TPU v7x, 32 devices: a whole 2x2x4 slice. The times are simulated.
32 devices in a mesh: ctx: 8 (over z, core), fsdp: 4 (over y, x).
Axes of the slice: x: 2, y: 2, z: 4, core: 2. Of those that a mesh axis runs over, the one named last changes fastest.
Arguments:
- hidden_in: bfloat16 [4, 2048, 2048], P('fsdp', 'ctx'), may hold values from -6 to 6
- weight_query: bfloat16 [2048, 2048], P('fsdp'), may hold values from -0.125 to 0.125
- key_weight_matrix: bfloat16 [2048, 1024], P('fsdp'), may hold values from -0.125 to 0.125
- weight_value: bfloat16 [2048, 1024], P('fsdp'), may hold values from -0.125 to 0.125
- weight_out: bfloat16 [2048, 2048], P(None, 'fsdp'), may hold values from -0.5 to 0.5
- weight_gate: bfloat16 [2048, 6144], P('fsdp'), may hold values from -0.125 to 0.125
- weight_up: bfloat16 [2048, 6144], P('fsdp'), may hold values from -0.125 to 0.125
- weight_down: bfloat16 [6144, 2048], P(None, 'fsdp'), may hold values from -0.078125 to 0.078125
- gain_attention: bfloat16 [2048], P('fsdp'), may hold values from 0.5 to 1.5
- gain_feed: bfloat16 [2048], P('fsdp'), may hold values from 0.5 to 1.5
- gain_query: bfloat16 [128], P('fsdp'), may hold values from 0.25 to 1.75
- gain_key: bfloat16 [128], P('fsdp'), may hold values from 0.25 to 1.75
- positions: int32 [4, 2048], P('fsdp', 'ctx'), may hold values from 0 to 4095
- token_block_index: int32 [4, 2048], P('fsdp', 'ctx'), may hold values from 0 to 15, never falling along the last dimension, each value on 1 to 256 neighbouring positions
- grad_out: bfloat16 [4, 2048, 2048], P('fsdp', 'ctx'), may hold values from -6 to 6
Outputs:
- hidden_out: bfloat16 [4, 2048, 2048], P('fsdp', 'ctx')
- grad_hidden: float32 [4, 2048, 2048], P('fsdp', 'ctx')
- grad_weight_query: float32 [2048, 2048], P('fsdp')
- grad_weight_key: float32 [2048, 1024], P('fsdp')
- grad_weight_value: float32 [2048, 1024], P('fsdp')
- grad_weight_out: float32 [2048, 2048], P(None, 'fsdp')
- grad_weight_gate: float32 [2048, 6144], P('fsdp')
- grad_weight_up: float32 [2048, 6144], P('fsdp')
- grad_weight_down: float32 [6144, 2048], P(None, 'fsdp')
- grad_gain_attention: float32 [2048], P('fsdp')
- grad_gain_feed: float32 [2048], P('fsdp')
- grad_gain_query: float32 [128], P('fsdp')
- grad_gain_key: float32 [128], P('fsdp')
Inputs may be any that keep to these rules, and one draw needn't show every extreme that they name: `token_block_index`: within each sequence the block ids never fall; each block holds 1 to 256 consecutive tokens and one holds exactly 256.
All inputs are finite; a program needn't handle non-finite values.
Results may differ from a plain program's by a relative error of at most 0.025.
Values may be sent and summed in bfloat16 or wider, within the bound.
A program may use at most 640 MiB of HBM per device.

v0:
```python
import jax
import jax.numpy as jnp
from jax import lax
from jax.sharding import PartitionSpec as P

D = 2048
QUERY_HEADS = 16
KEY_VALUE_HEADS = 8
HEAD_SIZE = 128
FF = 6144


EPS = 1e-06
THETA = 1000000.0
NEGATIVE_LARGE = -1e30


def from_behind(shard, axis, by):
    peers = lax.axis_size(axis)
    return lax.ppermute(shard, axis, [(i, (i + by) % peers) for i in range(peers)])


def tdot(left, right):
    return lax.dot_general(
        left, right, (((0,), (0,)), ((), ())), preferred_element_type=jnp.float32
    )


def rdot(left, right):
    return lax.dot_general(
        left, right, (((1,), (1,)), ((), ())), preferred_element_type=jnp.float32
    )


def tables(positions):
    half = HEAD_SIZE // 2
    freq = THETA ** (-(jnp.arange(half).astype(jnp.float32) * 2.0 / HEAD_SIZE))
    angle = positions.astype(jnp.float32)[..., None] * freq
    return (jnp.cos(angle), jnp.sin(angle))


def rotary(value, cosine_table, sine_table):
    half = value.shape[-1] // 2
    first = value[..., :half]
    second = value[..., half:]
    return jnp.concatenate(
        [first * cosine_table - second * sine_table, second * cosine_table + first * sine_table],
        axis=-1,
    )


def reverse_rotation(grad, cosine_table, sine_table):
    half = grad.shape[-1] // 2
    first = grad[..., :half]
    second = grad[..., half:]
    return jnp.concatenate(
        [first * cosine_table + second * sine_table, second * cosine_table - first * sine_table],
        axis=-1,
    )


def rms_forward(value, gain):
    inverse = lax.rsqrt(jnp.mean(value * value, axis=-1, keepdims=True) + EPS)
    return (value * inverse * gain, inverse)


def rms_backward(value, inverse, gain, grad):
    scaled = grad * gain
    inner = jnp.mean(scaled * value, axis=-1, keepdims=True)
    return (inverse * scaled - value * inverse * inverse * inverse * inner, grad * value * inverse)


def local(
    hidden_in,
    weight_query,
    key_weight_matrix,
    weight_value,
    weight_out,
    weight_gate,
    weight_up,
    weight_down,
    gain_attention,
    gain_feed,
    gain_query,
    gain_key,
    positions,
    token_block_index,
    grad_out,
):
    gathered = (
        lax.all_gather(weight_query, "fsdp", axis=0, tiled=True),
        lax.all_gather(key_weight_matrix, "fsdp", axis=0, tiled=True),
        lax.all_gather(weight_value, "fsdp", axis=0, tiled=True),
        lax.all_gather(weight_out, "fsdp", axis=1, tiled=True),
        lax.all_gather(weight_gate, "fsdp", axis=0, tiled=True),
        lax.all_gather(weight_up, "fsdp", axis=0, tiled=True),
        lax.all_gather(weight_down, "fsdp", axis=1, tiled=True),
        lax.all_gather(gain_attention, "fsdp", axis=0, tiled=True),
        lax.all_gather(gain_feed, "fsdp", axis=0, tiled=True),
        lax.all_gather(gain_query, "fsdp", axis=0, tiled=True),
        lax.all_gather(gain_key, "fsdp", axis=0, tiled=True),
    )
    full_query, full_key, full_value, full_out, full_gate, full_up, full_down = gathered[:7]
    norm_attention = gathered[7].astype(jnp.float32)
    norm_feed = gathered[8].astype(jnp.float32)
    norm_query = gathered[9].astype(jnp.float32)
    norm_key = gathered[10].astype(jnp.float32)
    residual = hidden_in.reshape(-1, D).astype(jnp.float32)
    local_row_count = residual.shape[0]
    query_group = QUERY_HEADS // KEY_VALUE_HEADS
    scale = HEAD_SIZE ** (-0.5)
    key_total_width = KEY_VALUE_HEADS * HEAD_SIZE
    cosine_table, sine_table = tables(positions.reshape(-1))
    cosine_table = cosine_table[:, None, :]
    sine_table = sine_table[:, None, :]
    query_ids = token_block_index.reshape(-1)
    key_ids = lax.all_gather(token_block_index, "ctx", axis=1, tiled=True).reshape(-1)
    normed, inverse_one = rms_forward(residual, norm_attention)
    normed_low = normed.astype(jnp.bfloat16)
    query_proj = jnp.dot(normed_low, full_query, preferred_element_type=jnp.float32).reshape(
        local_row_count, QUERY_HEADS, HEAD_SIZE
    )
    query_normed, inverse_query = rms_forward(query_proj, norm_query)
    query_matrix = (
        (rotary(query_normed, cosine_table, sine_table) * scale)
        .astype(jnp.bfloat16)
        .reshape(local_row_count, KEY_VALUE_HEADS, query_group, HEAD_SIZE)
    )
    key_projected = jnp.dot(normed_low, full_key, preferred_element_type=jnp.float32).reshape(
        local_row_count, KEY_VALUE_HEADS, HEAD_SIZE
    )
    key_normed, inverse_key = rms_forward(key_projected, norm_key)
    key_row_values = (
        rotary(key_normed, cosine_table, sine_table)
        .astype(jnp.bfloat16)
        .reshape(local_row_count, key_total_width)
    )
    value_row_values = jnp.dot(normed_low, full_value, preferred_element_type=jnp.float32).astype(
        jnp.bfloat16
    )
    portion_keys = lax.all_gather(key_row_values, "ctx", axis=0, tiled=True)
    portion_values = lax.all_gather(value_row_values, "ctx", axis=0, tiled=True)
    token_count = portion_keys.shape[0]
    piece_ids = key_ids
    previous_maximum = jnp.full(
        (local_row_count, KEY_VALUE_HEADS, query_group), NEGATIVE_LARGE, jnp.float32
    )
    scores = jnp.einsum(
        "qgrd,kgd->qgrk",
        query_matrix,
        portion_keys.reshape(token_count, KEY_VALUE_HEADS, HEAD_SIZE),
        preferred_element_type=jnp.float32,
    )
    allowed = (piece_ids[None, :] <= query_ids[:, None])[:, None, None, :]
    masked = jnp.where(allowed, scores, NEGATIVE_LARGE)
    new_max = jnp.maximum(previous_maximum, jnp.max(masked, axis=-1))
    weights = jnp.where(allowed, jnp.exp(masked - new_max[..., None]), 0.0)
    new_sum = jnp.sum(weights, axis=-1)
    new_acc = jnp.einsum(
        "qgrk,kgd->qgrd",
        weights.astype(jnp.bfloat16),
        portion_values.reshape(token_count, KEY_VALUE_HEADS, HEAD_SIZE),
        preferred_element_type=jnp.float32,
    )
    log_total = new_max + jnp.log(new_sum)
    context = (
        (new_acc / new_sum[..., None])
        .reshape(local_row_count, QUERY_HEADS * HEAD_SIZE)
        .astype(jnp.bfloat16)
    )
    middle = residual + jnp.dot(context, full_out, preferred_element_type=jnp.float32)
    normed_two, inverse_two = rms_forward(middle, norm_feed)
    normed_two_low = normed_two.astype(jnp.bfloat16)
    gate_proj = jnp.dot(normed_two_low, full_gate, preferred_element_type=jnp.float32)
    up_proj = jnp.dot(normed_two_low, full_up, preferred_element_type=jnp.float32)
    sigma = jax.nn.sigmoid(gate_proj)
    activation = (gate_proj * sigma * up_proj).astype(jnp.bfloat16)
    hidden_out = (
        middle + jnp.dot(activation, full_down, preferred_element_type=jnp.float32)
    ).astype(jnp.bfloat16)
    grad_low = grad_out.reshape(local_row_count, D)
    grad_act = rdot(grad_low, full_down)
    grad_gate = (grad_act * up_proj * sigma * (1.0 + gate_proj * (1.0 - sigma))).astype(
        jnp.bfloat16
    )
    grad_upward = (grad_act * gate_proj * sigma).astype(jnp.bfloat16)
    fsdp_count = lax.axis_size("fsdp")
    shard_rows = D // fsdp_count
    select = lambda array: array
    picked = select(normed_two_low)
    feed_shard = lax.psum_scatter(
        jnp.concatenate(
            [
                tdot(picked, grad_gate),
                tdot(picked, grad_upward),
                tdot(select(grad_low), activation),
            ],
            axis=1,
        ).astype(jnp.bfloat16),
        "fsdp",
        scatter_dimension=0,
        tiled=True,
    ).astype(jnp.float32)
    grad_normed_two = rdot(grad_gate, full_gate) + rdot(grad_upward, full_up)
    back_two, gain_two_terms = rms_backward(middle, inverse_two, norm_feed, grad_normed_two)
    grad_middle = grad_low.astype(jnp.float32) + back_two
    grad_attention = grad_middle.astype(jnp.bfloat16)
    context_gradient = rdot(grad_attention, full_out).astype(jnp.bfloat16)
    context_head_gradient = context_gradient.reshape(
        local_row_count, KEY_VALUE_HEADS, query_group, HEAD_SIZE
    )
    delta = jnp.sum(
        (context_gradient.astype(jnp.float32) * context.astype(jnp.float32)).reshape(
            local_row_count, KEY_VALUE_HEADS, query_group, HEAD_SIZE
        ),
        axis=-1,
    )
    own_index = lax.axis_index("ctx")
    cycle_size = lax.axis_size("ctx")

    def cycle_step(step_index, state):
        rotating_keys, rotating_values, key_gradient, grad_values, grad_queries = state
        source = (own_index - step_index) % cycle_size
        piece_ids = lax.dynamic_slice_in_dim(key_ids, source * local_row_count, local_row_count)
        acc_keys = key_gradient
        acc_values = grad_values
        acc_queries = grad_queries
        key_head_rows = rotating_keys.reshape(local_row_count, KEY_VALUE_HEADS, HEAD_SIZE)
        value_head_rows = rotating_values.reshape(local_row_count, KEY_VALUE_HEADS, HEAD_SIZE)
        scores = jnp.einsum(
            "qgrd,kgd->qgrk", query_matrix, key_head_rows, preferred_element_type=jnp.float32
        )
        allowed = (piece_ids[None, :] <= query_ids[:, None])[:, None, None, :]
        probs = jnp.where(
            allowed, jnp.exp(jnp.where(allowed, scores, NEGATIVE_LARGE) - log_total[..., None]), 0.0
        )
        grad_probs = jnp.einsum(
            "qgrd,kgd->qgrk",
            context_head_gradient,
            value_head_rows,
            preferred_element_type=jnp.float32,
        )
        grad_scores = (probs * (grad_probs - delta[..., None])).astype(jnp.bfloat16)
        acc_values = acc_values + jnp.einsum(
            "qgrk,qgrd->kgd",
            probs.astype(jnp.bfloat16),
            context_head_gradient,
            preferred_element_type=jnp.float32,
        ).reshape(local_row_count, key_total_width)
        acc_keys = acc_keys + jnp.einsum(
            "qgrk,qgrd->kgd", grad_scores, query_matrix, preferred_element_type=jnp.float32
        ).reshape(local_row_count, key_total_width)
        acc_queries = acc_queries + jnp.einsum(
            "qgrk,kgd->qgrd", grad_scores, key_head_rows, preferred_element_type=jnp.float32
        )
        rotating_keys, rotating_values = from_behind((rotating_keys, rotating_values), "ctx", 1)
        key_gradient, grad_values = (
            from_behind(acc_keys.astype(jnp.bfloat16), "ctx", 1).astype(jnp.float32),
            from_behind(acc_values.astype(jnp.bfloat16), "ctx", 1).astype(jnp.float32),
        )
        return (rotating_keys, rotating_values, key_gradient, grad_values, acc_queries)

    cycle_start = (
        key_row_values,
        value_row_values,
        jnp.zeros((local_row_count, key_total_width), jnp.float32),
        jnp.zeros((local_row_count, key_total_width), jnp.float32),
        jnp.zeros((local_row_count, KEY_VALUE_HEADS, query_group, HEAD_SIZE), jnp.float32),
    )
    cycle_final = lax.fori_loop(0, cycle_size, cycle_step, cycle_start)
    key_gradient, grad_values, grad_queries = (cycle_final[2], cycle_final[3], cycle_final[4])
    query_back = reverse_rotation(
        grad_queries.reshape(local_row_count, QUERY_HEADS, HEAD_SIZE) * scale,
        cosine_table,
        sine_table,
    )
    back_query, query_gain_terms = rms_backward(query_proj, inverse_query, norm_query, query_back)
    grad_query_low = back_query.reshape(local_row_count, QUERY_HEADS * HEAD_SIZE).astype(
        jnp.bfloat16
    )
    key_backward = reverse_rotation(
        key_gradient.reshape(local_row_count, KEY_VALUE_HEADS, HEAD_SIZE), cosine_table, sine_table
    )
    back_key, key_gain_terms = rms_backward(key_projected, inverse_key, norm_key, key_backward)
    grad_key_low = back_key.reshape(local_row_count, key_total_width).astype(jnp.bfloat16)
    grad_value_low = grad_values.astype(jnp.bfloat16)
    grad_normed_one = (
        rdot(grad_query_low, full_query)
        + rdot(grad_key_low, full_key)
        + rdot(grad_value_low, full_value)
    )
    back_one, gain_one_terms = rms_backward(residual, inverse_one, norm_attention, grad_normed_one)
    grad_hidden = (grad_middle + back_one).reshape(hidden_in.shape)
    select = lambda array: array
    picked = select(normed_low)
    attention_shard = lax.psum_scatter(
        jnp.concatenate(
            [
                tdot(picked, grad_query_low),
                tdot(picked, grad_key_low),
                tdot(picked, grad_value_low),
                tdot(select(grad_attention), context),
            ],
            axis=1,
        ).astype(jnp.bfloat16),
        "fsdp",
        scatter_dimension=0,
        tiled=True,
    ).astype(jnp.float32)
    attention_shard, feed_shard = (
        lax.psum(attention_shard.astype(jnp.bfloat16), "ctx").astype(jnp.float32),
        lax.psum(feed_shard.astype(jnp.bfloat16), "ctx").astype(jnp.float32),
    )
    gain_totals = lax.psum(
        (
            jnp.sum(gain_one_terms, axis=0),
            jnp.sum(gain_two_terms, axis=0),
            jnp.sum(query_gain_terms, axis=(0, 1)),
            jnp.sum(key_gain_terms, axis=(0, 1)),
        ),
        ("ctx", "fsdp"),
    )
    fsdp_index = lax.axis_index("fsdp")
    head_rows = HEAD_SIZE // fsdp_count
    query_width = QUERY_HEADS * HEAD_SIZE
    grad_gain_attention = lax.dynamic_slice_in_dim(
        gain_totals[0], fsdp_index * shard_rows, shard_rows
    )
    grad_gain_feed = lax.dynamic_slice_in_dim(gain_totals[1], fsdp_index * shard_rows, shard_rows)
    grad_gain_query = lax.dynamic_slice_in_dim(gain_totals[2], fsdp_index * head_rows, head_rows)
    grad_gain_key = lax.dynamic_slice_in_dim(gain_totals[3], fsdp_index * head_rows, head_rows)
    grad_weight_query = attention_shard[:, :query_width]
    grad_weight_key = attention_shard[:, query_width : query_width + key_total_width]
    grad_weight_value = attention_shard[
        :, query_width + key_total_width : query_width + 2 * key_total_width
    ]
    grad_weight_out = attention_shard[:, query_width + 2 * key_total_width :].T
    grad_weight_gate = feed_shard[:, :FF]
    grad_weight_up = feed_shard[:, FF : 2 * FF]
    grad_weight_down = feed_shard[:, 2 * FF :].T
    return (
        hidden_out.reshape(hidden_in.shape),
        grad_hidden,
        grad_weight_query,
        grad_weight_key,
        grad_weight_value,
        grad_weight_out,
        grad_weight_gate,
        grad_weight_up,
        grad_weight_down,
        grad_gain_attention,
        grad_gain_feed,
        grad_gain_query,
        grad_gain_key,
    )


def solution(mesh):
    return jax.shard_map(
        local,
        mesh=mesh,
        in_specs=(
            P("fsdp", "ctx", None),
            P("fsdp", None),
            P("fsdp", None),
            P("fsdp", None),
            P(None, "fsdp"),
            P("fsdp", None),
            P("fsdp", None),
            P(None, "fsdp"),
            P("fsdp"),
            P("fsdp"),
            P("fsdp"),
            P("fsdp"),
            P("fsdp", "ctx"),
            P("fsdp", "ctx"),
            P("fsdp", "ctx", None),
        ),
        out_specs=(
            P("fsdp", "ctx", None),
            P("fsdp", "ctx", None),
            P("fsdp", None),
            P("fsdp", None),
            P("fsdp", None),
            P(None, "fsdp"),
            P("fsdp", None),
            P("fsdp", None),
            P(None, "fsdp"),
            P("fsdp"),
            P("fsdp"),
            P("fsdp"),
            P("fsdp"),
        ),
        check_vma=False,
    )
```

profile of v0, /device:TPU:0, one launch (start us, length us, event | category | flops | bytes accessed | tf_op | source)
XLA Modules:
  0.0 2910.3 jit_solution(13086285690502229014)
XLA Ops:
  9.5 9.5 all-gather
  19.3 46.0 %all-gather.12.cloned.1.call-done = bf16[2048,1024]{1,0:T(8,128)(2,1)} async-done(((bf16[512,1024]{1,0:T(8,128)(2,1)}), bf16[2048,1024]{1,0:T(8,128)(2,1)}) %all-gather.12.cloned.1.call-update) | async-done | bytes 4194320 | tf_op jit(solution)/shard_map/all_gather | solution.py:93
  71.5 9.0 all-reduce.5
  80.9 39.0 %all-gather.16.cloned.1.call-done = bf16[2048,1024]{1,0:T(8,128)(2,1)} async-done(((bf16[512,1024]{1,0:T(8,128)(2,1)}), bf16[2048,1024]{1,0:T(8,128)(2,1)}) %all-gather.16.cloned.1.call-update) | async-done | bytes 4194320 | tf_op jit(solution)/shard_map/all_gather | solution.py:92
  119.9 6.4 copy.85
  135.3 7.8 all-gather.1
  143.1 11.9 all_gather.45
  156.6 52.9 %all-gather.20.cloned.1.call-done = bf16[2048,2048]{1,0:T(8,128)(2,1)} async-done(((bf16[512,2048]{1,0:T(8,128)(2,1)}), bf16[2048,2048]{1,0:T(8,128)(2,1)}) %all-gather.20.cloned.1.call-update) | async-done | bytes 8388624 | tf_op jit(solution)/shard_map/all_gather | solution.py:91
  209.5 12.3 copy.86
  221.7 5.9 multiply_reduce_fusion.5
  238.7 19.4 all-gather.14.cloned.1.call-done
  258.1 6.4 copy.117
  264.5 42.1 %all-gather.18.cloned.1.call-done = bf16[2048,1024]{0,1:T(8,128)(2,1)} async-done(((bf16[256,1024]{0,1:T(8,128)(2,1)}), bf16[2048,1024]{0,1:T(8,128)(2,1)}) %all-gather.18.cloned.1.call-update) | async-done | bytes 4194320 | tf_op jit(solution)/shard_map/all_gather | solution.py:141
  306.7 17.4 fusion.20
  324.1 14.3 fusion.21
  338.4 15.9 fusion.48
  355.7 38.3 %all-gather.22.cloned.1.call-done = bf16[2048,2048]{1,0:T(8,128)(2,1)} async-done(((bf16[2048,512]{1,0:T(8,128)(2,1)}), bf16[2048,2048]{1,0:T(8,128)(2,1)}) %all-gather.22.cloned.1.call-update) | async-done | bytes 8388624 | tf_op jit(solution)/shard_map/all_gather | solution.py:94
  394.1 6.2 multiply_reduce_fusion.4
  400.5 223.1 %all-gather.26.cloned.1.call-done = bf16[2048,6144]{1,0:T(8,128)(2,1)} async-done(((bf16[512,6144]{1,0:T(8,128)(2,1)}), bf16[2048,6144]{1,0:T(8,128)(2,1)}) %all-gather.26.cloned.1.call-update) | async-done | bytes 25165840 | tf_op jit(solution)/shard_map/all_gather | solution.py:96
  623.7 15.5 fusion.76
  639.2 214.1 %all-gather.24.cloned.1.call-done = bf16[2048,6144]{1,0:T(8,128)(2,1)} async-done(((bf16[512,6144]{1,0:T(8,128)(2,1)}), bf16[2048,6144]{1,0:T(8,128)(2,1)}) %all-gather.24.cloned.1.call-update) | async-done | bytes 25165840 | tf_op jit(solution)/shard_map/all_gather | solution.py:95
  853.3 15.5 fusion.75
  868.8 214.0 %all-gather.28.cloned.1.call-done = bf16[6144,2048]{1,0:T(8,128)(2,1)} async-done(((bf16[6144,512]{1,0:T(8,128)(2,1)}), bf16[6144,2048]{1,0:T(8,128)(2,1)}) %all-gather.28.cloned.1.call-update) | async-done | bytes 25165840 | tf_op jit(solution)/shard_map/all_gather | solution.py:97
  1082.8 20.8 multiply_convert_fusion
  1103.6 13.5 fusion.77
  1117.0 15.0 multiply_reduce_fusion.1
  1134.6 5.8 convolution_convert_fusion.2
  1146.5 5.0 reduce_sum.132
  1155.4 282.7 %while.24 = (s32[]{:T(128)}, bf16[256,1024]{1,0:T(8,128)(2,1)}, bf16[256,1024]{1,0:T(8,128)(2,1)}, f32[256,1024]{0,1:T(8,128)}, f32[256,1024]{0,1:T(8,128)S(1)},...) while((s32[]{:T(128)}, bf16[256,1024]{1,0:T(8,128)(2,1)}, ...), condition=%wide.region_9.10_spmd.clone, body=%wide.region_8.9_spmd.clone.sunk | while | flops 1355874304 | bytes 62640716 | solution.py:270
  1185.3 5.6 collective-permute-done.1
  1220.6 5.6 collective-permute-done.1
  1244.9 5.4 collective-permute-done.2
  1255.9 5.6 collective-permute-done.1
  1280.2 5.4 collective-permute-done.2
  1291.2 5.6 collective-permute-done.1
  1315.5 5.4 collective-permute-done.2
  1326.6 5.6 collective-permute-done.1
  1350.8 5.4 collective-permute-done.2
  1361.9 5.6 collective-permute-done.1
  1386.1 5.4 collective-permute-done.2
  1397.2 5.6 collective-permute-done.1
  1421.4 5.4 collective-permute-done.2
  1432.5 5.6 collective-permute-done.1
  1457.2 5.9 convolution_convert_fusion.3
  1463.1 18.0 pad_maximum_fusion.1
  1481.1 14.4 convert_bitcast_fusion
  1495.5 14.1 convolution_convert_fusion
  1509.6 14.1 convolution_convert_fusion.1
  1523.7 52.2 %pad_maximum_fusion = bf16[2048,18432]{1,0:T(8,128)(2,1)} fusion(bf16[2048,6144]{1,0:T(8,128)(2,1)} %convert_bitcast_fusion, bf16[2048,6144]{1,0:T(8,128)(2,1)} %convolution_convert_fusion, bf16[2048,6144]{1,0:T(8,128)(2,1)} %convolution_convert_fusion.1), kind=kLoop, calls=%fused_computation.25 | loop fusion | flops 226492416 | bytes 150994944 | tf_op jit(solution)/shard_map/concatenate | solution.py:192
  1576.2 124.1 %reduce-scatter.5.cloned.1.call-done = bf16[512,6144]{0,1:T(8,128)(2,1)} async-done(((bf16[2048,6144]{0,1:T(8,128)(2,1)}), bf16[512,6144]{0,1:T(8,128)(2,1)}) %reduce-scatter.5.cloned.1.call-update) | async-done | bytes 6291472 | tf_op jit(solution)/shard_map/reduce_scatter | solution.py:296
  1700.3 629.3 %reduce-scatter.7.cloned.1.call-done = bf16[512,18432]{1,0:T(8,128)(2,1)} async-done(((bf16[2048,18432]{1,0:T(8,128)(2,1)}), bf16[512,18432]{1,0:T(8,128)(2,1)}) %reduce-scatter.7.cloned.1.call-update) | async-done | bytes 18874384
  2329.7 6.2 fusion.78
  2342.0 40.7 %all-reduce.3 = (f32[2048]{0:T(1024)S(1)}, f32[2048]{0:T(1024)S(1)}, f32[128]{0:T(128)S(1)}, f32[128]{0:T(128)S(1)}) all-reduce(f32[2048]{0:T(1024)S(1)} %get-tuple-element.451, f32[2048]{0:T(1024)S(1)} %copy-done.41, f32[128]{0:T(128)S(1)} %get-tuple-element.447, ...), channel_id=1, replica_groups=mesh['ctx'=8,'fsdp'=4] {'ctx','fsdp'}, use_global_device_ids=true, to_apply=%region_18.19 | all-reduce | flops 4352 | bytes 34816 | tf_op jit(solution)/shard_map/psum | solution.py:314
  2385.2 4.5 fusion.40
  2389.6 13.0 fusion.34
  2402.7 421.8 %all-reduce.8.cloned.1.call-done = (bf16[512,6144]{0,1:T(8,128)(2,1)}, bf16[512,18432]{1,0:T(8,128)(2,1)}) async-done(((bf16[512,6144]{0,1:T(8,128)(2,1)}, bf16[512,18432]{1,0:T(8,128)(2,1)}), (bf16[512,6144]{0,1:T(8,128)(2,1)}, bf16[512,18432]{1,0:T(8,128)(2,1)})) %all-reduce.8.cloned.1.call-update) | async-done | bytes 25165840 | tf_op jit(solution)/shard_map/psum | solution.py:311
  2824.4 4.5 slice.68
  2833.2 9.5 convert_element_type.226
  2842.8 9.6 fusion.72
  2852.3 13.0 convert_element_type.227
  2865.3 5.3 copy.99
  2875.5 4.6 slice_bitcast_fusion.1
  2880.1 10.6 slice_bitcast_fusion
  2890.7 12.6 copy.102
  (423 shorter events, 284.5 us)
Async XLA Ops:
  7.2 11.8 copy-start.4
  7.2 58.1 %all-gather.12.cloned.1.call-start = ((), (), s32[]{:S(2)}) async-start(), calls=%async_computation.2 | async-start | bytes 5242880 | tf_op jit(solution)/shard_map/all_gather | solution.py:93
  7.9 112.0 %all-gather.16.cloned.1.call-start = ((), (), s32[]{:S(2)}) async-start(), calls=%async_computation.4 | async-start | bytes 5242880 | tf_op jit(solution)/shard_map/all_gather | solution.py:92
  8.7 200.8 %all-gather.20.cloned.1.call-start = ((), (), s32[]{:S(2)}) async-start(), calls=%async_computation.6 | async-start | bytes 10485760 | tf_op jit(solution)/shard_map/all_gather | solution.py:91
  9.4 248.7 %all-gather.14.cloned.1.call-start = ((), (), s32[]{:S(2)}) async-start(), calls=%async_computation.3 | async-start | bytes 4718592 | tf_op jit(solution)/shard_map/all_gather | solution.py:142
  19.0 202.7 %copy-start.30 = (f32[4,1,512]{2,1,0:T(1,128)}, f32[4,1,512]{2,1,0:T(1,128)S(1)}, u32[]{:S(2)}) copy-start(f32[4,1,512]{2,1,0:T(1,128)S(1)} %convert_element_type.229) | copy-start | bytes 24580
  19.3 202.4 %copy-start.36 = (f32[256]{0:T(256)}, f32[256]{0:T(256)S(1)}, u32[]{:S(2)}) copy-start(f32[256]{0:T(256)S(1)} %add_rsqrt_fusion.3) | copy-start | bytes 3076
  65.3 15.2 copy-start.48
  69.7 237.0 %all-gather.18.cloned.1.call-start = ((), (), s32[]{:S(2)}) async-start(), calls=%async_computation.5 | async-start | bytes 4718592 | tf_op jit(solution)/shard_map/all_gather | solution.py:141
  80.5 49.6 %copy-start.42 = (f32[128]{0:T(128)}, f32[128]{0:T(128)S(1)}, u32[]{:S(2)}) copy-start(f32[128]{0:T(128)S(1)} %convert_element_type.200) | copy-start | bytes 1540
  80.9 147.2 %copy-start.24 = (f32[256,64]{0,1:T(8,128)}, f32[256,64]{0,1:T(8,128)S(1)}, u32[]{:S(2)}) copy-start(f32[256,64]{0,1:T(8,128)S(1)} %get-tuple-element.504) | copy-start | bytes 196612
  80.9 147.2 %copy-start.26 = (f32[256,64]{0,1:T(8,128)}, f32[256,64]{0,1:T(8,128)S(1)}, u32[]{:S(2)}) copy-start(f32[256,64]{0,1:T(8,128)S(1)} %get-tuple-element.505) | copy-start | bytes 196612
  132.3 261.8 %all-gather.22.cloned.1.call-start = ((), (), s32[]{:S(2)}) async-start(), calls=%async_computation.7 | async-start | bytes 10485760 | tf_op jit(solution)/shard_map/all_gather | solution.py:94
  132.9 490.8 %all-gather.26.cloned.1.call-start = ((), (), s32[]{:S(2)}) async-start(), calls=%async_computation.9 | async-start | bytes 31457280 | tf_op jit(solution)/shard_map/all_gather | solution.py:96
  133.6 719.7 %all-gather.24.cloned.1.call-start = ((), (), s32[]{:S(2)}) async-start(), calls=%async_computation.8 | async-start | bytes 31457280 | tf_op jit(solution)/shard_map/all_gather | solution.py:95
  134.4 21.1 copy-start.20
  134.4 948.3 %all-gather.28.cloned.1.call-start = ((), (), s32[]{:S(2)}) async-start(), calls=%async_computation.10 | async-start | bytes 31457280 | tf_op jit(solution)/shard_map/all_gather | solution.py:97
  135.2 1565.1 %reduce-scatter.5.cloned.1.call-start = ((), (), s32[]{:S(2)}) async-start(), calls=%async_computation.11 | async-start | bytes 31457280 | tf_op jit(solution)/shard_map/reduce_scatter | solution.py:296
  135.3 92.4 %copy-start.44 = (f32[128]{0:T(128)}, f32[128]{0:T(128)S(1)}, u32[]{:S(2)}) copy-start(f32[128]{0:T(128)S(1)} %convert_element_type.205) | copy-start | bytes 1540
  155.1 66.7 %copy-start.38 = (s32[1,2048]{1,0:T(1,128)}, s32[1,2048]{1,0:T(1,128)S(1)}, u32[]{:S(2)}) copy-start(s32[1,2048]{1,0:T(1,128)S(1)} %all_gather.45) | copy-start | bytes 24580
  400.2 731.8 %copy-start.8 = (f32[256,2048]{1,0:T(8,128)}, f32[256,2048]{1,0:T(8,128)S(1)}, u32[]{:S(2)}) copy-start(f32[256,2048]{1,0:T(8,128)S(1)} %get-tuple-element.513) | copy-start | bytes 6291460
  400.5 452.8 %copy-start.15 = (bf16[256,2048]{1,0:T(8,128)(2,1)}, bf16[256,2048]{1,0:T(8,128)(2,1)S(1)}, u32[]{:S(2)}) copy-start(bf16[256,2048]{1,0:T(8,128)(2,1)S(1)} %multiply_convert_fusion.3) | copy-start | bytes 3145732
  1117.0 15.0 copy-start.21
  1155.3 282.8 %copy-start.25 = (f32[256,64]{0,1:T(8,128)S(1)}, f32[256,64]{0,1:T(8,128)}, u32[]{:S(2)}) copy-start(f32[256,64]{0,1:T(8,128)} %copy-done.24) | copy-start | bytes 196612
  1155.3 282.8 %copy-start.27 = (f32[256,64]{0,1:T(8,128)S(1)}, f32[256,64]{0,1:T(8,128)}, u32[]{:S(2)}) copy-start(f32[256,64]{0,1:T(8,128)} %copy-done.26) | copy-start | bytes 196612
  1155.4 284.3 %copy-start.35 = (f32[256,8]{0,1:T(8,128)S(1)}, f32[256,8]{0,1:T(8,128)}, u32[]{:S(2)}) copy-start(f32[256,8]{0,1:T(8,128)} %copy-done.34) | copy-start | bytes 24580
  1155.4 284.3 %copy-start.43 = (f32[128]{0:T(128)S(1)}, f32[128]{0:T(128)}, u32[]{:S(2)}) copy-start(f32[128]{0:T(128)} %copy-done.42) | copy-start | bytes 1540
  1162.4 13.0 collective-permute-start.3
  1169.0 10.7 collective-permute-start.2
  1170.6 14.7 collective-permute-start
  1170.6 20.4 collective-permute-start.1
  1197.7 11.9 collective-permute-start.3
  1204.3 10.7 collective-permute-start.2
  1204.3 16.3 collective-permute-start
  1204.3 21.9 collective-permute-start.1
  1233.0 10.7 collective-permute-start.3
  1239.6 10.7 collective-permute-start.2
  1239.6 16.3 collective-permute-start
  1239.6 21.9 collective-permute-start.1
  1268.3 10.7 collective-permute-start.3
  1274.9 10.7 collective-permute-start.2
  1274.9 16.3 collective-permute-start
  1274.9 21.9 collective-permute-start.1
  1303.6 10.7 collective-permute-start.3
  1310.2 10.7 collective-permute-start.2
  1310.2 16.3 collective-permute-start
  1310.2 21.9 collective-permute-start.1
  1339.0 10.7 collective-permute-start.3
  1345.5 10.7 collective-permute-start.2
  1345.5 16.3 collective-permute-start
  1345.5 21.9 collective-permute-start.1
  1374.3 10.7 collective-permute-start.3
  1380.8 10.7 collective-permute-start.2
  1380.8 16.3 collective-permute-start
  1380.8 21.9 collective-permute-start.1
  1409.6 10.7 collective-permute-start.3
  1416.1 10.7 collective-permute-start.2
  1416.1 16.3 collective-permute-start
  1416.2 21.9 collective-permute-start.1
  1481.1 848.6 %reduce-scatter.7.cloned.1.call-start = ((), (), s32[]{:S(2)}) async-start(), calls=%async_computation.12 | async-start | bytes 94371840
  1575.9 1248.5 %all-reduce.8.cloned.1.call-start = ((), (), s32[]{:S(2)}) async-start(), calls=%async_computation.13 | async-start | bytes 50331648 | tf_op jit(solution)/shard_map/psum | solution.py:311
  2824.4 18.3 slice-start
  2824.4 18.3 slice-start.1
  2828.9 13.8 slice-start.2
  (60 other events, 202.6 us)
Sparse Core Ops, SparseCore 0:
  9.9 55.3 all-gather.11
  67.2 52.6 all-gather.15
  121.7 87.6 all-gather.19
  210.9 47.1 all-gather.13
  260.1 46.5 all-gather.17
  308.3 85.6 all-gather.21
  395.9 227.7 all-gather.25
  625.5 227.7 all-gather.23
  855.1 227.5 all-gather.27
  1481.2 219.0 reduce-scatter.4
  1703.7 625.8 reduce-scatter.6
  2332.1 492.2 all-reduce.7
where the time goes:
time: 2920 us; the launch traced here: 2910 us
  waiting for transfers between devices  2180 us (75%)
  matrix products  284 us (10%)
  other arithmetic  176 us (6%)
  local copies, waits for them, and re-layouts  165 us (6%)
  blocking collectives  79 us (3%)
    unnamed x13, waiting for transfers between devices  634 us
    psum x1, waiting for transfers between devices, local(): lax.psum(attention_shard.astype(jnp.bfloat16), 'ctx').astype(jnp.float32)  422 us
    all_gather x1, waiting for transfers between devices, local(): lax.all_gather(weight_up, 'fsdp', axis=0, tiled=True)  223 us
    all_gather x1, waiting for transfers between devices, local(): lax.all_gather(weight_gate, 'fsdp', axis=0, tiled=True)  214 us
    all_gather x1, waiting for transfers between devices, local(): lax.all_gather(weight_down, 'fsdp', axis=1, tiled=True)  214 us
    reduce_scatter x1, waiting for transfers between devices, local(): lax.psum_scatter(jnp.concatenate([tdot(picked, grad_query_low), tdot(pick...  124 us
    ppermute x32, waiting for transfers between devices, from_behind(): lax.ppermute(shard, axis, [(i, (i + by) % peers) for i in range(peers)])  114 us
    dot_general x7, matrix products, rdot(): lax.dot_general(left, right, (((1,), (1,)), ((), ())), preferred_element_...  63.3 us
  transfers between devices with their start and end apart: 44, of which 42 were waited for; matrix products, arithmetic and copies ran while one was open for 13% of the time, Pallas kernels for 0%

commit v1 on v0

v1 whole, which is shorter than its diff:
```python
import jax
import jax.numpy as jnp
from jax import lax
from jax.sharding import PartitionSpec as P

D = 2048
QUERY_HEADS = 16
KEY_VALUE_HEADS = 8
HEAD_SIZE = 128
FF = 6144
EPS = 1e-06
THETA = 1000000.0
F32 = jnp.float32
BF16 = jnp.bfloat16


def dot(left, right):
    return jnp.dot(left, right, preferred_element_type=F32)


def tdot(left, right):
    return lax.dot_general(left, right, (((0,), (0,)), ((), ())), preferred_element_type=F32)


def rdot(left, right):
    return lax.dot_general(left, right, (((1,), (1,)), ((), ())), preferred_element_type=F32)


def tables(positions):
    half = HEAD_SIZE // 2
    freq = THETA ** (-(jnp.arange(half).astype(F32) * 2.0 / HEAD_SIZE))
    angle = positions.astype(F32)[..., None] * freq
    return jnp.cos(angle), jnp.sin(angle)


def rotary(value, cosine, sine):
    half = value.shape[-1] // 2
    first, second = value[..., :half], value[..., half:]
    return jnp.concatenate(
        [first * cosine - second * sine, second * cosine + first * sine], axis=-1
    )


def reverse_rotation(grad, cosine, sine):
    return rotary(grad, cosine, -sine)


def rms_forward(value, gain):
    inverse = lax.rsqrt(jnp.mean(value * value, axis=-1, keepdims=True) + EPS)
    return value * inverse * gain, inverse


def rms_backward(value, inverse, gain, grad):
    scaled = grad * gain
    inner = jnp.mean(scaled * value, axis=-1, keepdims=True)
    return inverse * scaled - value * inverse * inverse * inverse * inner, grad * value * inverse


def gather_ctx(piece):
    return lax.all_gather(piece, "ctx", axis=0, tiled=True)


def scatter_ctx(partial):
    return lax.psum_scatter(partial.astype(BF16), "ctx", scatter_dimension=0, tiled=True)


def own_columns(array, index, width):
    return lax.dynamic_slice_in_dim(array, index * width, width, axis=1)


def own_rows(array, index, width):
    return lax.dynamic_slice_in_dim(array, index * width, width, axis=0)


def local(
    hidden_in,
    weight_query,
    key_weight_matrix,
    weight_value,
    weight_out,
    weight_gate,
    weight_up,
    weight_down,
    gain_attention,
    gain_feed,
    gain_query,
    gain_key,
    positions,
    token_block_index,
    grad_out,
):
    parts = lax.axis_size("ctx")
    shards = lax.axis_size("fsdp")
    me = lax.axis_index("ctx")
    shard = lax.axis_index("fsdp")
    heads = QUERY_HEADS // parts
    sharers = parts // KEY_VALUE_HEADS
    key_head = me // sharers
    query_width = heads * HEAD_SIZE
    feed_width = FF // parts
    rows = D // shards
    scale = HEAD_SIZE ** (-0.5)

    def gather_rows(piece):
        return lax.all_gather(piece, "fsdp", axis=0, tiled=True)

    def gather_columns(piece):
        return lax.all_gather(piece, "fsdp", axis=1, tiled=True)

    gains = lax.all_gather(
        jnp.concatenate([gain_attention, gain_feed, gain_query, gain_key]), "fsdp", axis=0
    ).astype(F32)
    head_rows = HEAD_SIZE // shards
    norm_attention = gains[:, :rows].reshape(-1)
    norm_feed = gains[:, rows : 2 * rows].reshape(-1)
    norm_query = gains[:, 2 * rows : 2 * rows + head_rows].reshape(-1)
    norm_key = gains[:, 2 * rows + head_rows :].reshape(-1)

    qkv_weight = gather_rows(
        jnp.concatenate(
            [
                own_columns(weight_query, me, query_width),
                own_columns(key_weight_matrix, key_head, HEAD_SIZE),
                own_columns(weight_value, key_head, HEAD_SIZE),
            ],
            axis=1,
        )
    )
    out_weight = gather_columns(own_rows(weight_out, me, query_width))
    gate_weight = gather_rows(own_columns(weight_gate, me, feed_width))
    up_weight = gather_rows(own_columns(weight_up, me, feed_width))
    down_weight = gather_columns(own_rows(weight_down, me, feed_width))

    whole = lax.all_gather(jnp.stack([positions[0], token_block_index[0]]), "ctx", axis=1, tiled=True)
    cosine, sine = tables(whole[0])
    ids = whole[1]
    cosine = cosine[:, None, :]
    sine = sine[:, None, :]
    tokens = ids.shape[0]

    residual = hidden_in[0].astype(F32)
    normed, inverse_one = rms_forward(residual, norm_attention)
    normed_all = gather_ctx(normed.astype(BF16))
    grad_out_all = gather_ctx(grad_out[0])

    projected = dot(normed_all, qkv_weight)
    query_proj = projected[:, :query_width].reshape(tokens, heads, HEAD_SIZE)
    key_proj = projected[:, query_width : query_width + HEAD_SIZE].reshape(tokens, 1, HEAD_SIZE)
    values = projected[:, query_width + HEAD_SIZE :].astype(BF16)
    query_normed, inverse_query = rms_forward(query_proj, norm_query)
    queries = (rotary(query_normed, cosine, sine) * scale).astype(BF16)
    key_normed, inverse_key = rms_forward(key_proj, norm_key)
    keys = rotary(key_normed, cosine, sine).astype(BF16)[:, 0]

    allowed = (ids[None, :] <= ids[:, None])[:, None, :]
    scores = jnp.einsum("qrd,kd->qrk", queries, keys, preferred_element_type=F32)
    expon = jnp.where(allowed, jnp.exp(scores), 0.0)
    total = jnp.sum(expon, axis=-1)
    context = (
        jnp.einsum("qrk,kd->qrd", expon.astype(BF16), values, preferred_element_type=F32)
        / total[..., None]
    ).astype(BF16)

    middle = residual + scatter_ctx(dot(context.reshape(tokens, query_width), out_weight)).astype(F32)
    normed_two, inverse_two = rms_forward(middle, norm_feed)
    normed_two_all = gather_ctx(normed_two.astype(BF16))

    gate = dot(normed_two_all, gate_weight)
    up = dot(normed_two_all, up_weight)
    sigma = jax.nn.sigmoid(gate)
    activation = (gate * sigma * up).astype(BF16)
    grad_act = rdot(grad_out_all, down_weight)
    grad_gate = (grad_act * up * sigma * (1.0 + gate * (1.0 - sigma))).astype(BF16)
    grad_up = (grad_act * gate * sigma).astype(BF16)
    grad_normed_two = scatter_ctx(rdot(grad_gate, gate_weight) + rdot(grad_up, up_weight)).astype(F32)
    hidden_out = (middle + scatter_ctx(dot(activation, down_weight)).astype(F32)).astype(BF16)

    def sum_rows(grad):
        return lax.psum_scatter(grad.astype(BF16), "fsdp", scatter_dimension=0, tiled=True)

    feed_shard = sum_rows(
        jnp.concatenate(
            [
                tdot(normed_two_all, grad_gate),
                tdot(normed_two_all, grad_up),
                tdot(grad_out_all, activation),
            ],
            axis=1,
        )
    )
    feed_all = lax.all_gather(feed_shard, "ctx", axis=0)

    back_two, gain_two_terms = rms_backward(middle, inverse_two, norm_feed, grad_normed_two)
    grad_middle = grad_out[0].astype(F32) + back_two
    grad_attention_all = gather_ctx(grad_middle.astype(BF16))
    context_grad = rdot(grad_attention_all, out_weight).astype(BF16).reshape(tokens, heads, HEAD_SIZE)
    delta = jnp.sum(context_grad.astype(F32) * context.astype(F32), axis=-1)
    probs = expon / total[..., None]
    grad_probs = jnp.einsum("qrd,kd->qrk", context_grad, values, preferred_element_type=F32)
    grad_scores = (probs * (grad_probs - delta[..., None])).astype(BF16)
    grad_values = jnp.einsum(
        "qrk,qrd->kd", probs.astype(BF16), context_grad, preferred_element_type=F32
    )
    grad_keys = jnp.einsum("qrk,qrd->kd", grad_scores, queries, preferred_element_type=F32)
    grad_queries = jnp.einsum("qrk,kd->qrd", grad_scores, keys, preferred_element_type=F32)

    back_query, query_gain_terms = rms_backward(
        query_proj, inverse_query, norm_query, reverse_rotation(grad_queries * scale, cosine, sine)
    )
    back_key, key_gain_terms = rms_backward(
        key_proj, inverse_key, norm_key, reverse_rotation(grad_keys[:, None], cosine, sine)
    )
    grad_qkv = jnp.concatenate(
        [
            back_query.reshape(tokens, query_width).astype(BF16),
            back_key[:, 0].astype(BF16),
            grad_values.astype(BF16),
        ],
        axis=1,
    )
    grad_normed_one = scatter_ctx(rdot(grad_qkv, qkv_weight)).astype(F32)
    back_one, gain_one_terms = rms_backward(residual, inverse_one, norm_attention, grad_normed_one)
    grad_hidden = grad_middle + back_one

    attention_shard = sum_rows(
        jnp.concatenate(
            [
                tdot(normed_all, grad_qkv),
                tdot(grad_attention_all, context.reshape(tokens, query_width)),
            ],
            axis=1,
        )
    )
    attention_all = lax.all_gather(attention_shard, "ctx", axis=0)

    gain_totals = lax.psum(
        jnp.concatenate(
            [
                jnp.sum(gain_one_terms, axis=0),
                jnp.sum(gain_two_terms, axis=0),
                jnp.sum(query_gain_terms, axis=(0, 1)),
                jnp.sum(key_gain_terms, axis=(0, 1)),
            ]
        ),
        ("ctx", "fsdp"),
    )

    def columns(stacked):
        return stacked.astype(F32).transpose(1, 0, 2).reshape(rows, -1)

    def key_columns(stacked):
        summed = stacked.astype(F32).reshape(KEY_VALUE_HEADS, sharers, rows, HEAD_SIZE).sum(axis=1)
        return summed.transpose(1, 0, 2).reshape(rows, -1)

    def as_rows(stacked):
        return stacked.astype(F32).transpose(0, 2, 1).reshape(-1, rows)

    first, second = query_width, query_width + HEAD_SIZE
    third = second + HEAD_SIZE
    return (
        hidden_out[None],
        grad_hidden[None],
        columns(attention_all[:, :, :first]),
        key_columns(attention_all[:, :, first:second]),
        key_columns(attention_all[:, :, second:third]),
        as_rows(attention_all[:, :, third:]),
        columns(feed_all[:, :, :feed_width]),
        columns(feed_all[:, :, feed_width : 2 * feed_width]),
        as_rows(feed_all[:, :, 2 * feed_width :]),
        lax.dynamic_slice_in_dim(gain_totals, shard * rows, rows),
        lax.dynamic_slice_in_dim(gain_totals, D + shard * rows, rows),
        lax.dynamic_slice_in_dim(gain_totals, 2 * D + shard * head_rows, head_rows),
        lax.dynamic_slice_in_dim(gain_totals, 2 * D + HEAD_SIZE + shard * head_rows, head_rows),
    )


def solution(mesh):
    tokens = P("fsdp", "ctx", None)
    by_rows = P("fsdp", None)
    by_columns = P(None, "fsdp")
    per_token = P("fsdp", "ctx")
    vector = P("fsdp")
    weights = (by_rows, by_rows, by_rows, by_columns, by_rows, by_rows, by_columns)
    return jax.shard_map(
        local,
        mesh=mesh,
        in_specs=(tokens, *weights, vector, vector, vector, vector, per_token, per_token, tokens),
        out_specs=(tokens, tokens, *weights, vector, vector, vector, vector),
        check_vma=False,
    )
```

time: 2920 us -> 1560 us (0.53)
  waiting for transfers between devices: 2180 us -> 1010 us
  other arithmetic: 176 us -> 70.8 us
  matrix products: 284 us -> 231 us
    unnamed x13 -> x17, waiting for transfers between devices: 634 us -> 1.27 us
    psum x1 -> x0, waiting for transfers between devices: 422 us -> none  [local(): lax.psum(attention_shard.astype(jnp.bfloat16), 'ctx').astype(jnp.float32)]
    all_gather x9 -> x11, waiting for transfers between devices: 889 us -> 607 us  [the longest x4 321 us: gather_ctx(): return lax.all_gather(piece, 'ctx', axis=0, tiled=True)]
    reduce_scatter x1 -> x6, waiting for transfers between devices: 124 us -> 401 us  [the longest x4 314 us: scatter_ctx(): lax.psum_scatter(partial.astype(BF16), 'ctx', scatter_dimension=0, tiled=...]
    ppermute x32 -> x0, waiting for transfers between devices: 114 us -> none  [from_behind(): lax.ppermute(shard, axis, [(i, (i + by) % peers) for i in range(peers)])]
    convert_element_type x43 -> x5, other arithmetic: 67.8 us -> 7.62 us  [the longest x1 2.58 us: local(): normed_two_all = gather_ctx(normed_two.astype(BF16))]
    concatenate x3 -> x6, other arithmetic: 71 us -> 12.6 us  [the longest x2 5.5 us: rotary(): jnp.concatenate([first * cosine - second * sine, second * cosine + first...]
    reshape x2 -> x8, local copies, waits for them, and re-layouts: 9.18 us -> 60.6 us  [the longest x3 31.6 us: columns(): return stacked.astype(F32).transpose(1, 0, 2).reshape(rows, -1)]
  transfers between devices with their start and end apart: 44 -> 17, of which waited for: 42 -> 14; matrix products, arithmetic and copies ran while one was open for 13% -> 13% of each run, Pallas kernels for 0% -> 0%
where the time goes in v1:
time: 1560 us; the launch traced here: 1550 us
  waiting for transfers between devices  1010 us (65%)
  matrix products  231 us (15%)
  local copies, waits for them, and re-layouts  153 us (10%)
  other arithmetic  70.8 us (5%)
  blocking collectives  70.5 us (5%)
  between operations  15.9 us (1%)
    all_gather x4, waiting for transfers between devices, gather_ctx(): return lax.all_gather(piece, 'ctx', axis=0, tiled=True)  321 us
    reduce_scatter x4, waiting for transfers between devices, scatter_ctx(): lax.psum_scatter(partial.astype(BF16), 'ctx', scatter_dimension=0, tiled=...  314 us
    all_gather x1, waiting for transfers between devices, local(): feed_all = lax.all_gather(feed_shard, 'ctx', axis=0)  124 us
    reduce_scatter x2, waiting for transfers between devices, sum_rows(): lax.psum_scatter(grad.astype(BF16), 'fsdp', scatter_dimension=0, tiled=True)  87 us
    unnamed x143, local copies, waits for them, and re-layouts  74.7 us
    all_gather x3, waiting for transfers between devices, gather_rows(): return lax.all_gather(piece, 'fsdp', axis=0, tiled=True)  65.5 us
    all_gather x1, waiting for transfers between devices, local(): attention_all = lax.all_gather(attention_shard, 'ctx', axis=0)  59.1 us
    dot_general x5, matrix products, dot(): return jnp.dot(left, right, preferred_element_type=F32)  55.5 us
  transfers between devices with their start and end apart: 17, of which 14 were waited for; matrix products, arithmetic and copies ran while one was open for 13% of the time, Pallas kernels for 0%

profile of v1, /device:TPU:0, one launch (start us, length us, event | category | flops | bytes accessed | tf_op | source)
XLA Modules:
  0.0 1551.3 jit_solution(876755714289509284)
XLA Ops:
  12.7 2.8 concatenate.48
  15.7 17.5 %all-reduce = bf16[4352]{0:T(1024)(128)(2,1)S(1)} all-reduce(bf16[4352]{0:T(1024)(128)(2,1)S(1)} %dynamic-update-slice), channel_id=2, replica_groups=mesh['ctx'=8,'fsdp'=4] {'fsdp'}, use_global_device_ids=true, to_apply=%add | all-reduce | flops 4352 | bytes 17408
  37.3 13.1 all_gather.48
  50.4 4.1 broadcast_compare_fusion
  54.5 5.7 fusion.78
  60.2 73.0 %all-gather.16.cloned.1.call-done = bf16[2048,2048]{1,0:T(8,128)(2,1)} async-done(((bf16[256,2048]{1,0:T(8,128)(2,1)}), bf16[2048,2048]{1,0:T(8,128)(2,1)}) %all-gather.16.cloned.1.call-update) | async-done | bytes 8388624 | tf_op jit(solution)/shard_map/all_gather | solution.py:60
  133.2 7.6 fusion.94
  143.7 3.0 fusion.80
  153.0 16.6 %fusion.1 = (f32[2048,2]{0,1:T(2,128)S(1)}, f32[2048,2,2048]{0,2,1:T(8,128)}) fusion(pred[2048,2048]{0,1:T(8,128)(4,1)} %broadcast_compare_fusion, bf16[2048,2,128]{2,0,1:T(8,128)(2,1)S(1)} %fusion.55, bf16[2048,64]{0,1:T(8,128)(2,1)S(1)} %copy-done.25, bf16[2048,64]{0,1:T(8,128)(2,1)S(1)} %get-tuple-element.41), kind=kOutput, calls=%fused_computation.3 | convolution fusion | flops 2165305344 | bytes 39337984 | tf_op jit(solution)/shard_map/qrd,kd->qrk/dot_general | solution.py:156
  169.6 15.8 %divide_convert_fusion = bf16[2048,2,128]{0,2,1:T(8,128)(2,1)S(1)} fusion(f32[2048,2,2048]{0,2,1:T(8,128)} %get-tuple-element.57, pred[2048,2048]{0,1:T(8,128)(4,1)} %broadcast_compare_fusion, f32[2048,2]{0,1:T(2,128)S(1)} %get-tuple-element.56, f32[2048,512]{0,1:T(8,128)} %copy-done.4), kind=kOutput, calls=%fused_computation.100 | convolution fusion | flops 2165309440 | bytes 39337984 | tf_op jit(solution)/shard_map/qrk,kd->qrd/dot_general | solution.py:160
  185.5 7.4 convolution_convert_fusion.2
  197.8 83.3 %reduce-scatter.7.cloned.1.call-done = bf16[256,2048]{1,0:T(8,128)(2,1)} async-done(((bf16[2048,2048]{1,0:T(8,128)(2,1)}), bf16[256,2048]{1,0:T(8,128)(2,1)}) %reduce-scatter.7.cloned.1.call-update) | async-done | bytes 1048592 | tf_op jit(solution)/shard_map/reduce_scatter | solution.py:64
  282.7 2.6 multiply_convert_fusion.2
  287.5 38.0 %all-gather.28.cloned.1.call-done = bf16[768,2048]{1,0:T(8,128)(2,1)} async-done(((bf16[768,512]{1,0:T(8,128)(2,1)}), bf16[768,2048]{1,0:T(8,128)(2,1)}) %all-gather.28.cloned.1.call-update) | async-done | bytes 3145744 | tf_op jit(solution)/shard_map/all_gather | solution.py:108
  325.5 83.6 %all-gather.32.cloned.1.call-done = bf16[1,2048,2048]{2,1,0:T(8,128)(2,1)} async-done(((bf16[1,256,2048]{2,1,0:T(8,128)(2,1)}), bf16[1,2048,2048]{2,1,0:T(8,128)(2,1)}) %all-gather.32.cloned.1.call-update) | async-done | bytes 8388624 | tf_op jit(solution)/shard_map/all_gather | solution.py:60
  409.1 12.1 fusion.11
  421.2 32.8 %all-gather.26.cloned.1.call-done = bf16[2048,768]{1,0:T(8,128)(2,1)} async-done(((bf16[512,768]{1,0:T(8,128)(2,1)}), bf16[2048,768]{1,0:T(8,128)(2,1)}) %all-gather.26.cloned.1.call-update) | async-done | bytes 3145744 | tf_op jit(solution)/shard_map/all_gather | solution.py:105
  454.0 84.3 %all-gather.22.cloned.1.call-done = bf16[2048,2048]{1,0:T(8,128)(2,1)} async-done(((bf16[256,2048]{1,0:T(8,128)(2,1)}), bf16[2048,2048]{1,0:T(8,128)(2,1)}) %all-gather.22.cloned.1.call-update) | async-done | bytes 8388624 | tf_op jit(solution)/shard_map/all_gather | solution.py:60
  538.3 11.7 fusion.95
  550.0 32.7 %all-gather.24.cloned.1.call-done = bf16[2048,768]{1,0:T(8,128)(2,1)} async-done(((bf16[512,768]{1,0:T(8,128)(2,1)}), bf16[2048,768]{1,0:T(8,128)(2,1)}) %all-gather.24.cloned.1.call-update) | async-done | bytes 3145744 | tf_op jit(solution)/shard_map/all_gather | solution.py:105
  582.7 17.9 %fusion.18 = (bf16[2048,768]{1,0:T(8,128)(2,1)S(1)}, bf16[2048,768]{1,0:T(8,128)(2,1)S(1)}, bf16[2048,768]{1,0:T(8,128)(2,1)}) fusion(f32[768,2048]{0,1:T(8,128)} %fusion.11, f32[2048,768]{1,0:T(8,128)} %fusion.95, bf16[2048,2048]{1,0:T(8,128)(2,1)} %all-gather.22.cloned.1.call-done, bf16[2048,768]{1,0:T(8,128)(2,1)} %all-gather.24.cloned.1.call-done), kind=kOutput, calls=%fused_computation.29 | convolution fusion | flops 6467616768 | bytes 33554432 | tf_op jit(solution)/shard_map/dot_general | solution.py:18
  600.6 9.6 fusion.96
  610.2 12.5 add_convert_fusion
  622.8 89.7 %reduce-scatter.11.cloned.1.call-done = bf16[256,2048]{1,0:T(8,128)(2,1)} async-done(((bf16[2048,2048]{1,0:T(8,128)(2,1)}), bf16[256,2048]{1,0:T(8,128)(2,1)}) %reduce-scatter.11.cloned.1.call-update) | async-done | bytes 1048592 | tf_op jit(solution)/shard_map/reduce_scatter | solution.py:64
  712.5 2.6 fusion.46
  718.4 79.9 %all-gather.30.cloned.1.call-done = bf16[2048,2048]{1,0:T(8,128)(2,1)} async-done(((bf16[256,2048]{1,0:T(8,128)(2,1)}), bf16[2048,2048]{1,0:T(8,128)(2,1)}) %all-gather.30.cloned.1.call-update) | async-done | bytes 8388624 | tf_op jit(solution)/shard_map/all_gather | solution.py:60
  798.4 6.5 multiply_reduce_fusion.1
  804.8 16.0 %fusion.33 = bf16[2048,128]{0,1:T(8,128)(2,1)} fusion(bf16[2048,2,128]{0,2,1:T(8,128)(2,1)S(1)} %bitcast.233, f32[2048,2]{0,1:T(2,128)S(1)} %get-tuple-element.56, f32[2048,2,2048]{0,2,1:T(8,128)} %get-tuple-element.57, pred[2048,2048]{0,1:T(8,128)(4,1)} %broadcast_compare_fusion), kind=kOutput, calls=%fused_computation.63 | convolution fusion | flops 2172911616 | bytes 39337984 | tf_op jit(solution)/shard_map/qrk,qrd->kd/dot_general | solution.py:201
  820.8 19.9 %multiply_convert_fusion = bf16[2048,2,2048]{0,2,1:T(8,128)(2,1)} fusion(f32[2048,2]{0,1:T(2,128)S(1)} %get-tuple-element.58, bf16[2048,2,128]{0,2,1:T(8,128)(2,1)S(1)} %bitcast.234, f32[2048,2]{0,1:T(2,128)S(1)} %get-tuple-element.56, f32[2048,2,2048]{0,2,1:T(8,128)} %get-tuple-element.57, pred[2048,2048]{0,1:T(8,128)(4,1)} %broadcast_compare_fusion, ...), kind=kOutput, calls=%fused_computation | convolution fusion | flops 2189426688 | bytes 56131584 | tf_op jit(solution)/shard_map/qrd,kd->qrk/dot_general | solution.py:199
  840.7 11.5 convolution_bitcast_fusion
  852.3 8.4 convolution_multiply_fusion
  860.7 2.5 fusion.69
  870.8 2.7 fusion.54
  873.6 5.9 convolution_convert_fusion.6
  879.6 4.8 convolution_convert_fusion.5
  886.4 10.4 fusion.22
  896.9 9.5 convolution_convert_fusion.3
  906.4 7.5 convolution_convert_fusion.4
  914.0 4.4 pad_maximum_fusion
  918.4 8.6 convolution_convert_fusion
  928.9 10.9 convolution_convert_fusion.1
  940.6 87.0 %reduce-scatter.17.cloned.1.call-done = bf16[512,2304]{0,1:T(8,128)(2,1)} async-done(((bf16[2048,2304]{0,1:T(8,128)(2,1)}), bf16[512,2304]{0,1:T(8,128)(2,1)}) %reduce-scatter.17.cloned.1.call-update) | async-done | bytes 2359312 | tf_op jit(solution)/shard_map/reduce_scatter | solution.py:179
  1027.6 92.3 %reduce-scatter.13.cloned.1.call-done = bf16[256,2048]{1,0:T(8,128)(2,1)} async-done(((bf16[2048,2048]{1,0:T(8,128)(2,1)}), bf16[256,2048]{1,0:T(8,128)(2,1)}) %reduce-scatter.13.cloned.1.call-update) | async-done | bytes 1048592 | tf_op jit(solution)/shard_map/reduce_scatter | solution.py:64
  1121.9 39.9 %psum.7 = f32[4352]{0:T(1024)S(1)} all-reduce(f32[4352]{0:T(1024)S(1)} %pad_maximum_fusion.8), channel_id=1, replica_groups=mesh['ctx'=8,'fsdp'=4] {'ctx','fsdp'}, use_global_device_ids=true, to_apply=%region_21.22 | all-reduce | flops 4352 | bytes 34816 | tf_op jit(solution)/shard_map/psum | solution.py:236
  1163.0 48.7 %reduce-scatter.9.cloned.1.call-done = bf16[256,2048]{1,0:T(8,128)(2,1)} async-done(((bf16[2048,2048]{1,0:T(8,128)(2,1)}), bf16[256,2048]{1,0:T(8,128)(2,1)}) %reduce-scatter.9.cloned.1.call-update) | async-done | bytes 1048592 | tf_op jit(solution)/shard_map/reduce_scatter | solution.py:64
  1211.7 5.4 fusion.41
  1217.2 59.1 %all-gather.34.cloned.1.call-done = bf16[4096,768]{0,1:T(8,128)(2,1)} async-done(((bf16[512,768]{0,1:T(8,128)(2,1)}), bf16[4096,768]{0,1:T(8,128)(2,1)}) %all-gather.34.cloned.1.call-update) | async-done | bytes 6291472 | tf_op jit(solution)/shard_map/all_gather | solution.py:234
  1276.3 7.0 copy.88
  1287.3 3.5 copy.67
  1290.7 3.4 copy.97
  1294.1 2.4 copy.66
  1296.6 3.4 copy.98
  1300.0 4.8 convert_bitcast_fusion.3
  1304.8 4.4 copy.68
  1309.3 5.6 copy.65
  1314.8 6.2 copy.89
  1321.0 123.8 %all-gather.36.cloned.1.call-done = bf16[4096,2304]{0,1:T(8,128)(2,1)} async-done(((bf16[512,2304]{0,1:T(8,128)(2,1)}), bf16[4096,2304]{0,1:T(8,128)(2,1)}) %all-gather.36.cloned.1.call-update) | async-done | bytes 18874384 | tf_op jit(solution)/shard_map/all_gather | solution.py:191
  1444.8 13.5 copy.92
  1458.3 13.1 convert_bitcast_fusion
  1471.3 16.6 %copy.71 = f32[8,768,512]{2,1,0:T(8,128)} copy(f32[8,768,512]{2,0,1:T(8,128)} %get-tuple-element.21) | data formatting | bytes 25165824 | tf_op jit(solution)/shard_map/reshape | solution.py:256
  1488.0 13.0 copy.70
  1501.0 15.2 copy.94
  1516.2 13.0 copy.69
  1529.2 15.3 copy.93
  (222 shorter events, 49.4 us)
Async XLA Ops:
  7.2 26.1 %copy-start.2 = (bf16[1,256,2048]{2,1,0:T(8,128)(2,1)S(1)}, bf16[1,256,2048]{2,1,0:T(8,128)(2,1)}, u32[]{:S(2)}) copy-start(bf16[1,256,2048]{2,1,0:T(8,128)(2,1)} %param.15) | copy-start | bytes 3145732
  7.2 53.0 %all-gather.18.cloned.1.call-start = ((), (), s32[]{:S(2)}) async-start(), calls=%async_computation.7 | async-start | bytes 2621440 | tf_op jit(solution)/shard_map/all_gather | solution.py:105
  9.8 27.5 %copy-start.51 = (s32[1,256]{1,0:T(1,128)S(1)}, s32[1,256]{1,0:T(1,128)}, u32[]{:S(2)}) copy-start(s32[1,256]{1,0:T(1,128)} %param.28) | copy-start | bytes 3076
  9.8 27.5 %copy-start.52 = (s32[1,256]{1,0:T(1,128)S(1)}, s32[1,256]{1,0:T(1,128)}, u32[]{:S(2)}) copy-start(s32[1,256]{1,0:T(1,128)} %param.27) | copy-start | bytes 3076
  10.7 122.5 %all-gather.16.cloned.1.call-start = ((), (), s32[]{:S(2)}) async-start(), calls=%async_computation.6 | async-start | bytes 9437184 | tf_op jit(solution)/shard_map/all_gather | solution.py:60
  33.6 20.9 %copy-start.40 = (f32[256]{0:T(256)}, f32[256]{0:T(256)S(1)}, u32[]{:S(2)}) copy-start(f32[256]{0:T(256)S(1)} %add_rsqrt_fusion.3) | copy-start | bytes 3076
  35.2 150.2 %all-gather.20.cloned.1.call-start = ((), (), s32[]{:S(2)}) async-start(), calls=%async_computation.8 | async-start | bytes 1310720 | tf_op jit(solution)/shard_map/all_gather | solution.py:108
  37.0 244.1 %reduce-scatter.7.cloned.1.call-start = ((), (), s32[]{:S(2)}) async-start(), calls=%async_computation.9 | async-start | bytes 9437184 | tf_op jit(solution)/shard_map/reduce_scatter | solution.py:64
  37.0 106.7 %copy-start.48 = (f32[64]{0:T(128)}, f32[64]{0:T(128)S(1)}, u32[]{:S(2)}) copy-start(f32[64]{0:T(128)S(1)} %negate_power_fusion) | copy-start | bytes 772
  37.2 105.7 %copy-start.44 = (f32[128]{0:T(128)}, f32[128]{0:T(128)S(1)}, u32[]{:S(2)}) copy-start(f32[128]{0:T(128)S(1)} %mul.513) | copy-start | bytes 1540
  37.3 680.6 %copy-start.46 = (f32[128]{0:T(128)}, f32[128]{0:T(128)S(1)}, u32[]{:S(2)}) copy-start(f32[128]{0:T(128)S(1)} %mul.497) | copy-start | bytes 1540
  50.4 93.3 %copy-start.33 = (f32[1,2048]{1,0:T(1,128)}, f32[1,2048]{1,0:T(1,128)S(1)}, u32[]{:S(2)}) copy-start(f32[1,2048]{1,0:T(1,128)S(1)} %get-tuple-element.52) | copy-start | bytes 24580
  143.5 5.2 copy-start.29
  146.7 5.9 copy-start.23
  148.7 3.3 copy-start.9
  152.6 17.0 %copy-start.16 = (bf16[2048,2,128]{2,0,1:T(8,128)(2,1)}, bf16[2048,2,128]{2,0,1:T(8,128)(2,1)S(1)}, u32[]{:S(2)}) copy-start(bf16[2048,2,128]{2,0,1:T(8,128)(2,1)S(1)} %fusion.55) | copy-start | bytes 3145732
  185.4 7.4 copy-start.20
  192.9 132.7 %all-gather.28.cloned.1.call-start = ((), (), s32[]{:S(2)}) async-start(), calls=%async_computation.13 | async-start | bytes 3932160 | tf_op jit(solution)/shard_map/all_gather | solution.py:108
  195.0 214.1 %all-gather.32.cloned.1.call-start = ((), (), s32[]{:S(2)}) async-start(), calls=%async_computation.20 | async-start | bytes 9437184 | tf_op jit(solution)/shard_map/all_gather | solution.py:60
  195.6 258.4 %all-gather.26.cloned.1.call-start = ((), (), s32[]{:S(2)}) async-start(), calls=%async_computation.12 | async-start | bytes 3932160 | tf_op jit(solution)/shard_map/all_gather | solution.py:105
  197.7 340.6 %all-gather.22.cloned.1.call-start = ((), (), s32[]{:S(2)}) async-start(), calls=%async_computation.10 | async-start | bytes 9437184 | tf_op jit(solution)/shard_map/all_gather | solution.py:60
  197.8 517.3 %copy-start.27 = (f32[1,4,4,128]{3,1,2,0:T(4,128)}, f32[1,4,4,128]{3,1,2,0:T(4,128)S(1)}, u32[]{:S(2)}) copy-start(f32[1,4,4,128]{3,1,2,0:T(4,128)S(1)} %copy.87) | copy-start | bytes 24580
  282.7 432.4 %copy-start.38 = (f32[256]{0:T(256)}, f32[256]{0:T(256)S(1)}, u32[]{:S(2)}) copy-start(f32[256]{0:T(256)S(1)} %add_rsqrt_fusion.2) | copy-start | bytes 3076
  285.3 297.4 %all-gather.24.cloned.1.call-start = ((), (), s32[]{:S(2)}) async-start(), calls=%async_computation.11 | async-start | bytes 3932160 | tf_op jit(solution)/shard_map/all_gather | solution.py:105
  287.5 425.0 %reduce-scatter.11.cloned.1.call-start = ((), (), s32[]{:S(2)}) async-start(), calls=%async_computation.15 | async-start | bytes 9437184 | tf_op jit(solution)/shard_map/reduce_scatter | solution.py:64
  582.7 17.9 %copy-start.55 = (bf16[2048,768]{1,0:T(8,128)(2,1)S(1)}, bf16[2048,768]{1,0:T(8,128)(2,1)}, u32[]{:S(2)}) copy-start(bf16[2048,768]{1,0:T(8,128)(2,1)} %all-gather.24.cloned.1.call-done) | copy-start | bytes 9437188
  600.6 9.6 copy-start.56
  600.6 9.6 copy-start.58
  600.6 9.6 copy-start.54
  622.7 89.8 %copy-start.6 = (bf16[256,2048]{1,0:T(8,128)(2,1)S(1)}, bf16[256,2048]{1,0:T(8,128)(2,1)}, u32[]{:S(2)}) copy-start(bf16[256,2048]{1,0:T(8,128)(2,1)} %reduce-scatter.7.cloned.1.call-done) | copy-start | bytes 3145732
  622.7 93.0 %copy-start.11 = (bf16[1,256,2048]{2,1,0:T(8,128)(2,1)S(1)}, bf16[1,256,2048]{2,1,0:T(8,128)(2,1)}, u32[]{:S(2)}) copy-start(bf16[1,256,2048]{2,1,0:T(8,128)(2,1)} %param.29) | copy-start | bytes 3145732
  622.7 175.6 %all-gather.30.cloned.1.call-start = ((), (), s32[]{:S(2)}) async-start(), calls=%async_computation.16 | async-start | bytes 9437184 | tf_op jit(solution)/shard_map/all_gather | solution.py:60
  717.8 222.3 %reduce-scatter.15.cloned.1.call-start = ((), (), s32[]{:S(2)}) async-start(), calls=%async_computation.18 | async-start | bytes 3932160 | tf_op jit(solution)/shard_map/reduce_scatter | solution.py:179
  820.8 19.9 %copy-start.17 = (bf16[2048,2,128]{2,0,1:T(8,128)(2,1)S(1)}, bf16[2048,2,128]{2,0,1:T(8,128)(2,1)}, u32[]{:S(2)}) copy-start(bf16[2048,2,128]{2,0,1:T(8,128)(2,1)} %copy-done.16) | copy-start | bytes 3145732
  840.7 11.5 copy-start.24
  840.7 11.5 copy-start.26
  852.2 8.5 copy-start.34
  852.2 8.5 copy-start.49
  852.2 11.0 copy-start.14
  852.2 11.0 copy-start.18
  870.8 8.7 slice-start
  873.6 5.9 copy-start.22
  873.6 5.9 slice-start.1
  873.6 5.9 copy-start.60
  886.3 141.3 %reduce-scatter.17.cloned.1.call-start = ((), (), s32[]{:S(2)}) async-start(), calls=%async_computation.19 | async-start | bytes 11796480 | tf_op jit(solution)/shard_map/reduce_scatter | solution.py:179
  886.3 10.5 copy-start.59
  886.4 20.0 %slice-start.2 = ((s8[8388608]{0:T(1024)(128)(4,1)}), s8[4194304]{0:T(1024)(128)(4,1)S(1)}, s32[]{:S(2)}) async-start(s8[8388608]{0:T(1024)(128)(4,1)} %bitcast.231), calls=%async_computation.25 | async-start | bytes 8388608
  896.8 9.6 slice-start.3
  896.8 9.6 copy-start.57
  918.4 201.6 %reduce-scatter.13.cloned.1.call-start = ((), (), s32[]{:S(2)}) async-start(), calls=%async_computation.17 | async-start | bytes 9437184 | tf_op jit(solution)/shard_map/reduce_scatter | solution.py:64
  927.1 284.6 %reduce-scatter.9.cloned.1.call-start = ((), (), s32[]{:S(2)}) async-start(), calls=%async_computation.14 | async-start | bytes 9437184 | tf_op jit(solution)/shard_map/reduce_scatter | solution.py:64
  939.9 180.0 %copy-start.3 = (bf16[1,256,2048]{2,1,0:T(8,128)(2,1)S(1)}, bf16[1,256,2048]{2,1,0:T(8,128)(2,1)}, u32[]{:S(2)}) copy-start(bf16[1,256,2048]{2,1,0:T(8,128)(2,1)} %param.15) | copy-start | bytes 3145732
  939.9 180.0 %copy-start.36 = (f32[1,4,4,128]{3,1,2,0:T(4,128)S(1)}, f32[1,4,4,128]{3,1,2,0:T(4,128)}, u32[]{:S(2)}) copy-start(f32[1,4,4,128]{3,1,2,0:T(4,128)} %copy-done.35) | copy-start | bytes 24580
  939.9 180.0 %copy-start.41 = (f32[256]{0:T(256)S(1)}, f32[256]{0:T(256)}, u32[]{:S(2)}) copy-start(f32[256]{0:T(256)} %copy-done.40) | copy-start | bytes 3076
  940.0 181.9 %copy-start.37 = (f32[2048]{0:T(1024)S(1)}, f32[2048]{0:T(1024)}, u32[]{:S(2)}) copy-start(f32[2048]{0:T(1024)} %get-tuple-element.15) | copy-start | bytes 24580
  940.0 271.8 %copy-start.7 = (bf16[256,2048]{1,0:T(8,128)(2,1)S(1)}, bf16[256,2048]{1,0:T(8,128)(2,1)}, u32[]{:S(2)}) copy-start(bf16[256,2048]{1,0:T(8,128)(2,1)} %reduce-scatter.7.cloned.1.call-done) | copy-start | bytes 3145732
  940.0 271.8 %copy-start.12 = (bf16[1,256,2048]{2,1,0:T(8,128)(2,1)S(1)}, bf16[1,256,2048]{2,1,0:T(8,128)(2,1)}, u32[]{:S(2)}) copy-start(bf16[1,256,2048]{2,1,0:T(8,128)(2,1)} %param.29) | copy-start | bytes 3145732
  940.0 271.7 %copy-start.28 = (f32[1,4,4,128]{3,1,2,0:T(4,128)S(1)}, f32[1,4,4,128]{3,1,2,0:T(4,128)}, u32[]{:S(2)}) copy-start(f32[1,4,4,128]{3,1,2,0:T(4,128)} %copy-done.27) | copy-start | bytes 24580
  940.0 271.7 %copy-start.39 = (f32[256]{0:T(256)S(1)}, f32[256]{0:T(256)}, u32[]{:S(2)}) copy-start(f32[256]{0:T(256)} %copy-done.38) | copy-start | bytes 3076
  940.0 271.7 %copy-start.43 = (f32[256]{0:T(256)S(1)}, f32[256]{0:T(256)}, u32[]{:S(2)}) copy-start(f32[256]{0:T(256)} %copy-done.42) | copy-start | bytes 3076
  940.0 336.3 %all-gather.34.cloned.1.call-start = ((), (), s32[]{:S(2)}) async-start(), calls=%async_computation.21 | async-start | bytes 7077888 | tf_op jit(solution)/shard_map/all_gather | solution.py:234
  940.6 504.2 %all-gather.36.cloned.1.call-start = ((), (), s32[]{:S(2)}) async-start(), calls=%async_computation.22 | async-start | bytes 21233664 | tf_op jit(solution)/shard_map/all_gather | solution.py:191
  1283.2 4.0 copy-start.8
  1529.2 15.3 copy-start.1
  (18 other events, 35.8 us)
Sparse Core Ops, SparseCore 0:
  10.8 38.0 all-gather.17
  51.1 82.0 all-gather.15
  135.6 25.0 all-gather.19
  193.0 88.0 reduce-scatter.6
  283.3 42.1 all-gather.27
  327.0 82.0 all-gather.31
  411.5 42.4 all-gather.25
  456.2 82.0 all-gather.21
  540.2 42.4 all-gather.23
  622.9 89.5 reduce-scatter.10
  717.9 80.3 all-gather.29
  886.4 42.4 reduce-scatter.14
  932.6 94.9 reduce-scatter.16
  1030.3 89.5 reduce-scatter.12
  1122.7 89.0 reduce-scatter.8
  1213.2 63.0 all-gather.33
  1277.7 166.9 all-gather.35

commit v2 on v1

v2 whole, which is shorter than its diff:
```python
import functools

import jax
import jax.numpy as jnp
from jax import lax
from jax.experimental import pallas as pl
from jax.experimental.pallas import tpu as pltpu
from jax.sharding import PartitionSpec as P

D = 2048
QUERY_HEADS = 16
KEY_VALUE_HEADS = 8
HEAD_SIZE = 128
FF = 6144
EPS = 1e-06
THETA = 1000000.0
F32 = jnp.float32
BF16 = jnp.bfloat16
MESH = pl.DeviceIdType.MESH
VMEM = pltpu.VMEM
WHOLE = pl.BlockSpec(memory_space=pltpu.VMEM)
HBM = pl.BlockSpec(memory_space=pl.ANY)
CHUNKS = 4
WIDE = D // CHUNKS


def dot(left, right):
    return jnp.dot(left, right, preferred_element_type=F32)


def tdot(left, right):
    return lax.dot_general(left, right, (((0,), (0,)), ((), ())), preferred_element_type=F32)


def rdot(left, right):
    return lax.dot_general(left, right, (((1,), (1,)), ((), ())), preferred_element_type=F32)


def loop(count, body):
    def step(index, carry):
        body(index)
        return carry

    lax.fori_loop(0, count, step, 0)


def line_position():
    me = lax.axis_index("ctx")
    return me, me // 2, me % 2, lax.axis_size("ctx") // 2


def send(source, target, send_sem, recv_sem, axis, index):
    return pltpu.make_async_remote_copy(
        src_ref=source,
        dst_ref=target,
        send_sem=send_sem,
        recv_sem=recv_sem,
        device_id={axis: index},
        device_id_type=MESH,
    )


def line_barrier():
    me, chip, core, chips = line_position()
    barrier = pltpu.get_barrier_semaphore()

    def greet(index):
        pl.semaphore_signal(barrier, inc=1, device_id={"ctx": index}, device_id_type=MESH)

    greet(me + 1 - 2 * core)

    @pl.when(chip > 0)
    def _():
        greet(me - 2)

    @pl.when(chip < chips - 1)
    def _():
        greet(me + 2)

    peers = 1 + (chip > 0).astype(jnp.int32) + (chip < chips - 1).astype(jnp.int32)
    pl.semaphore_wait(barrier, peers)


def peers_of(axis):
    me, size = lax.axis_index(axis), lax.axis_size(axis)
    return size - 1, lambda i: (me + i + 1) % size, lambda i: (me + size - i - 1) % size


def full_barrier():
    barrier = pltpu.get_barrier_semaphore()
    total = 0
    for axis in ("fsdp", "ctx"):
        count, ahead, _ = peers_of(axis)
        loop(
            count,
            lambda i, axis=axis, ahead=ahead: pl.semaphore_signal(
                barrier, inc=1, device_id={axis: ahead(i)}, device_id_type=MESH
            ),
        )
        total += count
    pl.semaphore_wait(barrier, total)


def gather_scratch(chips):
    return [pltpu.SemaphoreType.DMA((chips,)) for _ in range(6)]


class Gather:
    def __init__(self, land, sems, consume=None, late=False):
        self.late = late
        self.land = land
        self.sems = sems
        self.consume = consume
        self.me, self.chip, self.core, self.chips = line_position()

    def right(self, step, source):
        ref = self.land.at[2 * source + self.core]
        return send(ref, ref, self.sems[0].at[step], self.sems[1].at[step], "ctx", self.me + 2)

    def left(self, step, source):
        ref = self.land.at[2 * source + self.core]
        return send(ref, ref, self.sems[2].at[step], self.sems[3].at[step], "ctx", self.me - 2)

    def across(self, source, core):
        ref = self.land.at[2 * source + core]
        other = self.me + 1 - 2 * self.core
        return send(ref, ref, self.sems[4].at[source], self.sems[5].at[source], "ctx", other)

    def step(self, step):
        chip, core, chips = self.chip, self.core, self.chips
        low, high = chip - step, chip + step
        has_low = low >= 0
        has_high = jnp.logical_and(high < chips, step > 0)

        @pl.when(jnp.logical_and(has_low, step > 0))
        def _():
            self.right(step - 1, low).wait_recv()

        @pl.when(jnp.logical_and(has_low, chip < chips - 1))
        def _():
            self.right(step, low).start()

        @pl.when(has_high)
        def _():
            self.left(step - 1, high).wait_recv()

        @pl.when(jnp.logical_and(high < chips, chip > 0))
        def _():
            self.left(step, high).start()

        @pl.when(has_low)
        def _():
            self.across(low, core).start()

        @pl.when(has_high)
        def _():
            self.across(high, core).start()

        if not self.late:
            self.use(step)
            return

        @pl.when(step > 0)
        def _():
            self.use(step - 1)

        @pl.when(step == chips - 1)
        def _():
            self.use(step)

    def use(self, step):
        chip, core, chips = self.chip, self.core, self.chips
        low, high = chip - step, chip + step

        def one(kind):
            upward = kind % 2
            crossed = kind // 2
            source = jnp.where(upward == 1, high, low)
            valid = jnp.where(upward == 1, jnp.logical_and(high < chips, step > 0), low >= 0)
            parity = jnp.where(crossed == 1, 1 - core, core)

            @pl.when(valid)
            def _():
                @pl.when(crossed == 1)
                def _():
                    self.across(source, parity).wait_recv()

                if self.consume is not None:
                    self.consume(2 * source + parity)

        loop(4, one)

    def finish(self):
        chip, core, chips = self.chip, self.core, self.chips

        def one(step):
            @pl.when(jnp.logical_and(chip - step >= 0, chip < chips - 1))
            def _():
                self.right(step, chip - step).wait_send()

            @pl.when(jnp.logical_and(chip + step < chips, chip > 0))
            def _():
                self.left(step, chip + step).wait_send()

            self.across(step, core).wait_send()

        loop(chips, one)


def scatter_scratch(chips, rows):
    buffers = [VMEM((count, CHUNKS, rows, WIDE), BF16) for count in (chips + 1, chips, chips)]
    return buffers + [pltpu.SemaphoreType.DMA((chips, CHUNKS)) for _ in range(6)]


class Scatter:
    def __init__(self, scratch, produce, total):
        self.line, self.out, self.other = scratch[:3]
        self.sems = scratch[3:]
        self.produce = produce
        self.total = total
        self.me, self.chip, self.core, self.chips = line_position()


    def right(self, step, chunk):
        ref = self.line.at[step, chunk]
        sems = self.sems
        return send(ref, ref, sems[0].at[step, chunk], sems[1].at[step, chunk], "ctx", self.me + 2)

    def left(self, step, chunk):
        ref = self.line.at[self.chips - step, chunk]
        sems = self.sems
        return send(ref, ref, sems[2].at[step, chunk], sems[3].at[step, chunk], "ctx", self.me - 2)

    def across(self, target, chunk):
        sems = self.sems
        return send(
            self.out.at[target, chunk],
            self.other.at[target, chunk],
            sems[4].at[target, chunk],
            sems[5].at[target, chunk],
            "ctx",
            self.me + 1 - 2 * self.core,
        )

    def begin(self):
        def clear(index):
            slot, chunk = index // CHUNKS, index % CHUNKS
            at_left = jnp.logical_and(self.chip == 0, slot < self.chips)
            at_right = jnp.logical_and(self.chip == self.chips - 1, slot > 0)

            @pl.when(jnp.logical_or(at_left, at_right))
            def _():
                self.line[slot, chunk] = jnp.zeros(self.line.shape[2:], BF16)

        loop((self.chips + 1) * CHUNKS, clear)

    def when_right(self, time):
        return jnp.logical_and(time >= self.chip, time < self.chips - 1)

    def when_left(self, time):
        return jnp.logical_and(time >= self.chips - 1 - self.chip, time < self.chips - 1)

    def prepare(self, time):
        def cross(target):
            def one(chunk):
                piece = 2 * target + 1 - self.core
                self.out[target, chunk] = self.produce(piece, chunk).astype(BF16)
                self.across(target, chunk).start()

            loop(CHUNKS, one)

        @pl.when(self.when_right(time))
        def _():
            cross(self.chips - 1 - time + self.chip)

        @pl.when(self.when_left(time))
        def _():
            cross(time - (self.chips - 1 - self.chip))

        @pl.when(time == self.chips - 1)
        def _():
            cross(self.chip)

    def step(self, time):
        chip, core, chips = self.chip, self.core, self.chips

        @pl.when(self.when_right(time))
        def _():
            step = time - chip
            target = chips - 1 - step

            def one(chunk):
                self.across(target, chunk).wait_recv()

                @pl.when(chip > 0)
                def _():
                    self.right(step, chunk).wait_recv()

                value = self.produce(2 * target + core, chunk) + self.other[target, chunk].astype(F32)
                value = value + self.line[step, chunk].astype(F32)
                self.line[step, chunk] = value.astype(BF16)
                self.right(step, chunk).start()

            loop(CHUNKS, one)

        @pl.when(self.when_left(time))
        def _():
            step = time - (chips - 1 - chip)

            def one(chunk):
                self.across(step, chunk).wait_recv()

                @pl.when(chip < chips - 1)
                def _():
                    self.left(step, chunk).wait_recv()

                value = self.produce(2 * step + core, chunk) + self.other[step, chunk].astype(F32)
                value = value + self.line[chips - step, chunk].astype(F32)
                self.line[chips - step, chunk] = value.astype(BF16)
                self.left(step, chunk).start()

            loop(CHUNKS, one)

    def finish(self):
        chip, core, chips = self.chip, self.core, self.chips
        last = chips - 1 - chip

        def one(chunk):
            self.across(chip, chunk).wait_recv()
            value = self.produce(2 * chip + core, chunk) + self.other[chip, chunk].astype(F32)

            @pl.when(chip > 0)
            def _():
                self.right(last, chunk).wait_recv()

            @pl.when(chip < chips - 1)
            def _():
                self.left(chip, chunk).wait_recv()

            value = value + self.line[last, chunk].astype(F32)
            value = value + self.line[chips - chip, chunk].astype(F32)
            self.total[:, pl.ds(pl.multiple_of(chunk * WIDE, WIDE), WIDE)] = value

        loop(CHUNKS, one)

        def drain(index):
            step, chunk = index // CHUNKS, index % CHUNKS

            @pl.when(step < last)
            def _():
                self.right(step, chunk).wait_send()

            @pl.when(step < chip)
            def _():
                self.left(step, chunk).wait_send()

            self.across(step, chunk).wait_send()

        loop(chips * CHUNKS, drain)


def row_blocks(rows, body, size=32):
    def one(index):
        body(pl.ds(pl.multiple_of(index * size, size), size))

    loop(rows // size, one)


def inverse_norm(value):
    return lax.rsqrt(jnp.mean(value * value, axis=-1, keepdims=True) + EPS)


def params(identity, megabytes):
    return pltpu.CompilerParams(
        collective_id=identity,
        has_side_effects=True,
        vmem_limit_bytes=megabytes * 1024 * 1024,
    )


def copy_in(source, target, sem):
    copy = pltpu.make_async_copy(source, target, sem)
    copy.start()
    return copy


def first_kernel(rows, width, *refs):
    x, gains, tokens, part, land, proj, weights, gain_rows, all_gains, all_tokens = refs[:10]
    sems, small = refs[10:16], refs[16:]
    me, _, _, chips = line_position()
    shard = lax.axis_index("fsdp")
    shards, ahead, behind = peers_of("fsdp")
    parts, next_part, past_part = peers_of("ctx")
    full_barrier()

    def gain_copy(i, slot):
        return send(gains, all_gains.at[slot], small[0].at[i], small[1].at[i], "fsdp", ahead(i))

    def token_copy(i, slot):
        return send(tokens, all_tokens.at[slot], small[2].at[i], small[3].at[i], "ctx", next_part(i))

    def weight_copy(i, owner):
        target = weights.at[pl.ds(pl.multiple_of(owner * rows, rows), rows), :]
        return send(part, target, small[4].at[i], small[5].at[i], "fsdp", ahead(i))

    loop(shards, lambda i: gain_copy(i, shard).start())
    loop(parts, lambda i: token_copy(i, me).start())
    loop(shards, lambda i: weight_copy(i, shard).start())
    all_gains[shard] = gains[...]
    all_tokens[me] = tokens[...]
    weights[pl.ds(pl.multiple_of(shard * rows, rows), rows), :] = part[...]
    loop(shards, lambda i: gain_copy(i, behind(i)).wait_recv())
    lanes = rows // 128
    for kind in range(2):
        for owner in range(shards + 1):
            for j in range(lanes):
                at = owner * rows + j * 128
                gain_rows[kind : kind + 1, at : at + 128] = all_gains[
                    owner, kind * lanes + j : kind * lanes + j + 1, :
                ]

    def norm(block):
        value = x[block, :].astype(F32)
        land[me, block] = (value * inverse_norm(value) * gain_rows[0:1, :]).astype(BF16)

    row_blocks(x.shape[0], norm)

    def consume(piece):
        proj[piece] = dot(land[piece], weights[:, :width])

    gather = Gather(land, sems, consume, late=True)

    def step(index):
        @pl.when(index == 1)
        def _():
            loop(shards, lambda i: weight_copy(i, behind(i)).wait_recv())

        gather.step(index)

    loop(chips, step)
    gather.finish()
    loop(shards, lambda i: gain_copy(i, shard).wait_send())
    loop(shards, lambda i: weight_copy(i, shard).wait_send())
    loop(parts, lambda i: token_copy(i, past_part(i)).wait_recv())
    loop(parts, lambda i: token_copy(i, me).wait_send())


def first(hidden, gains, tokens, part, shards, parts, width):
    count = hidden.shape[0]
    return pl.pallas_call(
        functools.partial(first_kernel, D // shards, width),
        out_shape=(
            jax.ShapeDtypeStruct((parts, count, D), BF16),
            jax.ShapeDtypeStruct((parts, count, width), F32),
            jax.ShapeDtypeStruct((D, part.shape[1]), BF16),
            jax.ShapeDtypeStruct((8, D), F32),
            jax.ShapeDtypeStruct((shards, *gains.shape), F32),
            jax.ShapeDtypeStruct((parts, *tokens.shape), jnp.int32),
        ),
        in_specs=[WHOLE] * 4,
        out_specs=(WHOLE,) * 6,
        scratch_shapes=gather_scratch(parts // 2)
        + [pltpu.SemaphoreType.DMA((shards,))] * 2
        + [pltpu.SemaphoreType.DMA((parts,))] * 2
        + [pltpu.SemaphoreType.DMA((shards,))] * 2,
        compiler_params=params(0, 60),
        name="gather_normed",
    )(hidden, gains, tokens, part)


def out_kernel(columns, *refs):
    context, weights, x, gain_rows, middle, normed = refs[:6]
    weight, weight_sem, total = refs[6:9]
    scratch = refs[9:]
    chips = line_position()[3]
    copy = copy_in(weights.at[:, columns], weight, weight_sem)

    def produce(piece, chunk):
        return rdot(context[piece], weight[pl.ds(pl.multiple_of(chunk * WIDE, WIDE), WIDE), :])

    scatter = Scatter(scratch, produce, total)
    scatter.begin()
    line_barrier()
    copy.wait()
    scatter.prepare(0)

    def step(time):
        scatter.step(time)
        scatter.prepare(time + 1)

    loop(chips - 1, step)
    scatter.finish()

    def norm(block):
        value = x[block, :].astype(F32) + total[block, :]
        middle[block, :] = value
        normed[block, :] = (value * inverse_norm(value) * gain_rows[1:2, :]).astype(BF16)

    row_blocks(x.shape[0], norm)


def attention_out(context, weights, hidden, gain_rows):
    parts, count, width = context.shape
    return pl.pallas_call(
        functools.partial(out_kernel, pl.ds(weights.shape[1] - width, width)),
        out_shape=(
            jax.ShapeDtypeStruct((count, D), F32),
            jax.ShapeDtypeStruct((count, D), BF16),
        ),
        in_specs=[WHOLE, HBM, WHOLE, WHOLE],
        out_specs=(WHOLE,) * 2,
        scratch_shapes=[VMEM((D, width), BF16), pltpu.SemaphoreType.DMA, VMEM((count, D), F32)]
        + scatter_scratch(parts // 2, count),
        compiler_params=params(1, 60),
        name="attention_out",
    )(context, weights, hidden, gain_rows)


def feed_kernel(width, *refs):
    x, grads, weights, land, activation, back = refs[:6]
    weight, weight_sem, grad, grad_sems = refs[6:10]
    sems = refs[10:]
    me, _, _, chips = line_position()
    copy = copy_in(weights, weight, weight_sem)

    def grad_copy(piece):
        return pltpu.make_async_copy(grads.at[piece], grad.at[piece], grad_sems.at[piece])

    loop(2 * chips, lambda piece: grad_copy(piece).start())
    land[me] = x[...]
    size = 256 if width % 256 == 0 else 128

    def consume(piece):
        grad_copy(piece).wait()

        def one(index):
            def columns(kind):
                return pl.ds(pl.multiple_of(kind * width + index * size, 128), size)

            gate = dot(land[piece], weight[:, columns(0)])
            up = dot(land[piece], weight[:, columns(1)])
            grad_act = dot(grad[piece], weight[:, columns(2)])
            sigma = 1.0 / (1.0 + jnp.exp(-gate))
            activation[piece, :, columns(0)] = (gate * sigma * up).astype(BF16)
            back[piece, :, columns(0)] = (
                grad_act * up * sigma * (1.0 + gate * (1.0 - sigma))
            ).astype(BF16)
            back[piece, :, columns(1)] = (grad_act * gate * sigma).astype(BF16)

        loop(width // size, one)

    line_barrier()
    gather = Gather(land, sems, consume)
    copy.wait()
    loop(chips, gather.step)
    gather.finish()


def feed(normed, grads, weights):
    parts, count, _ = grads.shape
    width = weights.shape[1] // 3
    return pl.pallas_call(
        functools.partial(feed_kernel, width),
        out_shape=(
            jax.ShapeDtypeStruct((parts, count, D), BF16),
            jax.ShapeDtypeStruct((parts, count, width), BF16),
            jax.ShapeDtypeStruct((parts, count, 2 * width), BF16),
        ),
        in_specs=[WHOLE, HBM, HBM],
        out_specs=(WHOLE,) * 3,
        scratch_shapes=[
            VMEM(weights.shape, BF16),
            pltpu.SemaphoreType.DMA,
            VMEM(grads.shape, BF16),
            pltpu.SemaphoreType.DMA((parts,)),
        ]
        + gather_scratch(parts // 2),
        compiler_params=params(2, 60),
        name="feed",
    )(normed, grads, weights)


def rms_back(value, gain, grad):
    inverse = inverse_norm(value)
    scaled = grad * gain
    inner = jnp.mean(scaled * value, axis=-1, keepdims=True)
    terms = grad * value * inverse
    return inverse * scaled - value * (inverse * inverse * inverse * inner), terms


def feed_back_kernel(columns, *refs):
    back, weights, middle, grad, gain_rows, grad_middle, low, gain_sum = refs[:8]
    weight, weight_sem, total = refs[8:11]
    scratch = refs[11:]
    chips = line_position()[3]
    copy = copy_in(weights.at[:, columns], weight, weight_sem)

    def produce(piece, chunk):
        return rdot(back[piece], weight[pl.ds(pl.multiple_of(chunk * WIDE, WIDE), WIDE), :])

    scatter = Scatter(scratch, produce, total)
    scatter.begin()
    line_barrier()
    copy.wait()
    scatter.prepare(0)

    def step(time):
        scatter.step(time)
        scatter.prepare(time + 1)

    loop(chips - 1, step)
    scatter.finish()
    gain_sum[...] = jnp.zeros_like(gain_sum)

    def norm(block):
        through, terms = rms_back(middle[block, :], gain_rows[1:2, :], total[block, :])
        value = grad[block, :].astype(F32) + through
        grad_middle[block, :] = value
        low[block, :] = value.astype(BF16)
        gain_sum[0:1, :] += jnp.sum(terms, axis=0, keepdims=True)

    row_blocks(middle.shape[0], norm)


def feed_back(back, weights, middle, grad, gain_rows):
    parts, count, width = back.shape
    return pl.pallas_call(
        functools.partial(feed_back_kernel, pl.ds(0, width)),
        out_shape=(
            jax.ShapeDtypeStruct((count, D), F32),
            jax.ShapeDtypeStruct((count, D), BF16),
            jax.ShapeDtypeStruct((8, D), F32),
        ),
        in_specs=[WHOLE, HBM, WHOLE, WHOLE, WHOLE],
        out_specs=(WHOLE,) * 3,
        scratch_shapes=[VMEM((D, width), BF16), pltpu.SemaphoreType.DMA, VMEM((count, D), F32)]
        + scatter_scratch(parts // 2, count),
        compiler_params=params(3, 60),
        name="feed_back",
    )(back, weights, middle, grad, gain_rows)


def turn_kernel(columns, down_columns, *refs):
    low, weights, activation, feed_weights, middle, land, context_grad, hidden = refs[:8]
    weight, weight_sem, down, down_sem, total = refs[8:13]
    gather_sems, scratch = refs[13:19], refs[19:]
    me, _, _, chips = line_position()
    copy = copy_in(weights.at[:, columns], weight, weight_sem)
    down_copy = copy_in(feed_weights.at[:, down_columns], down, down_sem)
    land[me] = low[...]

    def consume(piece):
        context_grad[piece] = dot(land[piece], weight[...]).astype(BF16)

    def produce(piece, chunk):
        return rdot(activation[piece], down[pl.ds(pl.multiple_of(chunk * WIDE, WIDE), WIDE), :])

    gather = Gather(land, gather_sems, consume)
    scatter = Scatter(scratch, produce, total)
    scatter.begin()
    line_barrier()
    copy.wait()
    down_copy.wait()
    scatter.prepare(0)

    def step(time):
        gather.step(time)
        scatter.step(time)
        scatter.prepare(time + 1)

    loop(chips - 1, step)
    gather.step(chips - 1)
    scatter.finish()
    gather.finish()

    def add(block):
        hidden[block, :] = (middle[block, :] + total[block, :]).astype(BF16)

    row_blocks(middle.shape[0], add)


def turn(low, weights, activation, feed_weights, middle, width):
    parts, count, feed_width = activation.shape
    return pl.pallas_call(
        functools.partial(
            turn_kernel, pl.ds(weights.shape[1] - width, width), pl.ds(2 * feed_width, feed_width)
        ),
        out_shape=(
            jax.ShapeDtypeStruct((parts, count, D), BF16),
            jax.ShapeDtypeStruct((parts, count, width), BF16),
            jax.ShapeDtypeStruct((count, D), BF16),
        ),
        in_specs=[WHOLE, HBM, WHOLE, HBM, WHOLE],
        out_specs=(WHOLE,) * 3,
        scratch_shapes=[
            VMEM((D, width), BF16),
            pltpu.SemaphoreType.DMA,
            VMEM((D, feed_width), BF16),
            pltpu.SemaphoreType.DMA,
            VMEM((count, D), F32),
        ]
        + gather_scratch(parts // 2)
        + scatter_scratch(parts // 2, count),
        compiler_params=params(4, 62),
        name="turn",
    )(low, weights, activation, feed_weights, middle)


def last_kernel(columns, *refs):
    back, weights, x, grad_middle, gain_rows, gain_two, gain_heads, hidden, gain_out = refs[:9]
    weight, weight_sem, total, gain_one, pack, pack_in, shard_sum, shard_in = refs[9:17]
    small, scratch = refs[17:21], refs[21:]
    chips = line_position()[3]
    copy = copy_in(weights.at[:, columns], weight, weight_sem)

    def produce(piece, chunk):
        return rdot(back[piece], weight[pl.ds(pl.multiple_of(chunk * WIDE, WIDE), WIDE), :])

    scatter = Scatter(scratch, produce, total)
    scatter.begin()
    full_barrier()
    copy.wait()
    scatter.prepare(0)

    def step(time):
        scatter.step(time)
        scatter.prepare(time + 1)

    loop(chips - 1, step)
    scatter.finish()
    gain_one[...] = jnp.zeros_like(gain_one)

    def norm(block):
        through, terms = rms_back(x[block, :].astype(F32), gain_rows[0:1, :], total[block, :])
        hidden[block, :] = grad_middle[block, :] + through
        gain_one[0:1, :] += jnp.sum(terms, axis=0, keepdims=True)

    row_blocks(x.shape[0], norm)

    shard = lax.axis_index("fsdp")
    shards, ahead, _ = peers_of("fsdp")
    parts, next_part, _ = peers_of("ctx")
    rows = D // (shards + 1)
    lanes = rows // 128
    pack[...] = jnp.zeros_like(pack)
    for owner in range(shards + 1):
        for j in range(lanes):
            at = owner * rows + j * 128
            pack[owner, j : j + 1, :] = gain_one[0:1, at : at + 128]
            pack[owner, lanes + j : lanes + j + 1, :] = gain_two[0:1, at : at + 128]
        pack[owner, 2 * lanes : 2 * lanes + 2, :] = gain_heads[0:2, :]

    def pack_copy(i):
        return send(pack.at[ahead(i)], pack_in.at[i], small[0].at[i], small[1].at[i], "fsdp", ahead(i))

    def sum_copy(i):
        return send(shard_sum, shard_in.at[i], small[2].at[i], small[3].at[i], "ctx", next_part(i))

    loop(shards, lambda i: pack_copy(i).start())
    shard_sum[...] = pack[shard]

    def add_pack(i):
        pack_copy(i).wait_recv()
        shard_sum[...] += pack_in[i]

    loop(shards, add_pack)
    loop(parts, lambda i: sum_copy(i).start())
    gain_out[...] = shard_sum[...]

    def add_sum(i):
        sum_copy(i).wait_recv()
        gain_out[...] += shard_in[i]

    loop(parts, add_sum)
    loop(shards, lambda i: pack_copy(i).wait_send())
    loop(parts, lambda i: sum_copy(i).wait_send())


def last(back, weights, hidden, grad_middle, gain_rows, gain_two, gain_heads, shards):
    parts, count, width = back.shape
    return pl.pallas_call(
        functools.partial(last_kernel, pl.ds(0, width)),
        out_shape=(
            jax.ShapeDtypeStruct((count, D), F32),
            jax.ShapeDtypeStruct((16, 128), F32),
        ),
        in_specs=[WHOLE, HBM] + [WHOLE] * 5,
        out_specs=(WHOLE,) * 2,
        scratch_shapes=[
            VMEM((D, width), BF16),
            pltpu.SemaphoreType.DMA,
            VMEM((count, D), F32),
            VMEM((8, D), F32),
            VMEM((shards, 16, 128), F32),
            VMEM((shards, 16, 128), F32),
            VMEM((16, 128), F32),
            VMEM((parts, 16, 128), F32),
        ]
        + [pltpu.SemaphoreType.DMA((shards,))] * 2
        + [pltpu.SemaphoreType.DMA((parts,))] * 2
        + scatter_scratch(parts // 2, count),
        compiler_params=params(5, 60),
        name="last",
    )(back, weights, hidden, grad_middle, gain_rows, gain_two, gain_heads)


QUERY_TILE = 256
KEY_TILE = 512


def reach(index, tokens):
    return jnp.minimum((index + 2) * QUERY_TILE + KEY_TILE - 1, tokens) // KEY_TILE


def head_norm(value, gain, cosine, sine):
    normed = value * inverse_norm(value) * gain
    return normed * cosine + pltpu.roll(normed, HEAD_SIZE // 2, 1) * sine


def attention_kernel(heads, proj, cosine, sine, gain, id_column, id_row, *refs):
    queries, keys, values, context, inverse = refs
    tokens = proj.shape[0]
    key_at = heads * HEAD_SIZE

    def prepare(index):
        block = pl.ds(pl.multiple_of(index * QUERY_TILE, QUERY_TILE), QUERY_TILE)
        c, s = cosine[block, :], sine[block, :]
        for h in range(heads):
            lanes = slice(h * HEAD_SIZE, (h + 1) * HEAD_SIZE)
            rotated = head_norm(proj[block, lanes], gain[0:1, :], c, s) * HEAD_SIZE ** (-0.5)
            queries[block, lanes] = rotated.astype(BF16)
        rotated = head_norm(proj[block, key_at : key_at + HEAD_SIZE], gain[1:2, :], c, s)
        keys[block, :] = rotated.astype(BF16)
        values[block, :] = proj[block, key_at + HEAD_SIZE : key_at + 2 * HEAD_SIZE].astype(BF16)

    loop(tokens // QUERY_TILE, prepare)

    def attend(index):
        block = pl.ds(pl.multiple_of(index * QUERY_TILE, QUERY_TILE), QUERY_TILE)
        query_ids = id_column[block, :]
        for h in range(heads):
            lanes = slice(h * HEAD_SIZE, (h + 1) * HEAD_SIZE)
            query = queries[block, lanes]

            def one(tile, carry):
                sums, total = carry
                span = pl.ds(pl.multiple_of(tile * KEY_TILE, KEY_TILE), KEY_TILE)
                scores = rdot(query, keys[span, :])
                expon = jnp.where(id_row[0:1, span] <= query_ids, jnp.exp(scores), 0.0)
                sums = sums + dot(expon.astype(BF16), values[span, :])
                return sums, total + jnp.sum(expon, axis=1, keepdims=True)

            start = (jnp.zeros((QUERY_TILE, HEAD_SIZE), F32), jnp.zeros((QUERY_TILE, 1), F32))
            sums, total = lax.fori_loop(0, reach(index, tokens), one, start)
            scale = 1.0 / total
            context[block, lanes] = (sums * scale).astype(BF16)
            inverse[h : h + 1, block] = jnp.broadcast_to(scale, (QUERY_TILE, HEAD_SIZE)).T[0:1, :]

    loop(tokens // QUERY_TILE, attend)


def attention(proj, cosine, sine, gain, id_column, id_row, heads):
    tokens = proj.shape[0]
    width = heads * HEAD_SIZE
    return pl.pallas_call(
        functools.partial(attention_kernel, heads),
        out_shape=(
            jax.ShapeDtypeStruct((tokens, width), BF16),
            jax.ShapeDtypeStruct((tokens, HEAD_SIZE), BF16),
            jax.ShapeDtypeStruct((tokens, HEAD_SIZE), BF16),
            jax.ShapeDtypeStruct((tokens, width), BF16),
            jax.ShapeDtypeStruct((8, tokens), F32),
        ),
        in_specs=[WHOLE] * 6,
        out_specs=(WHOLE,) * 5,
        compiler_params=pltpu.CompilerParams(vmem_limit_bytes=48 * 1024 * 1024),
        name="attention",
    )(proj, cosine, sine, gain, id_column, id_row)


def attention_back_kernel(heads, *refs):
    queries, keys, values, out_grad, inverse, context, proj, cosine, sine, gain = refs[:10]
    id_column, id_row, back, gain_sum, key_grad, value_grad, query_grad = refs[10:]
    tokens = proj.shape[0]
    key_at = heads * HEAD_SIZE
    key_grad[...] = jnp.zeros_like(key_grad)
    value_grad[...] = jnp.zeros_like(value_grad)
    gain_sum[...] = jnp.zeros_like(gain_sum)

    def through(block, lanes, grad, row):
        turned = pltpu.roll(grad, HEAD_SIZE // 2, 1)
        unrotated = grad * cosine[block, :] - turned * sine[block, :]
        result, terms = rms_back(proj[block, lanes], gain[row : row + 1, :], unrotated)
        back[block, lanes] = result.astype(BF16)
        gain_sum[row : row + 1, :] += jnp.sum(terms, axis=0, keepdims=True)

    def attend(index):
        block = pl.ds(pl.multiple_of(index * QUERY_TILE, QUERY_TILE), QUERY_TILE)
        query_ids = id_row[0:1, block]
        for h in range(heads):
            lanes = slice(h * HEAD_SIZE, (h + 1) * HEAD_SIZE)
            query = queries[block, lanes]
            grad = out_grad[block, lanes]
            scale = inverse[h : h + 1, block]
            products = grad.astype(F32) * context[block, lanes].astype(F32)
            shift = lax.dot_general(
                jnp.ones((8, HEAD_SIZE), F32),
                products,
                (((1,), (1,)), ((), ())),
                precision=lax.Precision.HIGHEST,
                preferred_element_type=F32,
            )[0:1, :]
            query_grad[...] = jnp.zeros_like(query_grad)

            def one(tile):
                span = pl.ds(pl.multiple_of(tile * KEY_TILE, KEY_TILE), KEY_TILE)
                key = keys[span, :]
                scores = rdot(key, query)
                probs = jnp.where(id_column[span, :] <= query_ids, jnp.exp(scores) * scale, 0.0)
                grad_scores = (probs * (rdot(values[span, :], grad) - shift)).astype(BF16)
                value_grad[span, :] += dot(probs.astype(BF16), grad)
                key_grad[span, :] += dot(grad_scores, query)
                query_grad[...] += tdot(grad_scores, key)

            loop(reach(index, tokens), one)
            through(block, lanes, query_grad[...] * HEAD_SIZE ** (-0.5), 0)

    loop(tokens // QUERY_TILE, attend)

    def finish(index):
        block = pl.ds(pl.multiple_of(index * QUERY_TILE, QUERY_TILE), QUERY_TILE)
        through(block, slice(key_at, key_at + HEAD_SIZE), key_grad[block, :], 1)
        back[block, key_at + HEAD_SIZE : key_at + 2 * HEAD_SIZE] = value_grad[block, :].astype(BF16)

    loop(tokens // QUERY_TILE, finish)


def attention_back(heads, *operands):
    tokens = operands[0].shape[0]
    width = heads * HEAD_SIZE
    return pl.pallas_call(
        functools.partial(attention_back_kernel, heads),
        out_shape=(
            jax.ShapeDtypeStruct((tokens, width + 2 * HEAD_SIZE), BF16),
            jax.ShapeDtypeStruct((8, HEAD_SIZE), F32),
        ),
        in_specs=[WHOLE] * len(operands),
        out_specs=(WHOLE,) * 2,
        scratch_shapes=[
            VMEM((tokens, HEAD_SIZE), F32),
            VMEM((tokens, HEAD_SIZE), F32),
            VMEM((QUERY_TILE, HEAD_SIZE), F32),
        ],
        compiler_params=pltpu.CompilerParams(vmem_limit_bytes=48 * 1024 * 1024),
        name="attention_back",
    )(*operands)


def spread_kernel(source, target):
    target[...] = source[0].astype(F32)


def spread_columns(stacked):
    parts, rows, width = stacked.shape
    return pl.pallas_call(
        spread_kernel,
        out_shape=jax.ShapeDtypeStruct((rows, parts * width), F32),
        grid=(parts,),
        in_specs=[pl.BlockSpec((1, rows, width), lambda i: (i, 0, 0))],
        out_specs=pl.BlockSpec((rows, width), lambda i: (0, i)),
        compiler_params=pltpu.CompilerParams(vmem_limit_bytes=32 * 1024 * 1024),
        name="spread",
    )(stacked)


def spread_heads_kernel(width, source, query, key, value):
    query[...] = source[0, :, :width].astype(F32)
    key[...] = source[0, :, width : width + HEAD_SIZE].astype(F32)
    value[...] = source[0, :, width + HEAD_SIZE :].astype(F32)


def spread_heads(stacked, width):
    parts, rows, total = stacked.shape
    widths = (width, HEAD_SIZE, HEAD_SIZE)
    return pl.pallas_call(
        functools.partial(spread_heads_kernel, width),
        out_shape=tuple(jax.ShapeDtypeStruct((rows, parts * w), F32) for w in widths),
        grid=(parts,),
        in_specs=[pl.BlockSpec((1, rows, total), lambda i: (i, 0, 0))],
        out_specs=tuple(pl.BlockSpec((rows, w), lambda i: (0, i)) for w in widths),
        compiler_params=pltpu.CompilerParams(vmem_limit_bytes=32 * 1024 * 1024),
        name="spread_heads",
    )(stacked)


def own_columns(array, index, width):
    return lax.dynamic_slice_in_dim(array, index * width, width, axis=1)


def own_rows(array, index, width):
    return lax.dynamic_slice_in_dim(array, index * width, width, axis=0)


def local(
    hidden_in,
    weight_query,
    key_weight_matrix,
    weight_value,
    weight_out,
    weight_gate,
    weight_up,
    weight_down,
    gain_attention,
    gain_feed,
    gain_query,
    gain_key,
    positions,
    token_block_index,
    grad_out,
):
    parts = lax.axis_size("ctx")
    shards = lax.axis_size("fsdp")
    me = lax.axis_index("ctx")
    shard = lax.axis_index("fsdp")
    heads = QUERY_HEADS // parts
    sharers = parts // KEY_VALUE_HEADS
    key_head = me // sharers
    width = heads * HEAD_SIZE
    feed_width = FF // parts
    rows = D // shards
    head_rows = HEAD_SIZE // shards
    count = hidden_in.shape[1]
    tokens = parts * count

    def gather_rows(piece):
        return lax.all_gather(piece, "fsdp", axis=0, tiled=True)

    def sum_rows(grad):
        return lax.psum_scatter(grad.astype(BF16), "fsdp", scatter_dimension=0, tiled=True)

    def gather_parts(piece):
        return lax.all_gather(piece, "ctx", axis=0)

    own_heads_weight = jnp.concatenate(
        [
            own_columns(weight_query, me, width),
            own_columns(key_weight_matrix, key_head, HEAD_SIZE),
            own_columns(weight_value, key_head, HEAD_SIZE),
            own_rows(weight_out, me, width).T,
        ],
        axis=1,
    )
    feed_weight = gather_rows(
        jnp.concatenate(
            [
                own_columns(weight_gate, me, feed_width),
                own_columns(weight_up, me, feed_width),
                own_rows(weight_down, me, feed_width).T,
            ],
            axis=1,
        )
    )

    own_gains = jnp.concatenate([gain_attention, gain_feed, gain_query, gain_key]).astype(F32)
    own_gains = jnp.pad(own_gains, (0, 2048 - own_gains.shape[0])).reshape(16, 128)
    own_tokens = jnp.pad(jnp.stack([positions[0], token_block_index[0]]), ((0, 6), (0, 0)))
    hidden, grad = hidden_in[0], grad_out[0]
    normed_all, proj, heads_weight, gain_rows, gains, whole = first(
        hidden, own_gains, own_tokens, own_heads_weight, shards, parts, width + 2 * HEAD_SIZE
    )
    grad_late, gains = lax.optimization_barrier((grad, gains))
    grad_all = gather_parts(grad_late)
    flat_gains = gains.reshape(shards, -1)
    norm_query = flat_gains[:, 2 * rows : 2 * rows + head_rows].reshape(1, -1)
    norm_key = flat_gains[:, 2 * rows + head_rows : 2 * rows + 2 * head_rows].reshape(1, -1)
    head_gains = jnp.concatenate([norm_query, norm_key, jnp.zeros((6, HEAD_SIZE), F32)])

    half = HEAD_SIZE // 2
    freq = THETA ** (-(jnp.arange(half).astype(F32) * 2.0 / HEAD_SIZE))
    angle = whole[:, 0].reshape(-1).astype(F32)[:, None] * freq
    cosine, sine = jnp.cos(angle), jnp.sin(angle)
    cosine = jnp.concatenate([cosine, cosine], axis=1)
    sine = jnp.concatenate([-sine, sine], axis=1)
    ids = whole[:, 1].reshape(-1)
    id_row, id_column = ids[None, :], ids[:, None]

    proj = proj.reshape(tokens, width + 2 * HEAD_SIZE)
    queries, keys, values, context, inverse = attention(
        proj, cosine, sine, head_gains, id_column, id_row, heads
    )
    middle, normed_two = attention_out(
        context.reshape(parts, count, width), heads_weight, hidden, gain_rows
    )
    normed_two_all, activation, back = feed(normed_two, grad_all, feed_weight)

    flat_grad = grad_all.reshape(tokens, D)
    flat_back = back.reshape(tokens, 2 * feed_width)
    flat_activation = activation.reshape(tokens, feed_width)
    grad_gate_up = tdot(normed_two_all.reshape(tokens, D), flat_back).astype(BF16)
    grad_down = tdot(flat_activation, flat_grad).astype(BF16)
    back, grad_gate_up, grad_down = lax.optimization_barrier((back, grad_gate_up, grad_down))
    grad_gate_up = sum_rows(grad_gate_up)
    grad_down = sum_rows(
        grad_down.reshape(feed_width, shards, rows).transpose(1, 0, 2).reshape(shards * feed_width, rows)
    )
    gate_parts = gather_parts(grad_gate_up[:, :feed_width])
    up_parts = gather_parts(grad_gate_up[:, feed_width:])
    grad_weight_down = lax.all_gather(grad_down, "ctx", axis=0, tiled=True).astype(F32)

    grad_middle, low, gain_two = feed_back(back, feed_weight, middle, grad, gain_rows)
    low_all, context_grad, hidden_out = turn(low, heads_weight, activation, feed_weight, middle, width)

    context_grad = context_grad.reshape(tokens, width)
    grad_qkv, gain_heads = attention_back(
        heads,
        queries,
        keys,
        values,
        context_grad,
        inverse,
        context,
        proj,
        cosine,
        sine,
        head_gains,
        id_column,
        id_row,
    )
    grad_hidden, gain_sums = last(
        grad_qkv.reshape(parts, count, -1),
        heads_weight,
        hidden,
        grad_middle,
        gain_rows,
        gain_two,
        gain_heads,
        shards,
    )

    grad_heads = sum_rows(tdot(normed_all.reshape(tokens, D), grad_qkv))
    grad_out_weight = sum_rows(
        tdot(context, low_all.reshape(tokens, D))
        .astype(BF16)
        .reshape(width, shards, rows)
        .transpose(1, 0, 2)
        .reshape(shards * width, rows)
    )
    head_parts = gather_parts(grad_heads)
    grad_weight_out = lax.all_gather(grad_out_weight, "ctx", axis=0, tiled=True).astype(F32)

    gain_sums = gain_sums.reshape(-1)
    def columns(stacked):
        return stacked.astype(F32).transpose(1, 0, 2).reshape(rows, -1)

    def key_columns(stacked):
        summed = stacked.astype(F32).reshape(KEY_VALUE_HEADS, sharers, rows, HEAD_SIZE).sum(axis=1)
        return summed.transpose(1, 0, 2).reshape(rows, -1)

    if sharers == 1:
        grad_query, grad_key, grad_value = spread_heads(head_parts, width)
    else:
        grad_query = columns(head_parts[:, :, :width])
        grad_key = key_columns(head_parts[:, :, width : width + HEAD_SIZE])
        grad_value = key_columns(head_parts[:, :, width + HEAD_SIZE :])
    return (
        hidden_out[None],
        grad_hidden[None],
        grad_query,
        grad_key,
        grad_value,
        grad_weight_out,
        spread_columns(gate_parts),
        spread_columns(up_parts),
        grad_weight_down,
        gain_sums[:rows],
        gain_sums[rows : 2 * rows],
        lax.dynamic_slice_in_dim(gain_sums, 2 * rows + shard * head_rows, head_rows),
        lax.dynamic_slice_in_dim(gain_sums, 2 * rows + HEAD_SIZE + shard * head_rows, head_rows),
    )


def solution(mesh):
    tokens = P("fsdp", "ctx", None)
    by_rows = P("fsdp", None)
    by_columns = P(None, "fsdp")
    per_token = P("fsdp", "ctx")
    vector = P("fsdp")
    weights = (by_rows, by_rows, by_rows, by_columns, by_rows, by_rows, by_columns)
    return jax.shard_map(
        local,
        mesh=mesh,
        in_specs=(tokens, *weights, vector, vector, vector, vector, per_token, per_token, tokens),
        out_specs=(tokens, tokens, *weights, vector, vector, vector, vector),
        check_vma=False,
    )
```

time: 1560 us -> 1170 us (0.75)
  Pallas kernels: 0 us -> 739 us
  waiting for transfers between devices: 1010 us -> 300 us
  matrix products: 231 us -> 44.4 us
  local copies, waits for them, and re-layouts: 153 us -> 43.5 us
  blocking collectives: 70.5 us -> 0 us
  other arithmetic: 70.8 us -> 22.4 us
    pallas_call x0 -> x11, Pallas kernels: none -> 739 us  [the longest x1 139 us: last(): pl.pallas_call(functools.partial(last_kernel, pl.ds(0, width)), out_shape...]
    all_gather x8 -> x6, waiting for transfers between devices: 542 us -> 152 us  [the longest x4 113 us: gather_parts(): return lax.all_gather(piece, 'ctx', axis=0)]
    reduce_scatter x4 -> x0, waiting for transfers between devices: 314 us -> none  [scatter_ctx(): lax.psum_scatter(partial.astype(BF16), 'ctx', scatter_dimension=0, tiled=...]
    dot_general x16 -> x0, matrix products: 193 us -> none  [the longest x5 55.5 us: dot(): return jnp.dot(left, right, preferred_element_type=F32)]
    all_gather x3 -> x1, waiting for transfers between devices: 65.5 us -> 0.02 us  [gather_rows(): return lax.all_gather(piece, 'fsdp', axis=0, tiled=True)]
    reduce_scatter x2 -> x4, waiting for transfers between devices: 87 us -> 146 us  [sum_rows(): lax.psum_scatter(grad.astype(BF16), 'fsdp', scatter_dimension=0, tiled=True)]
    unnamed x143 -> x53, local copies, waits for them, and re-layouts: 74.7 us -> 18.1 us
    reshape x8 -> x4, local copies, waits for them, and re-layouts: 60.6 us -> 7.67 us  [the longest x1 4.79 us: local(): grad_down.reshape(feed_width, shards, rows).transpose(1, 0, 2)]
  transfers between devices with their start and end apart: 17 -> 11, of which waited for: 14 -> 6; matrix products, arithmetic and copies ran while one was open for 13% -> 4% of each run, Pallas kernels for 0% -> 39%
where the time goes in v2:
time: 1170 us; the launch traced here: 1160 us
  Pallas kernels  739 us (63%)
  waiting for transfers between devices  300 us (26%)
  matrix products  44.4 us (4%)
  local copies, waits for them, and re-layouts  43.5 us (4%)
  other arithmetic  22.4 us (2%)
  between operations  14.6 us (1%)
    reduce_scatter x4, waiting for transfers between devices, sum_rows(): lax.psum_scatter(grad.astype(BF16), 'fsdp', scatter_dimension=0, tiled=True)  146 us
    pallas_call x1, Pallas kernels, last(): pl.pallas_call(functools.partial(last_kernel, pl.ds(0, width)), out_shape...  139 us
    pallas_call x1, Pallas kernels, first(): pl.pallas_call(functools.partial(first_kernel, D // shards, width), out_s...  124 us
    pallas_call x1, Pallas kernels, attention_out(): pl.pallas_call(functools.partial(out_kernel, pl.ds(weights.shape[1] - wid...  116 us
    all_gather x4, waiting for transfers between devices, gather_parts(): return lax.all_gather(piece, 'ctx', axis=0)  113 us
    pallas_call x1, Pallas kernels, turn(): pl.pallas_call(functools.partial(turn_kernel, pl.ds(weights.shape[1] - wi...  107 us
    pallas_call x1, Pallas kernels, feed(): pl.pallas_call(functools.partial(feed_kernel, width), out_shape=(jax.Shap...  87.2 us
    pallas_call x1, Pallas kernels, feed_back(): pl.pallas_call(functools.partial(feed_back_kernel, pl.ds(0, width)), out_...  85.3 us
  transfers between devices with their start and end apart: 11, of which 6 were waited for; matrix products, arithmetic and copies ran while one was open for 4% of the time, Pallas kernels for 39%

profile of v2, /device:TPU:0, one launch (start us, length us, event | category | flops | bytes accessed | tf_op | source)
XLA Modules:
  0.0 1164.3 jit_solution(10572281505919286226)
XLA Ops:
  7.2 1.2 constant_dynamic-slice_fusion
  8.4 0.3 copy.45
  8.7 1.5 constant_dynamic-slice_fusion.1
  10.3 1.6 pad_maximum_fusion
  11.9 1.0 constant_dynamic-slice_fusion.3
  12.9 0.1 copy.44
  13.0 0.6 pad.10.refs_2_
  13.7 0.1 concatenate.18
  13.8 0.6 bitcast_convert_fusion.2.refs_1_
  14.4 1.0 constant_dynamic-slice_fusion.6
  15.3 1.0 constant_dynamic-slice_fusion.4
  16.3 0.9 pad_maximum_fusion.3.refs_3_
  17.3 124.2 %gather_normed.1 = (bf16[8,256,2048]{2,1,0:T(8,128)(2,1)}, f32[8,256,512]{2,1,0:T(8,128)}, bf16[2048,768]{1,0:T(8,128)(2,1)}, f32[8,2048]{1,0:T(8,128)}, f32[4,16,128]{2,1,0:T(8,128)}, /*index=5*/s32[8,8,256]{2,1,0:T(8,128)}) custom-call(bf16[256,2048]{1,0:T(8,128)(2,1)} %bitcast.60, f32[16,128]{1,0:T(8,128)} %bitcast_convert_fusion.2.refs_1_, ...), custom_call_target="tpu_custom_call" | custom-call | tf_op jit(solution)/shard_map/gather_normed/pallas_call | solution.py:450
  141.6 0.8 copy.48
  142.6 0.9 fusion.2
  143.5 1.3 copy.35.id_column.refs_10_
  145.0 3.7 fusion
  148.8 0.3 pad_maximum_fusion.1.cosine.refs_7_
  149.1 0.3 pad_maximum_fusion.2.sine.refs_8_
  149.5 26.9 %attention.1 = (bf16[2048,256]{1,0:T(8,128)(2,1)S(1)}, bf16[2048,128]{1,0:T(8,128)(2,1)S(1)}, bf16[2048,128]{1,0:T(8,128)(2,1)S(1)}, bf16[2048,256]{1,0:T(8,128)(2,1)S(1)}, f32[8,2048]{1,0:T(8,128)S(1)}) custom-call(f32[2048,512]{1,0:T(8,128)} %bitcast.56, f32[2048,128]{1,0:T(8,128)S(1)} %pad_maximum_fusion.1.cosine.refs_7_, ...), custom_call_target="tpu_custom_call" | custom-call | tf_op jit(solution)/shard_map/attention/pallas_call | solution.py:865
  176.4 1.0 copy-done
  177.3 1.0 copy-done.8
  178.3 0.8 copy-done.11
  179.1 115.9 %attention_out.1 = (f32[256,2048]{1,0:T(8,128)}, bf16[256,2048]{1,0:T(8,128)(2,1)}) custom-call(bf16[8,256,256]{2,1,0:T(8,128)(2,1)} %bitcast.47, bf16[2048,768]{1,0:T(8,128)(2,1)} %get-tuple-element.52.refs_1_, bf16[256,2048]{1,0:T(8,128)(2,1)} %bitcast.61, f32[8,2048]{1,0:T(8,128)} %get-tuple-element.53.refs_3_.refs_4_), custom_call_target="tpu_custom_call" | custom-call | tf_op jit(solution)/shard_map/attention_out/pallas_call | solution.py:504
  295.0 87.2 %feed.1 = (bf16[8,256,2048]{2,1,0:T(8,128)(2,1)}, bf16[8,256,768]{2,1,0:T(8,128)(2,1)}, bf16[8,256,1536]{2,1,0:T(8,128)(2,1)}) custom-call(bf16[256,2048]{1,0:T(8,128)(2,1)} %get-tuple-element.54.refs_0_, bf16[8,256,2048]{2,1,0:T(8,128)(2,1)} %bitcast.63, bf16[2048,2304]{1,0:T(8,128)(2,1)} %all-gather.12.cloned.1.call-done.refs_2_.refs_1_.refs_3_), custom_call_target="tpu_custom_call" | custom-call | tf_op jit(solution)/shard_map/feed/pallas_call | solution.py:562
  382.3 12.1 %bitcast_convert_fusion.1 = bf16[768,2048]{1,0:T(8,128)(2,1)} fusion(bf16[8,256,768]{2,1,0:T(8,128)(2,1)} %get-tuple-element.58.refs_2_, bf16[8,256,2048]{2,1,0:T(8,128)(2,1)} %bitcast.64), kind=kOutput, calls=%fused_computation.1 | convolution fusion | flops 6444023808 | bytes 14680064 | tf_op jit(solution)/shard_map/dot_general | solution.py:32
  394.4 15.7 %bitcast_convert_fusion = bf16[2048,1536]{1,0:T(8,128)(2,1)} fusion(bf16[8,256,2048]{2,1,0:T(8,128)(2,1)S(1)} %copy-done.23, bf16[8,256,1536]{2,1,0:T(8,128)(2,1)S(1)} %copy-done.14), kind=kOutput, calls=%fused_computation | convolution fusion | flops 12888047616 | bytes 20971520 | tf_op jit(solution)/shard_map/dot_general | solution.py:32
  410.1 85.3 %feed_back.1 = (f32[256,2048]{1,0:T(8,128)}, bf16[256,2048]{1,0:T(8,128)(2,1)}, f32[8,2048]{1,0:T(8,128)}) custom-call(bf16[8,256,1536]{2,1,0:T(8,128)(2,1)} %get-tuple-element.59.refs_0_, bf16[2048,2304]{1,0:T(8,128)(2,1)} %all-gather.12.cloned.1.call-done.refs_2_.refs_1_.refs_3_, f32[256,2048]{1,0:T(8,128)} %get-tuple-element.60.refs_2_.refs_4_, ...), custom_call_target="tpu_custom_call" | custom-call | tf_op jit(solution)/shard_map/feed_back/pallas_call | solution.py:627
  495.4 107.1 %turn.1 = (bf16[8,256,2048]{2,1,0:T(8,128)(2,1)}, bf16[8,256,256]{2,1,0:T(8,128)(2,1)}, bf16[256,2048]{1,0:T(8,128)(2,1)}) custom-call(bf16[256,2048]{1,0:T(8,128)(2,1)} %get-tuple-element.61.refs_0_, bf16[2048,768]{1,0:T(8,128)(2,1)} %get-tuple-element.52.refs_1_, bf16[8,256,768]{2,1,0:T(8,128)(2,1)} %get-tuple-element.58.refs_2_, ...), custom_call_target="tpu_custom_call" | custom-call | tf_op jit(solution)/shard_map/turn/pallas_call | solution.py:684
  602.5 6.7 convolution_convert_fusion.1
  609.2 2.7 reshape.103
  611.9 2.4 copy.40
  614.4 1.2 copy-done.9
  615.6 1.2 copy-done.10
  616.9 1.0 copy-done.12
  617.9 37.8 %attention_back.1 = (bf16[2048,512]{1,0:T(8,128)(2,1)}, f32[8,128]{1,0:T(8,128)S(1)}) custom-call(bf16[2048,256]{1,0:T(8,128)(2,1)S(1)} %copy-done.9, bf16[2048,128]{1,0:T(8,128)(2,1)S(1)} %get-tuple-element.64.refs_1_, bf16[2048,128]{1,0:T(8,128)(2,1)S(1)} %copy-done.12, bf16[2048,256]{1,0:T(8,128)(2,1)S(1)} %bitcast.51, ...), custom_call_target="tpu_custom_call" | custom-call | tf_op jit(solution)/shard_map/attention_back/pallas_call | solution.py:941
  655.7 0.6 copy-done.13
  656.3 9.9 convolution_convert_fusion
  666.1 0.3 reduce-scatter.11.cloned.1.call-start
  666.4 4.8 reshape.105
  671.2 2.3 copy.41
  673.6 0.5 reduce-scatter.9.cloned.1.call-update
  674.2 0.7 all-gather.14.cloned.1.call-update
  674.9 24.8 %reduce-scatter.5.cloned.1.call-done = bf16[512,512]{1,0:T(8,128)(2,1)} async-done(((bf16[2048,512]{1,0:T(8,128)(2,1)}), bf16[512,512]{1,0:T(8,128)(2,1)}) %reduce-scatter.5.cloned.1.call-update) | async-done | bytes 524304 | tf_op jit(solution)/shard_map/reduce_scatter | solution.py:1039
  699.8 47.3 %reduce-scatter.11.cloned.1.call-done = bf16[768,512]{1,0:T(8,128)(2,1)} async-done(((bf16[3072,512]{1,0:T(8,128)(2,1)}), bf16[768,512]{1,0:T(8,128)(2,1)}) %reduce-scatter.11.cloned.1.call-update) | async-done | bytes 786448 | tf_op jit(solution)/shard_map/reduce_scatter | solution.py:1039
  747.2 73.6 %reduce-scatter.9.cloned.1.call-done = bf16[512,1536]{1,0:T(8,128)(2,1)} async-done(((bf16[2048,1536]{1,0:T(8,128)(2,1)}), bf16[512,1536]{1,0:T(8,128)(2,1)}) %reduce-scatter.9.cloned.1.call-update) | async-done | bytes 1572880 | tf_op jit(solution)/shard_map/reduce_scatter | solution.py:1039
  820.7 2.6 fusion.1
  823.4 0.7 all-gather.24.cloned.1.call-update
  824.1 138.9 %last.1 = (f32[256,2048]{1,0:T(8,128)}, f32[16,128]{1,0:T(8,128)}) custom-call(bf16[8,256,512]{2,1,0:T(8,128)(2,1)} %bitcast.71, bf16[2048,768]{1,0:T(8,128)(2,1)} %get-tuple-element.52.refs_1_, bf16[256,2048]{1,0:T(8,128)(2,1)} %bitcast.62, f32[256,2048]{1,0:T(8,128)} %get-tuple-element.69.refs_3_, f32[8,2048]{1,0:T(8,128)} %get-tuple-element.53.refs_3_.refs_4_, ...), custom_call_target="tpu_custom_call" | custom-call | tf_op jit(solution)/shard_map/last/pallas_call | solution.py:781
  963.1 1.4 fusion.4
  964.4 1.3 slice_bitcast_fusion
  965.7 4.2 convert_element_type.45
  969.9 2.2 copy-done.7
  972.1 4.3 spread_heads.1
  976.5 39.0 %all-gather.16.cloned.1.call-done = bf16[6144,512]{1,0:T(8,128)(2,1)} async-done(((bf16[768,512]{1,0:T(8,128)(2,1)}), bf16[6144,512]{1,0:T(8,128)(2,1)}) %all-gather.16.cloned.1.call-update) | async-done | bytes 6291472 | tf_op jit(solution)/shard_map/all_gather | solution.py:1108
  1015.4 9.7 convert_element_type.46
  1025.1 55.8 %all-gather.22.cloned.1.call-done = bf16[4096,768]{1,0:T(8,128)(2,1)} async-done(((bf16[512,768]{1,0:T(8,128)(2,1)}), bf16[4096,768]{1,0:T(8,128)(2,1)}) %all-gather.22.cloned.1.call-update) | async-done | bytes 6291472 | tf_op jit(solution)/shard_map/all_gather | solution.py:1042
  1080.9 2.8 copy-done.5
  1083.7 5.5 spread.2
  1089.2 57.4 %all-gather.24.cloned.1.call-done = bf16[4096,768]{1,0:T(8,128)(2,1)} async-done(((bf16[512,768]{1,0:T(8,128)(2,1)}), bf16[4096,768]{1,0:T(8,128)(2,1)}) %all-gather.24.cloned.1.call-update) | async-done | bytes 6291472 | tf_op jit(solution)/shard_map/all_gather | solution.py:1042
  1146.6 2.8 copy-done.6
  1149.4 5.6 spread.3
  1155.0 1.0 copy.51
  1156.0 1.3 copy.52
  (69 shorter events, 1.1 us)
Async XLA Ops:
  7.2 287.8 %all-gather.12.cloned.1.call-start = ((), (), s32[]{:S(2)}) async-start(), calls=%async_computation.4 | async-start | bytes 11796480 | tf_op jit(solution)/shard_map/all_gather | solution.py:1036
  10.2 2.8 copy-start.19
  10.2 2.8 copy-start.20
  10.2 3.4 copy-start.17
  10.2 3.4 copy-start.18
  10.2 3.4 copy-start.21
  10.3 3.4 copy-start.22
  11.8 283.2 %all-gather.18.cloned.1.call-start = ((), (), s32[]{:S(2)}) async-start(), calls=%async_computation.11 | async-start | bytes 9437184 | tf_op jit(solution)/shard_map/all_gather | solution.py:1042
  141.5 532.6 %reduce-scatter.7.cloned.1.call-start = ((), (), s32[]{:S(2)}) async-start(), calls=%async_computation.6 | async-start | bytes 1310720 | tf_op jit(solution)/shard_map/reduce_scatter | solution.py:1039
  149.1 27.2 %copy-start.3 = (f32[2048,128]{1,0:T(8,128)}, f32[2048,128]{1,0:T(8,128)S(1)}, u32[]{:S(2)}) copy-start(f32[2048,128]{1,0:T(8,128)S(1)} %pad_maximum_fusion.1.cosine.refs_7_) | copy-start | bytes 3145732
  149.5 26.9 %copy-start.2 = (f32[2048,128]{1,0:T(8,128)}, f32[2048,128]{1,0:T(8,128)S(1)}, u32[]{:S(2)}) copy-start(f32[2048,128]{1,0:T(8,128)S(1)} %pad_maximum_fusion.2.sine.refs_8_) | copy-start | bytes 3145732
  176.4 1.0 copy-start
  177.3 1.0 copy-start.8
  178.3 0.8 copy-start.11
  382.3 12.1 %copy-start.14 = (bf16[8,256,1536]{2,1,0:T(8,128)(2,1)S(1)}, bf16[8,256,1536]{2,1,0:T(8,128)(2,1)}, u32[]{:S(2)}) copy-start(bf16[8,256,1536]{2,1,0:T(8,128)(2,1)} %get-tuple-element.59.refs_0_) | copy-start | bytes 18874372
  382.3 12.1 %copy-start.23 = (bf16[8,256,2048]{2,1,0:T(8,128)(2,1)S(1)}, bf16[8,256,2048]{2,1,0:T(8,128)(2,1)}, u32[]{:S(2)}) copy-start(bf16[8,256,2048]{2,1,0:T(8,128)(2,1)} %get-tuple-element.57) | copy-start | bytes 25165828
  495.3 107.1 %copy-start.1 = (bf16[2048,256]{1,0:T(8,128)(2,1)S(1)}, bf16[2048,256]{1,0:T(8,128)(2,1)}, u32[]{:S(2)}) copy-start(bf16[2048,256]{1,0:T(8,128)(2,1)} %copy-done) | copy-start | bytes 3145732
  609.2 5.2 copy-start.4
  614.3 85.4 %reduce-scatter.5.cloned.1.call-start = ((), (), s32[]{:S(2)}) async-start(), calls=%async_computation.5 | async-start | bytes 2621440 | tf_op jit(solution)/shard_map/reduce_scatter | solution.py:1039
  614.4 1.2 copy-start.9
  615.6 1.2 copy-start.10
  616.9 1.0 copy-start.12
  655.7 0.6 copy-start.13
  666.1 80.9 %reduce-scatter.11.cloned.1.call-start = ((), (), s32[]{:S(2)}) async-start(), calls=%async_computation.9 | async-start | bytes 3932160 | tf_op jit(solution)/shard_map/reduce_scatter | solution.py:1039
  673.5 147.2 %reduce-scatter.9.cloned.1.call-start = ((), (), s32[]{:S(2)}) async-start(), calls=%async_computation.8 | async-start | bytes 7864320 | tf_op jit(solution)/shard_map/reduce_scatter | solution.py:1039
  674.1 291.6 %all-gather.14.cloned.1.call-start = ((), (), s32[]{:S(2)}) async-start(), calls=%async_computation.7 | async-start | bytes 2359296 | tf_op jit(solution)/shard_map/all_gather | solution.py:1149
  674.9 295.1 %all-gather.20.cloned.1.call-start = ((), (), s32[]{:S(2)}) async-start(), calls=%async_computation.12 | async-start | bytes 4718592 | tf_op jit(solution)/shard_map/all_gather | solution.py:1042
  699.7 315.7 %all-gather.16.cloned.1.call-start = ((), (), s32[]{:S(2)}) async-start(), calls=%async_computation.10 | async-start | bytes 7077888 | tf_op jit(solution)/shard_map/all_gather | solution.py:1108
  747.1 333.8 %all-gather.22.cloned.1.call-start = ((), (), s32[]{:S(2)}) async-start(), calls=%async_computation.13 | async-start | bytes 7077888 | tf_op jit(solution)/shard_map/all_gather | solution.py:1042
  823.4 323.2 %all-gather.24.cloned.1.call-start = ((), (), s32[]{:S(2)}) async-start(), calls=%async_computation.14 | async-start | bytes 7077888 | tf_op jit(solution)/shard_map/all_gather | solution.py:1042
  969.9 2.2 copy-start.7
  1080.9 2.8 copy-start.5
  1146.6 2.8 copy-start.6
  1149.4 5.6 copy-start.16
  1149.4 6.6 copy-start.15
Sparse Core Ops, SparseCore 0:
  12.0 129.7 all-gather.11
  143.4 111.9 all-gather.17
  614.5 25.9 reduce-scatter.6
  666.3 33.3 reduce-scatter.4
  703.1 43.9 reduce-scatter.10
  750.5 70.1 reduce-scatter.8
  822.3 40.2 all-gather.13
  864.2 81.1 all-gather.19
  947.0 68.3 all-gather.15
  1017.5 63.3 all-gather.21
  1083.2 63.3 all-gather.23

commit v3 on v2

--- a/solution.py
+++ b/solution.py
@@ -4,6 +4,7 @@
 import jax.numpy as jnp
 from jax import lax
 from jax.experimental import pallas as pl
+from jax.experimental.layout import Layout, with_layout_constraint
 from jax.experimental.pallas import tpu as pltpu
 from jax.sharding import PartitionSpec as P
 
@@ -378,6 +379,12 @@
     )
 
 
+def cost(microseconds):
+    return pl.CostEstimate(
+        flops=int(microseconds * 1.15e9), bytes_accessed=1024, transcendentals=0
+    )
+
+
 def copy_in(source, target, sem):
     copy = pltpu.make_async_copy(source, target, sem)
     copy.start()
@@ -425,19 +432,14 @@
 
     row_blocks(x.shape[0], norm)
 
-    def consume(piece):
+    gather = Gather(land, sems)
+    loop(chips, gather.step)
+    loop(shards, lambda i: weight_copy(i, behind(i)).wait_recv())
+
+    def project(piece):
         proj[piece] = dot(land[piece], weights[:, :width])
 
-    gather = Gather(land, sems, consume, late=True)
-
-    def step(index):
-        @pl.when(index == 1)
-        def _():
-            loop(shards, lambda i: weight_copy(i, behind(i)).wait_recv())
-
-        gather.step(index)
-
-    loop(chips, step)
+    loop(2 * chips, project)
     gather.finish()
     loop(shards, lambda i: gain_copy(i, shard).wait_send())
     loop(shards, lambda i: weight_copy(i, shard).wait_send())
@@ -464,6 +466,7 @@
         + [pltpu.SemaphoreType.DMA((parts,))] * 2
         + [pltpu.SemaphoreType.DMA((shards,))] * 2,
         compiler_params=params(0, 60),
+        cost_estimate=cost(85),
         name="gather_normed",
     )(hidden, gains, tokens, part)
 
@@ -512,6 +515,7 @@
         scratch_shapes=[VMEM((D, width), BF16), pltpu.SemaphoreType.DMA, VMEM((count, D), F32)]
         + scatter_scratch(parts // 2, count),
         compiler_params=params(1, 60),
+        cost_estimate=cost(90),
         name="attention_out",
     )(context, weights, hidden, gain_rows)
 
@@ -576,6 +580,7 @@
         ]
         + gather_scratch(parts // 2),
         compiler_params=params(2, 60),
+        cost_estimate=cost(90),
         name="feed",
     )(normed, grads, weights)
 
@@ -636,6 +641,7 @@
         scratch_shapes=[VMEM((D, width), BF16), pltpu.SemaphoreType.DMA, VMEM((count, D), F32)]
         + scatter_scratch(parts // 2, count),
         compiler_params=params(3, 60),
+        cost_estimate=cost(86),
         name="feed_back",
     )(back, weights, middle, grad, gain_rows)
 
@@ -702,6 +708,7 @@
         + gather_scratch(parts // 2)
         + scatter_scratch(parts // 2, count),
         compiler_params=params(4, 62),
+        cost_estimate=cost(107),
         name="turn",
     )(low, weights, activation, feed_weights, middle)
 
@@ -800,6 +807,7 @@
         + [pltpu.SemaphoreType.DMA((parts,))] * 2
         + scatter_scratch(parts // 2, count),
         compiler_params=params(5, 60),
+        cost_estimate=cost(90),
         name="last",
     )(back, weights, hidden, grad_middle, gain_rows, gain_two, gain_heads)
 
@@ -874,6 +882,7 @@
         in_specs=[WHOLE] * 6,
         out_specs=(WHOLE,) * 5,
         compiler_params=pltpu.CompilerParams(vmem_limit_bytes=48 * 1024 * 1024),
+        cost_estimate=cost(27),
         name="attention",
     )(proj, cosine, sine, gain, id_column, id_row)
 
@@ -952,31 +961,43 @@
             VMEM((QUERY_TILE, HEAD_SIZE), F32),
         ],
         compiler_params=pltpu.CompilerParams(vmem_limit_bytes=48 * 1024 * 1024),
+        cost_estimate=cost(38),
         name="attention_back",
     )(*operands)
 
 
-def spread_kernel(source, target):
-    target[...] = source[0].astype(F32)
-
-
-def spread_columns(stacked):
-    parts, rows, width = stacked.shape
+def spread_feed_kernel(width, source, gate, up, down):
+    gate[...] = source[0, :, :width].astype(F32)
+    up[...] = source[0, :, width : 2 * width].astype(F32)
+    down[...] = source[0, :, 2 * width :].astype(F32).T
+
+
+def spread_feed(stacked):
+    parts, rows, total = stacked.shape
+    width = total // 3
+    across = jax.ShapeDtypeStruct((rows, parts * width), F32)
     return pl.pallas_call(
-        spread_kernel,
-        out_shape=jax.ShapeDtypeStruct((rows, parts * width), F32),
+        functools.partial(spread_feed_kernel, width),
+        out_shape=(across, across, jax.ShapeDtypeStruct((parts * width, rows), F32)),
         grid=(parts,),
-        in_specs=[pl.BlockSpec((1, rows, width), lambda i: (i, 0, 0))],
-        out_specs=pl.BlockSpec((rows, width), lambda i: (0, i)),
+        in_specs=[pl.BlockSpec((1, rows, total), lambda i: (i, 0, 0))],
+        out_specs=(
+            pl.BlockSpec((rows, width), lambda i: (0, i)),
+            pl.BlockSpec((rows, width), lambda i: (0, i)),
+            pl.BlockSpec((width, rows), lambda i: (i, 0)),
+        ),
         compiler_params=pltpu.CompilerParams(vmem_limit_bytes=32 * 1024 * 1024),
-        name="spread",
+        name="spread_feed",
     )(stacked)
 
 
-def spread_heads_kernel(width, source, query, key, value):
+def spread_heads_kernel(width, source, query, key, value, out):
+    second = width + HEAD_SIZE
+    third = second + HEAD_SIZE
     query[...] = source[0, :, :width].astype(F32)
-    key[...] = source[0, :, width : width + HEAD_SIZE].astype(F32)
-    value[...] = source[0, :, width + HEAD_SIZE :].astype(F32)
+    key[...] = source[0, :, width:second].astype(F32)
+    value[...] = source[0, :, second:third].astype(F32)
+    out[...] = source[0, :, third:].astype(F32).T
 
 
 def spread_heads(stacked, width):
@@ -984,13 +1005,19 @@
     widths = (width, HEAD_SIZE, HEAD_SIZE)
     return pl.pallas_call(
         functools.partial(spread_heads_kernel, width),
-        out_shape=tuple(jax.ShapeDtypeStruct((rows, parts * w), F32) for w in widths),
+        out_shape=tuple(jax.ShapeDtypeStruct((rows, parts * w), F32) for w in widths)
+        + (jax.ShapeDtypeStruct((parts * width, rows), F32),),
         grid=(parts,),
         in_specs=[pl.BlockSpec((1, rows, total), lambda i: (i, 0, 0))],
-        out_specs=tuple(pl.BlockSpec((rows, w), lambda i: (0, i)) for w in widths),
+        out_specs=tuple(pl.BlockSpec((rows, w), lambda i: (0, i)) for w in widths)
+        + (pl.BlockSpec((width, rows), lambda i: (i, 0)),),
         compiler_params=pltpu.CompilerParams(vmem_limit_bytes=32 * 1024 * 1024),
         name="spread_heads",
     )(stacked)
+
+
+def by_row(array):
+    return with_layout_constraint(array, Layout(major_to_minor=(0, 1)))
 
 
 def own_columns(array, index, width):
@@ -1096,18 +1123,19 @@
     flat_grad = grad_all.reshape(tokens, D)
     flat_back = back.reshape(tokens, 2 * feed_width)
     flat_activation = activation.reshape(tokens, feed_width)
-    grad_gate_up = tdot(normed_two_all.reshape(tokens, D), flat_back).astype(BF16)
-    grad_down = tdot(flat_activation, flat_grad).astype(BF16)
-    back, grad_gate_up, grad_down = lax.optimization_barrier((back, grad_gate_up, grad_down))
-    grad_gate_up = sum_rows(grad_gate_up)
-    grad_down = sum_rows(
-        grad_down.reshape(feed_width, shards, rows).transpose(1, 0, 2).reshape(shards * feed_width, rows)
-    )
-    gate_parts = gather_parts(grad_gate_up[:, :feed_width])
-    up_parts = gather_parts(grad_gate_up[:, feed_width:])
-    grad_weight_down = lax.all_gather(grad_down, "ctx", axis=0, tiled=True).astype(F32)
+    feed_grad = jnp.concatenate(
+        [
+            by_row(tdot(normed_two_all.reshape(tokens, D), flat_back).astype(BF16)),
+            by_row(tdot(flat_grad, flat_activation).astype(BF16)),
+        ],
+        axis=1,
+    )
+    back, feed_grad = lax.optimization_barrier((back, feed_grad))
+    feed_shard = sum_rows(feed_grad)
 
     grad_middle, low, gain_two = feed_back(back, feed_weight, middle, grad, gain_rows)
+    low, feed_shard = lax.optimization_barrier((low, feed_shard))
+    feed_parts = gather_parts(feed_shard)
     low_all, context_grad, hidden_out = turn(low, heads_weight, activation, feed_weight, middle, width)
 
     context_grad = context_grad.reshape(tokens, width)
@@ -1126,6 +1154,15 @@
         id_column,
         id_row,
     )
+    head_grad = jnp.concatenate(
+        [
+            by_row(tdot(normed_all.reshape(tokens, D), grad_qkv).astype(BF16)),
+            by_row(tdot(low_all.reshape(tokens, D), context).astype(BF16)),
+        ],
+        axis=1,
+    )
+    grad_qkv, head_grad, feed_parts = lax.optimization_barrier((grad_qkv, head_grad, feed_parts))
+    head_shard = sum_rows(head_grad)
     grad_hidden, gain_sums = last(
         grad_qkv.reshape(parts, count, -1),
         heads_weight,
@@ -1137,41 +1174,25 @@
         shards,
     )
 
-    grad_heads = sum_rows(tdot(normed_all.reshape(tokens, D), grad_qkv))
-    grad_out_weight = sum_rows(
-        tdot(context, low_all.reshape(tokens, D))
-        .astype(BF16)
-        .reshape(width, shards, rows)
-        .transpose(1, 0, 2)
-        .reshape(shards * width, rows)
-    )
-    head_parts = gather_parts(grad_heads)
-    grad_weight_out = lax.all_gather(grad_out_weight, "ctx", axis=0, tiled=True).astype(F32)
-
+    head_parts = gather_parts(head_shard)
     gain_sums = gain_sums.reshape(-1)
-    def columns(stacked):
-        return stacked.astype(F32).transpose(1, 0, 2).reshape(rows, -1)
-
-    def key_columns(stacked):
-        summed = stacked.astype(F32).reshape(KEY_VALUE_HEADS, sharers, rows, HEAD_SIZE).sum(axis=1)
-        return summed.transpose(1, 0, 2).reshape(rows, -1)
-
-    if sharers == 1:
-        grad_query, grad_key, grad_value = spread_heads(head_parts, width)
-    else:
-        grad_query = columns(head_parts[:, :, :width])
-        grad_key = key_columns(head_parts[:, :, width : width + HEAD_SIZE])
-        grad_value = key_columns(head_parts[:, :, width + HEAD_SIZE :])
+    grad_gate, grad_up, grad_down = spread_feed(feed_parts)
+    grad_query, grad_key, grad_value, grad_out_weight = spread_heads(head_parts, width)
+    if sharers > 1:
+        grad_key, grad_value = (
+            part.reshape(rows, KEY_VALUE_HEADS, sharers, HEAD_SIZE).sum(axis=2).reshape(rows, -1)
+            for part in (grad_key, grad_value)
+        )
     return (
         hidden_out[None],
         grad_hidden[None],
         grad_query,
         grad_key,
         grad_value,
-        grad_weight_out,
-        spread_columns(gate_parts),
-        spread_columns(up_parts),
-        grad_weight_down,
+        grad_out_weight,
+        grad_gate,
+        grad_up,
+        grad_down,
         gain_sums[:rows],
         gain_sums[rows : 2 * rows],
         lax.dynamic_slice_in_dim(gain_sums, 2 * rows + shard * head_rows, head_rows),

time: 1170 us -> 1020 us (0.87)
  waiting for transfers between devices: 300 us -> 50.7 us
  Pallas kernels: 739 us -> 874 us
  local copies, waits for them, and re-layouts: 43.5 us -> 26.1 us
    pallas_call x1, Pallas kernels: 107 us -> 254 us  [turn(): pl.pallas_call(functools.partial(turn_kernel, pl.ds(weights.shape[1] - wi...]
    all_gather x4 -> x3, waiting for transfers between devices: 113 us -> 0.02 us  [gather_parts(): return lax.all_gather(piece, 'ctx', axis=0)]
    reduce_scatter x4 -> x2, waiting for transfers between devices: 146 us -> 50.6 us  [sum_rows(): lax.psum_scatter(grad.astype(BF16), 'fsdp', scatter_dimension=0, tiled=True)]
    all_gather x2 -> x0, waiting for transfers between devices: 39 us -> none  [the longest x1 39 us: local(): lax.all_gather(grad_down, 'ctx', axis=0, tiled=True).astype(F32)]
    pallas_call x1, Pallas kernels: 124 us -> 93.3 us  [first(): pl.pallas_call(functools.partial(first_kernel, D // shards, width), out_s...]
    pallas_call x1, Pallas kernels: 116 us -> 143 us  [attention_out(): pl.pallas_call(functools.partial(out_kernel, pl.ds(weights.shape[1] - wid...]
    pallas_call x1, Pallas kernels: 139 us -> 124 us  [last(): pl.pallas_call(functools.partial(last_kernel, pl.ds(0, width)), out_shape...]
    convert_element_type x2 -> x0, other arithmetic: 13.9 us -> none  [the longest x1 9.67 us: local(): lax.all_gather(grad_down, 'ctx', axis=0, tiled=True).astype(F32)]
  transfers between devices with their start and end apart: 11 -> 6, of which waited for: 6 -> 2; matrix products, arithmetic and copies ran while one was open for 4% -> 3% of each run, Pallas kernels for 39% -> 76%
where the time goes in v3:
time: 1020 us
  Pallas kernels  874 us (86%)
  waiting for transfers between devices  50.7 us (5%)
  matrix products  37.1 us (4%)
  local copies, waits for them, and re-layouts  26.1 us (3%)
  other arithmetic  14.9 us (1%)
  between operations  14.6 us (1%)
    pallas_call x1, Pallas kernels, turn(): pl.pallas_call(functools.partial(turn_kernel, pl.ds(weights.shape[1] - wi...  254 us
    pallas_call x1, Pallas kernels, attention_out(): pl.pallas_call(functools.partial(out_kernel, pl.ds(weights.shape[1] - wid...  143 us
    pallas_call x1, Pallas kernels, last(): pl.pallas_call(functools.partial(last_kernel, pl.ds(0, width)), out_shape...  124 us
    pallas_call x1, Pallas kernels, first(): pl.pallas_call(functools.partial(first_kernel, D // shards, width), out_s...  93.3 us
    pallas_call x1, Pallas kernels, feed(): pl.pallas_call(functools.partial(feed_kernel, width), out_shape=(jax.Shap...  91.1 us
    pallas_call x1, Pallas kernels, feed_back(): pl.pallas_call(functools.partial(feed_back_kernel, pl.ds(0, width)), out_...  86.2 us
    reduce_scatter x2, waiting for transfers between devices, sum_rows(): lax.psum_scatter(grad.astype(BF16), 'fsdp', scatter_dimension=0, tiled=True)  50.6 us
    pallas_call x1, Pallas kernels, attention_back(): pl.pallas_call(functools.partial(attention_back_kernel, heads), out_shape...  37.4 us
  transfers between devices with their start and end apart: 6, of which 2 were waited for; matrix products, arithmetic and copies ran while one was open for 3% of the time, Pallas kernels for 76%

profile of v3, /device:TPU:0, one launch (start us, length us, event | category | flops | bytes accessed | tf_op | source)
XLA Modules:
  0.0 1017.3 jit_solution(12820806739176523555)
XLA Ops:
  7.2 0.0 all-gather.8.cloned.1.call-start
  7.2 1.2 constant_dynamic-slice_fusion
  8.4 0.3 copy.41
  8.7 1.5 constant_dynamic-slice_fusion.1
  10.3 1.6 pad_maximum_fusion.2
  11.8 0.0 all-gather.8.cloned.1.call-update
  11.8 0.0 all-gather.10.cloned.1.call-start
  11.9 1.0 constant_dynamic-slice_fusion.3
  12.9 0.1 copy.40
  13.0 0.6 pad.10.refs_2_
  13.7 0.1 concatenate.24
  13.8 0.6 bitcast_convert_fusion.2.refs_1_
  14.4 1.0 constant_dynamic-slice_fusion.6
  15.3 1.0 constant_dynamic-slice_fusion.4
  16.3 0.9 pad_maximum_fusion.5.refs_3_
  17.3 93.3 %gather_normed.1 = (bf16[8,256,2048]{2,1,0:T(8,128)(2,1)}, f32[8,256,512]{2,1,0:T(8,128)}, bf16[2048,768]{1,0:T(8,128)(2,1)}, f32[8,2048]{1,0:T(8,128)}, f32[4,16,128]{2,1,0:T(8,128)}, /*index=5*/s32[8,8,256]{2,1,0:T(8,128)}) custom-call(bf16[256,2048]{1,0:T(8,128)(2,1)} %bitcast.61, f32[16,128]{1,0:T(8,128)} %bitcast_convert_fusion.2.refs_1_, ...), custom_call_target="tpu_custom_call" | custom-call | flops 97749999616 | bytes 1024 | tf_op jit(solution)/shard_map/gather_normed/pallas_call | solution.py:452
  110.6 0.0 all-gather.10.cloned.1.call-update
  110.6 0.0 reduce-scatter.3.cloned.1.call-start
  110.7 0.8 copy.44
  111.5 0.1 fusion.2
  111.5 0.1 reshape.84
  111.6 0.1 reshape.85
  111.7 0.9 fusion.1
  112.7 1.3 copy.33.id_column.refs_10_
  114.0 0.1 pad.20.clone
  114.1 0.1 maximum_maximum_fusion.gain.refs_9_
  114.2 3.7 fusion
  117.9 0.3 pad_maximum_fusion.3.cosine.refs_7_
  118.2 0.3 pad_maximum_fusion.4.sine.refs_8_
  118.6 26.3 %attention.1 = (bf16[2048,256]{1,0:T(8,128)(2,1)S(1)}, bf16[2048,128]{1,0:T(8,128)(2,1)S(1)}, bf16[2048,128]{1,0:T(8,128)(2,1)S(1)}, bf16[2048,256]{1,0:T(8,128)(2,1)S(1)}, f32[8,2048]{1,0:T(8,128)S(1)}) custom-call(f32[2048,512]{1,0:T(8,128)} %bitcast.68, f32[2048,128]{1,0:T(8,128)S(1)} %pad_maximum_fusion.3.cosine.refs_7_, ...), custom_call_target="tpu_custom_call" | custom-call | flops 31050000384 | bytes 1024 | tf_op jit(solution)/shard_map/attention/pallas_call | solution.py:873
  144.9 1.0 copy-done.9
  145.9 1.0 copy-done.12
  146.8 0.8 copy-done.14
  147.6 142.9 %attention_out.1 = (f32[256,2048]{1,0:T(8,128)}, bf16[256,2048]{1,0:T(8,128)(2,1)}) custom-call(bf16[8,256,256]{2,1,0:T(8,128)(2,1)} %bitcast.47, bf16[2048,768]{1,0:T(8,128)(2,1)} %get-tuple-element.60.refs_1_, bf16[256,2048]{1,0:T(8,128)(2,1)} %bitcast.62, f32[8,2048]{1,0:T(8,128)} %get-tuple-element.61.refs_3_.refs_4_), custom_call_target="tpu_custom_call" | custom-call | flops 103499997184 | bytes 1024 | tf_op jit(solution)/shard_map/attention_out/pallas_call | solution.py:507
  290.6 0.0 all-gather.8.cloned.1.call-done.refs_2_.refs_1_.refs_3_
  290.6 0.0 all-gather.10.cloned.1.call-done
  290.6 91.1 %feed.1 = (bf16[8,256,2048]{2,1,0:T(8,128)(2,1)}, bf16[8,256,768]{2,1,0:T(8,128)(2,1)}, bf16[8,256,1536]{2,1,0:T(8,128)(2,1)}) custom-call(bf16[256,2048]{1,0:T(8,128)(2,1)} %get-tuple-element.62.refs_0_, bf16[8,256,2048]{2,1,0:T(8,128)(2,1)} %bitcast.59, bf16[2048,2304]{1,0:T(8,128)(2,1)} %all-gather.8.cloned.1.call-done.refs_2_.refs_1_.refs_3_), custom_call_target="tpu_custom_call" | custom-call | flops 103499997184 | bytes 1024 | tf_op jit(solution)/shard_map/feed/pallas_call | solution.py:566
  381.8 10.4 %bitcast_convert_fusion.1 = bf16[2048,768]{1,0:T(8,128)(2,1)S(1)} fusion(bf16[8,256,2048]{2,1,0:T(8,128)(2,1)} %bitcast.60, bf16[8,256,768]{2,1,0:T(8,128)(2,1)} %get-tuple-element.66.refs_2_), kind=kOutput, calls=%fused_computation.2 | convolution fusion | flops 6444023808 | bytes 14680064 | tf_op jit(solution)/shard_map/dot_general | solution.py:33
  392.2 14.4 %bitcast_convert_fusion = bf16[2048,1536]{1,0:T(8,128)(2,1)S(1)} fusion(bf16[8,256,2048]{2,1,0:T(8,128)(2,1)S(1)} %copy-done.25, bf16[8,256,1536]{2,1,0:T(8,128)(2,1)S(1)} %copy-done.26), kind=kOutput, calls=%fused_computation | convolution fusion | flops 12888047616 | bytes 20971520 | tf_op jit(solution)/shard_map/dot_general | solution.py:33
  406.5 4.5 pad_maximum_fusion
  411.0 0.0 reduce-scatter.3.cloned.1.call-update
  411.1 0.0 all-gather.12.cloned.1.call-start
  411.1 86.2 %feed_back.1 = (f32[256,2048]{1,0:T(8,128)}, bf16[256,2048]{1,0:T(8,128)(2,1)}, f32[8,2048]{1,0:T(8,128)}) custom-call(bf16[8,256,1536]{2,1,0:T(8,128)(2,1)} %get-tuple-element.67.refs_0_, bf16[2048,2304]{1,0:T(8,128)(2,1)} %all-gather.8.cloned.1.call-done.refs_2_.refs_1_.refs_3_, f32[256,2048]{1,0:T(8,128)} %get-tuple-element.68.refs_2_.refs_4_, ...), custom_call_target="tpu_custom_call" | custom-call | flops 98900000768 | bytes 1024 | tf_op jit(solution)/shard_map/feed_back/pallas_call | solution.py:632
  497.3 7.4 reduce-scatter.3.cloned.1.call-done
  504.7 0.0 all-gather.12.cloned.1.call-update
  504.7 0.0 reduce-scatter.5.cloned.1.call-start
  504.8 254.5 %turn.1 = (bf16[8,256,2048]{2,1,0:T(8,128)(2,1)}, bf16[8,256,256]{2,1,0:T(8,128)(2,1)}, bf16[256,2048]{1,0:T(8,128)(2,1)}) custom-call(bf16[256,2048]{1,0:T(8,128)(2,1)} %get-tuple-element.71.refs_0_, bf16[2048,768]{1,0:T(8,128)(2,1)} %get-tuple-element.60.refs_1_, bf16[8,256,768]{2,1,0:T(8,128)(2,1)} %get-tuple-element.66.refs_2_, ...), custom_call_target="tpu_custom_call" | custom-call | flops 123050000384 | bytes 1024 | tf_op jit(solution)/shard_map/turn/pallas_call | solution.py:690
  759.3 6.0 convolution_convert_fusion.1
  765.5 37.4 %attention_back.1 = (bf16[2048,512]{1,0:T(8,128)(2,1)}, f32[8,128]{1,0:T(8,128)S(1)}) custom-call(bf16[2048,256]{1,0:T(8,128)(2,1)S(1)} %copy-done.13, bf16[2048,128]{1,0:T(8,128)(2,1)S(1)} %get-tuple-element.74.refs_1_, bf16[2048,128]{1,0:T(8,128)(2,1)S(1)} %copy-done.15, bf16[2048,256]{1,0:T(8,128)(2,1)S(1)} %bitcast.48, ...), custom_call_target="tpu_custom_call" | custom-call | flops 43699998720 | bytes 1024 | tf_op jit(solution)/shard_map/attention_back/pallas_call | solution.py:950
  802.9 6.3 convolution_convert_fusion
  809.3 1.9 pad_maximum_fusion.1
  811.2 0.0 reduce-scatter.5.cloned.1.call-update
  811.2 0.0 all-gather.14.cloned.1.call-start
  811.2 43.1 %reduce-scatter.5.cloned.1.call-done = bf16[512,768]{1,0:T(8,128)(2,1)} async-done(((bf16[2048,768]{1,0:T(8,128)(2,1)}), bf16[512,768]{1,0:T(8,128)(2,1)}) %reduce-scatter.5.cloned.1.call-update) | async-done | bytes 786448 | tf_op jit(solution)/shard_map/reduce_scatter | solution.py:1066
  854.3 0.0 all-gather.14.cloned.1.call-update
  854.4 6.4 copy-done
  860.7 13.1 %spread_feed.1 = (f32[512,6144]{1,0:T(8,128)}, f32[512,6144]{1,0:T(8,128)}, f32[6144,512]{1,0:T(8,128)}) custom-call(bf16[8,512,2304]{2,1,0:T(8,128)(2,1)S(1)} %bitcast.42), custom_call_target="tpu_custom_call" | custom-call | tf_op jit(solution)/shard_map/spread_feed/pallas_call | solution.py:979
  873.8 123.6 %last.1 = (f32[256,2048]{1,0:T(8,128)}, f32[16,128]{1,0:T(8,128)}) custom-call(bf16[8,256,512]{2,1,0:T(8,128)(2,1)} %bitcast.70, bf16[2048,768]{1,0:T(8,128)(2,1)} %get-tuple-element.60.refs_1_, bf16[256,2048]{1,0:T(8,128)(2,1)} %bitcast.63, f32[256,2048]{1,0:T(8,128)} %get-tuple-element.83.refs_3_, f32[8,2048]{1,0:T(8,128)} %get-tuple-element.61.refs_3_.refs_4_, ...), custom_call_target="tpu_custom_call" | custom-call | flops 103499997184 | bytes 1024 | tf_op jit(solution)/shard_map/last/pallas_call | solution.py:788
  997.4 1.3 fusion.3
  998.7 1.3 slice_bitcast_fusion
  1000.1 2.8 copy-done.1
  1002.8 5.3 spread_heads.1
  1008.1 1.0 copy.47
  1009.1 1.3 copy.48
  (59 shorter events, 0.2 us)
Async XLA Ops:
  7.2 283.4 %all-gather.8.cloned.1.call-start = ((), (), s32[]{:S(2)}) async-start(), calls=%async_computation.2 | async-start | bytes 11796480 | tf_op jit(solution)/shard_map/all_gather | solution.py:1063
  10.2 2.8 copy-start.21
  10.2 2.8 copy-start.22
  10.2 3.4 copy-start.19
  10.2 3.4 copy-start.20
  10.2 3.4 copy-start.23
  10.3 3.4 copy-start.24
  11.8 278.8 %all-gather.10.cloned.1.call-start = ((), (), s32[]{:S(2)}) async-start(), calls=%async_computation.5 | async-start | bytes 9437184 | tf_op jit(solution)/shard_map/all_gather | solution.py:1069
  110.6 394.1 %reduce-scatter.3.cloned.1.call-start = ((), (), s32[]{:S(2)}) async-start(), calls=%async_computation.3 | async-start | bytes 11796480 | tf_op jit(solution)/shard_map/reduce_scatter | solution.py:1066
  112.6 6.0 copy-start.5
  114.2 30.7 %copy-start.7 = (f32[8,128]{1,0:T(8,128)}, f32[8,128]{1,0:T(8,128)S(1)}, u32[]{:S(2)}) copy-start(f32[8,128]{1,0:T(8,128)S(1)} %maximum_maximum_fusion.gain.refs_9_) | copy-start | bytes 12292
  118.2 26.7 %copy-start.3 = (f32[2048,128]{1,0:T(8,128)}, f32[2048,128]{1,0:T(8,128)S(1)}, u32[]{:S(2)}) copy-start(f32[2048,128]{1,0:T(8,128)S(1)} %pad_maximum_fusion.3.cosine.refs_7_) | copy-start | bytes 3145732
  118.6 26.3 %copy-start.2 = (f32[2048,128]{1,0:T(8,128)}, f32[2048,128]{1,0:T(8,128)S(1)}, u32[]{:S(2)}) copy-start(f32[2048,128]{1,0:T(8,128)S(1)} %pad_maximum_fusion.4.sine.refs_8_) | copy-start | bytes 3145732
  144.9 1.0 copy-start.9
  145.9 1.0 copy-start.12
  146.8 0.8 copy-start.14
  381.7 10.4 %copy-start.25 = (bf16[8,256,2048]{2,1,0:T(8,128)(2,1)S(1)}, bf16[8,256,2048]{2,1,0:T(8,128)(2,1)}, u32[]{:S(2)}) copy-start(bf16[8,256,2048]{2,1,0:T(8,128)(2,1)} %get-tuple-element.65) | copy-start | bytes 25165828
  381.8 10.4 %copy-start.26 = (bf16[8,256,1536]{2,1,0:T(8,128)(2,1)S(1)}, bf16[8,256,1536]{2,1,0:T(8,128)(2,1)}, u32[]{:S(2)}) copy-start(bf16[8,256,1536]{2,1,0:T(8,128)(2,1)} %get-tuple-element.67.refs_0_) | copy-start | bytes 18874372
  411.1 400.1 %all-gather.12.cloned.1.call-start = ((), (), s32[]{:S(2)}) async-start(), calls=%async_computation.6 | async-start | bytes 21233664 | tf_op jit(solution)/shard_map/all_gather | solution.py:1069
  504.7 254.5 %copy-start.10 = (bf16[2048,256]{1,0:T(8,128)(2,1)S(1)}, bf16[2048,256]{1,0:T(8,128)(2,1)}, u32[]{:S(2)}) copy-start(bf16[2048,256]{1,0:T(8,128)(2,1)} %copy-done.9) | copy-start | bytes 3145732
  504.7 349.6 %reduce-scatter.5.cloned.1.call-start = ((), (), s32[]{:S(2)}) async-start(), calls=%async_computation.4 | async-start | bytes 3932160 | tf_op jit(solution)/shard_map/reduce_scatter | solution.py:1066
  759.3 6.1 copy-start.4
  759.3 6.1 copy-start.6
  759.3 6.1 copy-start.8
  759.3 6.1 copy-start.11
  759.3 6.1 copy-start.13
  759.3 6.1 copy-start.15
  759.3 43.6 %slice-start = ((s8[8388608]{0:T(1024)(128)(4,1)}), s8[4194304]{0:T(1024)(128)(4,1)S(1)}, s32[]{:S(2)}) async-start(s8[8388608]{0:T(1024)(128)(4,1)} %bitcast.64), calls=%async_computation.8 | async-start | bytes 8388608
  765.5 37.5 %slice-start.1 = ((s8[8388608]{0:T(1024)(128)(4,1)}), s8[4194304]{0:T(1024)(128)(4,1)S(1)}, s32[]{:S(2)}) async-start(s8[8388608]{0:T(1024)(128)(4,1)} %bitcast.64), calls=%async_computation.9 | async-start | bytes 8388608
  802.9 6.4 copy-start.16
  811.2 188.9 %all-gather.14.cloned.1.call-start = ((), (), s32[]{:S(2)}) async-start(), calls=%async_computation.7 | async-start | bytes 7077888 | tf_op jit(solution)/shard_map/all_gather | solution.py:1069
  854.4 6.4 copy-start
  873.8 134.3 %copy-start.18 = (bf16[256,2048]{1,0:T(8,128)(2,1)S(1)}, bf16[256,2048]{1,0:T(8,128)(2,1)}, u32[]{:S(2)}) copy-start(bf16[256,2048]{1,0:T(8,128)(2,1)} %get-tuple-element.72) | copy-start | bytes 3145732
  1000.1 2.8 copy-start.1
  1002.8 6.3 copy-start.17
Sparse Core Ops, SparseCore 0:
  12.0 129.7 all-gather.7
  143.3 140.6 all-gather.9
  411.2 93.4 reduce-scatter.2
  506.2 247.6 all-gather.11
  811.3 43.0 reduce-scatter.4
  855.8 91.2 all-gather.13

commit v4 on v3

--- a/solution.py
+++ b/solution.py
@@ -714,27 +714,53 @@
 
 
 def last_kernel(columns, *refs):
-    back, weights, x, grad_middle, gain_rows, gain_two, gain_heads, hidden, gain_out = refs[:9]
-    weight, weight_sem, total, gain_one, pack, pack_in, shard_sum, shard_in = refs[9:17]
-    small, scratch = refs[17:21], refs[21:]
-    chips = line_position()[3]
+    back, weights, x, grad_middle, gain_rows, gain_two, gain_heads, head_grad = refs[:8]
+    hidden, gain_out, land = refs[8:11]
+    weight, weight_sem, total, gain_one, pack, pack_in, shard_sum, shard_in, head_in = refs[11:20]
+    small, gather_sems, scratch = refs[20:26], refs[26:32], refs[32:]
+    me, _, _, chips = line_position()
+    shard = lax.axis_index("fsdp")
+    shards, ahead, _ = peers_of("fsdp")
+    parts, next_part, _ = peers_of("ctx")
     copy = copy_in(weights.at[:, columns], weight, weight_sem)
 
     def produce(piece, chunk):
         return rdot(back[piece], weight[pl.ds(pl.multiple_of(chunk * WIDE, WIDE), WIDE), :])
 
+    def head_copy(i):
+        return send(head_grad.at[ahead(i)], head_in.at[i], small[4].at[i], small[5].at[i], "fsdp", ahead(i))
+
+    def head_sum(block):
+        value = head_grad[shard, block].astype(F32)
+        for i in range(shards):
+            value = value + head_in[i, block].astype(F32)
+        land[me, block] = value.astype(BF16)
+
     scatter = Scatter(scratch, produce, total)
+    gather = Gather(land, gather_sems)
     scatter.begin()
     full_barrier()
     copy.wait()
     scatter.prepare(0)
+    loop(shards, lambda i: head_copy(i).start())
 
     def step(time):
         scatter.step(time)
+
+        @pl.when(time == 1)
+        def _():
+            loop(shards, lambda i: head_copy(i).wait_recv())
+            row_blocks(head_grad.shape[1], head_sum)
+
+        @pl.when(time >= 1)
+        def _():
+            gather.step(time - 1)
+
         scatter.prepare(time + 1)
 
     loop(chips - 1, step)
     scatter.finish()
+    gather.step(chips - 2)
     gain_one[...] = jnp.zeros_like(gain_one)
 
     def norm(block):
@@ -744,9 +770,6 @@
 
     row_blocks(x.shape[0], norm)
 
-    shard = lax.axis_index("fsdp")
-    shards, ahead, _ = peers_of("fsdp")
-    parts, next_part, _ = peers_of("ctx")
     rows = D // (shards + 1)
     lanes = rows // 128
     pack[...] = jnp.zeros_like(pack)
@@ -779,20 +802,25 @@
         gain_out[...] += shard_in[i]
 
     loop(parts, add_sum)
+    gather.step(chips - 1)
+    gather.finish()
+    loop(shards, lambda i: head_copy(i).wait_send())
     loop(shards, lambda i: pack_copy(i).wait_send())
     loop(parts, lambda i: sum_copy(i).wait_send())
 
 
-def last(back, weights, hidden, grad_middle, gain_rows, gain_two, gain_heads, shards):
+def last(back, weights, hidden, grad_middle, gain_rows, gain_two, gain_heads, head_grad):
     parts, count, width = back.shape
+    shards, rows, head_width = head_grad.shape
     return pl.pallas_call(
         functools.partial(last_kernel, pl.ds(0, width)),
         out_shape=(
             jax.ShapeDtypeStruct((count, D), F32),
             jax.ShapeDtypeStruct((16, 128), F32),
+            jax.ShapeDtypeStruct((parts, rows, head_width), BF16),
         ),
-        in_specs=[WHOLE, HBM] + [WHOLE] * 5,
-        out_specs=(WHOLE,) * 2,
+        in_specs=[WHOLE, HBM] + [WHOLE] * 6,
+        out_specs=(WHOLE,) * 3,
         scratch_shapes=[
             VMEM((D, width), BF16),
             pltpu.SemaphoreType.DMA,
@@ -802,14 +830,17 @@
             VMEM((shards, 16, 128), F32),
             VMEM((16, 128), F32),
             VMEM((parts, 16, 128), F32),
+            VMEM((shards - 1, rows, head_width), BF16),
         ]
         + [pltpu.SemaphoreType.DMA((shards,))] * 2
         + [pltpu.SemaphoreType.DMA((parts,))] * 2
+        + [pltpu.SemaphoreType.DMA((shards,))] * 2
+        + gather_scratch(parts // 2)
         + scatter_scratch(parts // 2, count),
         compiler_params=params(5, 60),
         cost_estimate=cost(90),
         name="last",
-    )(back, weights, hidden, grad_middle, gain_rows, gain_two, gain_heads)
+    )(back, weights, hidden, grad_middle, gain_rows, gain_two, gain_heads, head_grad)
 
 
 QUERY_TILE = 256
@@ -1134,10 +1165,10 @@
     feed_shard = sum_rows(feed_grad)
 
     grad_middle, low, gain_two = feed_back(back, feed_weight, middle, grad, gain_rows)
-    low, feed_shard = lax.optimization_barrier((low, feed_shard))
+    low_all, context_grad, hidden_out = turn(low, heads_weight, activation, feed_weight, middle, width)
+
+    context_grad, feed_shard = lax.optimization_barrier((context_grad, feed_shard))
     feed_parts = gather_parts(feed_shard)
-    low_all, context_grad, hidden_out = turn(low, heads_weight, activation, feed_weight, middle, width)
-
     context_grad = context_grad.reshape(tokens, width)
     grad_qkv, gain_heads = attention_back(
         heads,
@@ -1161,9 +1192,7 @@
         ],
         axis=1,
     )
-    grad_qkv, head_grad, feed_parts = lax.optimization_barrier((grad_qkv, head_grad, feed_parts))
-    head_shard = sum_rows(head_grad)
-    grad_hidden, gain_sums = last(
+    grad_hidden, gain_sums, head_parts = last(
         grad_qkv.reshape(parts, count, -1),
         heads_weight,
         hidden,
@@ -1171,10 +1200,9 @@
         gain_rows,
         gain_two,
         gain_heads,
-        shards,
-    )
-
-    head_parts = gather_parts(head_shard)
+        head_grad.reshape(shards, rows, -1),
+    )
+
     gain_sums = gain_sums.reshape(-1)
     grad_gate, grad_up, grad_down = spread_feed(feed_parts)
     grad_query, grad_key, grad_value, grad_out_weight = spread_heads(head_parts, width)

time: 1020 us -> 910 us (0.89)
  Pallas kernels: 874 us -> 818 us
  waiting for transfers between devices: 50.7 us -> 0.13 us
    pallas_call x1, Pallas kernels: 254 us -> 107 us  [turn(): pl.pallas_call(functools.partial(turn_kernel, pl.ds(weights.shape[1] - wi...]
    pallas_call x1, Pallas kernels: 124 us -> 215 us  [last(): pl.pallas_call(functools.partial(last_kernel, pl.ds(0, width)), out_shape...]
    reduce_scatter x2 -> x1, waiting for transfers between devices: 50.6 us -> 0.02 us  [sum_rows(): lax.psum_scatter(grad.astype(BF16), 'fsdp', scatter_dimension=0, tiled=True)]
  transfers between devices with their start and end apart: 6 -> 4, of which waited for: 2 -> 0; matrix products, arithmetic and copies ran while one was open for 3% -> 3% of each run, Pallas kernels for 76% -> 79%
where the time goes in v4:
time: 910 us; the launch traced here: 909 us
  Pallas kernels  818 us (90%)
  matrix products  37.1 us (4%)
  local copies, waits for them, and re-layouts  24.6 us (3%)
  other arithmetic  14.9 us (2%)
  between operations  14.3 us (2%)
    pallas_call x1, Pallas kernels, last(): pl.pallas_call(functools.partial(last_kernel, pl.ds(0, width)), out_shape...  215 us
    pallas_call x1, Pallas kernels, attention_out(): pl.pallas_call(functools.partial(out_kernel, pl.ds(weights.shape[1] - wid...  143 us
    pallas_call x1, Pallas kernels, turn(): pl.pallas_call(functools.partial(turn_kernel, pl.ds(weights.shape[1] - wi...  107 us
    pallas_call x1, Pallas kernels, first(): pl.pallas_call(functools.partial(first_kernel, D // shards, width), out_s...  93.3 us
    pallas_call x1, Pallas kernels, feed(): pl.pallas_call(functools.partial(feed_kernel, width), out_shape=(jax.Shap...  91.1 us
    pallas_call x1, Pallas kernels, feed_back(): pl.pallas_call(functools.partial(feed_back_kernel, pl.ds(0, width)), out_...  85.9 us
    pallas_call x1, Pallas kernels, attention_back(): pl.pallas_call(functools.partial(attention_back_kernel, heads), out_shape...  38.4 us
    dot_general x4, matrix products, tdot(): lax.dot_general(left, right, (((0,), (0,)), ((), ())), preferred_element_...  37.1 us
  transfers between devices with their start and end apart: 4, of which 0 were waited for; matrix products, arithmetic and copies ran while one was open for 3% of the time, Pallas kernels for 79%

profile of v4, /device:TPU:0, one launch (start us, length us, event | category | flops | bytes accessed | tf_op | source)
XLA Modules:
  0.0 909.4 jit_solution(6835949654765986647)
XLA Ops:
  7.2 0.0 all-gather.6.cloned.1.call-start
  7.2 1.2 constant_dynamic-slice_fusion
  8.4 0.3 copy.41
  8.7 1.5 constant_dynamic-slice_fusion.1
  10.2 0.0 copy-start.24
  10.3 0.0 copy-start.25
  10.3 1.6 pad_maximum_fusion.2
  11.8 0.0 all-gather.6.cloned.1.call-update
  11.8 0.0 all-gather.8.cloned.1.call-start
  11.9 0.6 pad.10.refs_2_
  12.5 1.0 constant_dynamic-slice_fusion.3
  13.5 0.1 copy.40
  13.7 0.1 concatenate.24
  13.8 0.6 bitcast_convert_fusion.2.refs_1_
  14.4 1.0 constant_dynamic-slice_fusion.6
  15.3 1.0 constant_dynamic-slice_fusion.4
  16.3 0.9 pad_maximum_fusion.5.refs_3_
  17.3 93.3 %gather_normed.1 = (bf16[8,256,2048]{2,1,0:T(8,128)(2,1)}, f32[8,256,512]{2,1,0:T(8,128)}, bf16[2048,768]{1,0:T(8,128)(2,1)}, f32[8,2048]{1,0:T(8,128)}, f32[4,16,128]{2,1,0:T(8,128)}, /*index=5*/s32[8,8,256]{2,1,0:T(8,128)}) custom-call(bf16[256,2048]{1,0:T(8,128)(2,1)} %bitcast.61, f32[16,128]{1,0:T(8,128)} %bitcast_convert_fusion.2.refs_1_, ...), custom_call_target="tpu_custom_call" | custom-call | flops 97749999616 | bytes 1024 | tf_op jit(solution)/shard_map/gather_normed/pallas_call | solution.py:452
  110.6 0.0 all-gather.8.cloned.1.call-update
  110.6 0.0 reduce-scatter.2.cloned.1.call-start
  110.6 0.8 copy.44
  111.4 0.1 fusion.2
  111.5 0.1 reshape.87
  111.6 0.1 reshape.88
  111.7 0.9 fusion.1
  112.6 1.3 copy.33.id_column.refs_10_
  113.9 0.1 pad.20.clone
  114.0 0.1 maximum_maximum_fusion.gain.refs_9_
  114.1 3.7 fusion
  117.8 0.3 pad_maximum_fusion.3.cosine.refs_7_
  118.2 0.3 pad_maximum_fusion.4.sine.refs_8_
  118.5 0.0 copy-start.2
  118.6 26.3 %attention.1 = (bf16[2048,256]{1,0:T(8,128)(2,1)S(1)}, bf16[2048,128]{1,0:T(8,128)(2,1)S(1)}, bf16[2048,128]{1,0:T(8,128)(2,1)S(1)}, bf16[2048,256]{1,0:T(8,128)(2,1)S(1)}, f32[8,2048]{1,0:T(8,128)S(1)}) custom-call(f32[2048,512]{1,0:T(8,128)} %bitcast.68, f32[2048,128]{1,0:T(8,128)S(1)} %pad_maximum_fusion.3.cosine.refs_7_, ...), custom_call_target="tpu_custom_call" | custom-call | flops 31050000384 | bytes 1024 | tf_op jit(solution)/shard_map/attention/pallas_call | solution.py:904
  144.8 1.0 copy-done.9
  145.8 1.0 copy-done.12
  146.8 0.8 copy-done.14
  147.6 143.0 %attention_out.1 = (f32[256,2048]{1,0:T(8,128)}, bf16[256,2048]{1,0:T(8,128)(2,1)}) custom-call(bf16[8,256,256]{2,1,0:T(8,128)(2,1)} %bitcast.46, bf16[2048,768]{1,0:T(8,128)(2,1)} %get-tuple-element.58.refs_1_, bf16[256,2048]{1,0:T(8,128)(2,1)} %bitcast.62, f32[8,2048]{1,0:T(8,128)} %get-tuple-element.59.refs_3_.refs_4_), custom_call_target="tpu_custom_call" | custom-call | flops 103499997184 | bytes 1024 | tf_op jit(solution)/shard_map/attention_out/pallas_call | solution.py:507
  290.6 0.0 all-gather.6.cloned.1.call-done.refs_2_.refs_1_.refs_3_
  290.6 0.0 all-gather.8.cloned.1.call-done
  290.7 91.1 %feed.1 = (bf16[8,256,2048]{2,1,0:T(8,128)(2,1)}, bf16[8,256,768]{2,1,0:T(8,128)(2,1)}, bf16[8,256,1536]{2,1,0:T(8,128)(2,1)}) custom-call(bf16[256,2048]{1,0:T(8,128)(2,1)} %get-tuple-element.60.refs_0_, bf16[8,256,2048]{2,1,0:T(8,128)(2,1)} %bitcast.59, bf16[2048,2304]{1,0:T(8,128)(2,1)} %all-gather.6.cloned.1.call-done.refs_2_.refs_1_.refs_3_), custom_call_target="tpu_custom_call" | custom-call | flops 103499997184 | bytes 1024 | tf_op jit(solution)/shard_map/feed/pallas_call | solution.py:566
  381.8 10.4 %bitcast_convert_fusion.1 = bf16[2048,768]{1,0:T(8,128)(2,1)S(1)} fusion(bf16[8,256,2048]{2,1,0:T(8,128)(2,1)} %bitcast.60, bf16[8,256,768]{2,1,0:T(8,128)(2,1)} %get-tuple-element.64.refs_2_), kind=kOutput, calls=%fused_computation.2 | convolution fusion | flops 6444023808 | bytes 14680064 | tf_op jit(solution)/shard_map/dot_general | solution.py:33
  392.2 14.3 %bitcast_convert_fusion = bf16[2048,1536]{1,0:T(8,128)(2,1)S(1)} fusion(bf16[8,256,2048]{2,1,0:T(8,128)(2,1)S(1)} %copy-done.26, bf16[8,256,1536]{2,1,0:T(8,128)(2,1)S(1)} %copy-done.27), kind=kOutput, calls=%fused_computation | convolution fusion | flops 12888047616 | bytes 20971520 | tf_op jit(solution)/shard_map/dot_general | solution.py:33
  406.5 4.5 pad_maximum_fusion
  411.0 0.0 reduce-scatter.2.cloned.1.call-update
  411.0 0.0 all-gather.10.cloned.1.call-start
  411.1 85.9 %feed_back.1 = (f32[256,2048]{1,0:T(8,128)}, bf16[256,2048]{1,0:T(8,128)(2,1)}, f32[8,2048]{1,0:T(8,128)}) custom-call(bf16[8,256,1536]{2,1,0:T(8,128)(2,1)} %get-tuple-element.65.refs_0_, bf16[2048,2304]{1,0:T(8,128)(2,1)} %all-gather.6.cloned.1.call-done.refs_2_.refs_1_.refs_3_, f32[256,2048]{1,0:T(8,128)} %get-tuple-element.66.refs_2_.refs_4_, ...), custom_call_target="tpu_custom_call" | custom-call | flops 98900000768 | bytes 1024 | tf_op jit(solution)/shard_map/feed_back/pallas_call | solution.py:632
  497.1 107.0 %turn.1 = (bf16[8,256,2048]{2,1,0:T(8,128)(2,1)}, bf16[8,256,256]{2,1,0:T(8,128)(2,1)}, bf16[256,2048]{1,0:T(8,128)(2,1)}) custom-call(bf16[256,2048]{1,0:T(8,128)(2,1)} %get-tuple-element.67.refs_0_, bf16[2048,768]{1,0:T(8,128)(2,1)} %get-tuple-element.58.refs_1_, bf16[8,256,768]{2,1,0:T(8,128)(2,1)} %get-tuple-element.64.refs_2_, ...), custom_call_target="tpu_custom_call" | custom-call | flops 123050000384 | bytes 1024 | tf_op jit(solution)/shard_map/turn/pallas_call | solution.py:690
  604.1 0.0 reduce-scatter.2.cloned.1.call-done
  604.1 0.0 all-gather.10.cloned.1.call-update
  604.2 0.0 copy-start.13
  604.2 0.0 copy-start.15
  604.3 6.1 convolution_convert_fusion.1
  610.4 38.4 %attention_back.1 = (bf16[2048,512]{1,0:T(8,128)(2,1)}, f32[8,128]{1,0:T(8,128)S(1)}) custom-call(bf16[2048,256]{1,0:T(8,128)(2,1)S(1)} %copy-done.13, bf16[2048,128]{1,0:T(8,128)(2,1)S(1)} %get-tuple-element.70.refs_1_, bf16[2048,128]{1,0:T(8,128)(2,1)S(1)} %copy-done.15, bf16[2048,256]{1,0:T(8,128)(2,1)S(1)} %bitcast.47, ...), custom_call_target="tpu_custom_call" | custom-call | flops 43699998720 | bytes 1024 | tf_op jit(solution)/shard_map/attention_back/pallas_call | solution.py:981
  648.8 6.4 convolution_convert_fusion
  655.2 1.9 pad_maximum_fusion.1
  657.0 215.4 %last.1 = (f32[256,2048]{1,0:T(8,128)}, f32[16,128]{1,0:T(8,128)}, bf16[8,512,768]{2,1,0:T(8,128)(2,1)}) custom-call(bf16[8,256,512]{2,1,0:T(8,128)(2,1)} %bitcast.70, bf16[2048,768]{1,0:T(8,128)(2,1)} %get-tuple-element.58.refs_1_, bf16[256,2048]{1,0:T(8,128)(2,1)} %bitcast.63, f32[256,2048]{1,0:T(8,128)} %get-tuple-element.77.refs_3_, ...), custom_call_target="tpu_custom_call" | custom-call | flops 103499997184 | bytes 1024 | tf_op jit(solution)/shard_map/last/pallas_call | solution.py:815
  872.4 2.8 copy-done.1
  875.2 5.3 spread_heads.1
  880.5 0.6 fusion.3
  881.1 0.6 slice_bitcast_fusion
  881.7 6.4 copy-done
  888.1 12.6 %spread_feed.1 = (f32[512,6144]{1,0:T(8,128)}, f32[512,6144]{1,0:T(8,128)}, f32[6144,512]{1,0:T(8,128)}) custom-call(bf16[8,512,2304]{2,1,0:T(8,128)(2,1)S(1)} %bitcast.42), custom_call_target="tpu_custom_call" | custom-call | tf_op jit(solution)/shard_map/spread_feed/pallas_call | solution.py:1010
  900.6 1.0 copy.47
  901.6 1.3 copy.48
  (55 shorter events, 0.1 us)
Async XLA Ops:
  7.2 283.5 %all-gather.6.cloned.1.call-start = ((), (), s32[]{:S(2)}) async-start(), calls=%async_computation.1 | async-start | bytes 11796480 | tf_op jit(solution)/shard_map/all_gather | solution.py:1094
  8.7 3.2 copy-start.22
  8.7 3.2 copy-start.23
  10.2 3.4 copy-start.20
  10.2 3.4 copy-start.21
  10.2 3.4 copy-start.24
  10.3 3.4 copy-start.25
  11.8 278.8 %all-gather.8.cloned.1.call-start = ((), (), s32[]{:S(2)}) async-start(), calls=%async_computation.3 | async-start | bytes 9437184 | tf_op jit(solution)/shard_map/all_gather | solution.py:1100
  110.6 493.5 %reduce-scatter.2.cloned.1.call-start = ((), (), s32[]{:S(2)}) async-start(), calls=%async_computation.2 | async-start | bytes 11796480 | tf_op jit(solution)/shard_map/reduce_scatter | solution.py:1097
  112.6 6.0 copy-start.5
  114.1 30.7 %copy-start.7 = (f32[8,128]{1,0:T(8,128)}, f32[8,128]{1,0:T(8,128)S(1)}, u32[]{:S(2)}) copy-start(f32[8,128]{1,0:T(8,128)S(1)} %maximum_maximum_fusion.gain.refs_9_) | copy-start | bytes 12292
  118.2 26.6 %copy-start.3 = (f32[2048,128]{1,0:T(8,128)}, f32[2048,128]{1,0:T(8,128)S(1)}, u32[]{:S(2)}) copy-start(f32[2048,128]{1,0:T(8,128)S(1)} %pad_maximum_fusion.3.cosine.refs_7_) | copy-start | bytes 3145732
  118.5 26.3 %copy-start.2 = (f32[2048,128]{1,0:T(8,128)}, f32[2048,128]{1,0:T(8,128)S(1)}, u32[]{:S(2)}) copy-start(f32[2048,128]{1,0:T(8,128)S(1)} %pad_maximum_fusion.4.sine.refs_8_) | copy-start | bytes 3145732
  144.8 1.0 copy-start.9
  145.8 1.0 copy-start.12
  146.8 0.8 copy-start.14
  381.7 10.4 %copy-start.26 = (bf16[8,256,2048]{2,1,0:T(8,128)(2,1)S(1)}, bf16[8,256,2048]{2,1,0:T(8,128)(2,1)}, u32[]{:S(2)}) copy-start(bf16[8,256,2048]{2,1,0:T(8,128)(2,1)} %get-tuple-element.63) | copy-start | bytes 25165828
  381.7 10.4 %copy-start.27 = (bf16[8,256,1536]{2,1,0:T(8,128)(2,1)S(1)}, bf16[8,256,1536]{2,1,0:T(8,128)(2,1)}, u32[]{:S(2)}) copy-start(bf16[8,256,1536]{2,1,0:T(8,128)(2,1)} %get-tuple-element.65.refs_0_) | copy-start | bytes 18874372
  411.0 470.6 %all-gather.10.cloned.1.call-start = ((), (), s32[]{:S(2)}) async-start(), calls=%async_computation.4 | async-start | bytes 21233664 | tf_op jit(solution)/shard_map/all_gather | solution.py:1100
  497.0 107.1 %copy-start.10 = (bf16[2048,256]{1,0:T(8,128)(2,1)S(1)}, bf16[2048,256]{1,0:T(8,128)(2,1)}, u32[]{:S(2)}) copy-start(bf16[2048,256]{1,0:T(8,128)(2,1)} %copy-done.9) | copy-start | bytes 3145732
  604.2 6.1 copy-start.4
  604.2 6.1 copy-start.6
  604.2 6.1 copy-start.8
  604.2 6.1 copy-start.11
  604.2 6.1 copy-start.13
  604.2 6.1 copy-start.15
  604.2 44.5 %slice-start = ((s8[8388608]{0:T(1024)(128)(4,1)}), s8[4194304]{0:T(1024)(128)(4,1)S(1)}, s32[]{:S(2)}) async-start(s8[8388608]{0:T(1024)(128)(4,1)} %bitcast.64), calls=%async_computation.5 | async-start | bytes 8388608
  610.4 38.4 %slice-start.1 = ((s8[8388608]{0:T(1024)(128)(4,1)}), s8[4194304]{0:T(1024)(128)(4,1)S(1)}, s32[]{:S(2)}) async-start(s8[8388608]{0:T(1024)(128)(4,1)} %bitcast.64), calls=%async_computation.6 | async-start | bytes 8388608
  648.7 6.4 copy-start.16
  872.4 2.8 copy-start.1
  875.2 5.3 copy-start.19
  881.7 6.4 copy-start
  888.1 12.6 %copy-start.18 = (bf16[256,2048]{1,0:T(8,128)(2,1)S(1)}, bf16[256,2048]{1,0:T(8,128)(2,1)}, u32[]{:S(2)}) copy-start(bf16[256,2048]{1,0:T(8,128)(2,1)} %get-tuple-element.68) | copy-start | bytes 3145732
  888.1 13.5 %copy-start.17 = (f32[256,2048]{1,0:T(8,128)S(1)}, f32[256,2048]{1,0:T(8,128)}, u32[]{:S(2)}) copy-start(f32[256,2048]{1,0:T(8,128)} %get-tuple-element.82) | copy-start | bytes 6291460
Sparse Core Ops, SparseCore 0:
  12.0 129.7 all-gather.5
  143.4 140.7 all-gather.7
  411.2 93.5 reduce-scatter.1
  604.3 245.3 all-gather.9

commit v5 on v4

--- a/solution.py
+++ b/solution.py
@@ -469,55 +469,6 @@
         cost_estimate=cost(85),
         name="gather_normed",
     )(hidden, gains, tokens, part)
-
-
-def out_kernel(columns, *refs):
-    context, weights, x, gain_rows, middle, normed = refs[:6]
-    weight, weight_sem, total = refs[6:9]
-    scratch = refs[9:]
-    chips = line_position()[3]
-    copy = copy_in(weights.at[:, columns], weight, weight_sem)
-
-    def produce(piece, chunk):
-        return rdot(context[piece], weight[pl.ds(pl.multiple_of(chunk * WIDE, WIDE), WIDE), :])
-
-    scatter = Scatter(scratch, produce, total)
-    scatter.begin()
-    line_barrier()
-    copy.wait()
-    scatter.prepare(0)
-
-    def step(time):
-        scatter.step(time)
-        scatter.prepare(time + 1)
-
-    loop(chips - 1, step)
-    scatter.finish()
-
-    def norm(block):
-        value = x[block, :].astype(F32) + total[block, :]
-        middle[block, :] = value
-        normed[block, :] = (value * inverse_norm(value) * gain_rows[1:2, :]).astype(BF16)
-
-    row_blocks(x.shape[0], norm)
-
-
-def attention_out(context, weights, hidden, gain_rows):
-    parts, count, width = context.shape
-    return pl.pallas_call(
-        functools.partial(out_kernel, pl.ds(weights.shape[1] - width, width)),
-        out_shape=(
-            jax.ShapeDtypeStruct((count, D), F32),
-            jax.ShapeDtypeStruct((count, D), BF16),
-        ),
-        in_specs=[WHOLE, HBM, WHOLE, WHOLE],
-        out_specs=(WHOLE,) * 2,
-        scratch_shapes=[VMEM((D, width), BF16), pltpu.SemaphoreType.DMA, VMEM((count, D), F32)]
-        + scatter_scratch(parts // 2, count),
-        compiler_params=params(1, 60),
-        cost_estimate=cost(90),
-        name="attention_out",
-    )(context, weights, hidden, gain_rows)
 
 
 def feed_kernel(width, *refs):
@@ -856,10 +807,21 @@
     return normed * cosine + pltpu.roll(normed, HEAD_SIZE // 2, 1) * sine
 
 
-def attention_kernel(heads, proj, cosine, sine, gain, id_column, id_row, *refs):
-    queries, keys, values, context, inverse = refs
+def attend_kernel(heads, columns, *refs):
+    proj, cosine, sine, gain, id_column, id_row, weights, x, grad, gain_rows = refs[:10]
+    queries, keys, values, context, inverse, middle, normed, land = refs[10:18]
+    weight, weight_sem, grad_sem, total = refs[18:22]
+    gather_sems, scratch = refs[22:28], refs[28:]
+    me, _, _, chips = line_position()
     tokens = proj.shape[0]
+    count = x.shape[0]
     key_at = heads * HEAD_SIZE
+    copy = copy_in(weights.at[:, columns], weight, weight_sem)
+    own = copy_in(grad, land.at[me], grad_sem)
+    gather = Gather(land, gather_sems)
+    line_barrier()
+    own.wait()
+    gather.step(0)
 
     def prepare(index):
         block = pl.ds(pl.multiple_of(index * QUERY_TILE, QUERY_TILE), QUERY_TILE)
@@ -897,25 +859,68 @@
 
     loop(tokens // QUERY_TILE, attend)
 
-
-def attention(proj, cosine, sine, gain, id_column, id_row, heads):
+    def produce(piece, chunk):
+        block = pl.ds(pl.multiple_of(piece * count, count), count)
+        return rdot(context[block, :], weight[pl.ds(pl.multiple_of(chunk * WIDE, WIDE), WIDE), :])
+
+    scatter = Scatter(scratch, produce, total)
+    scatter.begin()
+    copy.wait()
+    scatter.prepare(0)
+    gather.step(1)
+
+    def step(time):
+        scatter.step(time)
+
+        @pl.when(time + 2 < chips)
+        def _():
+            gather.step(time + 2)
+
+        scatter.prepare(time + 1)
+
+    loop(chips - 1, step)
+    scatter.finish()
+
+    def norm(block):
+        value = x[block, :].astype(F32) + total[block, :]
+        middle[block, :] = value
+        normed[block, :] = (value * inverse_norm(value) * gain_rows[1:2, :]).astype(BF16)
+
+    row_blocks(count, norm)
+    gather.finish()
+
+
+def attend(proj, cosine, sine, gain, id_column, id_row, weights, hidden, grad, gain_rows, heads):
     tokens = proj.shape[0]
     width = heads * HEAD_SIZE
+    count = hidden.shape[0]
+    parts = tokens // count
     return pl.pallas_call(
-        functools.partial(attention_kernel, heads),
+        functools.partial(attend_kernel, heads, pl.ds(weights.shape[1] - width, width)),
         out_shape=(
             jax.ShapeDtypeStruct((tokens, width), BF16),
             jax.ShapeDtypeStruct((tokens, HEAD_SIZE), BF16),
             jax.ShapeDtypeStruct((tokens, HEAD_SIZE), BF16),
             jax.ShapeDtypeStruct((tokens, width), BF16),
             jax.ShapeDtypeStruct((8, tokens), F32),
+            jax.ShapeDtypeStruct((count, D), F32),
+            jax.ShapeDtypeStruct((count, D), BF16),
+            jax.ShapeDtypeStruct((parts, count, D), BF16),
         ),
-        in_specs=[WHOLE] * 6,
-        out_specs=(WHOLE,) * 5,
-        compiler_params=pltpu.CompilerParams(vmem_limit_bytes=48 * 1024 * 1024),
-        cost_estimate=cost(27),
-        name="attention",
-    )(proj, cosine, sine, gain, id_column, id_row)
+        in_specs=[WHOLE] * 6 + [HBM, WHOLE, HBM, WHOLE],
+        out_specs=(WHOLE,) * 7 + (HBM,),
+        scratch_shapes=[
+            VMEM((D, width), BF16),
+            pltpu.SemaphoreType.DMA,
+            pltpu.SemaphoreType.DMA,
+            VMEM((count, D), F32),
+        ]
+        + gather_scratch(parts // 2)
+        + scatter_scratch(parts // 2, count),
+        compiler_params=params(1, 60),
+        cost_estimate=cost(110),
+        name="attend",
+    )(proj, cosine, sine, gain, id_column, id_row, weights, hidden, grad, gain_rows)
 
 
 def attention_back_kernel(heads, *refs):
@@ -1126,8 +1131,6 @@
     normed_all, proj, heads_weight, gain_rows, gains, whole = first(
         hidden, own_gains, own_tokens, own_heads_weight, shards, parts, width + 2 * HEAD_SIZE
     )
-    grad_late, gains = lax.optimization_barrier((grad, gains))
-    grad_all = gather_parts(grad_late)
     flat_gains = gains.reshape(shards, -1)
     norm_query = flat_gains[:, 2 * rows : 2 * rows + head_rows].reshape(1, -1)
     norm_key = flat_gains[:, 2 * rows + head_rows : 2 * rows + 2 * head_rows].reshape(1, -1)
@@ -1143,11 +1146,8 @@
     id_row, id_column = ids[None, :], ids[:, None]
 
     proj = proj.reshape(tokens, width + 2 * HEAD_SIZE)
-    queries, keys, values, context, inverse = attention(
-        proj, cosine, sine, head_gains, id_column, id_row, heads
-    )
-    middle, normed_two = attention_out(
-        context.reshape(parts, count, width), heads_weight, hidden, gain_rows
+    queries, keys, values, context, inverse, middle, normed_two, grad_all = attend(
+        proj, cosine, sine, head_gains, id_column, id_row, heads_weight, hidden, grad, gain_rows, heads
     )
     normed_two_all, activation, back = feed(normed_two, grad_all, feed_weight)
 

time: 910 us -> 881 us (0.968)
  Pallas kernels: 818 us -> 789 us
    pallas_call x2 -> x1, Pallas kernels: 169 us -> 144 us  [attend(): pl.pallas_call(functools.partial(attend_kernel, heads, pl.ds(weights.shap...]
  transfers between devices with their start and end apart: 4 -> 3, of which waited for: 0 -> 0; matrix products, arithmetic and copies ran while one was open for 3% -> 4% of each run, Pallas kernels for 79% -> 78%
where the time goes in v5:
time: 881 us; the launch traced here: 880 us
  Pallas kernels  789 us (90%)
  matrix products  37.5 us (4%)
  local copies, waits for them, and re-layouts  21.9 us (2%)
  other arithmetic  17.4 us (2%)
  between operations  14.2 us (2%)
    pallas_call x1, Pallas kernels, last(): pl.pallas_call(functools.partial(last_kernel, pl.ds(0, width)), out_shape...  213 us
    pallas_call x1, Pallas kernels, attend(): pl.pallas_call(functools.partial(attend_kernel, heads, pl.ds(weights.shap...  144 us
    pallas_call x1, Pallas kernels, turn(): pl.pallas_call(functools.partial(turn_kernel, pl.ds(weights.shape[1] - wi...  107 us
    pallas_call x1, Pallas kernels, first(): pl.pallas_call(functools.partial(first_kernel, D // shards, width), out_s...  93.2 us
    pallas_call x1, Pallas kernels, feed(): pl.pallas_call(functools.partial(feed_kernel, width), out_shape=(jax.Shap...  89.1 us
    pallas_call x1, Pallas kernels, feed_back(): pl.pallas_call(functools.partial(feed_back_kernel, pl.ds(0, width)), out_...  85.5 us
    pallas_call x1, Pallas kernels, attention_back(): pl.pallas_call(functools.partial(attention_back_kernel, heads), out_shape...  38.8 us
    dot_general x4, matrix products, tdot(): lax.dot_general(left, right, (((0,), (0,)), ((), ())), preferred_element_...  37.5 us
  transfers between devices with their start and end apart: 3, of which 0 were waited for; matrix products, arithmetic and copies ran while one was open for 4% of the time, Pallas kernels for 78%

profile of v5, /device:TPU:0, one launch (start us, length us, event | category | flops | bytes accessed | tf_op | source)
XLA Modules:
  0.0 879.9 jit_solution(8669139530216716653)
XLA Ops:
  7.2 0.0 all-gather.4.cloned.1.call-start
  7.2 1.2 constant_dynamic-slice_fusion
  8.4 0.3 copy.41
  8.7 0.0 copy-start.16
  8.7 0.0 copy-start.17
  8.7 0.0 copy-start.20
  8.7 0.0 copy-start.21
  8.7 0.0 copy-start.18
  8.8 0.0 copy-start.19
  8.8 1.5 constant_dynamic-slice_fusion.1
  10.3 1.6 pad_maximum_fusion.2
  11.8 0.0 all-gather.4.cloned.1.call-update
  11.9 0.0 reduce-scatter.2.cloned.1.call-start
  11.9 0.1 concatenate.24
  12.0 0.6 bitcast_convert_fusion.2.refs_1_
  12.7 0.6 pad.10.refs_2_
  13.3 1.0 constant_dynamic-slice_fusion.6
  14.2 1.0 constant_dynamic-slice_fusion.3
  15.2 0.1 copy.40
  15.3 1.0 constant_dynamic-slice_fusion.4
  16.4 0.9 pad_maximum_fusion.5.refs_3_
  17.3 93.2 %gather_normed.1 = (bf16[8,256,2048]{2,1,0:T(8,128)(2,1)}, f32[8,256,512]{2,1,0:T(8,128)}, bf16[2048,768]{1,0:T(8,128)(2,1)}, f32[8,2048]{1,0:T(8,128)}, f32[4,16,128]{2,1,0:T(8,128)}, /*index=5*/s32[8,8,256]{2,1,0:T(8,128)}) custom-call(bf16[256,2048]{1,0:T(8,128)(2,1)} %bitcast.56, f32[16,128]{1,0:T(8,128)} %bitcast_convert_fusion.2.refs_1_, ...), custom_call_target="tpu_custom_call" | custom-call | flops 97749999616 | bytes 1024 | tf_op jit(solution)/shard_map/gather_normed/pallas_call | solution.py:452
  110.5 0.8 copy.44
  111.3 0.1 fusion.2
  111.4 0.1 reshape.84
  111.5 0.1 reshape.85
  111.6 0.9 fusion.1
  112.5 0.0 copy-start.3
  112.5 1.3 copy.33.refs_4_.refs_10_
  113.8 0.1 pad.20.clone
  113.9 0.7 maximum_maximum_fusion.refs_3_.refs_9_
  114.6 3.7 fusion
  118.3 1.3 pad_maximum_fusion.3.refs_1_.refs_7_
  119.6 1.3 pad_maximum_fusion.4.refs_2_.refs_8_
  120.9 144.0 %attend.1 = (bf16[2048,256]{1,0:T(8,128)(2,1)}, bf16[2048,128]{1,0:T(8,128)(2,1)}, bf16[2048,128]{1,0:T(8,128)(2,1)}, bf16[2048,256]{1,0:T(8,128)(2,1)}, f32[8,2...) custom-call(f32[2048,512]{1,0:T(8,128)} %bitcast.63, ...), custom_call_target="tpu_custom_call" | custom-call | flops 126500003840 | bytes 1024 | tf_op jit(solution)/shard_map/attend/pallas_call | solution.py:898
  264.9 0.0 all-gather.4.cloned.1.call-done.refs_2_.refs_1_.refs_3_
  265.0 89.1 %feed.1 = (bf16[8,256,2048]{2,1,0:T(8,128)(2,1)}, bf16[8,256,768]{2,1,0:T(8,128)(2,1)}, bf16[8,256,1536]{2,1,0:T(8,128)(2,1)}) custom-call(bf16[256,2048]{1,0:T(8,128)(2,1)} %get-tuple-element.57.refs_0_, bf16[8,256,2048]{2,1,0:T(8,128)(2,1)} %get-tuple-element.58.refs_1_, bf16[2048,2304]{1,0:T(8,128)(2,1)} %all-gather.4.cloned.1.call-done.refs_2_.refs_1_.refs_3_), custom_call_target="tpu_custom_call" | custom-call | flops 103499997184 | bytes 1024 | tf_op jit(solution)/shard_map/feed/pallas_call | solution.py:517
  354.1 10.4 %bitcast_convert_fusion.1 = bf16[2048,768]{1,0:T(8,128)(2,1)S(1)} fusion(bf16[8,256,2048]{2,1,0:T(8,128)(2,1)} %get-tuple-element.58.refs_1_, bf16[8,256,768]{2,1,0:T(8,128)(2,1)} %get-tuple-element.61.refs_2_), kind=kOutput, calls=%fused_computation.2 | convolution fusion | flops 6444023808 | bytes 14680064 | tf_op jit(solution)/shard_map/dot_general | solution.py:33
  364.5 14.3 %bitcast_convert_fusion = bf16[2048,1536]{1,0:T(8,128)(2,1)S(1)} fusion(bf16[8,256,2048]{2,1,0:T(8,128)(2,1)S(1)} %copy-done.22, bf16[8,256,1536]{2,1,0:T(8,128)(2,1)S(1)} %copy-done.23), kind=kOutput, calls=%fused_computation | convolution fusion | flops 12888047616 | bytes 20971520 | tf_op jit(solution)/shard_map/dot_general | solution.py:33
  378.9 4.5 pad_maximum_fusion
  383.4 0.0 reduce-scatter.2.cloned.1.call-update
  383.4 0.0 all-gather.6.cloned.1.call-start
  383.5 85.5 %feed_back.1 = (f32[256,2048]{1,0:T(8,128)}, bf16[256,2048]{1,0:T(8,128)(2,1)}, f32[8,2048]{1,0:T(8,128)}) custom-call(bf16[8,256,1536]{2,1,0:T(8,128)(2,1)} %get-tuple-element.62.refs_0_, bf16[2048,2304]{1,0:T(8,128)(2,1)} %all-gather.4.cloned.1.call-done.refs_2_.refs_1_.refs_3_, f32[256,2048]{1,0:T(8,128)} %get-tuple-element.63.refs_2_.refs_4_, ...), custom_call_target="tpu_custom_call" | custom-call | flops 98900000768 | bytes 1024 | tf_op jit(solution)/shard_map/feed_back/pallas_call | solution.py:583
  469.0 107.0 %turn.1 = (bf16[8,256,2048]{2,1,0:T(8,128)(2,1)}, bf16[8,256,256]{2,1,0:T(8,128)(2,1)}, bf16[256,2048]{1,0:T(8,128)(2,1)}) custom-call(bf16[256,2048]{1,0:T(8,128)(2,1)} %get-tuple-element.64.refs_0_, bf16[2048,768]{1,0:T(8,128)(2,1)} %get-tuple-element.55.refs_6_.refs_1_, bf16[8,256,768]{2,1,0:T(8,128)(2,1)} %get-tuple-element.61.refs_2_, ...), custom_call_target="tpu_custom_call" | custom-call | flops 123050000384 | bytes 1024 | tf_op jit(solution)/shard_map/turn/pallas_call | solution.py:641
  576.0 0.0 reduce-scatter.2.cloned.1.call-done
  576.1 0.0 all-gather.6.cloned.1.call-update
  576.1 0.0 copy-start.2
  576.1 0.0 copy-start.4
  576.1 0.0 copy-start.5
  576.2 0.0 slice-start
  576.2 6.4 convolution_convert_fusion.1
  582.7 0.0 slice-start.1
  582.7 38.8 %attention_back.1 = (bf16[2048,512]{1,0:T(8,128)(2,1)}, f32[8,128]{1,0:T(8,128)S(1)}) custom-call(bf16[2048,256]{1,0:T(8,128)(2,1)S(1)} %copy-done.8, bf16[2048,128]{1,0:T(8,128)(2,1)S(1)} %copy-done.9, bf16[2048,128]{1,0:T(8,128)(2,1)S(1)} %copy-done.10, bf16[2048,256]{1,0:T(8,128)(2,1)S(1)} %bitcast.44, f32[8,2048]{1,0:T(8,128)S(1)} %copy-done.11, ...), custom_call_target="tpu_custom_call" | custom-call | flops 43699998720 | bytes 1024 | tf_op jit(solution)/shard_map/attention_back/pallas_call | solution.py:986
  621.6 6.3 convolution_convert_fusion
  627.9 1.9 pad_maximum_fusion.1
  629.8 213.1 %last.1 = (f32[256,2048]{1,0:T(8,128)}, f32[16,128]{1,0:T(8,128)}, bf16[8,512,768]{2,1,0:T(8,128)(2,1)}) custom-call(bf16[8,256,512]{2,1,0:T(8,128)(2,1)} %bitcast.65, bf16[2048,768]{1,0:T(8,128)(2,1)} %get-tuple-element.55.refs_6_.refs_1_, bf16[256,2048]{1,0:T(8,128)(2,1)} %bitcast.58, f32[256,2048]{1,0:T(8,128)} %get-tuple-element.75.refs_3_, ...), custom_call_target="tpu_custom_call" | custom-call | flops 103499997184 | bytes 1024 | tf_op jit(solution)/shard_map/last/pallas_call | solution.py:766
  842.9 2.8 copy-done.1
  845.7 5.3 spread_heads.1
  851.0 0.6 fusion.3
  851.5 0.6 slice_bitcast_fusion
  852.1 6.4 copy-done
  858.5 12.6 %spread_feed.1 = (f32[512,6144]{1,0:T(8,128)}, f32[512,6144]{1,0:T(8,128)}, f32[6144,512]{1,0:T(8,128)}) custom-call(bf16[8,512,2304]{2,1,0:T(8,128)(2,1)S(1)} %bitcast.40), custom_call_target="tpu_custom_call" | custom-call | tf_op jit(solution)/shard_map/spread_feed/pallas_call | solution.py:1015
  871.1 1.0 copy.47
  872.0 1.3 copy.48
  (43 shorter events, 0.1 us)
Async XLA Ops:
  7.2 257.8 %all-gather.4.cloned.1.call-start = ((), (), s32[]{:S(2)}) async-start(), calls=%async_computation.1 | async-start | bytes 11796480 | tf_op jit(solution)/shard_map/all_gather | solution.py:1099
  8.7 3.2 copy-start.16
  8.7 3.2 copy-start.17
  8.7 3.2 copy-start.20
  8.7 3.2 copy-start.21
  8.7 3.9 copy-start.18
  8.8 3.9 copy-start.19
  11.9 564.2 %reduce-scatter.2.cloned.1.call-start = ((), (), s32[]{:S(2)}) async-start(), calls=%async_computation.2 | async-start | bytes 11796480 | tf_op jit(solution)/shard_map/reduce_scatter | solution.py:1102
  112.5 8.5 copy-start.3
  354.1 10.4 %copy-start.22 = (bf16[8,256,2048]{2,1,0:T(8,128)(2,1)S(1)}, bf16[8,256,2048]{2,1,0:T(8,128)(2,1)}, u32[]{:S(2)}) copy-start(bf16[8,256,2048]{2,1,0:T(8,128)(2,1)} %get-tuple-element.60) | copy-start | bytes 25165828
  354.1 10.4 %copy-start.23 = (bf16[8,256,1536]{2,1,0:T(8,128)(2,1)S(1)}, bf16[8,256,1536]{2,1,0:T(8,128)(2,1)}, u32[]{:S(2)}) copy-start(bf16[8,256,1536]{2,1,0:T(8,128)(2,1)} %get-tuple-element.62.refs_0_) | copy-start | bytes 18874372
  383.4 468.7 %all-gather.6.cloned.1.call-start = ((), (), s32[]{:S(2)}) async-start(), calls=%async_computation.3 | async-start | bytes 21233664 | tf_op jit(solution)/shard_map/all_gather | solution.py:1105
  469.0 107.1 %copy-start.7 = (bf16[2048,256]{1,0:T(8,128)(2,1)S(1)}, bf16[2048,256]{1,0:T(8,128)(2,1)}, u32[]{:S(2)}) copy-start(bf16[2048,256]{1,0:T(8,128)(2,1)} %get-tuple-element.73.refs_5_) | copy-start | bytes 3145732
  576.1 6.5 copy-start.2
  576.1 6.5 copy-start.4
  576.1 6.5 copy-start.5
  576.1 6.5 copy-start.6
  576.1 6.5 copy-start.8
  576.2 6.5 copy-start.9
  576.2 6.5 copy-start.10
  576.2 6.5 copy-start.11
  576.2 45.4 %slice-start = ((s8[8388608]{0:T(1024)(128)(4,1)}), s8[4194304]{0:T(1024)(128)(4,1)S(1)}, s32[]{:S(2)}) async-start(s8[8388608]{0:T(1024)(128)(4,1)} %bitcast.59), calls=%async_computation.4 | async-start | bytes 8388608
  582.7 38.8 %slice-start.1 = ((s8[8388608]{0:T(1024)(128)(4,1)}), s8[4194304]{0:T(1024)(128)(4,1)S(1)}, s32[]{:S(2)}) async-start(s8[8388608]{0:T(1024)(128)(4,1)} %bitcast.59), calls=%async_computation.5 | async-start | bytes 8388608
  621.5 6.4 copy-start.12
  842.9 2.8 copy-start.1
  845.7 5.3 copy-start.15
  852.1 6.4 copy-start
  858.5 12.6 %copy-start.14 = (bf16[256,2048]{1,0:T(8,128)(2,1)S(1)}, bf16[256,2048]{1,0:T(8,128)(2,1)}, u32[]{:S(2)}) copy-start(bf16[256,2048]{1,0:T(8,128)(2,1)} %get-tuple-element.65) | copy-start | bytes 3145732
  858.5 13.5 %copy-start.13 = (f32[256,2048]{1,0:T(8,128)S(1)}, f32[256,2048]{1,0:T(8,128)}, u32[]{:S(2)}) copy-start(f32[256,2048]{1,0:T(8,128)} %get-tuple-element.80) | copy-start | bytes 6291460
Sparse Core Ops, SparseCore 0:
  12.0 129.7 all-gather.3
  383.5 94.4 reduce-scatter.1
  576.2 243.8 all-gather.5

commit v6 on v5

--- a/solution.py
+++ b/solution.py
@@ -383,6 +383,41 @@
     return pl.CostEstimate(
         flops=int(microseconds * 1.15e9), bytes_accessed=1024, transcendentals=0
     )
+
+
+class FsdpSum:
+    def __init__(self, grad, arrived, send_sems, recv_sems):
+        self.grad, self.arrived = grad, arrived
+        self.sems = send_sems, recv_sems
+        self.peers, self.ahead, _ = peers_of("fsdp")
+
+    def copy(self, i):
+        target = self.ahead(i)
+        return send(
+            self.grad.at[target], self.arrived.at[i], self.sems[0].at[i], self.sems[1].at[i], "fsdp", target
+        )
+
+    def start(self):
+        loop(self.peers, lambda i: self.copy(i).start())
+
+    def collect(self, land, slot):
+        shard = lax.axis_index("fsdp")
+        loop(self.peers, lambda i: self.copy(i).wait_recv())
+
+        def add(block):
+            value = self.grad[shard, block].astype(F32)
+            for i in range(self.peers):
+                value = value + self.arrived[i, block].astype(F32)
+            land[slot, block] = value.astype(BF16)
+
+        row_blocks(self.grad.shape[1], add)
+
+    def finish(self):
+        loop(self.peers, lambda i: self.copy(i).wait_send())
+
+
+def fsdp_scratch(shards, rows, width):
+    return [VMEM((shards - 1, rows, width), BF16)] + [pltpu.SemaphoreType.DMA((shards,))] * 2
 
 
 def copy_in(source, target, sem):
@@ -545,18 +580,21 @@
 
 
 def feed_back_kernel(columns, *refs):
-    back, weights, middle, grad, gain_rows, grad_middle, low, gain_sum = refs[:8]
-    weight, weight_sem, total = refs[8:11]
-    scratch = refs[11:]
-    chips = line_position()[3]
+    back, weights, middle, grad, gain_rows, down_grad, grad_middle, low, gain_sum, land = refs[:10]
+    weight, weight_sem, total = refs[10:13]
+    down_refs, gather_sems, scratch = refs[13:16], refs[16:22], refs[22:]
+    me, _, _, chips = line_position()
     copy = copy_in(weights.at[:, columns], weight, weight_sem)
 
     def produce(piece, chunk):
         return rdot(back[piece], weight[pl.ds(pl.multiple_of(chunk * WIDE, WIDE), WIDE), :])
 
+    down = FsdpSum(down_grad, *down_refs)
+    gather = Gather(land, gather_sems)
     scatter = Scatter(scratch, produce, total)
     scatter.begin()
-    line_barrier()
+    full_barrier()
+    down.start()
     copy.wait()
     scatter.prepare(0)
 
@@ -564,8 +602,17 @@
         scatter.step(time)
         scatter.prepare(time + 1)
 
+        @pl.when(time == 1)
+        def _():
+            down.collect(land, me)
+
+        @pl.when(time >= 1)
+        def _():
+            gather.step(time - 1)
+
     loop(chips - 1, step)
     scatter.finish()
+    gather.step(chips - 2)
     gain_sum[...] = jnp.zeros_like(gain_sum)
 
     def norm(block):
@@ -576,25 +623,32 @@
         gain_sum[0:1, :] += jnp.sum(terms, axis=0, keepdims=True)
 
     row_blocks(middle.shape[0], norm)
-
-
-def feed_back(back, weights, middle, grad, gain_rows):
+    gather.step(chips - 1)
+    gather.finish()
+    down.finish()
+
+
+def feed_back(back, weights, middle, grad, gain_rows, down_grad):
     parts, count, width = back.shape
+    shards, rows, down_width = down_grad.shape
     return pl.pallas_call(
         functools.partial(feed_back_kernel, pl.ds(0, width)),
         out_shape=(
             jax.ShapeDtypeStruct((count, D), F32),
             jax.ShapeDtypeStruct((count, D), BF16),
             jax.ShapeDtypeStruct((8, D), F32),
+            jax.ShapeDtypeStruct((parts, rows, down_width), BF16),
         ),
-        in_specs=[WHOLE, HBM, WHOLE, WHOLE, WHOLE],
-        out_specs=(WHOLE,) * 3,
+        in_specs=[WHOLE, HBM, WHOLE, WHOLE, WHOLE, WHOLE],
+        out_specs=(WHOLE,) * 4,
         scratch_shapes=[VMEM((D, width), BF16), pltpu.SemaphoreType.DMA, VMEM((count, D), F32)]
+        + fsdp_scratch(shards, rows, down_width)
+        + gather_scratch(parts // 2)
         + scatter_scratch(parts // 2, count),
-        compiler_params=params(3, 60),
-        cost_estimate=cost(86),
+        compiler_params=params(3, 62),
+        cost_estimate=cost(100),
         name="feed_back",
-    )(back, weights, middle, grad, gain_rows)
+    )(back, weights, middle, grad, gain_rows, down_grad)
 
 
 def turn_kernel(columns, down_columns, *refs):
@@ -667,8 +721,8 @@
 def last_kernel(columns, *refs):
     back, weights, x, grad_middle, gain_rows, gain_two, gain_heads, head_grad = refs[:8]
     hidden, gain_out, land = refs[8:11]
-    weight, weight_sem, total, gain_one, pack, pack_in, shard_sum, shard_in, head_in = refs[11:20]
-    small, gather_sems, scratch = refs[20:26], refs[26:32], refs[32:]
+    weight, weight_sem, total, gain_one, pack, pack_in, shard_sum, shard_in = refs[11:19]
+    small, head_refs, gather_sems, scratch = refs[19:23], refs[23:26], refs[26:32], refs[32:]
     me, _, _, chips = line_position()
     shard = lax.axis_index("fsdp")
     shards, ahead, _ = peers_of("fsdp")
@@ -678,30 +732,21 @@
     def produce(piece, chunk):
         return rdot(back[piece], weight[pl.ds(pl.multiple_of(chunk * WIDE, WIDE), WIDE), :])
 
-    def head_copy(i):
-        return send(head_grad.at[ahead(i)], head_in.at[i], small[4].at[i], small[5].at[i], "fsdp", ahead(i))
-
-    def head_sum(block):
-        value = head_grad[shard, block].astype(F32)
-        for i in range(shards):
-            value = value + head_in[i, block].astype(F32)
-        land[me, block] = value.astype(BF16)
-
+    heads = FsdpSum(head_grad, *head_refs)
     scatter = Scatter(scratch, produce, total)
     gather = Gather(land, gather_sems)
     scatter.begin()
     full_barrier()
     copy.wait()
     scatter.prepare(0)
-    loop(shards, lambda i: head_copy(i).start())
+    heads.start()
 
     def step(time):
         scatter.step(time)
 
         @pl.when(time == 1)
         def _():
-            loop(shards, lambda i: head_copy(i).wait_recv())
-            row_blocks(head_grad.shape[1], head_sum)
+            heads.collect(land, me)
 
         @pl.when(time >= 1)
         def _():
@@ -755,7 +800,7 @@
     loop(parts, add_sum)
     gather.step(chips - 1)
     gather.finish()
-    loop(shards, lambda i: head_copy(i).wait_send())
+    heads.finish()
     loop(shards, lambda i: pack_copy(i).wait_send())
     loop(parts, lambda i: sum_copy(i).wait_send())
 
@@ -781,11 +826,10 @@
             VMEM((shards, 16, 128), F32),
             VMEM((16, 128), F32),
             VMEM((parts, 16, 128), F32),
-            VMEM((shards - 1, rows, head_width), BF16),
         ]
         + [pltpu.SemaphoreType.DMA((shards,))] * 2
         + [pltpu.SemaphoreType.DMA((parts,))] * 2
-        + [pltpu.SemaphoreType.DMA((shards,))] * 2
+        + fsdp_scratch(shards, rows, head_width)
         + gather_scratch(parts // 2)
         + scatter_scratch(parts // 2, count),
         compiler_params=params(5, 60),
@@ -871,12 +915,11 @@
 
     def step(time):
         scatter.step(time)
-
-        @pl.when(time + 2 < chips)
-        def _():
-            gather.step(time + 2)
-
         scatter.prepare(time + 1)
+
+        @pl.when(time >= 1)
+        def _():
+            gather.step(time + 1)
 
     loop(chips - 1, step)
     scatter.finish()
@@ -1002,28 +1045,40 @@
     )(*operands)
 
 
-def spread_feed_kernel(width, source, gate, up, down):
+def spread_pair_kernel(width, source, gate, up):
     gate[...] = source[0, :, :width].astype(F32)
-    up[...] = source[0, :, width : 2 * width].astype(F32)
-    down[...] = source[0, :, 2 * width :].astype(F32).T
-
-
-def spread_feed(stacked):
+    up[...] = source[0, :, width:].astype(F32)
+
+
+def spread_pair(stacked):
     parts, rows, total = stacked.shape
-    width = total // 3
+    width = total // 2
     across = jax.ShapeDtypeStruct((rows, parts * width), F32)
     return pl.pallas_call(
-        functools.partial(spread_feed_kernel, width),
-        out_shape=(across, across, jax.ShapeDtypeStruct((parts * width, rows), F32)),
+        functools.partial(spread_pair_kernel, width),
+        out_shape=(across, across),
         grid=(parts,),
         in_specs=[pl.BlockSpec((1, rows, total), lambda i: (i, 0, 0))],
-        out_specs=(
-            pl.BlockSpec((rows, width), lambda i: (0, i)),
-            pl.BlockSpec((rows, width), lambda i: (0, i)),
-            pl.BlockSpec((width, rows), lambda i: (i, 0)),
-        ),
-        compiler_params=pltpu.CompilerParams(vmem_limit_bytes=32 * 1024 * 1024),
-        name="spread_feed",
+        out_specs=(pl.BlockSpec((rows, width), lambda i: (0, i)),) * 2,
+        compiler_params=pltpu.CompilerParams(vmem_limit_bytes=60 * 1024 * 1024),
+        name="spread_pair",
+    )(stacked)
+
+
+def spread_turned_kernel(source, target):
+    target[...] = source[0].astype(F32).T
+
+
+def spread_turned(stacked):
+    parts, rows, width = stacked.shape
+    return pl.pallas_call(
+        spread_turned_kernel,
+        out_shape=jax.ShapeDtypeStruct((parts * width, rows), F32),
+        grid=(parts,),
+        in_specs=[pl.BlockSpec((1, rows, width), lambda i: (i, 0, 0))],
+        out_specs=pl.BlockSpec((width, rows), lambda i: (i, 0)),
+        compiler_params=pltpu.CompilerParams(vmem_limit_bytes=60 * 1024 * 1024),
+        name="spread_turned",
     )(stacked)
 
 
@@ -1047,7 +1102,7 @@
         in_specs=[pl.BlockSpec((1, rows, total), lambda i: (i, 0, 0))],
         out_specs=tuple(pl.BlockSpec((rows, w), lambda i: (0, i)) for w in widths)
         + (pl.BlockSpec((width, rows), lambda i: (i, 0)),),
-        compiler_params=pltpu.CompilerParams(vmem_limit_bytes=32 * 1024 * 1024),
+        compiler_params=pltpu.CompilerParams(vmem_limit_bytes=60 * 1024 * 1024),
         name="spread_heads",
     )(stacked)
 
@@ -1154,20 +1209,19 @@
     flat_grad = grad_all.reshape(tokens, D)
     flat_back = back.reshape(tokens, 2 * feed_width)
     flat_activation = activation.reshape(tokens, feed_width)
-    feed_grad = jnp.concatenate(
-        [
-            by_row(tdot(normed_two_all.reshape(tokens, D), flat_back).astype(BF16)),
-            by_row(tdot(flat_grad, flat_activation).astype(BF16)),
-        ],
-        axis=1,
+    feed_grad = by_row(tdot(normed_two_all.reshape(tokens, D), flat_back).astype(BF16))
+    down_grad = by_row(tdot(flat_grad, flat_activation).astype(BF16))
+    back, feed_grad, down_grad = lax.optimization_barrier((back, feed_grad, down_grad))
+    feed_shard = sum_rows(feed_grad)
+
+    grad_middle, low, gain_two, down_parts = feed_back(
+        back, feed_weight, middle, grad, gain_rows, down_grad.reshape(shards, rows, feed_width)
     )
-    back, feed_grad = lax.optimization_barrier((back, feed_grad))
-    feed_shard = sum_rows(feed_grad)
-
-    grad_middle, low, gain_two = feed_back(back, feed_weight, middle, grad, gain_rows)
     low_all, context_grad, hidden_out = turn(low, heads_weight, activation, feed_weight, middle, width)
 
-    context_grad, feed_shard = lax.optimization_barrier((context_grad, feed_shard))
+    context_grad, feed_shard, down_parts = lax.optimization_barrier(
+        (context_grad, feed_shard, down_parts)
+    )
     feed_parts = gather_parts(feed_shard)
     context_grad = context_grad.reshape(tokens, width)
     grad_qkv, gain_heads = attention_back(
@@ -1192,6 +1246,8 @@
         ],
         axis=1,
     )
+    grad_down = spread_turned(down_parts)
+    grad_qkv, grad_down = lax.optimization_barrier((grad_qkv, grad_down))
     grad_hidden, gain_sums, head_parts = last(
         grad_qkv.reshape(parts, count, -1),
         heads_weight,
@@ -1204,7 +1260,7 @@
     )
 
     gain_sums = gain_sums.reshape(-1)
-    grad_gate, grad_up, grad_down = spread_feed(feed_parts)
+    grad_gate, grad_up = spread_pair(feed_parts)
     grad_query, grad_key, grad_value, grad_out_weight = spread_heads(head_parts, width)
     if sharers > 1:
         grad_key, grad_value = (

time: 881 us -> 916 us (1.040)
  Pallas kernels: 789 us -> 823 us
    pallas_call x1, Pallas kernels: 85.5 us -> 160 us  [feed_back(): pl.pallas_call(functools.partial(feed_back_kernel, pl.ds(0, width)), out_...]
    pallas_call x1, Pallas kernels: 213 us -> 154 us  [last(): pl.pallas_call(functools.partial(last_kernel, pl.ds(0, width)), out_shape...]
    pallas_call x1 -> x2, Pallas kernels: 12.6 us -> 24.7 us  [the longest x1 14.4 us: spread_pair(): pl.pallas_call(functools.partial(spread_pair_kernel, width), out_shape=(a...]
  transfers between devices with their start and end apart: 3 -> 3, of which waited for: 0 -> 0; matrix products, arithmetic and copies ran while one was open for 4% -> 4% of each run, Pallas kernels for 78% -> 79%
where the time goes in v6:
time: 916 us; the launch traced here: 908 us
  Pallas kernels  823 us (90%)
  matrix products  42.8 us (5%)
  local copies, waits for them, and re-layouts  15 us (2%)
  between operations  14.5 us (2%)
  other arithmetic  12.9 us (1%)
    pallas_call x1, Pallas kernels, feed_back(): pl.pallas_call(functools.partial(feed_back_kernel, pl.ds(0, width)), out_...  160 us
    pallas_call x1, Pallas kernels, last(): pl.pallas_call(functools.partial(last_kernel, pl.ds(0, width)), out_shape...  154 us
    pallas_call x1, Pallas kernels, attend(): pl.pallas_call(functools.partial(attend_kernel, heads, pl.ds(weights.shap...  145 us
    pallas_call x1, Pallas kernels, turn(): pl.pallas_call(functools.partial(turn_kernel, pl.ds(weights.shape[1] - wi...  110 us
    pallas_call x1, Pallas kernels, first(): pl.pallas_call(functools.partial(first_kernel, D // shards, width), out_s...  93.2 us
    pallas_call x1, Pallas kernels, feed(): pl.pallas_call(functools.partial(feed_kernel, width), out_shape=(jax.Shap...  89 us
    dot_general x4, matrix products, tdot(): lax.dot_general(left, right, (((0,), (0,)), ((), ())), preferred_element_...  42.8 us
    pallas_call x1, Pallas kernels, attention_back(): pl.pallas_call(functools.partial(attention_back_kernel, heads), out_shape...  37.5 us
  transfers between devices with their start and end apart: 3, of which 0 were waited for; matrix products, arithmetic and copies ran while one was open for 4% of the time, Pallas kernels for 79%

profile of v6, /device:TPU:0, one launch (start us, length us, event | category | flops | bytes accessed | tf_op | source)
XLA Modules:
  0.0 907.9 jit_solution(124765700262457061)
XLA Ops:
  7.2 0.0 all-gather.4.cloned.1.call-start
  7.2 1.2 constant_dynamic-slice_fusion
  8.4 0.3 copy.41
  8.7 1.5 constant_dynamic-slice_fusion.1
  10.2 0.0 copy-start.15
  10.2 0.0 copy-start.16
  10.2 0.0 copy-start.19
  10.2 0.0 copy-start.20
  10.2 0.0 copy-start.17
  10.2 0.0 copy-start.18
  10.3 1.6 pad_maximum_fusion.1
  11.8 0.0 all-gather.4.cloned.1.call-update
  11.8 0.0 reduce-scatter.2.cloned.1.call-start
  11.9 0.0 copy-done.15
  11.9 0.1 concatenate.21
  12.0 0.6 bitcast_convert_fusion.2.refs_1_
  12.6 0.6 pad.10.refs_2_
  13.2 1.0 constant_dynamic-slice_fusion.6
  14.2 1.0 constant_dynamic-slice_fusion.3
  15.2 0.1 copy.40
  15.3 1.0 constant_dynamic-slice_fusion.4
  16.3 0.9 pad_maximum_fusion.4.refs_3_
  17.3 93.2 %gather_normed.1 = (bf16[8,256,2048]{2,1,0:T(8,128)(2,1)}, f32[8,256,512]{2,1,0:T(8,128)}, bf16[2048,768]{1,0:T(8,128)(2,1)}, f32[8,2048]{1,0:T(8,128)}, f32[4,16,128]{2,1,0:T(8,128)}, /*index=5*/s32[8,8,256]{2,1,0:T(8,128)}) custom-call(bf16[256,2048]{1,0:T(8,128)(2,1)} %bitcast.57, f32[16,128]{1,0:T(8,128)} %bitcast_convert_fusion.2.refs_1_, ...), custom_call_target="tpu_custom_call" | custom-call | flops 97749999616 | bytes 1024 | tf_op jit(solution)/shard_map/gather_normed/pallas_call | solution.py:487
  110.5 0.8 copy.44
  111.3 0.1 fusion.2
  111.4 0.1 reshape.87
  111.5 0.1 reshape.88
  111.5 0.9 fusion.1
  112.5 0.0 copy-start.1
  112.5 1.3 copy.33.refs_4_.refs_10_
  113.8 0.1 pad.18.clone
  113.9 0.7 maximum_maximum_fusion.refs_3_.refs_9_
  114.6 3.7 fusion
  118.3 1.3 pad_maximum_fusion.2.refs_1_.refs_7_
  119.6 1.3 pad_maximum_fusion.3.refs_2_.refs_8_
  120.9 144.5 %attend.1 = (bf16[2048,256]{1,0:T(8,128)(2,1)}, bf16[2048,128]{1,0:T(8,128)(2,1)}, bf16[2048,128]{1,0:T(8,128)(2,1)}, bf16[2048,256]{1,0:T(8,128)(2,1)}, f32[8,2...) custom-call(f32[2048,512]{1,0:T(8,128)} %bitcast.62, ...), custom_call_target="tpu_custom_call" | custom-call | flops 126500003840 | bytes 1024 | tf_op jit(solution)/shard_map/attend/pallas_call | solution.py:941
  265.5 0.0 all-gather.4.cloned.1.call-done.refs_2_.refs_1_.refs_3_
  265.5 89.0 %feed.1 = (bf16[8,256,2048]{2,1,0:T(8,128)(2,1)}, bf16[8,256,768]{2,1,0:T(8,128)(2,1)}, bf16[8,256,1536]{2,1,0:T(8,128)(2,1)}) custom-call(bf16[256,2048]{1,0:T(8,128)(2,1)} %get-tuple-element.61.refs_0_, bf16[8,256,2048]{2,1,0:T(8,128)(2,1)} %get-tuple-element.62.refs_1_, bf16[2048,2304]{1,0:T(8,128)(2,1)} %all-gather.4.cloned.1.call-done.refs_2_.refs_1_.refs_3_), custom_call_target="tpu_custom_call" | custom-call | flops 103499997184 | bytes 1024 | tf_op jit(solution)/shard_map/feed/pallas_call | solution.py:552
  354.6 11.5 %bitcast_convert_fusion.1 = bf16[2048,768]{1,0:T(8,128)(2,1)} fusion(bf16[8,256,2048]{2,1,0:T(8,128)(2,1)} %get-tuple-element.62.refs_1_, bf16[8,256,768]{2,1,0:T(8,128)(2,1)} %get-tuple-element.65.refs_2_), kind=kOutput, calls=%fused_computation.1 | convolution fusion | flops 6444023808 | bytes 14680064 | tf_op jit(solution)/shard_map/dot_general | solution.py:33
  366.1 0.0 copy-done.21
  366.1 15.7 %bitcast_convert_fusion = bf16[2048,1536]{1,0:T(8,128)(2,1)} fusion(bf16[8,256,2048]{2,1,0:T(8,128)(2,1)S(1)} %copy-done.21, bf16[8,256,1536]{2,1,0:T(8,128)(2,1)S(1)} %copy-done.22), kind=kOutput, calls=%fused_computation | convolution fusion | flops 12888047616 | bytes 20971520 | tf_op jit(solution)/shard_map/dot_general | solution.py:33
  381.8 0.0 reduce-scatter.2.cloned.1.call-update
  381.8 0.0 all-gather.6.cloned.1.call-start
  381.8 160.3 %feed_back.1 = (f32[256,2048]{1,0:T(8,128)}, bf16[256,2048]{1,0:T(8,128)(2,1)}, f32[8,2048]{1,0:T(8,128)}, bf16[8,512,768]{2,1,0:T(8,128)(2,1)}) custom-call(bf16[8,256,1536]{2,1,0:T(8,128)(2,1)} %get-tuple-element.66.refs_0_, bf16[2048,2304]{1,0:T(8,128)(2,1)} %all-gather.4.cloned.1.call-done.refs_2_.refs_1_.refs_3_, ...), custom_call_target="tpu_custom_call" | custom-call | flops 115000000512 | bytes 1024 | tf_op jit(solution)/shard_map/feed_back/pallas_call | solution.py:634
  542.1 110.1 %turn.1 = (bf16[8,256,2048]{2,1,0:T(8,128)(2,1)}, bf16[8,256,256]{2,1,0:T(8,128)(2,1)}, bf16[256,2048]{1,0:T(8,128)(2,1)}) custom-call(bf16[256,2048]{1,0:T(8,128)(2,1)} %get-tuple-element.69.refs_0_, bf16[2048,768]{1,0:T(8,128)(2,1)} %get-tuple-element.59.refs_6_.refs_1_, bf16[8,256,768]{2,1,0:T(8,128)(2,1)} %get-tuple-element.65.refs_2_, ...), custom_call_target="tpu_custom_call" | custom-call | flops 123050000384 | bytes 1024 | tf_op jit(solution)/shard_map/turn/pallas_call | solution.py:695
  652.3 0.0 reduce-scatter.2.cloned.1.call-done
  652.3 0.0 all-gather.6.cloned.1.call-update
  652.3 6.9 convolution_convert_fusion.1
  659.2 10.3 %spread_turned.1 = f32[6144,512]{1,0:T(8,128)} custom-call(bf16[8,512,768]{2,1,0:T(8,128)(2,1)} %get-tuple-element.81.source), custom_call_target="tpu_custom_call" | custom-call | tf_op jit(solution)/shard_map/spread_turned/pallas_call | solution.py:1074
  669.5 0.0 copy-done.2
  669.6 1.2 copy-done.6
  670.8 1.0 copy-done.8
  671.8 37.5 %attention_back.1 = (bf16[2048,512]{1,0:T(8,128)(2,1)}, f32[8,128]{1,0:T(8,128)S(1)}) custom-call(bf16[2048,256]{1,0:T(8,128)(2,1)S(1)} %copy-done.6, bf16[2048,128]{1,0:T(8,128)(2,1)S(1)} %copy-done.7, bf16[2048,128]{1,0:T(8,128)(2,1)S(1)} %copy-done.8, bf16[2048,256]{1,0:T(8,128)(2,1)S(1)} %bitcast.44, f32[8,2048]{1,0:T(8,128)S(1)} %copy-done.9, ...), custom_call_target="tpu_custom_call" | custom-call | flops 43699998720 | bytes 1024 | tf_op jit(solution)/shard_map/attention_back/pallas_call | solution.py:1029
  709.3 8.8 convolution_convert_fusion
  718.0 0.0 copy-done.10
  718.0 0.0 copy-done.13
  718.1 1.9 pad_maximum_fusion
  719.9 154.3 %last.1 = (f32[256,2048]{1,0:T(8,128)}, f32[16,128]{1,0:T(8,128)}, bf16[8,512,768]{2,1,0:T(8,128)(2,1)}) custom-call(bf16[8,256,512]{2,1,0:T(8,128)(2,1)} %bitcast.65, bf16[2048,768]{1,0:T(8,128)(2,1)} %get-tuple-element.59.refs_6_.refs_1_, bf16[256,2048]{1,0:T(8,128)(2,1)} %bitcast.59, f32[256,2048]{1,0:T(8,128)} %get-tuple-element.83.refs_3_, ...), custom_call_target="tpu_custom_call" | custom-call | flops 103499997184 | bytes 1024 | tf_op jit(solution)/shard_map/last/pallas_call | solution.py:811
  874.2 8.8 spread_heads.1
  883.1 0.6 fusion.3
  883.7 0.6 slice_bitcast_fusion
  884.3 14.4 %spread_pair.1 = (f32[512,6144]{1,0:T(8,128)}, f32[512,6144]{1,0:T(8,128)}) custom-call(bf16[8,512,1536]{2,1,0:T(8,128)(2,1)} %bitcast.45), custom_call_target="tpu_custom_call" | custom-call | tf_op jit(solution)/shard_map/spread_pair/pallas_call | solution.py:1057
  898.7 1.0 copy.47
  899.7 1.3 copy.48
  (36 shorter events, 0.1 us)
Async XLA Ops:
  7.2 258.3 %all-gather.4.cloned.1.call-start = ((), (), s32[]{:S(2)}) async-start(), calls=%async_computation.1 | async-start | bytes 11796480 | tf_op jit(solution)/shard_map/all_gather | solution.py:1154
  10.2 1.7 copy-start.15
  10.2 1.7 copy-start.16
  10.2 1.7 copy-start.19
  10.2 1.7 copy-start.20
  10.2 2.4 copy-start.17
  10.2 2.4 copy-start.18
  11.8 640.4 %reduce-scatter.2.cloned.1.call-start = ((), (), s32[]{:S(2)}) async-start(), calls=%async_computation.2 | async-start | bytes 7864320 | tf_op jit(solution)/shard_map/reduce_scatter | solution.py:1157
  112.5 8.5 copy-start.1
  354.6 11.5 %copy-start.21 = (bf16[8,256,2048]{2,1,0:T(8,128)(2,1)S(1)}, bf16[8,256,2048]{2,1,0:T(8,128)(2,1)}, u32[]{:S(2)}) copy-start(bf16[8,256,2048]{2,1,0:T(8,128)(2,1)} %get-tuple-element.64) | copy-start | bytes 25165828
  354.6 11.5 %copy-start.22 = (bf16[8,256,1536]{2,1,0:T(8,128)(2,1)S(1)}, bf16[8,256,1536]{2,1,0:T(8,128)(2,1)}, u32[]{:S(2)}) copy-start(bf16[8,256,1536]{2,1,0:T(8,128)(2,1)} %get-tuple-element.66.refs_0_) | copy-start | bytes 18874372
  381.8 502.5 %all-gather.6.cloned.1.call-start = ((), (), s32[]{:S(2)}) async-start(), calls=%async_computation.3 | async-start | bytes 14155776 | tf_op jit(solution)/shard_map/all_gather | solution.py:1160
  542.1 110.2 %copy-start.5 = (bf16[2048,256]{1,0:T(8,128)(2,1)S(1)}, bf16[2048,256]{1,0:T(8,128)(2,1)}, u32[]{:S(2)}) copy-start(bf16[2048,256]{1,0:T(8,128)(2,1)} %get-tuple-element.79.refs_5_) | copy-start | bytes 3145732
  659.2 10.3 %copy-start = (f32[2048,128]{1,0:T(8,128)S(1)}, f32[2048,128]{1,0:T(8,128)}, u32[]{:S(2)}) copy-start(f32[2048,128]{1,0:T(8,128)} %pad_maximum_fusion.2.refs_1_.refs_7_) | copy-start | bytes 3145732
  659.2 10.3 %copy-start.2 = (s32[8,1,256]{2,1,0:T(1,128)S(1)}, s32[8,1,256]{2,1,0:T(1,128)}, u32[]{:S(2)}) copy-start(s32[8,1,256]{2,1,0:T(1,128)} %copy-done.1) | copy-start | bytes 24580
  659.2 10.3 %copy-start.3 = (f32[8,128]{1,0:T(8,128)S(1)}, f32[8,128]{1,0:T(8,128)}, u32[]{:S(2)}) copy-start(f32[8,128]{1,0:T(8,128)} %maximum_maximum_fusion.refs_3_.refs_9_) | copy-start | bytes 12292
  659.2 10.3 %copy-start.4 = (bf16[8,256,256]{2,1,0:T(8,128)(2,1)S(1)}, bf16[8,256,256]{2,1,0:T(8,128)(2,1)}, u32[]{:S(2)}) copy-start(bf16[8,256,256]{2,1,0:T(8,128)(2,1)} %get-tuple-element.77) | copy-start | bytes 3145732
  659.2 10.3 %copy-start.7 = (bf16[2048,128]{1,0:T(8,128)(2,1)S(1)}, bf16[2048,128]{1,0:T(8,128)(2,1)}, u32[]{:S(2)}) copy-start(bf16[2048,128]{1,0:T(8,128)(2,1)} %get-tuple-element.72.refs_1_) | copy-start | bytes 1572868
  659.2 10.3 %copy-start.9 = (f32[8,2048]{1,0:T(8,128)S(1)}, f32[8,2048]{1,0:T(8,128)}, u32[]{:S(2)}) copy-start(f32[8,2048]{1,0:T(8,128)} %get-tuple-element.78.refs_4_) | copy-start | bytes 196612
  669.5 1.2 copy-start.6
  670.8 1.0 copy-start.8
  709.3 8.8 copy-start.10
  709.3 8.8 copy-start.13
  874.2 8.9 copy-start.14
  884.3 14.4 %copy-start.12 = (bf16[256,2048]{1,0:T(8,128)(2,1)S(1)}, bf16[256,2048]{1,0:T(8,128)(2,1)}, u32[]{:S(2)}) copy-start(bf16[256,2048]{1,0:T(8,128)(2,1)} %get-tuple-element.70) | copy-start | bytes 3145732
  884.3 15.4 %copy-start.11 = (f32[256,2048]{1,0:T(8,128)S(1)}, f32[256,2048]{1,0:T(8,128)}, u32[]{:S(2)}) copy-start(f32[256,2048]{1,0:T(8,128)} %get-tuple-element.88) | copy-start | bytes 6291460
Sparse Core Ops, SparseCore 0:
  12.0 129.7 all-gather.3
  381.9 103.2 reduce-scatter.1
  652.4 142.7 all-gather.5

commit v7 on v6

--- a/solution.py
+++ b/solution.py
@@ -950,7 +950,7 @@
             jax.ShapeDtypeStruct((count, D), BF16),
             jax.ShapeDtypeStruct((parts, count, D), BF16),
         ),
-        in_specs=[WHOLE] * 6 + [HBM, WHOLE, HBM, WHOLE],
+        in_specs=[WHOLE] * 6 + [HBM, WHOLE, WHOLE, WHOLE],
         out_specs=(WHOLE,) * 7 + (HBM,),
         scratch_shapes=[
             VMEM((D, width), BF16),
@@ -1212,11 +1212,12 @@
     feed_grad = by_row(tdot(normed_two_all.reshape(tokens, D), flat_back).astype(BF16))
     down_grad = by_row(tdot(flat_grad, flat_activation).astype(BF16))
     back, feed_grad, down_grad = lax.optimization_barrier((back, feed_grad, down_grad))
-    feed_shard = sum_rows(feed_grad)
 
     grad_middle, low, gain_two, down_parts = feed_back(
         back, feed_weight, middle, grad, gain_rows, down_grad.reshape(shards, rows, feed_width)
     )
+    low, feed_grad = lax.optimization_barrier((low, feed_grad))
+    feed_shard = sum_rows(feed_grad)
     low_all, context_grad, hidden_out = turn(low, heads_weight, activation, feed_weight, middle, width)
 
     context_grad, feed_shard, down_parts = lax.optimization_barrier(

time: 916 us -> 855 us (0.933)
  Pallas kernels: 823 us -> 762 us
    pallas_call x1, Pallas kernels: 160 us -> 126 us  [feed_back(): pl.pallas_call(functools.partial(feed_back_kernel, pl.ds(0, width)), out_...]
    pallas_call x1, Pallas kernels: 145 us -> 118 us  [attend(): pl.pallas_call(functools.partial(attend_kernel, heads, pl.ds(weights.shap...]
  transfers between devices with their start and end apart: 3 -> 3, of which waited for: 0 -> 0; matrix products, arithmetic and copies ran while one was open for 4% -> 4% of each run, Pallas kernels for 79% -> 63%
where the time goes in v7:
time: 855 us; the launch traced here: 847 us
  Pallas kernels  762 us (89%)
  matrix products  42.7 us (5%)
  local copies, waits for them, and re-layouts  15 us (2%)
  between operations  14.5 us (2%)
  other arithmetic  12.9 us (2%)
    pallas_call x1, Pallas kernels, last(): pl.pallas_call(functools.partial(last_kernel, pl.ds(0, width)), out_shape...  154 us
    pallas_call x1, Pallas kernels, feed_back(): pl.pallas_call(functools.partial(feed_back_kernel, pl.ds(0, width)), out_...  126 us
    pallas_call x1, Pallas kernels, attend(): pl.pallas_call(functools.partial(attend_kernel, heads, pl.ds(weights.shap...  118 us
    pallas_call x1, Pallas kernels, turn(): pl.pallas_call(functools.partial(turn_kernel, pl.ds(weights.shape[1] - wi...  111 us
    pallas_call x1, Pallas kernels, first(): pl.pallas_call(functools.partial(first_kernel, D // shards, width), out_s...  93.2 us
    pallas_call x1, Pallas kernels, feed(): pl.pallas_call(functools.partial(feed_kernel, width), out_shape=(jax.Shap...  89.4 us
    dot_general x4, matrix products, tdot(): lax.dot_general(left, right, (((0,), (0,)), ((), ())), preferred_element_...  42.7 us
    pallas_call x1, Pallas kernels, attention_back(): pl.pallas_call(functools.partial(attention_back_kernel, heads), out_shape...  37.5 us
  transfers between devices with their start and end apart: 3, of which 0 were waited for; matrix products, arithmetic and copies ran while one was open for 4% of the time, Pallas kernels for 63%

profile of v7, /device:TPU:0, one launch (start us, length us, event | category | flops | bytes accessed | tf_op | source)
XLA Modules:
  0.0 846.9 jit_solution(5845151323674228184)
XLA Ops:
  7.2 0.0 all-gather.4.cloned.1.call-start
  7.2 1.2 constant_dynamic-slice_fusion
  8.4 0.3 copy.41
  8.7 1.5 constant_dynamic-slice_fusion.1
  10.2 0.0 copy-start.15
  10.2 0.0 copy-start.16
  10.2 0.0 copy-start.19
  10.2 0.0 copy-start.20
  10.2 0.0 copy-start.17
  10.2 0.0 copy-start.18
  10.3 1.6 pad_maximum_fusion.1
  11.8 0.0 all-gather.4.cloned.1.call-update
  11.8 0.0 reduce-scatter.2.cloned.1.call-start
  11.9 0.0 copy-done.15
  11.9 0.0 copy-done.16
  11.9 0.0 copy-done.19
  11.9 0.0 copy-done.20
  11.9 0.1 concatenate.21
  12.0 0.6 bitcast_convert_fusion.2.refs_1_
  12.6 0.0 copy-done.17
  12.6 0.6 pad.10.refs_2_
  13.2 1.0 constant_dynamic-slice_fusion.6
  14.2 1.0 constant_dynamic-slice_fusion.3
  15.2 0.1 copy.40
  15.3 1.0 constant_dynamic-slice_fusion.4
  16.3 0.9 pad_maximum_fusion.4.refs_3_
  17.3 93.2 %gather_normed.1 = (bf16[8,256,2048]{2,1,0:T(8,128)(2,1)}, f32[8,256,512]{2,1,0:T(8,128)}, bf16[2048,768]{1,0:T(8,128)(2,1)}, f32[8,2048]{1,0:T(8,128)}, f32[4,16,128]{2,1,0:T(8,128)}, /*index=5*/s32[8,8,256]{2,1,0:T(8,128)}) custom-call(bf16[256,2048]{1,0:T(8,128)(2,1)} %bitcast.57, f32[16,128]{1,0:T(8,128)} %bitcast_convert_fusion.2.refs_1_, ...), custom_call_target="tpu_custom_call" | custom-call | flops 97749999616 | bytes 1024 | tf_op jit(solution)/shard_map/gather_normed/pallas_call | solution.py:487
  110.5 0.8 copy.44
  111.3 0.1 fusion.2
  111.4 0.1 reshape.87
  111.5 0.1 reshape.88
  111.5 0.9 fusion.1
  112.5 0.0 copy-start.1
  112.5 1.3 copy.33.refs_4_.refs_10_
  113.8 0.1 pad.18.clone
  113.9 0.7 maximum_maximum_fusion.refs_3_.refs_9_
  114.6 3.7 fusion
  118.3 1.3 pad_maximum_fusion.2.refs_1_.refs_7_
  119.6 1.3 pad_maximum_fusion.3.refs_2_.refs_8_
  120.9 117.9 %attend.1 = (bf16[2048,256]{1,0:T(8,128)(2,1)}, bf16[2048,128]{1,0:T(8,128)(2,1)}, bf16[2048,128]{1,0:T(8,128)(2,1)}, bf16[2048,256]{1,0:T(8,128)(2,1)}, f32[8,2...) custom-call(f32[2048,512]{1,0:T(8,128)} %bitcast.62, ...), custom_call_target="tpu_custom_call" | custom-call | flops 126500003840 | bytes 1024 | tf_op jit(solution)/shard_map/attend/pallas_call | solution.py:941
  238.8 0.0 all-gather.4.cloned.1.call-done.refs_2_.refs_1_.refs_3_
  238.8 89.4 %feed.1 = (bf16[8,256,2048]{2,1,0:T(8,128)(2,1)}, bf16[8,256,768]{2,1,0:T(8,128)(2,1)}, bf16[8,256,1536]{2,1,0:T(8,128)(2,1)}) custom-call(bf16[256,2048]{1,0:T(8,128)(2,1)} %get-tuple-element.63.refs_0_, bf16[8,256,2048]{2,1,0:T(8,128)(2,1)} %get-tuple-element.64.refs_1_, bf16[2048,2304]{1,0:T(8,128)(2,1)} %all-gather.4.cloned.1.call-done.refs_2_.refs_1_.refs_3_), custom_call_target="tpu_custom_call" | custom-call | flops 103499997184 | bytes 1024 | tf_op jit(solution)/shard_map/feed/pallas_call | solution.py:552
  328.2 11.5 %bitcast_convert_fusion.1 = bf16[2048,768]{1,0:T(8,128)(2,1)} fusion(bf16[8,256,2048]{2,1,0:T(8,128)(2,1)} %get-tuple-element.64.refs_1_, bf16[8,256,768]{2,1,0:T(8,128)(2,1)} %get-tuple-element.67.refs_2_), kind=kOutput, calls=%fused_computation.1 | convolution fusion | flops 6444023808 | bytes 14680064 | tf_op jit(solution)/shard_map/dot_general | solution.py:33
  339.8 15.7 %bitcast_convert_fusion = bf16[2048,1536]{1,0:T(8,128)(2,1)} fusion(bf16[8,256,2048]{2,1,0:T(8,128)(2,1)S(1)} %copy-done.21, bf16[8,256,1536]{2,1,0:T(8,128)(2,1)S(1)} %copy-done.22), kind=kOutput, calls=%fused_computation | convolution fusion | flops 12888047616 | bytes 20971520 | tf_op jit(solution)/shard_map/dot_general | solution.py:33
  355.4 125.5 %feed_back.1 = (f32[256,2048]{1,0:T(8,128)}, bf16[256,2048]{1,0:T(8,128)(2,1)}, f32[8,2048]{1,0:T(8,128)}, bf16[8,512,768]{2,1,0:T(8,128)(2,1)}) custom-call(bf16[8,256,1536]{2,1,0:T(8,128)(2,1)} %get-tuple-element.68.refs_0_, bf16[2048,2304]{1,0:T(8,128)(2,1)} %all-gather.4.cloned.1.call-done.refs_2_.refs_1_.refs_3_, ...), custom_call_target="tpu_custom_call" | custom-call | flops 115000000512 | bytes 1024 | tf_op jit(solution)/shard_map/feed_back/pallas_call | solution.py:634
  481.0 0.0 reduce-scatter.2.cloned.1.call-update
  481.0 0.0 all-gather.6.cloned.1.call-start
  481.0 110.5 %turn.1 = (bf16[8,256,2048]{2,1,0:T(8,128)(2,1)}, bf16[8,256,256]{2,1,0:T(8,128)(2,1)}, bf16[256,2048]{1,0:T(8,128)(2,1)}) custom-call(bf16[256,2048]{1,0:T(8,128)(2,1)} %get-tuple-element.73.refs_0_, bf16[2048,768]{1,0:T(8,128)(2,1)} %get-tuple-element.61.refs_6_.refs_1_, bf16[8,256,768]{2,1,0:T(8,128)(2,1)} %get-tuple-element.67.refs_2_, ...), custom_call_target="tpu_custom_call" | custom-call | flops 123050000384 | bytes 1024 | tf_op jit(solution)/shard_map/turn/pallas_call | solution.py:695
  591.6 0.0 reduce-scatter.2.cloned.1.call-done
  591.6 0.0 all-gather.6.cloned.1.call-update
  591.6 6.9 convolution_convert_fusion.1
  598.5 10.6 %spread_turned.1 = f32[6144,512]{1,0:T(8,128)} custom-call(bf16[8,512,768]{2,1,0:T(8,128)(2,1)} %get-tuple-element.85.source), custom_call_target="tpu_custom_call" | custom-call | tf_op jit(solution)/shard_map/spread_turned/pallas_call | solution.py:1074
  609.2 1.2 copy-done.6
  610.4 1.0 copy-done.8
  611.4 37.5 %attention_back.1 = (bf16[2048,512]{1,0:T(8,128)(2,1)}, f32[8,128]{1,0:T(8,128)S(1)}) custom-call(bf16[2048,256]{1,0:T(8,128)(2,1)S(1)} %copy-done.6, bf16[2048,128]{1,0:T(8,128)(2,1)S(1)} %copy-done.7, bf16[2048,128]{1,0:T(8,128)(2,1)S(1)} %copy-done.8, bf16[2048,256]{1,0:T(8,128)(2,1)S(1)} %bitcast.44, f32[8,2048]{1,0:T(8,128)S(1)} %copy-done.9, ...), custom_call_target="tpu_custom_call" | custom-call | flops 43699998720 | bytes 1024 | tf_op jit(solution)/shard_map/attention_back/pallas_call | solution.py:1029
  648.9 8.7 %convolution_convert_fusion = bf16[2048,512]{1,0:T(8,128)(2,1)S(1)} fusion(bf16[2048,2048]{1,0:T(8,128)(2,1)} %bitcast.60, bf16[2048,512]{1,0:T(8,128)(2,1)} %get-tuple-element.86), kind=kOutput, calls=%fused_computation.3 | convolution fusion | flops 4296015872 | bytes 12582912 | tf_op jit(solution)/shard_map/dot_general | solution.py:33
  657.6 1.9 pad_maximum_fusion
  659.5 153.7 %last.1 = (f32[256,2048]{1,0:T(8,128)}, f32[16,128]{1,0:T(8,128)}, bf16[8,512,768]{2,1,0:T(8,128)(2,1)}) custom-call(bf16[8,256,512]{2,1,0:T(8,128)(2,1)} %bitcast.65, bf16[2048,768]{1,0:T(8,128)(2,1)} %get-tuple-element.61.refs_6_.refs_1_, bf16[256,2048]{1,0:T(8,128)(2,1)} %bitcast.59, f32[256,2048]{1,0:T(8,128)} %get-tuple-element.87.refs_3_, ...), custom_call_target="tpu_custom_call" | custom-call | flops 103499997184 | bytes 1024 | tf_op jit(solution)/shard_map/last/pallas_call | solution.py:811
  813.2 8.8 %spread_heads.1 = (f32[512,2048]{1,0:T(8,128)}, f32[512,1024]{1,0:T(8,128)}, f32[512,1024]{1,0:T(8,128)}, f32[2048,512]{1,0:T(8,128)}) custom-call(bf16[8,512,768]{2,1,0:T(8,128)(2,1)} %get-tuple-element.93.source), custom_call_target="tpu_custom_call" | custom-call | tf_op jit(solution)/shard_map/spread_heads/pallas_call | solution.py:1097
  822.0 0.6 fusion.3
  822.6 0.6 slice_bitcast_fusion
  823.2 14.4 %spread_pair.1 = (f32[512,6144]{1,0:T(8,128)}, f32[512,6144]{1,0:T(8,128)}) custom-call(bf16[8,512,1536]{2,1,0:T(8,128)(2,1)} %bitcast.45), custom_call_target="tpu_custom_call" | custom-call | tf_op jit(solution)/shard_map/spread_pair/pallas_call | solution.py:1057
  837.6 1.0 copy.47
  838.6 1.3 copy.48
  (36 shorter events, 0.1 us)
Async XLA Ops:
  7.2 231.7 %all-gather.4.cloned.1.call-start = ((), (), s32[]{:S(2)}) async-start(), calls=%async_computation.1 | async-start | bytes 11796480 | tf_op jit(solution)/shard_map/all_gather | solution.py:1154
  10.2 1.7 copy-start.15
  10.2 1.7 copy-start.16
  10.2 1.7 copy-start.19
  10.2 1.7 copy-start.20
  10.2 2.4 copy-start.17
  10.2 2.4 copy-start.18
  11.8 579.7 %reduce-scatter.2.cloned.1.call-start = ((), (), s32[]{:S(2)}) async-start(), calls=%async_computation.2 | async-start | bytes 7864320 | tf_op jit(solution)/shard_map/reduce_scatter | solution.py:1157
  112.5 8.5 copy-start.1
  328.2 11.5 %copy-start.21 = (bf16[8,256,2048]{2,1,0:T(8,128)(2,1)S(1)}, bf16[8,256,2048]{2,1,0:T(8,128)(2,1)}, u32[]{:S(2)}) copy-start(bf16[8,256,2048]{2,1,0:T(8,128)(2,1)} %get-tuple-element.66) | copy-start | bytes 25165828
  328.2 11.5 %copy-start.22 = (bf16[8,256,1536]{2,1,0:T(8,128)(2,1)S(1)}, bf16[8,256,1536]{2,1,0:T(8,128)(2,1)}, u32[]{:S(2)}) copy-start(bf16[8,256,1536]{2,1,0:T(8,128)(2,1)} %get-tuple-element.68.refs_0_) | copy-start | bytes 18874372
  481.0 110.6 %copy-start.5 = (bf16[2048,256]{1,0:T(8,128)(2,1)S(1)}, bf16[2048,256]{1,0:T(8,128)(2,1)}, u32[]{:S(2)}) copy-start(bf16[2048,256]{1,0:T(8,128)(2,1)} %get-tuple-element.83.refs_5_) | copy-start | bytes 3145732
  481.0 342.2 %all-gather.6.cloned.1.call-start = ((), (), s32[]{:S(2)}) async-start(), calls=%async_computation.3 | async-start | bytes 14155776 | tf_op jit(solution)/shard_map/all_gather | solution.py:1160
  598.5 10.7 %copy-start = (f32[2048,128]{1,0:T(8,128)S(1)}, f32[2048,128]{1,0:T(8,128)}, u32[]{:S(2)}) copy-start(f32[2048,128]{1,0:T(8,128)} %pad_maximum_fusion.2.refs_1_.refs_7_) | copy-start | bytes 3145732
  598.5 10.7 %copy-start.2 = (s32[8,1,256]{2,1,0:T(1,128)S(1)}, s32[8,1,256]{2,1,0:T(1,128)}, u32[]{:S(2)}) copy-start(s32[8,1,256]{2,1,0:T(1,128)} %copy-done.1) | copy-start | bytes 24580
  598.5 10.7 %copy-start.3 = (f32[8,128]{1,0:T(8,128)S(1)}, f32[8,128]{1,0:T(8,128)}, u32[]{:S(2)}) copy-start(f32[8,128]{1,0:T(8,128)} %maximum_maximum_fusion.refs_3_.refs_9_) | copy-start | bytes 12292
  598.5 10.7 %copy-start.4 = (bf16[8,256,256]{2,1,0:T(8,128)(2,1)S(1)}, bf16[8,256,256]{2,1,0:T(8,128)(2,1)}, u32[]{:S(2)}) copy-start(bf16[8,256,256]{2,1,0:T(8,128)(2,1)} %get-tuple-element.81) | copy-start | bytes 3145732
  598.5 10.7 %copy-start.7 = (bf16[2048,128]{1,0:T(8,128)(2,1)S(1)}, bf16[2048,128]{1,0:T(8,128)(2,1)}, u32[]{:S(2)}) copy-start(bf16[2048,128]{1,0:T(8,128)(2,1)} %get-tuple-element.76.refs_1_) | copy-start | bytes 1572868
  598.5 10.7 %copy-start.9 = (f32[8,2048]{1,0:T(8,128)S(1)}, f32[8,2048]{1,0:T(8,128)}, u32[]{:S(2)}) copy-start(f32[8,2048]{1,0:T(8,128)} %get-tuple-element.82.refs_4_) | copy-start | bytes 196612
  609.2 1.2 copy-start.6
  610.4 1.0 copy-start.8
  648.9 8.7 %copy-start.10 = (f32[8,128]{1,0:T(8,128)}, f32[8,128]{1,0:T(8,128)S(1)}, u32[]{:S(2)}) copy-start(f32[8,128]{1,0:T(8,128)S(1)} %get-tuple-element.89.refs_6_) | copy-start | bytes 12292
  648.9 8.7 %copy-start.13 = (bf16[2048,256]{1,0:T(8,128)(2,1)S(1)}, bf16[2048,256]{1,0:T(8,128)(2,1)}, u32[]{:S(2)}) copy-start(bf16[2048,256]{1,0:T(8,128)(2,1)} %convolution_convert_fusion.1) | copy-start | bytes 3145732
  813.2 8.9 %copy-start.14 = (f32[16,128]{1,0:T(8,128)S(1)}, f32[16,128]{1,0:T(8,128)}, u32[]{:S(2)}) copy-start(f32[16,128]{1,0:T(8,128)} %get-tuple-element.102) | copy-start | bytes 24580
  823.2 14.4 %copy-start.12 = (bf16[256,2048]{1,0:T(8,128)(2,1)S(1)}, bf16[256,2048]{1,0:T(8,128)(2,1)}, u32[]{:S(2)}) copy-start(bf16[256,2048]{1,0:T(8,128)(2,1)} %get-tuple-element.74) | copy-start | bytes 3145732
  823.2 15.4 %copy-start.11 = (f32[256,2048]{1,0:T(8,128)S(1)}, f32[256,2048]{1,0:T(8,128)}, u32[]{:S(2)}) copy-start(f32[256,2048]{1,0:T(8,128)} %get-tuple-element.92) | copy-start | bytes 6291460
Sparse Core Ops, SparseCore 0:
  12.0 129.7 all-gather.3
  481.1 68.5 reduce-scatter.1
  591.7 141.5 all-gather.5

commit v8 on v7

--- a/solution.py
+++ b/solution.py
@@ -209,7 +209,7 @@
 
 
 def scatter_scratch(chips, rows):
-    buffers = [VMEM((count, CHUNKS, rows, WIDE), BF16) for count in (chips + 1, chips, chips)]
+    buffers = [VMEM((count, CHUNKS, rows, WIDE), BF16) for count in (chips + 1, 2, chips)]
     return buffers + [pltpu.SemaphoreType.DMA((chips, CHUNKS)) for _ in range(6)]
 
 
@@ -232,10 +232,10 @@
         sems = self.sems
         return send(ref, ref, sems[2].at[step, chunk], sems[3].at[step, chunk], "ctx", self.me - 2)
 
-    def across(self, target, chunk):
+    def across(self, target, chunk, slot=0):
         sems = self.sems
         return send(
-            self.out.at[target, chunk],
+            self.out.at[slot, chunk],
             self.other.at[target, chunk],
             sems[4].at[target, chunk],
             sems[5].at[target, chunk],
@@ -262,25 +262,33 @@
         return jnp.logical_and(time >= self.chips - 1 - self.chip, time < self.chips - 1)
 
     def prepare(self, time):
-        def cross(target):
+        chip, chips = self.chip, self.chips
+
+        def cross(target, slot, before, used):
             def one(chunk):
+                @pl.when(used)
+                def _():
+                    self.across(before, chunk, slot).wait_send()
+
                 piece = 2 * target + 1 - self.core
-                self.out[target, chunk] = self.produce(piece, chunk).astype(BF16)
-                self.across(target, chunk).start()
+                self.out[slot, chunk] = self.produce(piece, chunk).astype(BF16)
+                self.across(target, chunk, slot).start()
 
             loop(CHUNKS, one)
 
         @pl.when(self.when_right(time))
         def _():
-            cross(self.chips - 1 - time + self.chip)
+            target = chips - 1 - time + chip
+            cross(target, 0, target + 1, time > chip)
 
         @pl.when(self.when_left(time))
         def _():
-            cross(time - (self.chips - 1 - self.chip))
-
-        @pl.when(time == self.chips - 1)
-        def _():
-            cross(self.chip)
+            target = time - (chips - 1 - chip)
+            cross(target, 1, target - 1, target > 0)
+
+        @pl.when(time == chips - 1)
+        def _():
+            cross(chip, 0, chip + 1, chip < chips - 1)
 
     def step(self, time):
         chip, core, chips = self.chip, self.core, self.chips
@@ -355,7 +363,9 @@
             def _():
                 self.left(step, chunk).wait_send()
 
-            self.across(step, chunk).wait_send()
+            @pl.when(jnp.logical_or(step == chip, step == chip - 1))
+            def _():
+                self.across(step, chunk, jnp.where(step == chip, 0, 1)).wait_send()
 
         loop(chips * CHUNKS, drain)
 
@@ -386,8 +396,9 @@
 
 
 class FsdpSum:
-    def __init__(self, grad, arrived, send_sems, recv_sems):
+    def __init__(self, grad, arrived, send_sems, recv_sems, own=None):
         self.grad, self.arrived = grad, arrived
+        self.own = grad.at[lax.axis_index("fsdp")] if own is None else own
         self.sems = send_sems, recv_sems
         self.peers, self.ahead, _ = peers_of("fsdp")
 
@@ -400,17 +411,19 @@
     def start(self):
         loop(self.peers, lambda i: self.copy(i).start())
 
-    def collect(self, land, slot):
-        shard = lax.axis_index("fsdp")
+    def arrive(self):
         loop(self.peers, lambda i: self.copy(i).wait_recv())
 
+    def collect(self, target):
+        self.arrive()
+
         def add(block):
-            value = self.grad[shard, block].astype(F32)
+            value = self.own[block, :].astype(F32)
             for i in range(self.peers):
                 value = value + self.arrived[i, block].astype(F32)
-            land[slot, block] = value.astype(BF16)
-
-        row_blocks(self.grad.shape[1], add)
+            target[block, :] = value.astype(BF16)
+
+        row_blocks(self.own.shape[0], add)
 
     def finish(self):
         loop(self.peers, lambda i: self.copy(i).wait_send())
@@ -579,23 +592,43 @@
     return inverse * scaled - value * (inverse * inverse * inverse * inner), terms
 
 
-def feed_back_kernel(columns, *refs):
-    back, weights, middle, grad, gain_rows, down_grad, grad_middle, low, gain_sum, land = refs[:10]
-    weight, weight_sem, total = refs[10:13]
-    down_refs, gather_sems, scratch = refs[13:16], refs[16:22], refs[22:]
+def turn_kernel(columns, *refs):
+    back, feed_weights, activation, weights, middle, grad, gain_rows, down_grad, pair_grad = refs[:9]
+    grad_middle, land, gain_sum, down_land, context_grad, hidden, pair_in = refs[9:16]
+    weight, data, head_weight, total, low, piece_in, own_down, down_sum, sems = refs[16:25]
+    down_refs, down_sems, gather_sems = refs[25:28], refs[28:34], refs[34:40]
+    pair_sems, first_scratch, second_scratch = refs[40:42], refs[42:51], refs[51:]
     me, _, _, chips = line_position()
-    copy = copy_in(weights.at[:, columns], weight, weight_sem)
+    width = back.shape[2] // 2
+    weight_copy = copy_in(feed_weights.at[:, pl.ds(0, 2 * width)], weight, sems.at[0])
+    data_copy = copy_in(back, data, sems.at[1])
+    head_copy = copy_in(weights.at[:, columns], head_weight, sems.at[2])
+    own_copy = copy_in(down_grad.at[lax.axis_index("fsdp")], own_down, sems.at[3])
 
     def produce(piece, chunk):
-        return rdot(back[piece], weight[pl.ds(pl.multiple_of(chunk * WIDE, WIDE), WIDE), :])
-
-    down = FsdpSum(down_grad, *down_refs)
-    gather = Gather(land, gather_sems)
-    scatter = Scatter(scratch, produce, total)
+        return rdot(data[piece], weight[pl.ds(pl.multiple_of(chunk * WIDE, WIDE), WIDE), :])
+
+    def produce_hidden(piece, chunk):
+        block = pl.ds(pl.multiple_of(chunk * WIDE, WIDE), WIDE)
+        return rdot(data[piece, :, :width], weight[block, :width])
+
+    def consume(piece):
+        copy = copy_in(land.at[piece], piece_in, sems.at[4])
+        copy.wait()
+        context_grad[piece] = dot(piece_in[...], head_weight[...]).astype(BF16)
+
+    down = FsdpSum(down_grad, *down_refs, own=own_down)
+    pair = FsdpSum(pair_grad, pair_in, *pair_sems, own=own_down)
+    down_gather = Gather(down_land, down_sems)
+    gather = Gather(land, gather_sems, consume)
+    scatter = Scatter(first_scratch, produce, total)
+    hidden_scatter = Scatter(second_scratch, produce_hidden, total)
     scatter.begin()
+    hidden_scatter.begin()
     full_barrier()
     down.start()
-    copy.wait()
+    weight_copy.wait()
+    data_copy.wait()
     scatter.prepare(0)
 
     def step(time):
@@ -604,15 +637,22 @@
 
         @pl.when(time == 1)
         def _():
-            down.collect(land, me)
+            own_copy.wait()
+            down.collect(down_sum)
+            pair.start()
+            copy = copy_in(down_sum, down_land.at[me], sems.at[3])
+            copy.wait()
 
         @pl.when(time >= 1)
         def _():
-            gather.step(time - 1)
+            down_gather.step(time - 1)
 
     loop(chips - 1, step)
     scatter.finish()
-    gather.step(chips - 2)
+    down_copy = copy_in(
+        feed_weights.at[:, pl.ds(2 * width, width)], weight.at[:, pl.ds(0, width)], sems.at[0]
+    )
+    act_copy = copy_in(activation, data.at[:, :, pl.ds(0, width)], sems.at[1])
     gain_sum[...] = jnp.zeros_like(gain_sum)
 
     def norm(block):
@@ -623,99 +663,74 @@
         gain_sum[0:1, :] += jnp.sum(terms, axis=0, keepdims=True)
 
     row_blocks(middle.shape[0], norm)
-    gather.step(chips - 1)
+    low_copy = copy_in(low, land.at[me], sems.at[3])
+    low_copy.wait()
+    head_copy.wait()
+    gather.step(0)
+    down_copy.wait()
+    act_copy.wait()
+    hidden_scatter.prepare(0)
+
+    def turn_step(time):
+        hidden_scatter.step(time)
+        hidden_scatter.prepare(time + 1)
+        gather.step(time + 1)
+
+        @pl.when(time < 2)
+        def _():
+            down_gather.step(chips - 2 + time)
+
+    loop(chips - 1, turn_step)
+    hidden_scatter.finish()
     gather.finish()
+    down_gather.finish()
     down.finish()
-
-
-def feed_back(back, weights, middle, grad, gain_rows, down_grad):
-    parts, count, width = back.shape
-    shards, rows, down_width = down_grad.shape
+    pair.arrive()
+    pair.finish()
+
+    def add(block):
+        hidden[block, :] = (middle[block, :] + total[block, :]).astype(BF16)
+
+    row_blocks(middle.shape[0], add)
+
+
+def turn(back, feed_weights, activation, weights, middle, grad, gain_rows, down_grad, pair_grad, width):
+    parts, count, feed_width = activation.shape
+    shards, rows, _ = down_grad.shape
     return pl.pallas_call(
-        functools.partial(feed_back_kernel, pl.ds(0, width)),
+        functools.partial(turn_kernel, pl.ds(weights.shape[1] - width, width)),
         out_shape=(
             jax.ShapeDtypeStruct((count, D), F32),
-            jax.ShapeDtypeStruct((count, D), BF16),
+            jax.ShapeDtypeStruct((parts, count, D), BF16),
             jax.ShapeDtypeStruct((8, D), F32),
-            jax.ShapeDtypeStruct((parts, rows, down_width), BF16),
-        ),
-        in_specs=[WHOLE, HBM, WHOLE, WHOLE, WHOLE, WHOLE],
-        out_specs=(WHOLE,) * 4,
-        scratch_shapes=[VMEM((D, width), BF16), pltpu.SemaphoreType.DMA, VMEM((count, D), F32)]
-        + fsdp_scratch(shards, rows, down_width)
-        + gather_scratch(parts // 2)
-        + scatter_scratch(parts // 2, count),
-        compiler_params=params(3, 62),
-        cost_estimate=cost(100),
-        name="feed_back",
-    )(back, weights, middle, grad, gain_rows, down_grad)
-
-
-def turn_kernel(columns, down_columns, *refs):
-    low, weights, activation, feed_weights, middle, land, context_grad, hidden = refs[:8]
-    weight, weight_sem, down, down_sem, total = refs[8:13]
-    gather_sems, scratch = refs[13:19], refs[19:]
-    me, _, _, chips = line_position()
-    copy = copy_in(weights.at[:, columns], weight, weight_sem)
-    down_copy = copy_in(feed_weights.at[:, down_columns], down, down_sem)
-    land[me] = low[...]
-
-    def consume(piece):
-        context_grad[piece] = dot(land[piece], weight[...]).astype(BF16)
-
-    def produce(piece, chunk):
-        return rdot(activation[piece], down[pl.ds(pl.multiple_of(chunk * WIDE, WIDE), WIDE), :])
-
-    gather = Gather(land, gather_sems, consume)
-    scatter = Scatter(scratch, produce, total)
-    scatter.begin()
-    line_barrier()
-    copy.wait()
-    down_copy.wait()
-    scatter.prepare(0)
-
-    def step(time):
-        gather.step(time)
-        scatter.step(time)
-        scatter.prepare(time + 1)
-
-    loop(chips - 1, step)
-    gather.step(chips - 1)
-    scatter.finish()
-    gather.finish()
-
-    def add(block):
-        hidden[block, :] = (middle[block, :] + total[block, :]).astype(BF16)
-
-    row_blocks(middle.shape[0], add)
-
-
-def turn(low, weights, activation, feed_weights, middle, width):
-    parts, count, feed_width = activation.shape
-    return pl.pallas_call(
-        functools.partial(
-            turn_kernel, pl.ds(weights.shape[1] - width, width), pl.ds(2 * feed_width, feed_width)
-        ),
-        out_shape=(
-            jax.ShapeDtypeStruct((parts, count, D), BF16),
+            jax.ShapeDtypeStruct((parts, rows, feed_width), BF16),
             jax.ShapeDtypeStruct((parts, count, width), BF16),
             jax.ShapeDtypeStruct((count, D), BF16),
+            jax.ShapeDtypeStruct((shards - 1, rows, 2 * feed_width), BF16),
         ),
-        in_specs=[WHOLE, HBM, WHOLE, HBM, WHOLE],
-        out_specs=(WHOLE,) * 3,
+        in_specs=[HBM, HBM, HBM, HBM, WHOLE, WHOLE, WHOLE, HBM, HBM],
+        out_specs=(WHOLE, HBM, WHOLE, HBM, WHOLE, WHOLE, HBM),
         scratch_shapes=[
+            VMEM((D, 2 * feed_width), BF16),
+            VMEM((parts, count, 2 * feed_width), BF16),
             VMEM((D, width), BF16),
-            pltpu.SemaphoreType.DMA,
-            VMEM((D, feed_width), BF16),
-            pltpu.SemaphoreType.DMA,
             VMEM((count, D), F32),
+            VMEM((count, D), BF16),
+            VMEM((count, D), BF16),
+            VMEM((rows, feed_width), BF16),
+            VMEM((rows, feed_width), BF16),
+            pltpu.SemaphoreType.DMA((5,)),
         ]
+        + fsdp_scratch(shards, rows, feed_width)
         + gather_scratch(parts // 2)
+        + gather_scratch(parts // 2)
+        + [pltpu.SemaphoreType.DMA((shards,))] * 2
+        + scatter_scratch(parts // 2, count)
         + scatter_scratch(parts // 2, count),
-        compiler_params=params(4, 62),
-        cost_estimate=cost(107),
+        compiler_params=params(3, 63),
+        cost_estimate=cost(185),
         name="turn",
-    )(low, weights, activation, feed_weights, middle)
+    )(back, feed_weights, activation, weights, middle, grad, gain_rows, down_grad, pair_grad)
 
 
 def last_kernel(columns, *refs):
@@ -746,7 +761,7 @@
 
         @pl.when(time == 1)
         def _():
-            heads.collect(land, me)
+            heads.collect(land.at[me])
 
         @pl.when(time >= 1)
         def _():
@@ -1153,9 +1168,6 @@
     def gather_rows(piece):
         return lax.all_gather(piece, "fsdp", axis=0, tiled=True)
 
-    def sum_rows(grad):
-        return lax.psum_scatter(grad.astype(BF16), "fsdp", scatter_dimension=0, tiled=True)
-
     def gather_parts(piece):
         return lax.all_gather(piece, "ctx", axis=0)
 
@@ -1212,14 +1224,21 @@
     feed_grad = by_row(tdot(normed_two_all.reshape(tokens, D), flat_back).astype(BF16))
     down_grad = by_row(tdot(flat_grad, flat_activation).astype(BF16))
     back, feed_grad, down_grad = lax.optimization_barrier((back, feed_grad, down_grad))
-
-    grad_middle, low, gain_two, down_parts = feed_back(
-        back, feed_weight, middle, grad, gain_rows, down_grad.reshape(shards, rows, feed_width)
-    )
-    low, feed_grad = lax.optimization_barrier((low, feed_grad))
-    feed_shard = sum_rows(feed_grad)
-    low_all, context_grad, hidden_out = turn(low, heads_weight, activation, feed_weight, middle, width)
-
+    feed_grad = feed_grad.reshape(shards, rows, 2 * feed_width)
+    grad_middle, low_all, gain_two, down_parts, context_grad, hidden_out, pair_in = turn(
+        back,
+        feed_weight,
+        activation,
+        heads_weight,
+        middle,
+        grad,
+        gain_rows,
+        down_grad.reshape(shards, rows, feed_width),
+        feed_grad,
+        width,
+    )
+    own_pair = lax.dynamic_index_in_dim(feed_grad, shard, keepdims=False)
+    feed_shard = (own_pair.astype(F32) + jnp.sum(pair_in.astype(F32), axis=0)).astype(BF16)
     context_grad, feed_shard, down_parts = lax.optimization_barrier(
         (context_grad, feed_shard, down_parts)
     )

time: 855 us -> 840 us (0.982)
  Pallas kernels: 762 us -> 740 us
    pallas_call x1 -> x0, Pallas kernels: 126 us -> none  [feed_back(): pl.pallas_call(functools.partial(feed_back_kernel, pl.ds(0, width)), out_...]
    pallas_call x1, Pallas kernels: 111 us -> 213 us  [turn(): pl.pallas_call(functools.partial(turn_kernel, pl.ds(weights.shape[1] - wi...]
  transfers between devices with their start and end apart: 3 -> 2, of which waited for: 0 -> 0; matrix products, arithmetic and copies ran while one was open for 4% -> 4% of each run, Pallas kernels for 63% -> 51%
where the time goes in v8:
time: 840 us; the launch traced here: 832 us
  Pallas kernels  740 us (88%)
  matrix products  41.8 us (5%)
  other arithmetic  19.4 us (2%)
  local copies, waits for them, and re-layouts  15.1 us (2%)
  between operations  14.9 us (2%)
    pallas_call x1, Pallas kernels, turn(): pl.pallas_call(functools.partial(turn_kernel, pl.ds(weights.shape[1] - wi...  213 us
    pallas_call x1, Pallas kernels, last(): pl.pallas_call(functools.partial(last_kernel, pl.ds(0, width)), out_shape...  156 us
    pallas_call x1, Pallas kernels, attend(): pl.pallas_call(functools.partial(attend_kernel, heads, pl.ds(weights.shap...  118 us
    pallas_call x1, Pallas kernels, first(): pl.pallas_call(functools.partial(first_kernel, D // shards, width), out_s...  93.1 us
    pallas_call x1, Pallas kernels, feed(): pl.pallas_call(functools.partial(feed_kernel, width), out_shape=(jax.Shap...  89.5 us
    dot_general x4, matrix products, tdot(): lax.dot_general(left, right, (((0,), (0,)), ((), ())), preferred_element_...  41.8 us
    pallas_call x1, Pallas kernels, attention_back(): pl.pallas_call(functools.partial(attention_back_kernel, heads), out_shape...  37.4 us
  transfers between devices with their start and end apart: 2, of which 0 were waited for; matrix products, arithmetic and copies ran while one was open for 4% of the time, Pallas kernels for 51%

profile of v8, /device:TPU:0, one launch (start us, length us, event | category | flops | bytes accessed | tf_op | source)
XLA Modules:
  0.0 831.5 jit_solution(306045521172719648)
XLA Ops:
  7.2 0.0 all-gather.4.cloned.1.call-start
  7.2 1.2 constant_dynamic-slice_fusion
  8.4 0.3 copy.41
  8.7 1.5 constant_dynamic-slice_fusion.1
  10.2 0.0 copy-start.14
  10.2 0.0 copy-start.15
  10.2 0.0 copy-start.18
  10.2 0.0 copy-start.19
  10.2 0.0 copy-start.16
  10.2 0.0 copy-start.17
  10.3 1.6 pad_maximum_fusion.1
  11.8 0.0 all-gather.4.cloned.1.call-update
  11.8 0.0 all-gather.6.cloned.1.call-start
  11.9 1.0 constant_dynamic-slice_fusion.3
  12.9 0.1 copy.40
  13.0 1.0 constant_dynamic-slice_fusion.6
  14.0 0.1 concatenate.21
  14.1 0.6 bitcast_convert_fusion.2.refs_1_
  14.7 0.6 pad.10.refs_2_
  15.3 1.0 constant_dynamic-slice_fusion.4
  16.3 0.9 pad_maximum_fusion.4.refs_3_
  17.3 93.1 %gather_normed.1 = (bf16[8,256,2048]{2,1,0:T(8,128)(2,1)}, f32[8,256,512]{2,1,0:T(8,128)}, bf16[2048,768]{1,0:T(8,128)(2,1)}, f32[8,2048]{1,0:T(8,128)}, f32[4,16,128]{2,1,0:T(8,128)}, /*index=5*/s32[8,8,256]{2,1,0:T(8,128)}) custom-call(bf16[256,2048]{1,0:T(8,128)(2,1)} %bitcast.63, f32[16,128]{1,0:T(8,128)} %bitcast_convert_fusion.2.refs_1_, ...), custom_call_target="tpu_custom_call" | custom-call | flops 97749999616 | bytes 1024 | tf_op jit(solution)/shard_map/gather_normed/pallas_call | solution.py:500
  110.4 0.8 copy.44
  111.2 0.1 fusion.3
  111.3 0.1 reshape.92
  111.4 0.1 reshape.93
  111.4 0.9 fusion.2
  112.4 0.0 copy-start.1
  112.4 1.3 copy.33.refs_4_.refs_10_
  113.7 0.1 pad.18.clone
  113.8 0.7 maximum_maximum_fusion.refs_3_.refs_9_
  114.5 3.7 fusion.1
  118.2 1.3 pad_maximum_fusion.2.refs_1_.refs_7_
  119.5 1.3 pad_maximum_fusion.3.refs_2_.refs_8_
  120.8 117.9 %attend.1 = (bf16[2048,256]{1,0:T(8,128)(2,1)}, bf16[2048,128]{1,0:T(8,128)(2,1)}, bf16[2048,128]{1,0:T(8,128)(2,1)}, bf16[2048,256]{1,0:T(8,128)(2,1)}, f32[8,2...) custom-call(f32[2048,512]{1,0:T(8,128)} %bitcast.68, ...), custom_call_target="tpu_custom_call" | custom-call | flops 126500003840 | bytes 1024 | tf_op jit(solution)/shard_map/attend/pallas_call | solution.py:956
  238.8 0.0 all-gather.4.cloned.1.call-done.refs_2_.refs_1_
  238.8 89.5 %feed.1 = (bf16[8,256,2048]{2,1,0:T(8,128)(2,1)}, bf16[8,256,768]{2,1,0:T(8,128)(2,1)}, bf16[8,256,1536]{2,1,0:T(8,128)(2,1)}) custom-call(bf16[256,2048]{1,0:T(8,128)(2,1)} %get-tuple-element.61.refs_0_, bf16[8,256,2048]{2,1,0:T(8,128)(2,1)} %get-tuple-element.62.refs_1_, bf16[2048,2304]{1,0:T(8,128)(2,1)} %all-gather.4.cloned.1.call-done.refs_2_.refs_1_), custom_call_target="tpu_custom_call" | custom-call | flops 103499997184 | bytes 1024 | tf_op jit(solution)/shard_map/feed/pallas_call | solution.py:565
  328.3 0.0 copy-start.21
  328.3 0.0 copy-start.22
  328.3 11.5 %bitcast_convert_fusion.1 = bf16[2048,768]{1,0:T(8,128)(2,1)} fusion(bf16[8,256,2048]{2,1,0:T(8,128)(2,1)} %get-tuple-element.62.refs_1_, bf16[8,256,768]{2,1,0:T(8,128)(2,1)} %get-tuple-element.65.refs_2_), kind=kOutput, calls=%fused_computation.2 | convolution fusion | flops 6444023808 | bytes 14680064 | tf_op jit(solution)/shard_map/dot_general | solution.py:33
  339.8 0.0 copy-done.22
  339.8 15.7 %bitcast_convert_fusion = bf16[2048,1536]{1,0:T(8,128)(2,1)} fusion(bf16[8,256,2048]{2,1,0:T(8,128)(2,1)S(1)} %copy-done.21, bf16[8,256,1536]{2,1,0:T(8,128)(2,1)S(1)} %copy-done.22), kind=kOutput, calls=%fused_computation | convolution fusion | flops 12888047616 | bytes 20971520 | tf_op jit(solution)/shard_map/dot_general | solution.py:33
  355.5 213.2 %turn.1 = (f32[256,2048]{1,0:T(8,128)}, bf16[8,256,2048]{2,1,0:T(8,128)(2,1)}, f32[8,2048]{1,0:T(8,128)}, bf16[8,512,768]{2,1,0:T(8,128)(2,1)}, bf16[8,256,256]{...) custom-call(bf16[8,256,1536]{2,1,0:T(8,128)(2,1)} %get-tuple-element.66.refs_0_, ...), custom_call_target="tpu_custom_call" | custom-call | flops 212749991936 | bytes 1024 | tf_op jit(solution)/shard_map/turn/pallas_call | solution.py:700
  568.7 3.5 convert_reduce_fusion
  572.1 3.0 fusion
  575.2 0.0 all-gather.6.cloned.1.call-update
  575.2 0.0 copy-start
  575.2 0.0 copy-start.2
  575.2 0.0 copy-start.3
  575.3 9.9 %spread_turned.1 = f32[6144,512]{1,0:T(8,128)} custom-call(bf16[8,512,768]{2,1,0:T(8,128)(2,1)} %get-tuple-element.81.source), custom_call_target="tpu_custom_call" | custom-call | tf_op jit(solution)/shard_map/spread_turned/pallas_call | solution.py:1089
  585.2 0.0 copy-done.2
  585.2 1.3 copy-done.6
  586.6 1.0 copy-done.8
  587.6 37.4 %attention_back.1 = (bf16[2048,512]{1,0:T(8,128)(2,1)}, f32[8,128]{1,0:T(8,128)S(1)}) custom-call(bf16[2048,256]{1,0:T(8,128)(2,1)S(1)} %copy-done.6, bf16[2048,128]{1,0:T(8,128)(2,1)S(1)} %copy-done.7, bf16[2048,128]{1,0:T(8,128)(2,1)S(1)} %copy-done.8, bf16[2048,256]{1,0:T(8,128)(2,1)S(1)} %bitcast.48, f32[8,2048]{1,0:T(8,128)S(1)} %copy-done.9, ...), custom_call_target="tpu_custom_call" | custom-call | flops 43699998720 | bytes 1024 | tf_op jit(solution)/shard_map/attention_back/pallas_call | solution.py:1044
  625.0 6.1 convolution_convert_fusion.1
  631.1 8.6 %convolution_convert_fusion = bf16[2048,512]{1,0:T(8,128)(2,1)S(1)} fusion(bf16[2048,2048]{1,0:T(8,128)(2,1)} %bitcast.66, bf16[2048,512]{1,0:T(8,128)(2,1)S(1)} %copy-done.20), kind=kOutput, calls=%fused_computation.6 | convolution fusion | flops 4296015872 | bytes 12582912 | tf_op jit(solution)/shard_map/dot_general | solution.py:33
  639.7 1.9 pad_maximum_fusion
  641.5 155.9 %last.1 = (f32[256,2048]{1,0:T(8,128)}, f32[16,128]{1,0:T(8,128)}, bf16[8,512,768]{2,1,0:T(8,128)(2,1)}) custom-call(bf16[8,256,512]{2,1,0:T(8,128)(2,1)} %bitcast.71, bf16[2048,768]{1,0:T(8,128)(2,1)} %get-tuple-element.59.refs_6_.refs_3_.refs_1_, bf16[256,2048]{1,0:T(8,128)(2,1)} %bitcast.65, f32[256,2048]{1,0:T(8,128)} %get-tuple-element.83.refs_3_, ...), custom_call_target="tpu_custom_call" | custom-call | flops 103499997184 | bytes 1024 | tf_op jit(solution)/shard_map/last/pallas_call | solution.py:826
  797.5 8.8 %spread_heads.1 = (f32[512,2048]{1,0:T(8,128)}, f32[512,1024]{1,0:T(8,128)}, f32[512,1024]{1,0:T(8,128)}, f32[2048,512]{1,0:T(8,128)}) custom-call(bf16[8,512,768]{2,1,0:T(8,128)(2,1)} %get-tuple-element.89.source), custom_call_target="tpu_custom_call" | custom-call | tf_op jit(solution)/shard_map/spread_heads/pallas_call | solution.py:1112
  806.4 0.6 fusion.4
  806.9 0.6 slice_bitcast_fusion
  807.5 14.4 %spread_pair.1 = (f32[512,6144]{1,0:T(8,128)}, f32[512,6144]{1,0:T(8,128)}) custom-call(bf16[8,512,1536]{2,1,0:T(8,128)(2,1)} %bitcast.49), custom_call_target="tpu_custom_call" | custom-call | tf_op jit(solution)/shard_map/spread_pair/pallas_call | solution.py:1072
  822.0 1.0 copy.47
  822.9 1.3 copy.48
  (34 shorter events, 0.1 us)
Async XLA Ops:
  7.2 231.6 %all-gather.4.cloned.1.call-start = ((), (), s32[]{:S(2)}) async-start(), calls=%async_computation | async-start | bytes 11796480 | tf_op jit(solution)/shard_map/all_gather | solution.py:1169
  10.2 3.8 copy-start.14
  10.2 3.8 copy-start.15
  10.2 3.8 copy-start.18
  10.2 3.8 copy-start.19
  10.2 4.5 copy-start.16
  10.2 4.5 copy-start.17
  11.8 795.7 %all-gather.6.cloned.1.call-start = ((), (), s32[]{:S(2)}) async-start(), calls=%async_computation.1 | async-start | bytes 14155776 | tf_op jit(solution)/shard_map/all_gather | solution.py:1172
  112.4 8.5 %copy-start.1 = (s32[8,1,256]{2,1,0:T(1,128)}, s32[8,1,256]{2,1,0:T(1,128)S(1)}, u32[]{:S(2)}) copy-start(s32[8,1,256]{2,1,0:T(1,128)S(1)} %get-tuple-element.99) | copy-start | bytes 24580
  328.3 11.5 %copy-start.21 = (bf16[8,256,2048]{2,1,0:T(8,128)(2,1)S(1)}, bf16[8,256,2048]{2,1,0:T(8,128)(2,1)}, u32[]{:S(2)}) copy-start(bf16[8,256,2048]{2,1,0:T(8,128)(2,1)} %get-tuple-element.64) | copy-start | bytes 25165828
  328.3 11.5 %copy-start.22 = (bf16[8,256,1536]{2,1,0:T(8,128)(2,1)S(1)}, bf16[8,256,1536]{2,1,0:T(8,128)(2,1)}, u32[]{:S(2)}) copy-start(bf16[8,256,1536]{2,1,0:T(8,128)(2,1)} %get-tuple-element.66.refs_0_) | copy-start | bytes 18874372
  575.2 10.0 %copy-start = (f32[2048,128]{1,0:T(8,128)S(1)}, f32[2048,128]{1,0:T(8,128)}, u32[]{:S(2)}) copy-start(f32[2048,128]{1,0:T(8,128)} %pad_maximum_fusion.2.refs_1_.refs_7_) | copy-start | bytes 3145732
  575.2 10.0 %copy-start.2 = (s32[8,1,256]{2,1,0:T(1,128)S(1)}, s32[8,1,256]{2,1,0:T(1,128)}, u32[]{:S(2)}) copy-start(s32[8,1,256]{2,1,0:T(1,128)} %copy-done.1) | copy-start | bytes 24580
  575.2 10.0 %copy-start.3 = (f32[8,128]{1,0:T(8,128)S(1)}, f32[8,128]{1,0:T(8,128)}, u32[]{:S(2)}) copy-start(f32[8,128]{1,0:T(8,128)} %maximum_maximum_fusion.refs_3_.refs_9_) | copy-start | bytes 12292
  575.2 10.0 %copy-start.4 = (bf16[8,256,256]{2,1,0:T(8,128)(2,1)S(1)}, bf16[8,256,256]{2,1,0:T(8,128)(2,1)}, u32[]{:S(2)}) copy-start(bf16[8,256,256]{2,1,0:T(8,128)(2,1)} %get-tuple-element.77) | copy-start | bytes 3145732
  575.2 10.0 %copy-start.5 = (bf16[2048,256]{1,0:T(8,128)(2,1)S(1)}, bf16[2048,256]{1,0:T(8,128)(2,1)}, u32[]{:S(2)}) copy-start(bf16[2048,256]{1,0:T(8,128)(2,1)} %get-tuple-element.79.refs_5_) | copy-start | bytes 3145732
  575.3 10.0 %copy-start.7 = (bf16[2048,128]{1,0:T(8,128)(2,1)S(1)}, bf16[2048,128]{1,0:T(8,128)(2,1)}, u32[]{:S(2)}) copy-start(bf16[2048,128]{1,0:T(8,128)(2,1)} %get-tuple-element.72.refs_1_) | copy-start | bytes 1572868
  575.3 10.0 %copy-start.9 = (f32[8,2048]{1,0:T(8,128)S(1)}, f32[8,2048]{1,0:T(8,128)}, u32[]{:S(2)}) copy-start(f32[8,2048]{1,0:T(8,128)} %get-tuple-element.78.refs_4_) | copy-start | bytes 196612
  585.2 1.3 copy-start.6
  586.5 1.0 copy-start.8
  625.0 6.1 copy-start.10
  625.0 6.1 copy-start.20
  797.5 8.9 %copy-start.13 = (f32[16,128]{1,0:T(8,128)S(1)}, f32[16,128]{1,0:T(8,128)}, u32[]{:S(2)}) copy-start(f32[16,128]{1,0:T(8,128)} %get-tuple-element.98) | copy-start | bytes 24580
  807.5 14.4 %copy-start.12 = (bf16[256,2048]{1,0:T(8,128)(2,1)S(1)}, bf16[256,2048]{1,0:T(8,128)(2,1)}, u32[]{:S(2)}) copy-start(bf16[256,2048]{1,0:T(8,128)(2,1)} %get-tuple-element.70) | copy-start | bytes 3145732
  807.5 15.4 %copy-start.11 = (f32[256,2048]{1,0:T(8,128)S(1)}, f32[256,2048]{1,0:T(8,128)}, u32[]{:S(2)}) copy-start(f32[256,2048]{1,0:T(8,128)} %get-tuple-element.88) | copy-start | bytes 6291460
Sparse Core Ops, SparseCore 0:
  12.0 129.7 all-gather.3
  575.3 144.1 all-gather.5

commit v9 on v8

--- a/solution.py
+++ b/solution.py
@@ -107,8 +107,7 @@
 
 
 class Gather:
-    def __init__(self, land, sems, consume=None, late=False):
-        self.late = late
+    def __init__(self, land, sems, consume=None):
         self.land = land
         self.sems = sems
         self.consume = consume
@@ -128,6 +127,10 @@
         return send(ref, ref, self.sems[4].at[source], self.sems[5].at[source], "ctx", other)
 
     def step(self, step):
+        self.move(step)
+        self.use(step)
+
+    def move(self, step):
         chip, core, chips = self.chip, self.core, self.chips
         low, high = chip - step, chip + step
         has_low = low >= 0
@@ -156,18 +159,6 @@
         @pl.when(has_high)
         def _():
             self.across(high, core).start()
-
-        if not self.late:
-            self.use(step)
-            return
-
-        @pl.when(step > 0)
-        def _():
-            self.use(step - 1)
-
-        @pl.when(step == chips - 1)
-        def _():
-            self.use(step)
 
     def use(self, step):
         chip, core, chips = self.chip, self.core, self.chips
@@ -370,6 +361,10 @@
         loop(chips * CHUNKS, drain)
 
 
+def tile(index, size):
+    return pl.ds(pl.multiple_of(index * size, size), size)
+
+
 def row_blocks(rows, body, size=32):
     def one(index):
         body(pl.ds(pl.multiple_of(index * size, size), size))
@@ -433,39 +428,133 @@
     return [VMEM((shards - 1, rows, width), BF16)] + [pltpu.SemaphoreType.DMA((shards,))] * 2
 
 
+def sine_cosine(angle):
+    count = jnp.floor(angle * 0.6366197723675814 + 0.5)
+    rest = angle - count * 1.5703125
+    rest = rest - count * 4.837512969970703e-4
+    rest = rest - count * 7.549789948768648e-8
+    square = rest * rest
+    sine = -1.9515295891e-4 * square + 8.3321608736e-3
+    sine = rest + rest * square * (sine * square - 1.6666654611e-1)
+    cosine = 2.443315711809948e-5 * square - 1.388731625493765e-3
+    cosine = 1.0 - 0.5 * square + square * square * (cosine * square + 4.166664568298827e-2)
+    quarter = jnp.bitwise_and(count.astype(jnp.int32), 3)
+    odd = jnp.bitwise_and(quarter, 1) == 1
+    sine, cosine = jnp.where(odd, cosine, sine), jnp.where(odd, sine, cosine)
+    sine = jnp.where(quarter >= 2, -sine, sine)
+    cosine = jnp.where(jnp.logical_or(quarter == 1, quarter == 2), -cosine, cosine)
+    return sine, cosine
+
+
+class Shares:
+    def __init__(self, source, target_of, own_sem, sems):
+        self.source, self.target_of = source, target_of
+        self.own_sem, self.sems = own_sem, sems
+        self.peers, self.ahead, self.behind = peers_of("fsdp")
+        self.shard = lax.axis_index("fsdp")
+
+    def copy(self, i, owner):
+        sems = self.sems
+        target = self.target_of(owner)
+        return send(self.source, target, sems[0].at[i], sems[1].at[i], "fsdp", self.ahead(i))
+
+    def own(self):
+        return pltpu.make_async_copy(self.source, self.target_of(self.shard), self.own_sem)
+
+    def start(self):
+        loop(self.peers, lambda i: self.copy(i, self.shard).start())
+        self.own().start()
+
+    def arrive(self):
+        self.own().wait()
+        loop(self.peers, lambda i: self.copy(i, self.behind(i)).wait_recv())
+
+    def finish(self):
+        loop(self.peers, lambda i: self.copy(i, self.shard).wait_send())
+
+
+def shares_scratch(count, shards):
+    return [pltpu.SemaphoreType.DMA((count,))] + [pltpu.SemaphoreType.DMA((shards,))] * (2 * count)
+
+
 def copy_in(source, target, sem):
     copy = pltpu.make_async_copy(source, target, sem)
     copy.start()
     return copy
 
 
-def first_kernel(rows, width, *refs):
-    x, gains, tokens, part, land, proj, weights, gain_rows, all_gains, all_tokens = refs[:10]
-    sems, small = refs[10:16], refs[16:]
+QUERY_TILE = 256
+KEY_TILE = 512
+
+
+def reach(index, tokens):
+    return jnp.minimum((index + 2) * QUERY_TILE + KEY_TILE - 1, tokens) // KEY_TILE
+
+
+def head_norm(value, gain, cosine, sine):
+    normed = value * inverse_norm(value) * gain
+    return normed * cosine + pltpu.roll(normed, HEAD_SIZE // 2, 1) * sine
+
+
+def forward_kernel(heads, *refs):
+    x, grad, gains, token_info, freq = refs[:5]
+    sources, refs = refs[5:12], refs[12:]
+    normed_land, grad_land, two_land, activation, back = refs[:5]
+    proj, cosine, sine, queries, keys, values, context, inverse = refs[5:13]
+    middle, gain_rows, all_gains, all_tokens = refs[13:17]
+    head_weight, out_weight, pair_weight, down_weight = refs[17:21]
+    refs = refs[21:]
+    pair, down, own, piece_in, grad_in, act_out, back_out, total, sems = refs[:9]
+    small, refs = refs[9:13], refs[13:]
+    share_own, share_sems, refs = refs[0], refs[1:15], refs[15:]
+    first_sems, grad_sems, two_sems, scratch = refs[:6], refs[6:12], refs[12:18], refs[18:]
     me, _, _, chips = line_position()
     shard = lax.axis_index("fsdp")
     shards, ahead, behind = peers_of("fsdp")
     parts, next_part, past_part = peers_of("ctx")
-    full_barrier()
+    count = x.shape[0]
+    tokens = 2 * chips * count
+    width = heads * HEAD_SIZE
+    feed_width = down.shape[0]
+    rows = D // (shards + 1)
+    lanes = rows // 128
+    key_head = me // (2 * chips // KEY_VALUE_HEADS)
 
     def gain_copy(i, slot):
         return send(gains, all_gains.at[slot], small[0].at[i], small[1].at[i], "fsdp", ahead(i))
 
     def token_copy(i, slot):
-        return send(tokens, all_tokens.at[slot], small[2].at[i], small[3].at[i], "ctx", next_part(i))
-
-    def weight_copy(i, owner):
-        target = weights.at[pl.ds(pl.multiple_of(owner * rows, rows), rows), :]
-        return send(part, target, small[4].at[i], small[5].at[i], "fsdp", ahead(i))
-
+        return send(token_info, all_tokens.at[slot], small[2].at[i], small[3].at[i], "ctx", next_part(i))
+
+    def by_row(target, at, size):
+        return lambda owner: target.at[tile(owner, rows), pl.ds(at, size)]
+
+    def by_column(target):
+        return lambda owner: target.at[:, tile(owner, rows)]
+
+    places = (
+        (sources[0].at[:, tile(me, width)], by_row(head_weight, 0, width)),
+        (sources[1].at[:, tile(key_head, HEAD_SIZE)], by_row(head_weight, width, HEAD_SIZE)),
+        (sources[2].at[:, tile(key_head, HEAD_SIZE)], by_row(head_weight, width + HEAD_SIZE, HEAD_SIZE)),
+        (sources[3].at[tile(me, width), :], by_column(out_weight)),
+        (sources[4].at[:, tile(me, feed_width)], by_row(pair, 0, feed_width)),
+        (sources[5].at[:, tile(me, feed_width)], by_row(pair, feed_width, feed_width)),
+        (sources[6].at[tile(me, feed_width), :], by_column(down)),
+    )
+    shares = [
+        Shares(source, target_of, share_own.at[i], share_sems[2 * i : 2 * i + 2])
+        for i, (source, target_of) in enumerate(places)
+    ]
+
+    full_barrier()
     loop(shards, lambda i: gain_copy(i, shard).start())
     loop(parts, lambda i: token_copy(i, me).start())
-    loop(shards, lambda i: weight_copy(i, shard).start())
+    for share in shares[:4]:
+        share.start()
+    grad_copy = copy_in(grad, grad_land.at[me], sems.at[0])
     all_gains[shard] = gains[...]
-    all_tokens[me] = tokens[...]
-    weights[pl.ds(pl.multiple_of(shard * rows, rows), rows), :] = part[...]
+    all_tokens[me] = token_info[...]
     loop(shards, lambda i: gain_copy(i, behind(i)).wait_recv())
-    lanes = rows // 128
     for kind in range(2):
         for owner in range(shards + 1):
             for j in range(lanes):
@@ -473,115 +562,243 @@
                 gain_rows[kind : kind + 1, at : at + 128] = all_gains[
                     owner, kind * lanes + j : kind * lanes + j + 1, :
                 ]
+    size = HEAD_SIZE // (shards + 1)
+    for kind in range(2):
+        gain_rows[2 + kind : 3 + kind, 0:HEAD_SIZE] = jnp.concatenate(
+            [
+                all_gains[
+                    owner, 2 * lanes : 2 * lanes + 1, kind * size : (kind + 1) * size
+                ]
+                for owner in range(shards + 1)
+            ],
+            axis=1,
+        )
 
     def norm(block):
         value = x[block, :].astype(F32)
-        land[me, block] = (value * inverse_norm(value) * gain_rows[0:1, :]).astype(BF16)
-
-    row_blocks(x.shape[0], norm)
-
-    gather = Gather(land, sems)
-    loop(chips, gather.step)
-    loop(shards, lambda i: weight_copy(i, behind(i)).wait_recv())
+        own[block, :] = (value * inverse_norm(value) * gain_rows[0:1, :]).astype(BF16)
+
+    row_blocks(count, norm)
+    own_copy = copy_in(own, normed_land.at[me], sems.at[1])
+    own_copy.wait()
+
+    def column(piece, row):
+        values_in_lanes = all_tokens[piece, row : row + 1, :].astype(F32)
+        return jnp.broadcast_to(values_in_lanes, (128, count)).T
 
     def project(piece):
-        proj[piece] = dot(land[piece], weights[:, :width])
-
-    loop(2 * chips, project)
-    gather.finish()
+        copy = copy_in(normed_land.at[piece], piece_in, sems.at[1])
+        block = tile(piece, count)
+        s, c = sine_cosine(column(piece, 0) * freq[0:1, :])
+        lane = lax.broadcasted_iota(jnp.int32, s.shape, 1)
+        s = jnp.where(lane < HEAD_SIZE // 2, -s, s)
+        cosine[block, :] = c
+        sine[block, :] = s
+        copy.wait()
+        proj[piece] = dot(piece_in[...], head_weight[...])
+
+        def turned(at, row):
+            return head_norm(proj[piece, :, at : at + HEAD_SIZE], gain_rows[row : row + 1, 0:HEAD_SIZE], c, s)
+
+        for h in range(heads):
+            at = h * HEAD_SIZE
+            queries[block, at : at + HEAD_SIZE] = (turned(at, 2) * HEAD_SIZE ** (-0.5)).astype(BF16)
+        keys[block, :] = turned(width, 3).astype(BF16)
+        values[block, :] = proj[piece, :, width + HEAD_SIZE : width + 2 * HEAD_SIZE].astype(BF16)
+
+    first_gather = Gather(normed_land, first_sems, project)
+    grad_gather = Gather(grad_land, grad_sems)
+    first_gather.move(0)
+    loop(parts, lambda i: token_copy(i, past_part(i)).wait_recv())
+
+    def first_step(step):
+        first_gather.move(step + 1)
+
+        @pl.when(step == 0)
+        def _():
+            for share in shares[:4]:
+                share.arrive()
+            for share in shares[4:]:
+                share.start()
+
+        first_gather.use(step)
+
+    loop(chips - 1, first_step)
+    grad_copy.wait()
+    grad_gather.step(0)
+    first_gather.use(chips - 1)
+
+    def attend(index):
+        block = tile(index, QUERY_TILE)
+        query_ids = column(index, 1)[:, 0:1]
+        for h in range(heads):
+            head = slice(h * HEAD_SIZE, (h + 1) * HEAD_SIZE)
+            query = queries[block, head]
+
+            def one(key_tile, carry):
+                sums, total = carry
+                span = tile(key_tile, KEY_TILE)
+                scores = rdot(query, keys[span, :])
+                key_ids = jnp.concatenate(
+                    [all_tokens[key_tile * each + j, 1:2, :] for j in range(each)], axis=1
+                ).astype(F32)
+                expon = jnp.where(key_ids <= query_ids, jnp.exp(scores), 0.0)
+                sums = sums + dot(expon.astype(BF16), values[span, :])
+                return sums, total + jnp.sum(expon, axis=1, keepdims=True)
+
+            each = KEY_TILE // count
+            start = (jnp.zeros((QUERY_TILE, HEAD_SIZE), F32), jnp.zeros((QUERY_TILE, 1), F32))
+            sums, total = lax.fori_loop(0, reach(index, tokens), one, start)
+            scale = 1.0 / total
+            context[block, head] = (sums * scale).astype(BF16)
+            inverse[h : h + 1, block] = jnp.broadcast_to(scale, (QUERY_TILE, HEAD_SIZE)).T[0:1, :]
+
+    loop(tokens // QUERY_TILE, attend)
+
+    def produce(piece, chunk):
+        return dot(context[tile(piece, count), :], out_weight[:, tile(chunk, WIDE)])
+
+    scatter = Scatter(scratch, produce, total)
+    scatter.begin()
+    scatter.prepare(0)
+    grad_gather.step(1)
+
+    def scatter_step(time):
+        scatter.step(time)
+        scatter.prepare(time + 1)
+
+        @pl.when(time >= 1)
+        def _():
+            grad_gather.step(time + 1)
+
+    loop(chips - 1, scatter_step)
+    scatter.finish()
+
+    def norm_two(block):
+        value = x[block, :].astype(F32) + total[block, :]
+        middle[block, :] = value
+        own[block, :] = (value * inverse_norm(value) * gain_rows[1:2, :]).astype(BF16)
+
+    row_blocks(count, norm_two)
+    two_copy = copy_in(own, two_land.at[me], sems.at[1])
+    two_copy.wait()
+    for share in shares[4:]:
+        share.arrive()
+    outs = [
+        copy_in(head_weight, refs_out, sems.at[2 + i])
+        for i, (head_weight, refs_out) in enumerate(((pair, pair_weight), (down, down_weight)))
+    ]
+    feed_size = 256 if feed_width % 256 == 0 else 128
+
+    def act_copy(piece):
+        return pltpu.make_async_copy(act_out, activation.at[piece], sems.at[6])
+
+    def back_copy(piece):
+        return pltpu.make_async_copy(back_out, back.at[piece], sems.at[7])
+
+    def feed(piece):
+        copies = (
+            copy_in(two_land.at[piece], piece_in, sems.at[4]),
+            copy_in(grad_land.at[piece], grad_in, sems.at[5]),
+        )
+        for copy in copies:
+            copy.wait()
+
+        @pl.when(piece != me)
+        def _():
+            act_copy(piece).wait()
+            back_copy(piece).wait()
+
+        def one(index):
+            def columns(kind):
+                return pl.ds(pl.multiple_of(kind * feed_width + index * feed_size, 128), feed_size)
+
+            gate = dot(piece_in[...], pair[:, columns(0)])
+            up = dot(piece_in[...], pair[:, columns(1)])
+            grad_act = rdot(grad_in[...], down[tile(index, feed_size), :])
+            sigma = 1.0 / (1.0 + jnp.exp(-gate))
+            act_out[:, columns(0)] = (gate * sigma * up).astype(BF16)
+            back_out[:, columns(0)] = (
+                grad_act * up * sigma * (1.0 + gate * (1.0 - sigma))
+            ).astype(BF16)
+            back_out[:, columns(1)] = (grad_act * gate * sigma).astype(BF16)
+
+        loop(feed_width // feed_size, one)
+        act_copy(piece).start()
+        back_copy(piece).start()
+
+    two_gather = Gather(two_land, two_sems, feed)
+    loop(chips, two_gather.step)
+    act_copy(0).wait()
+    back_copy(0).wait()
+    first_gather.finish()
+    grad_gather.finish()
+    two_gather.finish()
+    for out in outs:
+        out.wait()
+    for share in shares:
+        share.finish()
     loop(shards, lambda i: gain_copy(i, shard).wait_send())
-    loop(shards, lambda i: weight_copy(i, shard).wait_send())
-    loop(parts, lambda i: token_copy(i, past_part(i)).wait_recv())
     loop(parts, lambda i: token_copy(i, me).wait_send())
 
 
-def first(hidden, gains, tokens, part, shards, parts, width):
+def forward(hidden, grad, gains, token_info, freq, weights, shards, parts, heads):
     count = hidden.shape[0]
+    tokens = parts * count
+    width = heads * HEAD_SIZE
+    total_width = width + 2 * HEAD_SIZE
+    feed_width = FF // parts
+    chips = parts // 2
+    shape = jax.ShapeDtypeStruct
     return pl.pallas_call(
-        functools.partial(first_kernel, D // shards, width),
+        functools.partial(forward_kernel, heads),
         out_shape=(
-            jax.ShapeDtypeStruct((parts, count, D), BF16),
-            jax.ShapeDtypeStruct((parts, count, width), F32),
-            jax.ShapeDtypeStruct((D, part.shape[1]), BF16),
-            jax.ShapeDtypeStruct((8, D), F32),
-            jax.ShapeDtypeStruct((shards, *gains.shape), F32),
-            jax.ShapeDtypeStruct((parts, *tokens.shape), jnp.int32),
+            shape((parts, count, D), BF16),
+            shape((parts, count, D), BF16),
+            shape((parts, count, D), BF16),
+            shape((parts, count, feed_width), BF16),
+            shape((parts, count, 2 * feed_width), BF16),
+            shape((parts, count, total_width), F32),
+            shape((tokens, HEAD_SIZE), F32),
+            shape((tokens, HEAD_SIZE), F32),
+            shape((tokens, width), BF16),
+            shape((tokens, HEAD_SIZE), BF16),
+            shape((tokens, HEAD_SIZE), BF16),
+            shape((tokens, width), BF16),
+            shape((8, tokens), F32),
+            shape((count, D), F32),
+            shape((8, D), F32),
+            shape((shards, *gains.shape), F32),
+            shape((parts, *token_info.shape), jnp.int32),
+            shape((D, total_width), BF16),
+            shape((width, D), BF16),
+            shape((D, 2 * feed_width), BF16),
+            shape((feed_width, D), BF16),
         ),
-        in_specs=[WHOLE] * 4,
-        out_specs=(WHOLE,) * 6,
-        scratch_shapes=gather_scratch(parts // 2)
+        in_specs=[WHOLE] * 5 + [HBM] * 7,
+        out_specs=(HBM,) * 5 + (WHOLE,) * 14 + (HBM,) * 2,
+        scratch_shapes=[
+            VMEM((D, 2 * feed_width), BF16),
+            VMEM((feed_width, D), BF16),
+            VMEM((count, D), BF16),
+            VMEM((count, D), BF16),
+            VMEM((count, D), BF16),
+            VMEM((count, feed_width), BF16),
+            VMEM((count, 2 * feed_width), BF16),
+            VMEM((count, D), F32),
+            pltpu.SemaphoreType.DMA((8,)),
+        ]
         + [pltpu.SemaphoreType.DMA((shards,))] * 2
         + [pltpu.SemaphoreType.DMA((parts,))] * 2
-        + [pltpu.SemaphoreType.DMA((shards,))] * 2,
-        compiler_params=params(0, 60),
-        cost_estimate=cost(85),
-        name="gather_normed",
-    )(hidden, gains, tokens, part)
-
-
-def feed_kernel(width, *refs):
-    x, grads, weights, land, activation, back = refs[:6]
-    weight, weight_sem, grad, grad_sems = refs[6:10]
-    sems = refs[10:]
-    me, _, _, chips = line_position()
-    copy = copy_in(weights, weight, weight_sem)
-
-    def grad_copy(piece):
-        return pltpu.make_async_copy(grads.at[piece], grad.at[piece], grad_sems.at[piece])
-
-    loop(2 * chips, lambda piece: grad_copy(piece).start())
-    land[me] = x[...]
-    size = 256 if width % 256 == 0 else 128
-
-    def consume(piece):
-        grad_copy(piece).wait()
-
-        def one(index):
-            def columns(kind):
-                return pl.ds(pl.multiple_of(kind * width + index * size, 128), size)
-
-            gate = dot(land[piece], weight[:, columns(0)])
-            up = dot(land[piece], weight[:, columns(1)])
-            grad_act = dot(grad[piece], weight[:, columns(2)])
-            sigma = 1.0 / (1.0 + jnp.exp(-gate))
-            activation[piece, :, columns(0)] = (gate * sigma * up).astype(BF16)
-            back[piece, :, columns(0)] = (
-                grad_act * up * sigma * (1.0 + gate * (1.0 - sigma))
-            ).astype(BF16)
-            back[piece, :, columns(1)] = (grad_act * gate * sigma).astype(BF16)
-
-        loop(width // size, one)
-
-    line_barrier()
-    gather = Gather(land, sems, consume)
-    copy.wait()
-    loop(chips, gather.step)
-    gather.finish()
-
-
-def feed(normed, grads, weights):
-    parts, count, _ = grads.shape
-    width = weights.shape[1] // 3
-    return pl.pallas_call(
-        functools.partial(feed_kernel, width),
-        out_shape=(
-            jax.ShapeDtypeStruct((parts, count, D), BF16),
-            jax.ShapeDtypeStruct((parts, count, width), BF16),
-            jax.ShapeDtypeStruct((parts, count, 2 * width), BF16),
-        ),
-        in_specs=[WHOLE, HBM, HBM],
-        out_specs=(WHOLE,) * 3,
-        scratch_shapes=[
-            VMEM(weights.shape, BF16),
-            pltpu.SemaphoreType.DMA,
-            VMEM(grads.shape, BF16),
-            pltpu.SemaphoreType.DMA((parts,)),
-        ]
-        + gather_scratch(parts // 2),
-        compiler_params=params(2, 60),
-        cost_estimate=cost(90),
-        name="feed",
-    )(normed, grads, weights)
+        + shares_scratch(7, shards)
+        + gather_scratch(chips)
+        + gather_scratch(chips)
+        + gather_scratch(chips)
+        + scatter_scratch(chips, count),
+        compiler_params=params(0, 63),
+        cost_estimate=cost(280),
+        name="forward",
+    )(hidden, grad, gains, token_info, freq, *weights)
 
 
 def rms_back(value, gain, grad):
@@ -592,30 +809,38 @@
     return inverse * scaled - value * (inverse * inverse * inverse * inner), terms
 
 
-def turn_kernel(columns, *refs):
-    back, feed_weights, activation, weights, middle, grad, gain_rows, down_grad, pair_grad = refs[:9]
-    grad_middle, land, gain_sum, down_land, context_grad, hidden, pair_in = refs[9:16]
-    weight, data, head_weight, total, low, piece_in, own_down, down_sum, sems = refs[16:25]
+def turn_kernel(*refs):
+    back, pair_weight, down_weight, activation, out_weight = refs[:5]
+    middle, grad, gain_rows, down_grad, pair_grad = refs[5:10]
+    grad_middle, land, gain_sum, down_land, context_grad, hidden, pair_in = refs[10:17]
+    weight, data, total, low, piece_in, own_down, down_sum, sems = refs[17:25]
     down_refs, down_sems, gather_sems = refs[25:28], refs[28:34], refs[34:40]
     pair_sems, first_scratch, second_scratch = refs[40:42], refs[42:51], refs[51:]
     me, _, _, chips = line_position()
     width = back.shape[2] // 2
-    weight_copy = copy_in(feed_weights.at[:, pl.ds(0, 2 * width)], weight, sems.at[0])
+    weight_copy = copy_in(pair_weight, weight, sems.at[0])
     data_copy = copy_in(back, data, sems.at[1])
-    head_copy = copy_in(weights.at[:, columns], head_weight, sems.at[2])
     own_copy = copy_in(down_grad.at[lax.axis_index("fsdp")], own_down, sems.at[3])
 
     def produce(piece, chunk):
         return rdot(data[piece], weight[pl.ds(pl.multiple_of(chunk * WIDE, WIDE), WIDE), :])
 
+    each = 2 * width // WIDE
+
+    def down_block(chunk):
+        return tile(chunk // each, width), tile(chunk % each, WIDE)
+
+    def down_copy(chunk):
+        source = down_weight.at[:, tile(chunk, WIDE)]
+        return pltpu.make_async_copy(source, weight.at[down_block(chunk)], sems.at[5 + chunk])
+
     def produce_hidden(piece, chunk):
-        block = pl.ds(pl.multiple_of(chunk * WIDE, WIDE), WIDE)
-        return rdot(data[piece, :, :width], weight[block, :width])
+        return dot(data[piece, :, :width], weight[down_block(chunk)])
 
     def consume(piece):
         copy = copy_in(land.at[piece], piece_in, sems.at[4])
         copy.wait()
-        context_grad[piece] = dot(piece_in[...], head_weight[...]).astype(BF16)
+        context_grad[piece] = rdot(piece_in[...], out_weight[...]).astype(BF16)
 
     down = FsdpSum(down_grad, *down_refs, own=own_down)
     pair = FsdpSum(pair_grad, pair_in, *pair_sems, own=own_down)
@@ -649,9 +874,8 @@
 
     loop(chips - 1, step)
     scatter.finish()
-    down_copy = copy_in(
-        feed_weights.at[:, pl.ds(2 * width, width)], weight.at[:, pl.ds(0, width)], sems.at[0]
-    )
+    for chunk in range(CHUNKS):
+        down_copy(chunk).start()
     act_copy = copy_in(activation, data.at[:, :, pl.ds(0, width)], sems.at[1])
     gain_sum[...] = jnp.zeros_like(gain_sum)
 
@@ -665,9 +889,9 @@
     row_blocks(middle.shape[0], norm)
     low_copy = copy_in(low, land.at[me], sems.at[3])
     low_copy.wait()
-    head_copy.wait()
     gather.step(0)
-    down_copy.wait()
+    for chunk in range(CHUNKS):
+        down_copy(chunk).wait()
     act_copy.wait()
     hidden_scatter.prepare(0)
 
@@ -694,11 +918,12 @@
     row_blocks(middle.shape[0], add)
 
 
-def turn(back, feed_weights, activation, weights, middle, grad, gain_rows, down_grad, pair_grad, width):
+def turn(back, pair_weight, down_weight, activation, out_weight, middle, grad, gain_rows, down_grad, pair_grad):
     parts, count, feed_width = activation.shape
     shards, rows, _ = down_grad.shape
+    width = out_weight.shape[0]
     return pl.pallas_call(
-        functools.partial(turn_kernel, pl.ds(weights.shape[1] - width, width)),
+        turn_kernel,
         out_shape=(
             jax.ShapeDtypeStruct((count, D), F32),
             jax.ShapeDtypeStruct((parts, count, D), BF16),
@@ -708,18 +933,17 @@
             jax.ShapeDtypeStruct((count, D), BF16),
             jax.ShapeDtypeStruct((shards - 1, rows, 2 * feed_width), BF16),
         ),
-        in_specs=[HBM, HBM, HBM, HBM, WHOLE, WHOLE, WHOLE, HBM, HBM],
+        in_specs=[HBM] * 4 + [WHOLE] * 4 + [HBM] * 2,
         out_specs=(WHOLE, HBM, WHOLE, HBM, WHOLE, WHOLE, HBM),
         scratch_shapes=[
             VMEM((D, 2 * feed_width), BF16),
             VMEM((parts, count, 2 * feed_width), BF16),
-            VMEM((D, width), BF16),
             VMEM((count, D), F32),
             VMEM((count, D), BF16),
             VMEM((count, D), BF16),
             VMEM((rows, feed_width), BF16),
             VMEM((rows, feed_width), BF16),
-            pltpu.SemaphoreType.DMA((5,)),
+            pltpu.SemaphoreType.DMA((5 + CHUNKS,)),
         ]
         + fsdp_scratch(shards, rows, feed_width)
         + gather_scratch(parts // 2)
@@ -730,10 +954,21 @@
         compiler_params=params(3, 63),
         cost_estimate=cost(185),
         name="turn",
-    )(back, feed_weights, activation, weights, middle, grad, gain_rows, down_grad, pair_grad)
-
-
-def last_kernel(columns, *refs):
+    )(
+        back,
+        pair_weight,
+        down_weight,
+        activation,
+        out_weight,
+        middle,
+        grad,
+        gain_rows,
+        down_grad,
+        pair_grad,
+    )
+
+
+def last_kernel(*refs):
     back, weights, x, grad_middle, gain_rows, gain_two, gain_heads, head_grad = refs[:8]
     hidden, gain_out, land = refs[8:11]
     weight, weight_sem, total, gain_one, pack, pack_in, shard_sum, shard_in = refs[11:19]
@@ -742,7 +977,7 @@
     shard = lax.axis_index("fsdp")
     shards, ahead, _ = peers_of("fsdp")
     parts, next_part, _ = peers_of("ctx")
-    copy = copy_in(weights.at[:, columns], weight, weight_sem)
+    copy = copy_in(weights, weight, weight_sem)
 
     def produce(piece, chunk):
         return rdot(back[piece], weight[pl.ds(pl.multiple_of(chunk * WIDE, WIDE), WIDE), :])
@@ -824,7 +1059,7 @@
     parts, count, width = back.shape
     shards, rows, head_width = head_grad.shape
     return pl.pallas_call(
-        functools.partial(last_kernel, pl.ds(0, width)),
+        last_kernel,
         out_shape=(
             jax.ShapeDtypeStruct((count, D), F32),
             jax.ShapeDtypeStruct((16, 128), F32),
@@ -853,134 +1088,6 @@
     )(back, weights, hidden, grad_middle, gain_rows, gain_two, gain_heads, head_grad)
 
 
-QUERY_TILE = 256
-KEY_TILE = 512
-
-
-def reach(index, tokens):
-    return jnp.minimum((index + 2) * QUERY_TILE + KEY_TILE - 1, tokens) // KEY_TILE
-
-
-def head_norm(value, gain, cosine, sine):
-    normed = value * inverse_norm(value) * gain
-    return normed * cosine + pltpu.roll(normed, HEAD_SIZE // 2, 1) * sine
-
-
-def attend_kernel(heads, columns, *refs):
-    proj, cosine, sine, gain, id_column, id_row, weights, x, grad, gain_rows = refs[:10]
-    queries, keys, values, context, inverse, middle, normed, land = refs[10:18]
-    weight, weight_sem, grad_sem, total = refs[18:22]
-    gather_sems, scratch = refs[22:28], refs[28:]
-    me, _, _, chips = line_position()
-    tokens = proj.shape[0]
-    count = x.shape[0]
-    key_at = heads * HEAD_SIZE
-    copy = copy_in(weights.at[:, columns], weight, weight_sem)
-    own = copy_in(grad, land.at[me], grad_sem)
-    gather = Gather(land, gather_sems)
-    line_barrier()
-    own.wait()
-    gather.step(0)
-
-    def prepare(index):
-        block = pl.ds(pl.multiple_of(index * QUERY_TILE, QUERY_TILE), QUERY_TILE)
-        c, s = cosine[block, :], sine[block, :]
-        for h in range(heads):
-            lanes = slice(h * HEAD_SIZE, (h + 1) * HEAD_SIZE)
-            rotated = head_norm(proj[block, lanes], gain[0:1, :], c, s) * HEAD_SIZE ** (-0.5)
-            queries[block, lanes] = rotated.astype(BF16)
-        rotated = head_norm(proj[block, key_at : key_at + HEAD_SIZE], gain[1:2, :], c, s)
-        keys[block, :] = rotated.astype(BF16)
-        values[block, :] = proj[block, key_at + HEAD_SIZE : key_at + 2 * HEAD_SIZE].astype(BF16)
-
-    loop(tokens // QUERY_TILE, prepare)
-
-    def attend(index):
-        block = pl.ds(pl.multiple_of(index * QUERY_TILE, QUERY_TILE), QUERY_TILE)
-        query_ids = id_column[block, :]
-        for h in range(heads):
-            lanes = slice(h * HEAD_SIZE, (h + 1) * HEAD_SIZE)
-            query = queries[block, lanes]
-
-            def one(tile, carry):
-                sums, total = carry
-                span = pl.ds(pl.multiple_of(tile * KEY_TILE, KEY_TILE), KEY_TILE)
-                scores = rdot(query, keys[span, :])
-                expon = jnp.where(id_row[0:1, span] <= query_ids, jnp.exp(scores), 0.0)
-                sums = sums + dot(expon.astype(BF16), values[span, :])
-                return sums, total + jnp.sum(expon, axis=1, keepdims=True)
-
-            start = (jnp.zeros((QUERY_TILE, HEAD_SIZE), F32), jnp.zeros((QUERY_TILE, 1), F32))
-            sums, total = lax.fori_loop(0, reach(index, tokens), one, start)
-            scale = 1.0 / total
-            context[block, lanes] = (sums * scale).astype(BF16)
-            inverse[h : h + 1, block] = jnp.broadcast_to(scale, (QUERY_TILE, HEAD_SIZE)).T[0:1, :]
-
-    loop(tokens // QUERY_TILE, attend)
-
-    def produce(piece, chunk):
-        block = pl.ds(pl.multiple_of(piece * count, count), count)
-        return rdot(context[block, :], weight[pl.ds(pl.multiple_of(chunk * WIDE, WIDE), WIDE), :])
-
-    scatter = Scatter(scratch, produce, total)
-    scatter.begin()
-    copy.wait()
-    scatter.prepare(0)
-    gather.step(1)
-
-    def step(time):
-        scatter.step(time)
-        scatter.prepare(time + 1)
-
-        @pl.when(time >= 1)
-        def _():
-            gather.step(time + 1)
-
-    loop(chips - 1, step)
-    scatter.finish()
-
-    def norm(block):
-        value = x[block, :].astype(F32) + total[block, :]
-        middle[block, :] = value
-        normed[block, :] = (value * inverse_norm(value) * gain_rows[1:2, :]).astype(BF16)
-
-    row_blocks(count, norm)
-    gather.finish()
-
-
-def attend(proj, cosine, sine, gain, id_column, id_row, weights, hidden, grad, gain_rows, heads):
-    tokens = proj.shape[0]
-    width = heads * HEAD_SIZE
-    count = hidden.shape[0]
-    parts = tokens // count
-    return pl.pallas_call(
-        functools.partial(attend_kernel, heads, pl.ds(weights.shape[1] - width, width)),
-        out_shape=(
-            jax.ShapeDtypeStruct((tokens, width), BF16),
-            jax.ShapeDtypeStruct((tokens, HEAD_SIZE), BF16),
-            jax.ShapeDtypeStruct((tokens, HEAD_SIZE), BF16),
-            jax.ShapeDtypeStruct((tokens, width), BF16),
-            jax.ShapeDtypeStruct((8, tokens), F32),
-            jax.ShapeDtypeStruct((count, D), F32),
-            jax.ShapeDtypeStruct((count, D), BF16),
-            jax.ShapeDtypeStruct((parts, count, D), BF16),
-        ),
-        in_specs=[WHOLE] * 6 + [HBM, WHOLE, WHOLE, WHOLE],
-        out_specs=(WHOLE,) * 7 + (HBM,),
-        scratch_shapes=[
-            VMEM((D, width), BF16),
-            pltpu.SemaphoreType.DMA,
-            pltpu.SemaphoreType.DMA,
-            VMEM((count, D), F32),
-        ]
-        + gather_scratch(parts // 2)
-        + scatter_scratch(parts // 2, count),
-        compiler_params=params(1, 60),
-        cost_estimate=cost(110),
-        name="attend",
-    )(proj, cosine, sine, gain, id_column, id_row, weights, hidden, grad, gain_rows)
-
-
 def attention_back_kernel(heads, *refs):
     queries, keys, values, out_grad, inverse, context, proj, cosine, sine, gain = refs[:10]
     id_column, id_row, back, gain_sum, key_grad, value_grad, query_grad = refs[10:]
@@ -1126,14 +1233,6 @@
     return with_layout_constraint(array, Layout(major_to_minor=(0, 1)))
 
 
-def own_columns(array, index, width):
-    return lax.dynamic_slice_in_dim(array, index * width, width, axis=1)
-
-
-def own_rows(array, index, width):
-    return lax.dynamic_slice_in_dim(array, index * width, width, axis=0)
-
-
 def local(
     hidden_in,
     weight_query,
@@ -1153,11 +1252,9 @@
 ):
     parts = lax.axis_size("ctx")
     shards = lax.axis_size("fsdp")
-    me = lax.axis_index("ctx")
     shard = lax.axis_index("fsdp")
     heads = QUERY_HEADS // parts
     sharers = parts // KEY_VALUE_HEADS
-    key_head = me // sharers
     width = heads * HEAD_SIZE
     feed_width = FF // parts
     rows = D // shards
@@ -1165,58 +1262,52 @@
     count = hidden_in.shape[1]
     tokens = parts * count
 
-    def gather_rows(piece):
-        return lax.all_gather(piece, "fsdp", axis=0, tiled=True)
-
     def gather_parts(piece):
         return lax.all_gather(piece, "ctx", axis=0)
-
-    own_heads_weight = jnp.concatenate(
-        [
-            own_columns(weight_query, me, width),
-            own_columns(key_weight_matrix, key_head, HEAD_SIZE),
-            own_columns(weight_value, key_head, HEAD_SIZE),
-            own_rows(weight_out, me, width).T,
-        ],
-        axis=1,
-    )
-    feed_weight = gather_rows(
-        jnp.concatenate(
-            [
-                own_columns(weight_gate, me, feed_width),
-                own_columns(weight_up, me, feed_width),
-                own_rows(weight_down, me, feed_width).T,
-            ],
-            axis=1,
-        )
-    )
 
     own_gains = jnp.concatenate([gain_attention, gain_feed, gain_query, gain_key]).astype(F32)
     own_gains = jnp.pad(own_gains, (0, 2048 - own_gains.shape[0])).reshape(16, 128)
     own_tokens = jnp.pad(jnp.stack([positions[0], token_block_index[0]]), ((0, 6), (0, 0)))
-    hidden, grad = hidden_in[0], grad_out[0]
-    normed_all, proj, heads_weight, gain_rows, gains, whole = first(
-        hidden, own_gains, own_tokens, own_heads_weight, shards, parts, width + 2 * HEAD_SIZE
-    )
-    flat_gains = gains.reshape(shards, -1)
-    norm_query = flat_gains[:, 2 * rows : 2 * rows + head_rows].reshape(1, -1)
-    norm_key = flat_gains[:, 2 * rows + head_rows : 2 * rows + 2 * head_rows].reshape(1, -1)
-    head_gains = jnp.concatenate([norm_query, norm_key, jnp.zeros((6, HEAD_SIZE), F32)])
-
     half = HEAD_SIZE // 2
     freq = THETA ** (-(jnp.arange(half).astype(F32) * 2.0 / HEAD_SIZE))
-    angle = whole[:, 0].reshape(-1).astype(F32)[:, None] * freq
-    cosine, sine = jnp.cos(angle), jnp.sin(angle)
-    cosine = jnp.concatenate([cosine, cosine], axis=1)
-    sine = jnp.concatenate([-sine, sine], axis=1)
+    freq = jnp.broadcast_to(jnp.concatenate([freq, freq]), (8, HEAD_SIZE))
+    hidden, grad = hidden_in[0], grad_out[0]
+    weights = (
+        weight_query,
+        key_weight_matrix,
+        weight_value,
+        weight_out,
+        weight_gate,
+        weight_up,
+        weight_down,
+    )
+    (
+        normed_all,
+        grad_all,
+        normed_two_all,
+        activation,
+        back,
+        proj,
+        cosine,
+        sine,
+        queries,
+        keys,
+        values,
+        context,
+        inverse,
+        middle,
+        gain_rows,
+        gains,
+        whole,
+        heads_weight,
+        out_weight,
+        pair_weight,
+        down_weight,
+    ) = forward(hidden, grad, own_gains, own_tokens, freq, weights, shards, parts, heads)
+    head_gains = gain_rows[2:4, :HEAD_SIZE]
     ids = whole[:, 1].reshape(-1)
     id_row, id_column = ids[None, :], ids[:, None]
-
     proj = proj.reshape(tokens, width + 2 * HEAD_SIZE)
-    queries, keys, values, context, inverse, middle, normed_two, grad_all = attend(
-        proj, cosine, sine, head_gains, id_column, id_row, heads_weight, hidden, grad, gain_rows, heads
-    )
-    normed_two_all, activation, back = feed(normed_two, grad_all, feed_weight)
 
     flat_grad = grad_all.reshape(tokens, D)
     flat_back = back.reshape(tokens, 2 * feed_width)
@@ -1227,15 +1318,15 @@
     feed_grad = feed_grad.reshape(shards, rows, 2 * feed_width)
     grad_middle, low_all, gain_two, down_parts, context_grad, hidden_out, pair_in = turn(
         back,
-        feed_weight,
+        pair_weight,
+        down_weight,
         activation,
-        heads_weight,
+        out_weight,
         middle,
         grad,
         gain_rows,
         down_grad.reshape(shards, rows, feed_width),
         feed_grad,
-        width,
     )
     own_pair = lax.dynamic_index_in_dim(feed_grad, shard, keepdims=False)
     feed_shard = (own_pair.astype(F32) + jnp.sum(pair_in.astype(F32), axis=0)).astype(BF16)

time: 840 us -> 795 us (0.946)
  Pallas kernels: 740 us -> 715 us
  other arithmetic: 19.4 us -> 9.67 us
    pallas_call x5 -> x3, Pallas kernels: 670 us -> 645 us  [the longest x1 277 us: forward(): pl.pallas_call(functools.partial(forward_kernel, heads), out_shape=(shape...]
  transfers between devices with their start and end apart: 2 -> 1, of which waited for: 0 -> 0; matrix products, arithmetic and copies ran while one was open for 4% -> 3% of each run, Pallas kernels for 51% -> 26%
where the time goes in v9:
time: 795 us; the launch traced here: 794 us
  Pallas kernels  715 us (90%)
  matrix products  41.7 us (5%)
  between operations  14.2 us (2%)
  local copies, waits for them, and re-layouts  12.6 us (2%)
  other arithmetic  9.67 us (1%)
    pallas_call x1, Pallas kernels, forward(): pl.pallas_call(functools.partial(forward_kernel, heads), out_shape=(shape...  277 us
    pallas_call x1, Pallas kernels, turn(): pl.pallas_call(turn_kernel, out_shape=(jax.ShapeDtypeStruct((count, D), F...  213 us
    pallas_call x1, Pallas kernels, last(): pl.pallas_call(last_kernel, out_shape=(jax.ShapeDtypeStruct((count, D), F...  154 us
    dot_general x4, matrix products, tdot(): lax.dot_general(left, right, (((0,), (0,)), ((), ())), preferred_element_...  41.7 us
    pallas_call x1, Pallas kernels, attention_back(): pl.pallas_call(functools.partial(attention_back_kernel, heads), out_shape...  37.5 us
  transfers between devices with their start and end apart: 1, of which 0 were waited for; matrix products, arithmetic and copies ran while one was open for 3% of the time, Pallas kernels for 26%

profile of v9, /device:TPU:0, one launch (start us, length us, event | category | flops | bytes accessed | tf_op | source)
XLA Modules:
  0.0 793.7 jit_solution(2584720112939648174)
XLA Ops:
  7.2 0.0 all-gather.3.cloned.1.call-start
  7.2 2.8 concatenate.9
  10.0 0.6 bitcast_convert_fusion.2.refs_2_
  10.6 0.1 pad_maximum_fusion.1
  10.7 0.7 pad_add_fusion
  11.4 0.6 pad.10.refs_3_
  12.0 0.6 broadcast_in_dim.9.refs_4_
  12.6 277.3 %forward.1 = (bf16[8,256,2048]{2,1,0:T(8,128)(2,1)}, bf16[8,256,2048]{2,1,0:T(8,128)(2,1)}, bf16[8,256,2048]{2,1,0:T(8,128)(2,1)}, bf16[8,256,768]{2,1,0:T(8,128...) custom-call(bf16[256,2048]{1,0:T(8,128)(2,1)} %bitcast.50, ...), custom_call_target="tpu_custom_call" | custom-call | flops 321999994880 | bytes 1024 | tf_op jit(solution)/shard_map/forward/pallas_call | solution.py:753
  290.0 0.0 copy-start.12
  290.0 0.0 copy-start.13
  290.0 11.5 %bitcast_convert_fusion.1 = bf16[2048,768]{1,0:T(8,128)(2,1)} fusion(bf16[8,256,2048]{2,1,0:T(8,128)(2,1)} %get-tuple-element.61, bf16[8,256,768]{2,1,0:T(8,128)(2,1)} %get-tuple-element.62.refs_3_), kind=kOutput, calls=%fused_computation.2 | convolution fusion | flops 6444023808 | bytes 14680064 | tf_op jit(solution)/shard_map/dot_general | solution.py:33
  301.5 0.0 copy-done.12
  301.5 0.0 copy-done.13
  301.5 15.6 %bitcast_convert_fusion = bf16[2048,1536]{1,0:T(8,128)(2,1)} fusion(bf16[8,256,2048]{2,1,0:T(8,128)(2,1)S(1)} %copy-done.12, bf16[8,256,1536]{2,1,0:T(8,128)(2,1)S(1)} %copy-done.13), kind=kOutput, calls=%fused_computation | convolution fusion | flops 12888047616 | bytes 20971520 | tf_op jit(solution)/shard_map/dot_general | solution.py:33
  317.1 213.3 %turn.1 = (f32[256,2048]{1,0:T(8,128)}, bf16[8,256,2048]{2,1,0:T(8,128)(2,1)}, f32[8,2048]{1,0:T(8,128)}, bf16[8,512,768]{2,1,0:T(8,128)(2,1)}, bf16[8,256,256]{...) custom-call(bf16[8,256,1536]{2,1,0:T(8,128)(2,1)} %get-tuple-element.63.refs_0_, ...), custom_call_target="tpu_custom_call" | custom-call | flops 212749991936 | bytes 1024 | tf_op jit(solution)/shard_map/turn/pallas_call | solution.py:925
  530.5 3.4 convert_reduce_fusion
  533.9 3.0 fusion
  536.9 0.0 all-gather.3.cloned.1.call-update
  536.9 0.7 slice.18.refs_9_
  537.6 0.8 slice.19
  538.4 1.3 copy.32.refs_10_
  539.8 0.0 copy-start
  539.8 0.0 copy-start.1
  539.8 0.0 copy-start.2
  539.8 0.0 copy-start.4
  539.8 0.0 copy-start.6
  539.8 10.1 %spread_turned.1 = f32[6144,512]{1,0:T(8,128)} custom-call(bf16[8,512,768]{2,1,0:T(8,128)(2,1)} %get-tuple-element.86.source), custom_call_target="tpu_custom_call" | custom-call | tf_op jit(solution)/shard_map/spread_turned/pallas_call | solution.py:1196
  549.9 0.0 copy-done
  549.9 0.0 copy-done.1
  549.9 0.0 copy-done.2
  549.9 0.0 copy-done.4
  549.9 0.0 copy-done.6
  549.9 0.0 copy-start.3
  549.9 1.2 copy-done.3
  551.2 0.0 copy-start.5
  551.2 1.0 copy-done.5
  552.2 37.5 %attention_back.1 = (bf16[2048,512]{1,0:T(8,128)(2,1)}, f32[8,128]{1,0:T(8,128)S(1)}) custom-call(bf16[2048,256]{1,0:T(8,128)(2,1)S(1)} %copy-done.3, bf16[2048,128]{1,0:T(8,128)(2,1)S(1)} %copy-done.4, bf16[2048,128]{1,0:T(8,128)(2,1)S(1)} %copy-done.5, bf16[2048,256]{1,0:T(8,128)(2,1)S(1)} %bitcast.40, f32[8,2048]{1,0:T(8,128)S(1)} %copy-done.6, ...), custom_call_target="tpu_custom_call" | custom-call | flops 43699998720 | bytes 1024 | tf_op jit(solution)/shard_map/attention_back/pallas_call | solution.py:1151
  589.7 0.0 copy-start.7
  589.7 0.0 copy-start.11
  589.7 6.0 convolution_convert_fusion.1
  595.8 0.0 copy-done.7
  595.8 0.0 copy-done.11
  595.8 8.5 %convolution_convert_fusion = bf16[2048,512]{1,0:T(8,128)(2,1)S(1)} fusion(bf16[2048,2048]{1,0:T(8,128)(2,1)} %bitcast.52, bf16[2048,512]{1,0:T(8,128)(2,1)S(1)} %copy-done.11), kind=kOutput, calls=%fused_computation.6 | convolution fusion | flops 4296015872 | bytes 12582912 | tf_op jit(solution)/shard_map/dot_general | solution.py:33
  604.3 1.9 pad_maximum_fusion
  606.2 153.9 %last.1 = (f32[256,2048]{1,0:T(8,128)}, f32[16,128]{1,0:T(8,128)}, bf16[8,512,768]{2,1,0:T(8,128)(2,1)}) custom-call(bf16[8,256,512]{2,1,0:T(8,128)(2,1)} %bitcast.56, bf16[2048,512]{1,0:T(8,128)(2,1)} %get-tuple-element.88.refs_1_, bf16[256,2048]{1,0:T(8,128)(2,1)} %bitcast.51, f32[256,2048]{1,0:T(8,128)} %get-tuple-element.89.refs_3_, ...), custom_call_target="tpu_custom_call" | custom-call | flops 103499997184 | bytes 1024 | tf_op jit(solution)/shard_map/last/pallas_call | solution.py:1061
  760.1 0.0 copy-start.10
  760.1 8.8 %spread_heads.1 = (f32[512,2048]{1,0:T(8,128)}, f32[512,1024]{1,0:T(8,128)}, f32[512,1024]{1,0:T(8,128)}, f32[2048,512]{1,0:T(8,128)}) custom-call(bf16[8,512,768]{2,1,0:T(8,128)(2,1)} %get-tuple-element.95.source), custom_call_target="tpu_custom_call" | custom-call | tf_op jit(solution)/shard_map/spread_heads/pallas_call | solution.py:1219
  768.9 0.0 copy-done.10
  768.9 0.6 fusion.1
  769.5 0.6 slice_bitcast_fusion
  770.1 0.0 all-gather.3.cloned.1.call-done
  770.1 0.0 copy-start.9
  770.1 0.0 copy-start.8
  770.1 14.4 %spread_pair.1 = (f32[512,6144]{1,0:T(8,128)}, f32[512,6144]{1,0:T(8,128)}) custom-call(bf16[8,512,1536]{2,1,0:T(8,128)(2,1)} %bitcast.41), custom_call_target="tpu_custom_call" | custom-call | tf_op jit(solution)/shard_map/spread_pair/pallas_call | solution.py:1179
  784.5 0.0 copy-done.9
  784.5 1.0 copy.37
  785.5 0.0 copy-done.8
  785.5 1.3 copy.38
  (1 shorter events, 0.0 us)
Async XLA Ops:
  7.2 762.9 %all-gather.3.cloned.1.call-start = ((), (), s32[]{:S(2)}) async-start(), calls=%async_computation | async-start | bytes 14155776 | tf_op jit(solution)/shard_map/all_gather | solution.py:1266
  290.0 11.5 %copy-start.12 = (bf16[8,256,2048]{2,1,0:T(8,128)(2,1)S(1)}, bf16[8,256,2048]{2,1,0:T(8,128)(2,1)}, u32[]{:S(2)}) copy-start(bf16[8,256,2048]{2,1,0:T(8,128)(2,1)} %get-tuple-element.60) | copy-start | bytes 25165828
  290.0 11.5 %copy-start.13 = (bf16[8,256,1536]{2,1,0:T(8,128)(2,1)S(1)}, bf16[8,256,1536]{2,1,0:T(8,128)(2,1)}, u32[]{:S(2)}) copy-start(bf16[8,256,1536]{2,1,0:T(8,128)(2,1)} %get-tuple-element.63.refs_0_) | copy-start | bytes 18874372
  539.8 10.1 %copy-start = (bf16[8,256,256]{2,1,0:T(8,128)(2,1)S(1)}, bf16[8,256,256]{2,1,0:T(8,128)(2,1)}, u32[]{:S(2)}) copy-start(bf16[8,256,256]{2,1,0:T(8,128)(2,1)} %get-tuple-element.78) | copy-start | bytes 3145732
  539.8 10.1 %copy-start.1 = (bf16[2048,256]{1,0:T(8,128)(2,1)S(1)}, bf16[2048,256]{1,0:T(8,128)(2,1)}, u32[]{:S(2)}) copy-start(bf16[2048,256]{1,0:T(8,128)(2,1)} %get-tuple-element.80.refs_5_) | copy-start | bytes 3145732
  539.8 10.1 %copy-start.2 = (f32[2048,128]{1,0:T(8,128)S(1)}, f32[2048,128]{1,0:T(8,128)}, u32[]{:S(2)}) copy-start(f32[2048,128]{1,0:T(8,128)} %get-tuple-element.82.refs_7_) | copy-start | bytes 3145732
  539.8 10.1 %copy-start.4 = (bf16[2048,128]{1,0:T(8,128)(2,1)S(1)}, bf16[2048,128]{1,0:T(8,128)(2,1)}, u32[]{:S(2)}) copy-start(bf16[2048,128]{1,0:T(8,128)(2,1)} %get-tuple-element.73.refs_1_) | copy-start | bytes 1572868
  539.8 10.1 %copy-start.6 = (f32[8,2048]{1,0:T(8,128)S(1)}, f32[8,2048]{1,0:T(8,128)}, u32[]{:S(2)}) copy-start(f32[8,2048]{1,0:T(8,128)} %get-tuple-element.79.refs_4_) | copy-start | bytes 196612
  549.9 1.2 copy-start.3
  551.2 1.0 copy-start.5
  589.7 6.1 copy-start.7
  589.7 6.1 copy-start.11
  760.1 8.9 %copy-start.10 = (f32[16,128]{1,0:T(8,128)S(1)}, f32[16,128]{1,0:T(8,128)}, u32[]{:S(2)}) copy-start(f32[16,128]{1,0:T(8,128)} %get-tuple-element.104) | copy-start | bytes 24580
  770.1 14.4 %copy-start.9 = (bf16[256,2048]{1,0:T(8,128)(2,1)S(1)}, bf16[256,2048]{1,0:T(8,128)(2,1)}, u32[]{:S(2)}) copy-start(bf16[256,2048]{1,0:T(8,128)(2,1)} %get-tuple-element.71) | copy-start | bytes 3145732
  770.1 15.4 %copy-start.8 = (f32[256,2048]{1,0:T(8,128)S(1)}, f32[256,2048]{1,0:T(8,128)}, u32[]{:S(2)}) copy-start(f32[256,2048]{1,0:T(8,128)} %get-tuple-element.94) | copy-start | bytes 6291460
Sparse Core Ops, SparseCore 0:
  537.0 141.4 all-gather.2

commit v10 on v9

--- a/solution.py
+++ b/solution.py
@@ -205,7 +205,8 @@
 
 
 class Scatter:
-    def __init__(self, scratch, produce, total):
+    def __init__(self, scratch, produce, total, ready=None):
+        self.ready = ready
         self.line, self.out, self.other = scratch[:3]
         self.sems = scratch[3:]
         self.produce = produce
@@ -256,6 +257,9 @@
         chip, chips = self.chip, self.chips
 
         def cross(target, slot, before, used):
+            if self.ready is not None:
+                self.ready(target)
+
             def one(chunk):
                 @pl.when(used)
                 def _():
@@ -653,23 +657,21 @@
             context[block, head] = (sums * scale).astype(BF16)
             inverse[h : h + 1, block] = jnp.broadcast_to(scale, (QUERY_TILE, HEAD_SIZE)).T[0:1, :]
 
-    loop(tokens // QUERY_TILE, attend)
+    def ready(target):
+        each = 2 * count // QUERY_TILE
+        loop(each, lambda i: attend(target * each + i))
 
     def produce(piece, chunk):
         return dot(context[tile(piece, count), :], out_weight[:, tile(chunk, WIDE)])
 
-    scatter = Scatter(scratch, produce, total)
+    scatter = Scatter(scratch, produce, total, ready)
     scatter.begin()
     scatter.prepare(0)
-    grad_gather.step(1)
 
     def scatter_step(time):
         scatter.step(time)
         scatter.prepare(time + 1)
-
-        @pl.when(time >= 1)
-        def _():
-            grad_gather.step(time + 1)
+        grad_gather.step(time + 1)
 
     loop(chips - 1, scatter_step)
     scatter.finish()
@@ -801,6 +803,66 @@
     )(hidden, grad, gains, token_info, freq, *weights)
 
 
+def slab_size(parts):
+    return 256 if parts <= 8 else 128
+
+
+class Slabs:
+    def __init__(self, sources, buffers, out, target, sems, products):
+        self.sources, self.buffers, self.out, self.target = sources, buffers, out, target
+        self.sems, self.products = sems, products
+        self.size = out.shape[0]
+        self.count = D // self.size
+
+    def copies(self, index):
+        slot = index % 2
+        return [
+            pltpu.make_async_copy(
+                source.at[:, :, tile(index, self.size)], buffer.at[slot], self.sems.at[2 * i + slot]
+            )
+            for i, (source, buffer) in enumerate(zip(self.sources, self.buffers))
+        ]
+
+    def fetch(self, index):
+        for copy in self.copies(index):
+            copy.start()
+
+    def leave(self, index):
+        each = self.target.shape[1] // self.size
+        target = self.target.at[index // each, tile(index % each, self.size), :]
+        return pltpu.make_async_copy(self.out, target, self.sems.at[2 * len(self.sources)])
+
+    def run(self, begin, end):
+        def one(index, carry):
+            for copy in self.copies(index):
+                copy.wait()
+
+            @pl.when(index + 1 < self.count)
+            def _():
+                self.fetch(index + 1)
+
+            @pl.when(index > 0)
+            def _():
+                self.leave(index - 1).wait()
+
+            at = 0
+            for left, right in self.products(index % 2):
+                left = left.reshape(-1, self.size)
+                right = right.reshape(left.shape[0], -1)
+                width = right.shape[1]
+                self.out[:, at : at + width] = tdot(left, right).astype(BF16)
+                at += width
+            self.leave(index).start()
+
+            @pl.when(index == self.count - 1)
+            def _():
+                self.leave(index).wait()
+
+            return carry
+
+        lax.fori_loop(begin, end, one, 0)
+
+
 def rms_back(value, gain, grad):
     inverse = inverse_norm(value)
     scaled = grad * gain
@@ -811,11 +873,12 @@
 
 def turn_kernel(*refs):
     back, pair_weight, down_weight, activation, out_weight = refs[:5]
-    middle, grad, gain_rows, down_grad, pair_grad = refs[5:10]
-    grad_middle, land, gain_sum, down_land, context_grad, hidden, pair_in = refs[10:17]
-    weight, data, total, low, piece_in, own_down, down_sum, sems = refs[17:25]
-    down_refs, down_sems, gather_sems = refs[25:28], refs[28:34], refs[34:40]
-    pair_sems, first_scratch, second_scratch = refs[40:42], refs[42:51], refs[51:]
+    middle, grad, gain_rows, down_grad, normed = refs[5:10]
+    grad_middle, land, gain_sum, down_land, context_grad, hidden, pair_in, pair_grad = refs[10:18]
+    weight, data, total, low, own_down, sems = refs[18:24]
+    slab, slab_out, slab_sems = refs[24:27]
+    down_refs, down_sems, gather_sems = refs[27:30], refs[30:36], refs[36:42]
+    pair_sems, first_scratch, second_scratch = refs[42:44], refs[44:53], refs[53:]
     me, _, _, chips = line_position()
     width = back.shape[2] // 2
     weight_copy = copy_in(pair_weight, weight, sems.at[0])
@@ -838,10 +901,14 @@
         return dot(data[piece, :, :width], weight[down_block(chunk)])
 
     def consume(piece):
-        copy = copy_in(land.at[piece], piece_in, sems.at[4])
+        copy = copy_in(land.at[piece], low, sems.at[4])
         copy.wait()
-        context_grad[piece] = rdot(piece_in[...], out_weight[...]).astype(BF16)
-
+        context_grad[piece] = rdot(low[...], out_weight[...]).astype(BF16)
+
+    def products(slot):
+        return ((slab[slot], data[...]),)
+
+    slabs = Slabs((normed,), (slab,), slab_out, pair_grad, slab_sems, products)
     down = FsdpSum(down_grad, *down_refs, own=own_down)
     pair = FsdpSum(pair_grad, pair_in, *pair_sems, own=own_down)
     down_gather = Gather(down_land, down_sems)
@@ -852,6 +919,7 @@
     hidden_scatter.begin()
     full_barrier()
     down.start()
+    slabs.fetch(0)
     weight_copy.wait()
     data_copy.wait()
     scatter.prepare(0)
@@ -863,14 +931,21 @@
         @pl.when(time == 1)
         def _():
             own_copy.wait()
-            down.collect(down_sum)
+            down.collect(own_down)
+            copy = copy_in(own_down, down_land.at[me], sems.at[3])
+            copy.wait()
+
+        @pl.when(time >= 1)
+        def _():
+            down_gather.step(time - 1)
+
+        @pl.when(time < 3)
+        def _():
+            slabs.run(time * slabs.count // 3, (time + 1) * slabs.count // 3)
+
+        @pl.when(time == 2)
+        def _():
             pair.start()
-            copy = copy_in(down_sum, down_land.at[me], sems.at[3])
-            copy.wait()
-
-        @pl.when(time >= 1)
-        def _():
-            down_gather.step(time - 1)
 
     loop(chips - 1, step)
     scatter.finish()
@@ -918,7 +993,7 @@
     row_blocks(middle.shape[0], add)
 
 
-def turn(back, pair_weight, down_weight, activation, out_weight, middle, grad, gain_rows, down_grad, pair_grad):
+def turn(back, pair_weight, down_weight, activation, out_weight, middle, grad, gain_rows, down_grad, normed):
     parts, count, feed_width = activation.shape
     shards, rows, _ = down_grad.shape
     width = out_weight.shape[0]
@@ -932,18 +1007,20 @@
             jax.ShapeDtypeStruct((parts, count, width), BF16),
             jax.ShapeDtypeStruct((count, D), BF16),
             jax.ShapeDtypeStruct((shards - 1, rows, 2 * feed_width), BF16),
+            jax.ShapeDtypeStruct((shards, rows, 2 * feed_width), BF16),
         ),
         in_specs=[HBM] * 4 + [WHOLE] * 4 + [HBM] * 2,
-        out_specs=(WHOLE, HBM, WHOLE, HBM, WHOLE, WHOLE, HBM),
+        out_specs=(WHOLE, HBM, WHOLE, HBM, WHOLE, WHOLE, HBM, HBM),
         scratch_shapes=[
             VMEM((D, 2 * feed_width), BF16),
             VMEM((parts, count, 2 * feed_width), BF16),
             VMEM((count, D), F32),
             VMEM((count, D), BF16),
-            VMEM((count, D), BF16),
-            VMEM((rows, feed_width), BF16),
             VMEM((rows, feed_width), BF16),
             pltpu.SemaphoreType.DMA((5 + CHUNKS,)),
+            VMEM((2, parts, count, slab_size(parts)), BF16),
+            VMEM((slab_size(parts), 2 * feed_width), BF16),
+            pltpu.SemaphoreType.DMA((3,)),
         ]
         + fsdp_scratch(shards, rows, feed_width)
         + gather_scratch(parts // 2)
@@ -964,15 +1041,17 @@
         grad,
         gain_rows,
         down_grad,
-        pair_grad,
+        normed,
     )
 
 
 def last_kernel(*refs):
-    back, weights, x, grad_middle, gain_rows, gain_two, gain_heads, head_grad = refs[:8]
-    hidden, gain_out, land = refs[8:11]
-    weight, weight_sem, total, gain_one, pack, pack_in, shard_sum, shard_in = refs[11:19]
-    small, head_refs, gather_sems, scratch = refs[19:23], refs[23:26], refs[26:32], refs[32:]
+    back, weights, x, grad_middle, gain_rows, gain_two, gain_heads, context, normed, low = refs[:10]
+    hidden, gain_out, head_grad, query_out, key_out, value_out, out_out = refs[10:17]
+    weight, weight_sem, total, gain_one, pack, pack_in, shard_sum, shard_in, land = refs[17:26]
+    slabs_in, slab_out, slab_sems, own_head = refs[26:28], refs[28], refs[29], refs[30]
+    stages, stage_sems, refs = refs[31:35], refs[35], refs[36:]
+    small, head_refs, gather_sems, scratch = refs[:4], refs[4:7], refs[7:13], refs[13:]
     me, _, _, chips = line_position()
     shard = lax.axis_index("fsdp")
     shards, ahead, _ = peers_of("fsdp")
@@ -982,17 +1061,58 @@
     def produce(piece, chunk):
         return rdot(back[piece], weight[pl.ds(pl.multiple_of(chunk * WIDE, WIDE), WIDE), :])
 
-    heads = FsdpSum(head_grad, *head_refs)
+    def products(slot):
+        return (slabs_in[0][slot], back[...]), (slabs_in[1][slot], context[...])
+
+    width = context.shape[2]
+
+    def stage_copies(piece):
+        targets = (
+            query_out.at[:, tile(piece, width)],
+            key_out.at[:, tile(piece, HEAD_SIZE)],
+            value_out.at[:, tile(piece, HEAD_SIZE)],
+            out_out.at[tile(piece, width), :],
+        )
+        return [
+            pltpu.make_async_copy(stage, target, stage_sems.at[i])
+            for i, (stage, target) in enumerate(zip(stages, targets))
+        ]
+
+    def consume(piece):
+        @pl.when(piece != me)
+        def _():
+            for copy in stage_copies(piece):
+                copy.wait()
+
+        second = width + HEAD_SIZE
+        third = second + HEAD_SIZE
+        stages[0][...] = land[piece, :, :width].astype(F32)
+        stages[1][...] = land[piece, :, width:second].astype(F32)
+        stages[2][...] = land[piece, :, second:third].astype(F32)
+        stages[3][...] = land[piece, :, third:].astype(F32).T
+        for copy in stage_copies(piece):
+            copy.start()
+
+    slabs = Slabs((normed, low), slabs_in, slab_out, head_grad, slab_sems, products)
+    heads = FsdpSum(head_grad, *head_refs, own=own_head)
     scatter = Scatter(scratch, produce, total)
-    gather = Gather(land, gather_sems)
+    gather = Gather(land, gather_sems, consume)
     scatter.begin()
+    slabs.fetch(0)
     full_barrier()
     copy.wait()
     scatter.prepare(0)
-    heads.start()
 
     def step(time):
         scatter.step(time)
+        scatter.prepare(time + 1)
+
+        @pl.when(time == 0)
+        def _():
+            slabs.run(0, slabs.count)
+            heads.start()
+            own = copy_in(head_grad.at[shard], own_head, weight_sem)
+            own.wait()
 
         @pl.when(time == 1)
         def _():
@@ -1001,8 +1121,6 @@
         @pl.when(time >= 1)
         def _():
             gather.step(time - 1)
-
-        scatter.prepare(time + 1)
 
     loop(chips - 1, step)
     scatter.finish()
@@ -1050,23 +1168,31 @@
     loop(parts, add_sum)
     gather.step(chips - 1)
     gather.finish()
+    for stage in stage_copies(0):
+        stage.wait()
     heads.finish()
     loop(shards, lambda i: pack_copy(i).wait_send())
     loop(parts, lambda i: sum_copy(i).wait_send())
 
 
-def last(back, weights, hidden, grad_middle, gain_rows, gain_two, gain_heads, head_grad):
+def last(back, weights, hidden, grad_middle, gain_rows, gain_two, gain_heads, context, normed, low, shards):
     parts, count, width = back.shape
-    shards, rows, head_width = head_grad.shape
+    rows = D // shards
+    query_width = context.shape[2]
+    head_width = width + query_width
     return pl.pallas_call(
         last_kernel,
         out_shape=(
             jax.ShapeDtypeStruct((count, D), F32),
             jax.ShapeDtypeStruct((16, 128), F32),
-            jax.ShapeDtypeStruct((parts, rows, head_width), BF16),
+            jax.ShapeDtypeStruct((shards, rows, head_width), BF16),
+            jax.ShapeDtypeStruct((rows, parts * query_width), F32),
+            jax.ShapeDtypeStruct((rows, parts * HEAD_SIZE), F32),
+            jax.ShapeDtypeStruct((rows, parts * HEAD_SIZE), F32),
+            jax.ShapeDtypeStruct((parts * query_width, rows), F32),
         ),
-        in_specs=[WHOLE, HBM] + [WHOLE] * 6,
-        out_specs=(WHOLE,) * 3,
+        in_specs=[WHOLE, HBM] + [WHOLE] * 6 + [HBM] * 2,
+        out_specs=(WHOLE,) * 2 + (HBM,) * 5,
         scratch_shapes=[
             VMEM((D, width), BF16),
             pltpu.SemaphoreType.DMA,
@@ -1076,6 +1202,17 @@
             VMEM((shards, 16, 128), F32),
             VMEM((16, 128), F32),
             VMEM((parts, 16, 128), F32),
+            VMEM((parts, rows, head_width), BF16),
+            VMEM((2, parts, count, slab_size(parts)), BF16),
+            VMEM((2, parts, count, slab_size(parts)), BF16),
+            VMEM((slab_size(parts), head_width), BF16),
+            pltpu.SemaphoreType.DMA((5,)),
+            VMEM((rows, head_width), BF16),
+            VMEM((rows, query_width), F32),
+            VMEM((rows, HEAD_SIZE), F32),
+            VMEM((rows, HEAD_SIZE), F32),
+            VMEM((query_width, rows), F32),
+            pltpu.SemaphoreType.DMA((4,)),
         ]
         + [pltpu.SemaphoreType.DMA((shards,))] * 2
         + [pltpu.SemaphoreType.DMA((parts,))] * 2
@@ -1085,7 +1222,7 @@
         compiler_params=params(5, 60),
         cost_estimate=cost(90),
         name="last",
-    )(back, weights, hidden, grad_middle, gain_rows, gain_two, gain_heads, head_grad)
+    )(back, weights, hidden, grad_middle, gain_rows, gain_two, gain_heads, context, normed, low)
 
 
 def attention_back_kernel(heads, *refs):
@@ -1201,31 +1338,6 @@
         out_specs=pl.BlockSpec((width, rows), lambda i: (i, 0)),
         compiler_params=pltpu.CompilerParams(vmem_limit_bytes=60 * 1024 * 1024),
         name="spread_turned",
-    )(stacked)
-
-
-def spread_heads_kernel(width, source, query, key, value, out):
-    second = width + HEAD_SIZE
-    third = second + HEAD_SIZE
-    query[...] = source[0, :, :width].astype(F32)
-    key[...] = source[0, :, width:second].astype(F32)
-    value[...] = source[0, :, second:third].astype(F32)
-    out[...] = source[0, :, third:].astype(F32).T
-
-
-def spread_heads(stacked, width):
-    parts, rows, total = stacked.shape
-    widths = (width, HEAD_SIZE, HEAD_SIZE)
-    return pl.pallas_call(
-        functools.partial(spread_heads_kernel, width),
-        out_shape=tuple(jax.ShapeDtypeStruct((rows, parts * w), F32) for w in widths)
-        + (jax.ShapeDtypeStruct((parts * width, rows), F32),),
-        grid=(parts,),
-        in_specs=[pl.BlockSpec((1, rows, total), lambda i: (i, 0, 0))],
-        out_specs=tuple(pl.BlockSpec((rows, w), lambda i: (0, i)) for w in widths)
-        + (pl.BlockSpec((width, rows), lambda i: (i, 0)),),
-        compiler_params=pltpu.CompilerParams(vmem_limit_bytes=60 * 1024 * 1024),
-        name="spread_heads",
     )(stacked)
 
 
@@ -1310,13 +1422,9 @@
     proj = proj.reshape(tokens, width + 2 * HEAD_SIZE)
 
     flat_grad = grad_all.reshape(tokens, D)
-    flat_back = back.reshape(tokens, 2 * feed_width)
     flat_activation = activation.reshape(tokens, feed_width)
-    feed_grad = by_row(tdot(normed_two_all.reshape(tokens, D), flat_back).astype(BF16))
     down_grad = by_row(tdot(flat_grad, flat_activation).astype(BF16))
-    back, feed_grad, down_grad = lax.optimization_barrier((back, feed_grad, down_grad))
-    feed_grad = feed_grad.reshape(shards, rows, 2 * feed_width)
-    grad_middle, low_all, gain_two, down_parts, context_grad, hidden_out, pair_in = turn(
+    grad_middle, low_all, gain_two, down_parts, context_grad, hidden_out, pair_in, pair_grad = turn(
         back,
         pair_weight,
         down_weight,
@@ -1326,9 +1434,9 @@
         grad,
         gain_rows,
         down_grad.reshape(shards, rows, feed_width),
-        feed_grad,
+        normed_two_all,
     )
-    own_pair = lax.dynamic_index_in_dim(feed_grad, shard, keepdims=False)
+    own_pair = lax.dynamic_index_in_dim(pair_grad, shard, keepdims=False)
     feed_shard = (own_pair.astype(F32) + jnp.sum(pair_in.astype(F32), axis=0)).astype(BF16)
     context_grad, feed_shard, down_parts = lax.optimization_barrier(
         (context_grad, feed_shard, down_parts)
@@ -1350,16 +1458,9 @@
         id_column,
         id_row,
     )
-    head_grad = jnp.concatenate(
-        [
-            by_row(tdot(normed_all.reshape(tokens, D), grad_qkv).astype(BF16)),
-            by_row(tdot(low_all.reshape(tokens, D), context).astype(BF16)),
-        ],
-        axis=1,
-    )
     grad_down = spread_turned(down_parts)
     grad_qkv, grad_down = lax.optimization_barrier((grad_qkv, grad_down))
-    grad_hidden, gain_sums, head_parts = last(
+    grad_hidden, gain_sums, _, grad_query, grad_key, grad_value, grad_out_weight = last(
         grad_qkv.reshape(parts, count, -1),
         heads_weight,
         hidden,
@@ -1367,12 +1468,14 @@
         gain_rows,
         gain_two,
         gain_heads,
-        head_grad.reshape(shards, rows, -1),
+        context.reshape(parts, count, width),
+        normed_all,
+        low_all,
+        shards,
     )
 
     gain_sums = gain_sums.reshape(-1)
     grad_gate, grad_up = spread_pair(feed_parts)
-    grad_query, grad_key, grad_value, grad_out_weight = spread_heads(head_parts, width)
     if sharers > 1:
         grad_key, grad_value = (
             part.reshape(rows, KEY_VALUE_HEADS, sharers, HEAD_SIZE).sum(axis=2).reshape(rows, -1)

time: 795 us -> 778 us (0.979)
  matrix products: 41.7 us -> 11.4 us
  local copies, waits for them, and re-layouts: 12.6 us -> 25.8 us
    dot_general x4 -> x1, matrix products: 41.7 us -> 11.4 us  [tdot(): lax.dot_general(left, right, (((0,), (0,)), ((), ())), preferred_element_...]
    pallas_call x1, Pallas kernels: 154 us -> 166 us  [last(): pl.pallas_call(last_kernel, out_shape=(jax.ShapeDtypeStruct((count, D), F...]
    unnamed x30 -> x34, local copies, waits for them, and re-layouts: 4.59 us -> 16.3 us
    pallas_call x1 -> x0, Pallas kernels: 8.85 us -> none  [spread_heads(): pl.pallas_call(functools.partial(spread_heads_kernel, width), out_shape=t...]
  transfers between devices with their start and end apart: 1 -> 1, of which waited for: 0 -> 0; matrix products, arithmetic and copies ran while one was open for 3% -> 1% of each run, Pallas kernels for 26% -> 28%
where the time goes in v10:
time: 778 us; the launch traced here: 776 us
  Pallas kernels  717 us (92%)
  local copies, waits for them, and re-layouts  25.8 us (3%)
  between operations  14.1 us (2%)
  matrix products  11.4 us (1%)
  other arithmetic  7.8 us (1%)
    pallas_call x1, Pallas kernels, forward(): pl.pallas_call(functools.partial(forward_kernel, heads), out_shape=(shape...  275 us
    pallas_call x1, Pallas kernels, turn(): pl.pallas_call(turn_kernel, out_shape=(jax.ShapeDtypeStruct((count, D), F...  214 us
    pallas_call x1, Pallas kernels, last(): pl.pallas_call(last_kernel, out_shape=(jax.ShapeDtypeStruct((count, D), F...  166 us
    pallas_call x1, Pallas kernels, attention_back(): pl.pallas_call(functools.partial(attention_back_kernel, heads), out_shape...  37.4 us
    unnamed x34, local copies, waits for them, and re-layouts  16.3 us
  transfers between devices with their start and end apart: 1, of which 0 were waited for; matrix products, arithmetic and copies ran while one was open for 1% of the time, Pallas kernels for 28%

profile of v10, /device:TPU:0, one launch (start us, length us, event | category | flops | bytes accessed | tf_op | source)
XLA Modules:
  0.0 775.8 jit_solution(3603373023891281890)
XLA Ops:
  7.2 0.0 all-gather.3.cloned.1.call-start
  7.2 2.8 concatenate.6
  10.0 0.6 bitcast_convert_fusion.1.refs_2_
  10.6 0.1 pad_maximum_fusion
  10.7 0.7 pad_add_fusion
  11.4 0.6 pad.10.refs_3_
  12.0 0.6 broadcast_in_dim.9.refs_4_
  12.6 274.6 %forward.1 = (bf16[8,256,2048]{2,1,0:T(8,128)(2,1)}, bf16[8,256,2048]{2,1,0:T(8,128)(2,1)}, bf16[8,256,2048]{2,1,0:T(8,128)(2,1)}, bf16[8,256,768]{2,1,0:T(8,128...) custom-call(bf16[256,2048]{1,0:T(8,128)(2,1)} %bitcast.37, ...), custom_call_target="tpu_custom_call" | custom-call | flops 321999994880 | bytes 1024 | tf_op jit(solution)/shard_map/forward/pallas_call | solution.py:755
  287.2 11.4 %bitcast_convert_fusion = bf16[2048,768]{1,0:T(8,128)(2,1)} fusion(bf16[8,256,2048]{2,1,0:T(8,128)(2,1)} %get-tuple-element.63, bf16[8,256,768]{2,1,0:T(8,128)(2,1)} %get-tuple-element.59.refs_3_), kind=kOutput, calls=%fused_computation.1 | convolution fusion | flops 6444023808 | bytes 14680064 | tf_op jit(solution)/shard_map/dot_general | solution.py:33
  298.6 214.2 %turn.1 = (f32[256,2048]{1,0:T(8,128)}, bf16[8,256,2048]{2,1,0:T(8,128)(2,1)}, f32[8,2048]{1,0:T(8,128)}, bf16[8,512,768]{2,1,0:T(8,128)(2,1)}, bf16[8,256,256]{...) custom-call(bf16[8,256,1536]{2,1,0:T(8,128)(2,1)} %get-tuple-element.56, ...), custom_call_target="tpu_custom_call" | custom-call | flops 212749991936 | bytes 1024 | tf_op jit(solution)/shard_map/turn/pallas_call | solution.py:1000
  512.8 3.4 convert_reduce_fusion
  516.2 3.0 fusion
  519.2 0.0 all-gather.3.cloned.1.call-update
  519.3 0.7 slice.18.refs_9_
  519.9 0.0 copy-start
  519.9 0.0 copy-start.1
  519.9 0.0 copy-start.2
  519.9 0.0 copy-start.6
  519.9 10.1 %spread_turned.1 = f32[6144,512]{1,0:T(8,128)} custom-call(bf16[8,512,768]{2,1,0:T(8,128)(2,1)} %get-tuple-element.81.source), custom_call_target="tpu_custom_call" | custom-call | tf_op jit(solution)/shard_map/spread_turned/pallas_call | solution.py:1333
  530.0 0.8 slice.19
  530.9 1.3 copy.30.refs_10_
  532.2 0.0 copy-done
  532.2 0.0 copy-done.1
  532.2 0.0 copy-done.2
  532.2 0.0 copy-done.6
  532.2 0.0 copy-start.3
  532.3 1.2 copy-done.3
  533.5 0.0 copy-start.4
  533.5 1.1 copy-done.4
  534.6 0.0 copy-start.5
  534.6 1.0 copy-done.5
  535.6 37.4 %attention_back.1 = (bf16[2048,512]{1,0:T(8,128)(2,1)}, f32[8,128]{1,0:T(8,128)S(1)}) custom-call(bf16[2048,256]{1,0:T(8,128)(2,1)S(1)} %copy-done.3, bf16[2048,128]{1,0:T(8,128)(2,1)S(1)} %copy-done.4, bf16[2048,128]{1,0:T(8,128)(2,1)S(1)} %copy-done.5, bf16[2048,256]{1,0:T(8,128)(2,1)S(1)} %bitcast.30, f32[8,2048]{1,0:T(8,128)S(1)} %copy-done.6, ...), custom_call_target="tpu_custom_call" | custom-call | flops 43699998720 | bytes 1024 | tf_op jit(solution)/shard_map/attention_back/pallas_call | solution.py:1288
  573.0 0.0 copy-start.7
  573.0 0.6 copy-done.7
  573.6 166.0 %last.1 = (f32[256,2048]{1,0:T(8,128)}, f32[16,128]{1,0:T(8,128)}, bf16[4,512,768]{2,1,0:T(8,128)(2,1)}, f32[512,2048]{1,0:T(8,128)}, f32[512,1024]{1,0:T(8,128)...) custom-call(bf16[8,256,512]{2,1,0:T(8,128)(2,1)} %bitcast.41, bf16[2048,512]{1,0:T(8,128)(2,1)} %get-tuple-element.83.refs_1_, ...), custom_call_target="tpu_custom_call" | custom-call | flops 103499997184 | bytes 1024 | tf_op jit(solution)/shard_map/last/pallas_call | solution.py:1183
  739.6 1.3 fusion.1
  740.9 1.3 slice_bitcast_fusion
  742.3 0.0 all-gather.3.cloned.1.call-done
  742.3 0.0 copy-start.13
  742.3 0.0 copy-start.12
  742.3 14.4 %spread_pair.1 = (f32[512,6144]{1,0:T(8,128)}, f32[512,6144]{1,0:T(8,128)}) custom-call(bf16[8,512,1536]{2,1,0:T(8,128)(2,1)} %bitcast.31), custom_call_target="tpu_custom_call" | custom-call | tf_op jit(solution)/shard_map/spread_pair/pallas_call | solution.py:1316
  756.7 0.0 copy-start.9
  756.7 0.0 copy-done.13
  756.7 1.0 copy.38
  757.7 0.0 copy-done.12
  757.7 1.3 copy.39
  759.0 1.0 copy-done.9
  760.0 0.0 copy-start.11
  760.0 0.0 copy-start.10
  760.0 2.1 copy.40
  762.1 1.0 copy-done.11
  763.1 0.0 copy-start.8
  763.1 1.3 copy.41
  764.4 0.0 copy-done.10
  764.4 1.3 copy.42
  765.7 1.2 copy-done.8
  767.0 2.0 copy.43
  (1 shorter events, 0.0 us)
Async XLA Ops:
  7.2 735.1 %all-gather.3.cloned.1.call-start = ((), (), s32[]{:S(2)}) async-start(), calls=%async_computation | async-start | bytes 14155776 | tf_op jit(solution)/shard_map/all_gather | solution.py:1378
  519.9 12.3 %copy-start = (bf16[2048,256]{1,0:T(8,128)(2,1)S(1)}, bf16[2048,256]{1,0:T(8,128)(2,1)}, u32[]{:S(2)}) copy-start(bf16[2048,256]{1,0:T(8,128)(2,1)} %get-tuple-element.75.refs_5_) | copy-start | bytes 3145732
  519.9 12.3 %copy-start.1 = (bf16[8,256,256]{2,1,0:T(8,128)(2,1)S(1)}, bf16[8,256,256]{2,1,0:T(8,128)(2,1)}, u32[]{:S(2)}) copy-start(bf16[8,256,256]{2,1,0:T(8,128)(2,1)} %get-tuple-element.73) | copy-start | bytes 3145732
  519.9 12.3 %copy-start.2 = (f32[2048,128]{1,0:T(8,128)S(1)}, f32[2048,128]{1,0:T(8,128)}, u32[]{:S(2)}) copy-start(f32[2048,128]{1,0:T(8,128)} %get-tuple-element.77.refs_7_) | copy-start | bytes 3145732
  519.9 12.3 %copy-start.6 = (f32[8,2048]{1,0:T(8,128)S(1)}, f32[8,2048]{1,0:T(8,128)}, u32[]{:S(2)}) copy-start(f32[8,2048]{1,0:T(8,128)} %get-tuple-element.74.refs_4_) | copy-start | bytes 196612
  532.2 1.2 copy-start.3
  533.5 1.1 copy-start.4
  534.6 1.0 copy-start.5
  573.0 0.6 copy-start.7
  742.3 14.4 %copy-start.13 = (bf16[256,2048]{1,0:T(8,128)(2,1)S(1)}, bf16[256,2048]{1,0:T(8,128)(2,1)}, u32[]{:S(2)}) copy-start(bf16[256,2048]{1,0:T(8,128)(2,1)} %get-tuple-element.65) | copy-start | bytes 3145732
  742.3 15.4 %copy-start.12 = (f32[256,2048]{1,0:T(8,128)S(1)}, f32[256,2048]{1,0:T(8,128)}, u32[]{:S(2)}) copy-start(f32[256,2048]{1,0:T(8,128)} %get-tuple-element.89) | copy-start | bytes 6291460
  756.7 3.3 copy-start.9
  760.0 3.1 copy-start.11
  760.0 4.4 copy-start.10
  763.1 3.9 copy-start.8
Sparse Core Ops, SparseCore 0:
  519.4 155.5 all-gather.2

commit v11 on v10

--- a/solution.py
+++ b/solution.py
@@ -107,22 +107,26 @@
 
 
 class Gather:
-    def __init__(self, land, sems, consume=None):
+    def __init__(self, land, sems, consume=None, part=None):
+        self.part = part
         self.land = land
         self.sems = sems
         self.consume = consume
         self.me, self.chip, self.core, self.chips = line_position()
 
+    def place(self, piece):
+        return self.land.at[piece] if self.part is None else self.land.at[piece, self.part]
+
     def right(self, step, source):
-        ref = self.land.at[2 * source + self.core]
+        ref = self.place(2 * source + self.core)
         return send(ref, ref, self.sems[0].at[step], self.sems[1].at[step], "ctx", self.me + 2)
 
     def left(self, step, source):
-        ref = self.land.at[2 * source + self.core]
+        ref = self.place(2 * source + self.core)
         return send(ref, ref, self.sems[2].at[step], self.sems[3].at[step], "ctx", self.me - 2)
 
     def across(self, source, core):
-        ref = self.land.at[2 * source + core]
+        ref = self.place(2 * source + core)
         other = self.me + 1 - 2 * self.core
         return send(ref, ref, self.sems[4].at[source], self.sems[5].at[source], "ctx", other)
 
@@ -395,8 +399,8 @@
 
 
 class FsdpSum:
-    def __init__(self, grad, arrived, send_sems, recv_sems, own=None):
-        self.grad, self.arrived = grad, arrived
+    def __init__(self, grad, arrived, send_sems, recv_sems, own=None, part=slice(None)):
+        self.grad, self.arrived, self.part = grad, arrived, part
         self.own = grad.at[lax.axis_index("fsdp")] if own is None else own
         self.sems = send_sems, recv_sems
         self.peers, self.ahead, _ = peers_of("fsdp")
@@ -404,7 +408,7 @@
     def copy(self, i):
         target = self.ahead(i)
         return send(
-            self.grad.at[target], self.arrived.at[i], self.sems[0].at[i], self.sems[1].at[i], "fsdp", target
+            self.grad.at[target, self.part], self.arrived.at[i], self.sems[0].at[i], self.sems[1].at[i], "fsdp", target
         )
 
     def start(self):
@@ -874,11 +878,11 @@
 def turn_kernel(*refs):
     back, pair_weight, down_weight, activation, out_weight = refs[:5]
     middle, grad, gain_rows, down_grad, normed = refs[5:10]
-    grad_middle, land, gain_sum, down_land, context_grad, hidden, pair_in, pair_grad = refs[10:18]
-    weight, data, total, low, own_down, sems = refs[18:24]
-    slab, slab_out, slab_sems = refs[24:27]
-    down_refs, down_sems, gather_sems = refs[27:30], refs[30:36], refs[36:42]
-    pair_sems, first_scratch, second_scratch = refs[42:44], refs[44:53], refs[53:]
+    grad_middle, land, gain_sum, down_land, context_grad, hidden, pair_in, pair_grad, pair_sum = refs[10:19]
+    weight, data, total, low, own_down, sems = refs[19:25]
+    slab, slab_out, slab_sems, sum_sems = refs[25:29]
+    down_refs, down_sems = (refs[29:32], refs[32:35]), (refs[35:41], refs[41:47])
+    gather_sems, pair_sems, first_scratch, second_scratch = refs[47:53], refs[53:55], refs[55:64], refs[64:]
     me, _, _, chips = line_position()
     width = back.shape[2] // 2
     weight_copy = copy_in(pair_weight, weight, sems.at[0])
@@ -909,16 +913,28 @@
         return ((slab[slot], data[...]),)
 
     slabs = Slabs((normed,), (slab,), slab_out, pair_grad, slab_sems, products)
-    down = FsdpSum(down_grad, *down_refs, own=own_down)
+    half = own_down.shape[0] // 2
+    halves = [pl.ds(h * half, half) for h in range(2)]
+    downs = [
+        FsdpSum(down_grad, *down_refs[h], own=own_down.at[halves[h]], part=halves[h]) for h in range(2)
+    ]
+    down_gathers = [Gather(down_land, down_sems[h], part=halves[h]) for h in range(2)]
+
+    def down_ready(h):
+        downs[h].collect(own_down.at[halves[h]])
+        copy = copy_in(own_down.at[halves[h]], down_land.at[me, halves[h]], sems.at[3])
+        copy.wait()
+        down_gathers[h].step(0)
+
     pair = FsdpSum(pair_grad, pair_in, *pair_sems, own=own_down)
-    down_gather = Gather(down_land, down_sems)
     gather = Gather(land, gather_sems, consume)
     scatter = Scatter(first_scratch, produce, total)
     hidden_scatter = Scatter(second_scratch, produce_hidden, total)
     scatter.begin()
     hidden_scatter.begin()
     full_barrier()
-    down.start()
+    for down in downs:
+        down.start()
     slabs.fetch(0)
     weight_copy.wait()
     data_copy.wait()
@@ -928,16 +944,22 @@
         scatter.step(time)
         scatter.prepare(time + 1)
 
+        @pl.when(time == 0)
+        def _():
+            own_copy.wait()
+            down_ready(0)
+
+        @pl.when(time >= 1)
+        def _():
+            down_gathers[0].step(time)
+
         @pl.when(time == 1)
         def _():
-            own_copy.wait()
-            down.collect(own_down)
-            copy = copy_in(own_down, down_land.at[me], sems.at[3])
-            copy.wait()
-
-        @pl.when(time >= 1)
-        def _():
-            down_gather.step(time - 1)
+            down_ready(1)
+
+        @pl.when(time >= 2)
+        def _():
+            down_gathers[1].step(time - 1)
 
         @pl.when(time < 3)
         def _():
@@ -949,6 +971,8 @@
 
     loop(chips - 1, step)
     scatter.finish()
+    down_gathers[0].step(chips - 1)
+    down_gathers[1].step(chips - 2)
     for chunk in range(CHUNKS):
         down_copy(chunk).start()
     act_copy = copy_in(activation, data.at[:, :, pl.ds(0, width)], sems.at[1])
@@ -970,21 +994,86 @@
     act_copy.wait()
     hidden_scatter.prepare(0)
 
+    def add_pairs():
+        pair.arrive()
+        shard = lax.axis_index("fsdp")
+        count, size = slab.shape[2], slab.shape[3]
+        per = own_down.shape[0] // count
+        tiles = 2 * width // size
+
+        def arrivals(index):
+            slot = index % 2
+            copies = []
+            for i in range(pair.peers + 1):
+                source = pair_grad.at[shard] if i == 0 else pair_in.at[i - 1]
+                for j in range(per):
+                    at = i * per + j
+                    block = source.at[pl.ds(j * count, count), tile(index, size)]
+                    copies.append(
+                        pltpu.make_async_copy(block, slab.at[slot, at], sum_sems.at[slot, at])
+                    )
+            return copies
+
+        def leave(index):
+            slot = index % 2
+            return [
+                pltpu.make_async_copy(
+                    slab.at[slot, j],
+                    pair_sum.at[pl.ds(j * count, count), tile(index, size)],
+                    sum_sems.at[slot, j],
+                )
+                for j in range(per)
+            ]
+
+        for copy in arrivals(0):
+            copy.start()
+
+        def one(index):
+            @pl.when(index > 0)
+            def _():
+                for copy in leave(index - 1):
+                    copy.wait()
+
+            @pl.when(index + 1 < tiles)
+            def _():
+                for copy in arrivals(index + 1):
+                    copy.start()
+
+            for copy in arrivals(index):
+                copy.wait()
+            slot = index % 2
+            for j in range(per):
+                value = slab[slot, j].astype(F32)
+                for i in range(1, pair.peers + 1):
+                    value = value + slab[slot, i * per + j].astype(F32)
+                slab[slot, j] = value.astype(BF16)
+            for copy in leave(index):
+                copy.start()
+
+        loop(tiles, one)
+        for copy in leave(tiles - 1):
+            copy.wait()
+
     def turn_step(time):
         hidden_scatter.step(time)
         hidden_scatter.prepare(time + 1)
+
+        @pl.when(time == chips - 2)
+        def _():
+            add_pairs()
+
         gather.step(time + 1)
 
-        @pl.when(time < 2)
-        def _():
-            down_gather.step(chips - 2 + time)
+        @pl.when(time == 1)
+        def _():
+            down_gathers[1].step(chips - 1)
 
     loop(chips - 1, turn_step)
     hidden_scatter.finish()
     gather.finish()
-    down_gather.finish()
-    down.finish()
-    pair.arrive()
+    for h in range(2):
+        down_gathers[h].finish()
+        downs[h].finish()
     pair.finish()
 
     def add(block):
@@ -1008,9 +1097,10 @@
             jax.ShapeDtypeStruct((count, D), BF16),
             jax.ShapeDtypeStruct((shards - 1, rows, 2 * feed_width), BF16),
             jax.ShapeDtypeStruct((shards, rows, 2 * feed_width), BF16),
+            jax.ShapeDtypeStruct((rows, 2 * feed_width), BF16),
         ),
         in_specs=[HBM] * 4 + [WHOLE] * 4 + [HBM] * 2,
-        out_specs=(WHOLE, HBM, WHOLE, HBM, WHOLE, WHOLE, HBM, HBM),
+        out_specs=(WHOLE, HBM, WHOLE, HBM, WHOLE, WHOLE, HBM, HBM, HBM),
         scratch_shapes=[
             VMEM((D, 2 * feed_width), BF16),
             VMEM((parts, count, 2 * feed_width), BF16),
@@ -1021,8 +1111,11 @@
             VMEM((2, parts, count, slab_size(parts)), BF16),
             VMEM((slab_size(parts), 2 * feed_width), BF16),
             pltpu.SemaphoreType.DMA((3,)),
+            pltpu.SemaphoreType.DMA((2, parts)),
         ]
-        + fsdp_scratch(shards, rows, feed_width)
+        + fsdp_scratch(shards, rows // 2, feed_width)
+        + fsdp_scratch(shards, rows // 2, feed_width)
+        + gather_scratch(parts // 2)
         + gather_scratch(parts // 2)
         + gather_scratch(parts // 2)
         + [pltpu.SemaphoreType.DMA((shards,))] * 2
@@ -1047,10 +1140,9 @@
 
 def last_kernel(*refs):
     back, weights, x, grad_middle, gain_rows, gain_two, gain_heads, context, normed, low = refs[:10]
-    hidden, gain_out, head_grad, query_out, key_out, value_out, out_out = refs[10:17]
-    weight, weight_sem, total, gain_one, pack, pack_in, shard_sum, shard_in, land = refs[17:26]
-    slabs_in, slab_out, slab_sems, own_head = refs[26:28], refs[28], refs[29], refs[30]
-    stages, stage_sems, refs = refs[31:35], refs[35], refs[36:]
+    hidden, gain_out, head_grad, land = refs[10:14]
+    weight, weight_sem, total, gain_one, pack, pack_in, shard_sum, shard_in = refs[14:22]
+    slabs_in, slab_out, slab_sems, own_head, refs = refs[22:24], refs[24], refs[25], refs[26], refs[27:]
     small, head_refs, gather_sems, scratch = refs[:4], refs[4:7], refs[7:13], refs[13:]
     me, _, _, chips = line_position()
     shard = lax.axis_index("fsdp")
@@ -1064,55 +1156,23 @@
     def products(slot):
         return (slabs_in[0][slot], back[...]), (slabs_in[1][slot], context[...])
 
-    width = context.shape[2]
-
-    def stage_copies(piece):
-        targets = (
-            query_out.at[:, tile(piece, width)],
-            key_out.at[:, tile(piece, HEAD_SIZE)],
-            value_out.at[:, tile(piece, HEAD_SIZE)],
-            out_out.at[tile(piece, width), :],
-        )
-        return [
-            pltpu.make_async_copy(stage, target, stage_sems.at[i])
-            for i, (stage, target) in enumerate(zip(stages, targets))
-        ]
-
-    def consume(piece):
-        @pl.when(piece != me)
-        def _():
-            for copy in stage_copies(piece):
-                copy.wait()
-
-        second = width + HEAD_SIZE
-        third = second + HEAD_SIZE
-        stages[0][...] = land[piece, :, :width].astype(F32)
-        stages[1][...] = land[piece, :, width:second].astype(F32)
-        stages[2][...] = land[piece, :, second:third].astype(F32)
-        stages[3][...] = land[piece, :, third:].astype(F32).T
-        for copy in stage_copies(piece):
-            copy.start()
-
     slabs = Slabs((normed, low), slabs_in, slab_out, head_grad, slab_sems, products)
     heads = FsdpSum(head_grad, *head_refs, own=own_head)
     scatter = Scatter(scratch, produce, total)
-    gather = Gather(land, gather_sems, consume)
+    gather = Gather(land, gather_sems)
     scatter.begin()
     slabs.fetch(0)
     full_barrier()
     copy.wait()
+    slabs.run(0, slabs.count)
+    heads.start()
+    own = copy_in(head_grad.at[shard], own_head, weight_sem)
+    own.wait()
     scatter.prepare(0)
 
     def step(time):
         scatter.step(time)
         scatter.prepare(time + 1)
-
-        @pl.when(time == 0)
-        def _():
-            slabs.run(0, slabs.count)
-            heads.start()
-            own = copy_in(head_grad.at[shard], own_head, weight_sem)
-            own.wait()
 
         @pl.when(time == 1)
         def _():
@@ -1168,8 +1228,6 @@
     loop(parts, add_sum)
     gather.step(chips - 1)
     gather.finish()
-    for stage in stage_copies(0):
-        stage.wait()
     heads.finish()
     loop(shards, lambda i: pack_copy(i).wait_send())
     loop(parts, lambda i: sum_copy(i).wait_send())
@@ -1186,13 +1244,10 @@
             jax.ShapeDtypeStruct((count, D), F32),
             jax.ShapeDtypeStruct((16, 128), F32),
             jax.ShapeDtypeStruct((shards, rows, head_width), BF16),
-            jax.ShapeDtypeStruct((rows, parts * query_width), F32),
-            jax.ShapeDtypeStruct((rows, parts * HEAD_SIZE), F32),
-            jax.ShapeDtypeStruct((rows, parts * HEAD_SIZE), F32),
-            jax.ShapeDtypeStruct((parts * query_width, rows), F32),
+            jax.ShapeDtypeStruct((parts, rows, head_width), BF16),
         ),
         in_specs=[WHOLE, HBM] + [WHOLE] * 6 + [HBM] * 2,
-        out_specs=(WHOLE,) * 2 + (HBM,) * 5,
+        out_specs=(WHOLE, WHOLE, HBM, WHOLE),
         scratch_shapes=[
             VMEM((D, width), BF16),
             pltpu.SemaphoreType.DMA,
@@ -1202,17 +1257,11 @@
             VMEM((shards, 16, 128), F32),
             VMEM((16, 128), F32),
             VMEM((parts, 16, 128), F32),
-            VMEM((parts, rows, head_width), BF16),
             VMEM((2, parts, count, slab_size(parts)), BF16),
             VMEM((2, parts, count, slab_size(parts)), BF16),
             VMEM((slab_size(parts), head_width), BF16),
             pltpu.SemaphoreType.DMA((5,)),
             VMEM((rows, head_width), BF16),
-            VMEM((rows, query_width), F32),
-            VMEM((rows, HEAD_SIZE), F32),
-            VMEM((rows, HEAD_SIZE), F32),
-            VMEM((query_width, rows), F32),
-            pltpu.SemaphoreType.DMA((4,)),
         ]
         + [pltpu.SemaphoreType.DMA((shards,))] * 2
         + [pltpu.SemaphoreType.DMA((parts,))] * 2
@@ -1304,41 +1353,51 @@
     )(*operands)
 
 
-def spread_pair_kernel(width, source, gate, up):
-    gate[...] = source[0, :, :width].astype(F32)
-    up[...] = source[0, :, width:].astype(F32)
-
-
-def spread_pair(stacked):
-    parts, rows, total = stacked.shape
-    width = total // 2
-    across = jax.ShapeDtypeStruct((rows, parts * width), F32)
+def spread_kernel(width, head_source, pair_source, down_source, *targets):
+    query, key, value, out, gate, up, down = targets
+    second = width + HEAD_SIZE
+    third = second + HEAD_SIZE
+    query[...] = head_source[0, :, :width].astype(F32)
+    key[...] = head_source[0, :, width:second].astype(F32)
+    value[...] = head_source[0, :, second:third].astype(F32)
+    out[...] = head_source[0, :, third:].astype(F32).T
+    feed_width = gate.shape[1]
+    gate[...] = pair_source[0, :, :feed_width].astype(F32)
+    up[...] = pair_source[0, :, feed_width:].astype(F32)
+    down[...] = down_source[0].astype(F32).T
+
+
+def spread(head_parts, pair_parts, down_parts, width):
+    parts, rows, _ = head_parts.shape
+    feed_width = down_parts.shape[2]
+    sources = (head_parts, pair_parts, down_parts)
+
+    def side_by_side(columns):
+        shape = jax.ShapeDtypeStruct((rows, parts * columns), F32)
+        return shape, pl.BlockSpec((rows, columns), lambda i: (0, i))
+
+    def stacked(columns):
+        shape = jax.ShapeDtypeStruct((parts * columns, rows), F32)
+        return shape, pl.BlockSpec((columns, rows), lambda i: (i, 0))
+
+    outs = (
+        side_by_side(width),
+        side_by_side(HEAD_SIZE),
+        side_by_side(HEAD_SIZE),
+        stacked(width),
+        side_by_side(feed_width),
+        side_by_side(feed_width),
+        stacked(feed_width),
+    )
     return pl.pallas_call(
-        functools.partial(spread_pair_kernel, width),
-        out_shape=(across, across),
+        functools.partial(spread_kernel, width),
+        out_shape=tuple(shape for shape, _ in outs),
         grid=(parts,),
-        in_specs=[pl.BlockSpec((1, rows, total), lambda i: (i, 0, 0))],
-        out_specs=(pl.BlockSpec((rows, width), lambda i: (0, i)),) * 2,
+        in_specs=[pl.BlockSpec((1, *source.shape[1:]), lambda i: (i, 0, 0)) for source in sources],
+        out_specs=tuple(spec for _, spec in outs),
         compiler_params=pltpu.CompilerParams(vmem_limit_bytes=60 * 1024 * 1024),
-        name="spread_pair",
-    )(stacked)
-
-
-def spread_turned_kernel(source, target):
-    target[...] = source[0].astype(F32).T
-
-
-def spread_turned(stacked):
-    parts, rows, width = stacked.shape
-    return pl.pallas_call(
-        spread_turned_kernel,
-        out_shape=jax.ShapeDtypeStruct((parts * width, rows), F32),
-        grid=(parts,),
-        in_specs=[pl.BlockSpec((1, rows, width), lambda i: (i, 0, 0))],
-        out_specs=pl.BlockSpec((width, rows), lambda i: (i, 0)),
-        compiler_params=pltpu.CompilerParams(vmem_limit_bytes=60 * 1024 * 1024),
-        name="spread_turned",
-    )(stacked)
+        name="spread",
+    )(*sources)
 
 
 def by_row(array):
@@ -1424,7 +1483,7 @@
     flat_grad = grad_all.reshape(tokens, D)
     flat_activation = activation.reshape(tokens, feed_width)
     down_grad = by_row(tdot(flat_grad, flat_activation).astype(BF16))
-    grad_middle, low_all, gain_two, down_parts, context_grad, hidden_out, pair_in, pair_grad = turn(
+    grad_middle, low_all, gain_two, down_parts, context_grad, hidden_out, _, _, feed_shard = turn(
         back,
         pair_weight,
         down_weight,
@@ -1435,11 +1494,6 @@
         gain_rows,
         down_grad.reshape(shards, rows, feed_width),
         normed_two_all,
-    )
-    own_pair = lax.dynamic_index_in_dim(pair_grad, shard, keepdims=False)
-    feed_shard = (own_pair.astype(F32) + jnp.sum(pair_in.astype(F32), axis=0)).astype(BF16)
-    context_grad, feed_shard, down_parts = lax.optimization_barrier(
-        (context_grad, feed_shard, down_parts)
     )
     feed_parts = gather_parts(feed_shard)
     context_grad = context_grad.reshape(tokens, width)
@@ -1458,9 +1512,7 @@
         id_column,
         id_row,
     )
-    grad_down = spread_turned(down_parts)
-    grad_qkv, grad_down = lax.optimization_barrier((grad_qkv, grad_down))
-    grad_hidden, gain_sums, _, grad_query, grad_key, grad_value, grad_out_weight = last(
+    grad_hidden, gain_sums, _, head_parts = last(
         grad_qkv.reshape(parts, count, -1),
         heads_weight,
         hidden,
@@ -1475,7 +1527,9 @@
     )
 
     gain_sums = gain_sums.reshape(-1)
-    grad_gate, grad_up = spread_pair(feed_parts)
+    grad_query, grad_key, grad_value, grad_out_weight, grad_gate, grad_up, grad_down = spread(
+        head_parts, feed_parts, down_parts, width
+    )
     if sharers > 1:
         grad_key, grad_value = (
             part.reshape(rows, KEY_VALUE_HEADS, sharers, HEAD_SIZE).sum(axis=2).reshape(rows, -1)

time: 778 us -> 773 us (level)
  Pallas kernels: 717 us -> 726 us
    pallas_call x1, Pallas kernels: 166 us -> 175 us  [last(): pl.pallas_call(last_kernel, out_shape=(jax.ShapeDtypeStruct((count, D), F...]
    unnamed x34 -> x22, local copies, waits for them, and re-layouts: 16.3 us -> 9.13 us
    pallas_call x2 -> x1, Pallas kernels: 24.5 us -> 26.3 us  [spread(): pl.pallas_call(functools.partial(spread_kernel, width), out_shape=tuple((...]
where the time goes in v11:
time: 773 us; the launch traced here: 771 us
  Pallas kernels  726 us (94%)
  local copies, waits for them, and re-layouts  18.7 us (2%)
  between operations  14.1 us (2%)
  matrix products  11.4 us (1%)
    pallas_call x1, Pallas kernels, forward(): pl.pallas_call(functools.partial(forward_kernel, heads), out_shape=(shape...  275 us
    pallas_call x1, Pallas kernels, turn(): pl.pallas_call(turn_kernel, out_shape=(jax.ShapeDtypeStruct((count, D), F...  211 us
    pallas_call x1, Pallas kernels, last(): pl.pallas_call(last_kernel, out_shape=(jax.ShapeDtypeStruct((count, D), F...  175 us
    pallas_call x1, Pallas kernels, attention_back(): pl.pallas_call(functools.partial(attention_back_kernel, heads), out_shape...  38.1 us
    pallas_call x1, Pallas kernels, spread(): pl.pallas_call(functools.partial(spread_kernel, width), out_shape=tuple((...  26.3 us
  transfers between devices with their start and end apart: 1, of which 0 were waited for; matrix products, arithmetic and copies ran while one was open for 1% of the time, Pallas kernels for 28%

profile of v11, /device:TPU:0, one launch (start us, length us, event | category | flops | bytes accessed | tf_op | source)
XLA Modules:
  0.0 771.1 jit_solution(14288846812626609795)
XLA Ops:
  7.2 0.0 all-gather.3.cloned.1.call-start
  7.2 2.8 concatenate.6
  10.0 0.6 bitcast_convert_fusion.1.refs_2_
  10.6 0.1 pad_maximum_fusion
  10.7 0.7 pad_add_fusion
  11.4 0.6 pad.10.refs_3_
  12.0 0.6 broadcast_in_dim.9.refs_4_
  12.6 274.7 %forward.1 = (bf16[8,256,2048]{2,1,0:T(8,128)(2,1)}, bf16[8,256,2048]{2,1,0:T(8,128)(2,1)}, bf16[8,256,2048]{2,1,0:T(8,128)(2,1)}, bf16[8,256,768]{2,1,0:T(8,128...) custom-call(bf16[256,2048]{1,0:T(8,128)(2,1)} %bitcast.34, ...), custom_call_target="tpu_custom_call" | custom-call | flops 321999994880 | bytes 1024 | tf_op jit(solution)/shard_map/forward/pallas_call | solution.py:759
  287.3 11.4 %bitcast_convert_fusion = bf16[2048,768]{1,0:T(8,128)(2,1)} fusion(bf16[8,256,2048]{2,1,0:T(8,128)(2,1)} %get-tuple-element.59, bf16[8,256,768]{2,1,0:T(8,128)(2,1)} %get-tuple-element.55.refs_3_), kind=kOutput, calls=%fused_computation | convolution fusion | flops 6444023808 | bytes 14680064 | tf_op jit(solution)/shard_map/dot_general | solution.py:33
  298.7 0.0 copy-start.4
  298.7 0.0 copy-start.6
  298.7 211.4 %turn.1 = (f32[256,2048]{1,0:T(8,128)}, bf16[8,256,2048]{2,1,0:T(8,128)(2,1)}, f32[8,2048]{1,0:T(8,128)}, bf16[8,512,768]{2,1,0:T(8,128)(2,1)}, bf16[8,256,256]{...) custom-call(bf16[8,256,1536]{2,1,0:T(8,128)(2,1)} %get-tuple-element, ...), custom_call_target="tpu_custom_call" | custom-call | flops 212749991936 | bytes 1024 | tf_op jit(solution)/shard_map/turn/pallas_call | solution.py:1089
  510.1 0.0 all-gather.3.cloned.1.call-update
  510.1 0.7 slice.18.refs_9_
  510.8 0.8 slice.19
  511.6 1.3 copy.30.refs_10_
  513.0 0.0 copy-done.4
  513.0 0.0 copy-done.6
  513.0 0.0 copy-start
  513.0 1.2 copy-done
  514.2 0.0 copy-start.1
  514.2 1.2 copy-done.1
  515.4 0.0 copy-start.2
  515.4 1.3 copy-done.2
  516.8 0.0 copy-start.3
  516.8 1.4 copy-done.3
  518.1 0.0 copy-start.5
  518.2 1.1 copy-done.5
  519.2 38.1 %attention_back.1 = (bf16[2048,512]{1,0:T(8,128)(2,1)}, f32[8,128]{1,0:T(8,128)S(1)}) custom-call(bf16[2048,256]{1,0:T(8,128)(2,1)S(1)} %copy-done.3, bf16[2048,128]{1,0:T(8,128)(2,1)S(1)} %copy-done.4, bf16[2048,128]{1,0:T(8,128)(2,1)S(1)} %copy-done.5, bf16[2048,256]{1,0:T(8,128)(2,1)S(1)} %bitcast.27, f32[8,2048]{1,0:T(8,128)S(1)} %copy-done.6, ...), custom_call_target="tpu_custom_call" | custom-call | flops 43699998720 | bytes 1024 | tf_op jit(solution)/shard_map/attention_back/pallas_call | solution.py:1337
  557.3 0.0 copy-start.7
  557.3 0.6 copy-done.7
  557.9 175.1 %last.1 = (f32[256,2048]{1,0:T(8,128)}, f32[16,128]{1,0:T(8,128)}, bf16[4,512,768]{2,1,0:T(8,128)(2,1)}, bf16[8,512,768]{2,1,0:T(8,128)(2,1)}) custom-call(bf16[8,256,512]{2,1,0:T(8,128)(2,1)} %bitcast.38, bf16[2048,512]{1,0:T(8,128)(2,1)} %get-tuple-element.73.refs_1_, bf16[256,2048]{1,0:T(8,128)(2,1)} %bitcast.35, f32[256,2048]{1,0:T(8,128)} %get-tuple-element.74.refs_3_, ...), custom_call_target="tpu_custom_call" | custom-call | flops 103499997184 | bytes 1024 | tf_op jit(solution)/shard_map/last/pallas_call | solution.py:1241
  733.0 1.3 fusion
  734.4 1.3 slice_bitcast_fusion
  735.7 0.0 all-gather.3.cloned.1.call-done
  735.7 0.0 copy-start.9
  735.7 0.0 copy-start.8
  735.7 26.3 %spread.1 = (f32[512,2048]{1,0:T(8,128)}, f32[512,1024]{1,0:T(8,128)}, f32[512,1024]{1,0:T(8,128)}, f32[2048,512]{1,0:T(8,128)}, f32[512,6144]{1,0:T(8,128)}, /*index=5*/f32[512,6144]{1,0:T(8,128)}, f32[6144,512]{1,0:T(8,128)}) custom-call(bf16[8,512,768]{2,1,0:T(8,128)(2,1)} %get-tuple-element.80.head_source, bf16[8,512,1536]{2,1,0:T(8,128)(2,1)} %bitcast.28, ...), custom_call_target="tpu_custom_call" | custom-call | tf_op jit(solution)/shard_map/spread/pallas_call | solution.py:1392
  762.0 0.0 copy-done.9
  762.0 1.0 copy.34
  763.0 0.0 copy-done.8
  763.0 1.3 copy.35
  (1 shorter events, 0.0 us)
Async XLA Ops:
  7.2 728.5 %all-gather.3.cloned.1.call-start = ((), (), s32[]{:S(2)}) async-start(), calls=%async_computation | async-start | bytes 14155776 | tf_op jit(solution)/shard_map/all_gather | solution.py:1437
  298.7 214.3 %copy-start.4 = (bf16[2048,128]{1,0:T(8,128)(2,1)S(1)}, bf16[2048,128]{1,0:T(8,128)(2,1)}, u32[]{:S(2)}) copy-start(bf16[2048,128]{1,0:T(8,128)(2,1)} %get-tuple-element.63.refs_1_) | copy-start | bytes 1572868
  298.7 214.3 %copy-start.6 = (f32[8,2048]{1,0:T(8,128)S(1)}, f32[8,2048]{1,0:T(8,128)}, u32[]{:S(2)}) copy-start(f32[8,2048]{1,0:T(8,128)} %get-tuple-element.66.refs_4_) | copy-start | bytes 196612
  513.0 1.2 copy-start
  514.2 1.2 copy-start.1
  515.4 1.3 copy-start.2
  516.8 1.4 copy-start.3
  518.1 1.1 copy-start.5
  557.3 0.6 copy-start.7
  735.7 26.3 %copy-start.9 = (bf16[256,2048]{1,0:T(8,128)(2,1)S(1)}, bf16[256,2048]{1,0:T(8,128)(2,1)}, u32[]{:S(2)}) copy-start(bf16[256,2048]{1,0:T(8,128)(2,1)} %get-tuple-element.61) | copy-start | bytes 3145732
  735.7 27.2 %copy-start.8 = (f32[256,2048]{1,0:T(8,128)S(1)}, f32[256,2048]{1,0:T(8,128)}, u32[]{:S(2)}) copy-start(f32[256,2048]{1,0:T(8,128)} %get-tuple-element.79) | copy-start | bytes 6291460
Sparse Core Ops, SparseCore 0:
  510.2 147.8 all-gather.2

commit v12 on v11

--- a/solution.py
+++ b/solution.py
@@ -419,14 +419,16 @@
 
     def collect(self, target):
         self.arrive()
-
-        def add(block):
+        self.add(target)
+
+    def add(self, target):
+        def one(block):
             value = self.own[block, :].astype(F32)
             for i in range(self.peers):
                 value = value + self.arrived[i, block].astype(F32)
             target[block, :] = value.astype(BF16)
 
-        row_blocks(self.own.shape[0], add)
+        row_blocks(self.own.shape[0], one)
 
     def finish(self):
         loop(self.peers, lambda i: self.copy(i).wait_send())
@@ -639,24 +641,26 @@
     def attend(index):
         block = tile(index, QUERY_TILE)
         query_ids = column(index, 1)[:, 0:1]
-        for h in range(heads):
-            head = slice(h * HEAD_SIZE, (h + 1) * HEAD_SIZE)
-            query = queries[block, head]
-
-            def one(key_tile, carry):
-                sums, total = carry
-                span = tile(key_tile, KEY_TILE)
-                scores = rdot(query, keys[span, :])
-                key_ids = jnp.concatenate(
-                    [all_tokens[key_tile * each + j, 1:2, :] for j in range(each)], axis=1
-                ).astype(F32)
-                expon = jnp.where(key_ids <= query_ids, jnp.exp(scores), 0.0)
-                sums = sums + dot(expon.astype(BF16), values[span, :])
-                return sums, total + jnp.sum(expon, axis=1, keepdims=True)
-
-            each = KEY_TILE // count
-            start = (jnp.zeros((QUERY_TILE, HEAD_SIZE), F32), jnp.zeros((QUERY_TILE, 1), F32))
-            sums, total = lax.fori_loop(0, reach(index, tokens), one, start)
+        each = KEY_TILE // count
+        lanes_of = [slice(h * HEAD_SIZE, (h + 1) * HEAD_SIZE) for h in range(heads)]
+
+        def one(key_tile, carry):
+            span = tile(key_tile, KEY_TILE)
+            key, value = keys[span, :], values[span, :]
+            key_ids = jnp.concatenate(
+                [all_tokens[key_tile * each + j, 1:2, :] for j in range(each)], axis=1
+            ).astype(F32)
+            allowed = key_ids <= query_ids
+            result = []
+            for head, (sums, total) in zip(lanes_of, carry):
+                expon = jnp.where(allowed, jnp.exp(rdot(queries[block, head], key)), 0.0)
+                sums = sums + dot(expon.astype(BF16), value)
+                result.append((sums, total + jnp.sum(expon, axis=1, keepdims=True)))
+            return tuple(result)
+
+        start = (jnp.zeros((QUERY_TILE, HEAD_SIZE), F32), jnp.zeros((QUERY_TILE, 1), F32))
+        results = lax.fori_loop(0, reach(index, tokens), one, (start,) * heads)
+        for h, (head, (sums, total)) in enumerate(zip(lanes_of, results)):
             scale = 1.0 / total
             context[block, head] = (sums * scale).astype(BF16)
             inverse[h : h + 1, block] = jnp.broadcast_to(scale, (QUERY_TILE, HEAD_SIZE)).T[0:1, :]
@@ -812,7 +816,8 @@
 
 
 class Slabs:
-    def __init__(self, sources, buffers, out, target, sems, products):
+    def __init__(self, sources, buffers, out, target, sems, products, place=lambda index: index):
+        self.place = place
         self.sources, self.buffers, self.out, self.target = sources, buffers, out, target
         self.sems, self.products = sems, products
         self.size = out.shape[0]
@@ -822,7 +827,7 @@
         slot = index % 2
         return [
             pltpu.make_async_copy(
-                source.at[:, :, tile(index, self.size)], buffer.at[slot], self.sems.at[2 * i + slot]
+                source.at[:, :, tile(self.place(index), self.size)], buffer.at[slot], self.sems.at[2 * i + slot]
             )
             for i, (source, buffer) in enumerate(zip(self.sources, self.buffers))
         ]
@@ -833,7 +838,8 @@
 
     def leave(self, index):
         each = self.target.shape[1] // self.size
-        target = self.target.at[index // each, tile(index % each, self.size), :]
+        place = self.place(index)
+        target = self.target.at[place // each, tile(place % each, self.size), :]
         return pltpu.make_async_copy(self.out, target, self.sems.at[2 * len(self.sources)])
 
     def run(self, begin, end):
@@ -845,7 +851,7 @@
             def _():
                 self.fetch(index + 1)
 
-            @pl.when(index > 0)
+            @pl.when(index > begin)
             def _():
                 self.leave(index - 1).wait()
 
@@ -857,14 +863,12 @@
                 self.out[:, at : at + width] = tdot(left, right).astype(BF16)
                 at += width
             self.leave(index).start()
-
-            @pl.when(index == self.count - 1)
-            def _():
-                self.leave(index).wait()
-
             return carry
 
         lax.fori_loop(begin, end, one, 0)
+
+    def settle(self, index):
+        self.leave(index - 1).wait()
 
 
 def rms_back(value, gain, grad):
@@ -921,7 +925,10 @@
     down_gathers = [Gather(down_land, down_sems[h], part=halves[h]) for h in range(2)]
 
     def down_ready(h):
-        downs[h].collect(own_down.at[halves[h]])
+        downs[h].arrive()
+        if h == 0:
+            downs[1].start()
+        downs[h].add(own_down.at[halves[h]])
         copy = copy_in(own_down.at[halves[h]], down_land.at[me, halves[h]], sems.at[3])
         copy.wait()
         down_gathers[h].step(0)
@@ -933,8 +940,7 @@
     scatter.begin()
     hidden_scatter.begin()
     full_barrier()
-    for down in downs:
-        down.start()
+    downs[0].start()
     slabs.fetch(0)
     weight_copy.wait()
     data_copy.wait()
@@ -964,6 +970,7 @@
         @pl.when(time < 3)
         def _():
             slabs.run(time * slabs.count // 3, (time + 1) * slabs.count // 3)
+            slabs.settle((time + 1) * slabs.count // 3)
 
         @pl.when(time == 2)
         def _():
@@ -1143,7 +1150,8 @@
     hidden, gain_out, head_grad, land = refs[10:14]
     weight, weight_sem, total, gain_one, pack, pack_in, shard_sum, shard_in = refs[14:22]
     slabs_in, slab_out, slab_sems, own_head, refs = refs[22:24], refs[24], refs[25], refs[26], refs[27:]
-    small, head_refs, gather_sems, scratch = refs[:4], refs[4:7], refs[7:13], refs[13:]
+    small, head_refs, refs = refs[:4], (refs[4:7], refs[7:10]), refs[10:]
+    gather_sems, scratch = (refs[:6], refs[6:12]), refs[12:]
     me, _, _, chips = line_position()
     shard = lax.axis_index("fsdp")
     shards, ahead, _ = peers_of("fsdp")
@@ -1156,16 +1164,33 @@
     def products(slot):
         return (slabs_in[0][slot], back[...]), (slabs_in[1][slot], context[...])
 
-    slabs = Slabs((normed, low), slabs_in, slab_out, head_grad, slab_sems, products)
-    heads = FsdpSum(head_grad, *head_refs, own=own_head)
+    half = own_head.shape[0] // 2
+    halves = [pl.ds(h * half, half) for h in range(2)]
+    per_half = (D // half) // 2 * half // slab_out.shape[0]
+    inner = half // slab_out.shape[0]
+
+    def place(index):
+        side, rest = index // per_half, index % per_half
+        return (rest // inner) * 2 * inner + side * inner + rest % inner
+
+    slabs = Slabs((normed, low), slabs_in, slab_out, head_grad, slab_sems, products, place)
+    heads = [
+        FsdpSum(head_grad, *head_refs[h], own=own_head.at[halves[h]], part=halves[h]) for h in range(2)
+    ]
+    gathers = [Gather(land, gather_sems[h], part=halves[h]) for h in range(2)]
+
+    def head_ready(h):
+        heads[h].collect(land.at[me, halves[h]])
+        gathers[h].step(0)
     scatter = Scatter(scratch, produce, total)
-    gather = Gather(land, gather_sems)
     scatter.begin()
     slabs.fetch(0)
     full_barrier()
     copy.wait()
-    slabs.run(0, slabs.count)
-    heads.start()
+    for h in range(2):
+        slabs.run(h * per_half, (h + 1) * per_half)
+        slabs.settle((h + 1) * per_half)
+        heads[h].start()
     own = copy_in(head_grad.at[shard], own_head, weight_sem)
     own.wait()
     scatter.prepare(0)
@@ -1174,17 +1199,26 @@
         scatter.step(time)
         scatter.prepare(time + 1)
 
+        @pl.when(time == 0)
+        def _():
+            head_ready(0)
+
+        @pl.when(time >= 1)
+        def _():
+            gathers[0].step(time)
+
         @pl.when(time == 1)
         def _():
-            heads.collect(land.at[me])
-
-        @pl.when(time >= 1)
-        def _():
-            gather.step(time - 1)
+            head_ready(1)
+
+        @pl.when(time >= 2)
+        def _():
+            gathers[1].step(time - 1)
 
     loop(chips - 1, step)
     scatter.finish()
-    gather.step(chips - 2)
+    gathers[0].step(chips - 1)
+    gathers[1].step(chips - 2)
     gain_one[...] = jnp.zeros_like(gain_one)
 
     def norm(block):
@@ -1226,9 +1260,10 @@
         gain_out[...] += shard_in[i]
 
     loop(parts, add_sum)
-    gather.step(chips - 1)
-    gather.finish()
-    heads.finish()
+    gathers[1].step(chips - 1)
+    for h in range(2):
+        gathers[h].finish()
+        heads[h].finish()
     loop(shards, lambda i: pack_copy(i).wait_send())
     loop(parts, lambda i: sum_copy(i).wait_send())
 
@@ -1265,7 +1300,9 @@
         ]
         + [pltpu.SemaphoreType.DMA((shards,))] * 2
         + [pltpu.SemaphoreType.DMA((parts,))] * 2
-        + fsdp_scratch(shards, rows, head_width)
+        + fsdp_scratch(shards, rows // 2, head_width)
+        + fsdp_scratch(shards, rows // 2, head_width)
+        + gather_scratch(parts // 2)
         + gather_scratch(parts // 2)
         + scatter_scratch(parts // 2, count),
         compiler_params=params(5, 60),
@@ -1275,8 +1312,8 @@
 
 
 def attention_back_kernel(heads, *refs):
-    queries, keys, values, out_grad, inverse, context, proj, cosine, sine, gain = refs[:10]
-    id_column, id_row, back, gain_sum, key_grad, value_grad, query_grad = refs[10:]
+    queries, keys, values, out_grad, inverse, context, proj, cosine, sine, gain_rows = refs[:10]
+    token_info, back, gain_sum, key_grad, value_grad, query_grad = refs[10:]
     tokens = proj.shape[0]
     key_at = heads * HEAD_SIZE
     key_grad[...] = jnp.zeros_like(key_grad)
@@ -1286,19 +1323,20 @@
     def through(block, lanes, grad, row):
         turned = pltpu.roll(grad, HEAD_SIZE // 2, 1)
         unrotated = grad * cosine[block, :] - turned * sine[block, :]
-        result, terms = rms_back(proj[block, lanes], gain[row : row + 1, :], unrotated)
+        result, terms = rms_back(proj[block, lanes], gain_rows[row + 2 : row + 3, :HEAD_SIZE], unrotated)
         back[block, lanes] = result.astype(BF16)
         gain_sum[row : row + 1, :] += jnp.sum(terms, axis=0, keepdims=True)
 
+    count = token_info.shape[2]
+    each = KEY_TILE // count
+
     def attend(index):
-        block = pl.ds(pl.multiple_of(index * QUERY_TILE, QUERY_TILE), QUERY_TILE)
-        query_ids = id_row[0:1, block]
+        block = tile(index, QUERY_TILE)
+        query_ids = token_info[index, 1:2, :].astype(F32)
+        shifts = []
         for h in range(heads):
             lanes = slice(h * HEAD_SIZE, (h + 1) * HEAD_SIZE)
-            query = queries[block, lanes]
-            grad = out_grad[block, lanes]
-            scale = inverse[h : h + 1, block]
-            products = grad.astype(F32) * context[block, lanes].astype(F32)
+            products = out_grad[block, lanes].astype(F32) * context[block, lanes].astype(F32)
             shift = lax.dot_general(
                 jnp.ones((8, HEAD_SIZE), F32),
                 products,
@@ -1306,20 +1344,36 @@
                 precision=lax.Precision.HIGHEST,
                 preferred_element_type=F32,
             )[0:1, :]
-            query_grad[...] = jnp.zeros_like(query_grad)
-
-            def one(tile):
-                span = pl.ds(pl.multiple_of(tile * KEY_TILE, KEY_TILE), KEY_TILE)
-                key = keys[span, :]
-                scores = rdot(key, query)
-                probs = jnp.where(id_column[span, :] <= query_ids, jnp.exp(scores) * scale, 0.0)
-                grad_scores = (probs * (rdot(values[span, :], grad) - shift)).astype(BF16)
+            shifts.append(shift)
+        query_grad[...] = jnp.zeros_like(query_grad)
+
+        def one(key_tile):
+            span = tile(key_tile, KEY_TILE)
+            key, value = keys[span, :], values[span, :]
+            key_ids = jnp.concatenate(
+                [
+                    jnp.broadcast_to(
+                        token_info[key_tile * each + j, 1:2, :].astype(F32), (128, count)
+                    ).T[:, 0:1]
+                    for j in range(each)
+                ],
+                axis=0,
+            )
+            allowed = key_ids <= query_ids
+            for h in range(heads):
+                lanes = slice(h * HEAD_SIZE, (h + 1) * HEAD_SIZE)
+                query, grad = queries[block, lanes], out_grad[block, lanes]
+                expon = jnp.exp(rdot(key, query)) * inverse[h : h + 1, block]
+                probs = jnp.where(allowed, expon, 0.0)
+                grad_scores = (probs * (rdot(value, grad) - shifts[h])).astype(BF16)
                 value_grad[span, :] += dot(probs.astype(BF16), grad)
                 key_grad[span, :] += dot(grad_scores, query)
-                query_grad[...] += tdot(grad_scores, key)
-
-            loop(reach(index, tokens), one)
-            through(block, lanes, query_grad[...] * HEAD_SIZE ** (-0.5), 0)
+                query_grad[:, lanes] += tdot(grad_scores, key)
+
+        loop(reach(index, tokens), one)
+        for h in range(heads):
+            lanes = slice(h * HEAD_SIZE, (h + 1) * HEAD_SIZE)
+            through(block, lanes, query_grad[:, lanes] * HEAD_SIZE ** (-0.5), 0)
 
     loop(tokens // QUERY_TILE, attend)
 
@@ -1345,9 +1399,9 @@
         scratch_shapes=[
             VMEM((tokens, HEAD_SIZE), F32),
             VMEM((tokens, HEAD_SIZE), F32),
-            VMEM((QUERY_TILE, HEAD_SIZE), F32),
+            VMEM((QUERY_TILE, width), F32),
         ],
-        compiler_params=pltpu.CompilerParams(vmem_limit_bytes=48 * 1024 * 1024),
+        compiler_params=pltpu.CompilerParams(vmem_limit_bytes=62 * 1024 * 1024),
         cost_estimate=cost(38),
         name="attention_back",
     )(*operands)
@@ -1475,9 +1529,6 @@
         pair_weight,
         down_weight,
     ) = forward(hidden, grad, own_gains, own_tokens, freq, weights, shards, parts, heads)
-    head_gains = gain_rows[2:4, :HEAD_SIZE]
-    ids = whole[:, 1].reshape(-1)
-    id_row, id_column = ids[None, :], ids[:, None]
     proj = proj.reshape(tokens, width + 2 * HEAD_SIZE)
 
     flat_grad = grad_all.reshape(tokens, D)
@@ -1508,9 +1559,8 @@
         proj,
         cosine,
         sine,
-        head_gains,
-        id_column,
-        id_row,
+        gain_rows,
+        whole,
     )
     grad_hidden, gain_sums, _, head_parts = last(
         grad_qkv.reshape(parts, count, -1),

time: 773 us -> 770 us (level)
  local copies, waits for them, and re-layouts: 18.7 us -> 8.97 us
    pallas_call x1, Pallas kernels: 175 us -> 185 us  [last(): pl.pallas_call(last_kernel, out_shape=(jax.ShapeDtypeStruct((count, D), F...]
  transfers between devices with their start and end apart: 1 -> 1, of which waited for: 0 -> 0; matrix products, arithmetic and copies ran while one was open for 1% -> 0% of each run, Pallas kernels for 28% -> 29%
where the time goes in v12:
time: 770 us; the launch traced here: 769 us
  Pallas kernels  733 us (95%)
  between operations  14.1 us (2%)
  matrix products  11.4 us (1%)
  local copies, waits for them, and re-layouts  8.97 us (1%)
    pallas_call x1, Pallas kernels, forward(): pl.pallas_call(functools.partial(forward_kernel, heads), out_shape=(shape...  272 us
    pallas_call x1, Pallas kernels, turn(): pl.pallas_call(turn_kernel, out_shape=(jax.ShapeDtypeStruct((count, D), F...  212 us
    pallas_call x1, Pallas kernels, last(): pl.pallas_call(last_kernel, out_shape=(jax.ShapeDtypeStruct((count, D), F...  185 us
    pallas_call x1, Pallas kernels, attention_back(): pl.pallas_call(functools.partial(attention_back_kernel, heads), out_shape...  37.7 us
    pallas_call x1, Pallas kernels, spread(): pl.pallas_call(functools.partial(spread_kernel, width), out_shape=tuple((...  26.3 us
  transfers between devices with their start and end apart: 1, of which 0 were waited for; matrix products, arithmetic and copies ran while one was open for 0% of the time, Pallas kernels for 29%

profile of v12, /device:TPU:0, one launch (start us, length us, event | category | flops | bytes accessed | tf_op | source)
XLA Modules:
  0.0 768.8 jit_solution(2809525055863661431)
XLA Ops:
  7.2 0.0 all-gather.3.cloned.1.call-start
  7.2 2.8 concatenate.6
  10.0 0.6 bitcast_convert_fusion.1.refs_2_
  10.6 0.1 pad_maximum_fusion
  10.7 0.7 pad_add_fusion
  11.4 0.6 pad.10.refs_3_
  12.0 0.6 broadcast_in_dim.9.refs_4_
  12.6 272.2 %forward.1 = (bf16[8,256,2048]{2,1,0:T(8,128)(2,1)}, bf16[8,256,2048]{2,1,0:T(8,128)(2,1)}, bf16[8,256,2048]{2,1,0:T(8,128)(2,1)}, bf16[8,256,768]{2,1,0:T(8,128...) custom-call(bf16[256,2048]{1,0:T(8,128)(2,1)} %bitcast.28, ...), custom_call_target="tpu_custom_call" | custom-call | flops 321999994880 | bytes 1024 | tf_op jit(solution)/shard_map/forward/pallas_call | solution.py:763
  284.8 11.4 %bitcast_convert_fusion = bf16[2048,768]{1,0:T(8,128)(2,1)} fusion(bf16[8,256,2048]{2,1,0:T(8,128)(2,1)} %get-tuple-element.59, bf16[8,256,768]{2,1,0:T(8,128)(2,1)} %get-tuple-element.55.refs_3_), kind=kOutput, calls=%fused_computation | convolution fusion | flops 6444023808 | bytes 14680064 | tf_op jit(solution)/shard_map/dot_general | solution.py:33
  296.2 212.2 %turn.1 = (f32[256,2048]{1,0:T(8,128)}, bf16[8,256,2048]{2,1,0:T(8,128)(2,1)}, f32[8,2048]{1,0:T(8,128)}, bf16[8,512,768]{2,1,0:T(8,128)(2,1)}, bf16[8,256,256]{...) custom-call(bf16[8,256,1536]{2,1,0:T(8,128)(2,1)} %get-tuple-element, ...), custom_call_target="tpu_custom_call" | custom-call | flops 212749991936 | bytes 1024 | tf_op jit(solution)/shard_map/turn/pallas_call | solution.py:1096
  508.4 0.0 all-gather.3.cloned.1.call-update
  508.5 37.7 %attention_back.1 = (bf16[2048,512]{1,0:T(8,128)(2,1)}, f32[8,128]{1,0:T(8,128)}) custom-call(bf16[2048,256]{1,0:T(8,128)(2,1)} %get-tuple-element.62.refs_0_, bf16[2048,128]{1,0:T(8,128)(2,1)} %get-tuple-element.63.refs_1_, bf16[2048,128]{1,0:T(8,128)(2,1)} %get-tuple-element.64.refs_2_, bf16[2048,256]{1,0:T(8,128)(2,1)} %bitcast.34, ...), custom_call_target="tpu_custom_call" | custom-call | flops 43699998720 | bytes 1024 | tf_op jit(solution)/shard_map/attention_back/pallas_call | solution.py:1391
  546.1 184.5 %last.1 = (f32[256,2048]{1,0:T(8,128)}, f32[16,128]{1,0:T(8,128)}, bf16[4,512,768]{2,1,0:T(8,128)(2,1)}, bf16[8,512,768]{2,1,0:T(8,128)(2,1)}) custom-call(bf16[8,256,512]{2,1,0:T(8,128)(2,1)} %bitcast.32, bf16[2048,512]{1,0:T(8,128)(2,1)} %get-tuple-element.73.refs_1_, bf16[256,2048]{1,0:T(8,128)(2,1)} %bitcast.29, f32[256,2048]{1,0:T(8,128)} %get-tuple-element.74.refs_3_, ...), custom_call_target="tpu_custom_call" | custom-call | flops 103499997184 | bytes 1024 | tf_op jit(solution)/shard_map/last/pallas_call | solution.py:1276
  730.7 1.3 fusion
  732.0 1.3 slice_bitcast_fusion
  733.3 0.0 all-gather.3.cloned.1.call-done
  733.3 0.0 copy-start.1
  733.3 0.0 copy-start
  733.3 26.3 %spread.1 = (f32[512,2048]{1,0:T(8,128)}, f32[512,1024]{1,0:T(8,128)}, f32[512,1024]{1,0:T(8,128)}, f32[2048,512]{1,0:T(8,128)}, f32[512,6144]{1,0:T(8,128)}, /*index=5*/f32[512,6144]{1,0:T(8,128)}, f32[6144,512]{1,0:T(8,128)}) custom-call(bf16[8,512,768]{2,1,0:T(8,128)(2,1)} %get-tuple-element.80.head_source, bf16[8,512,1536]{2,1,0:T(8,128)(2,1)} %bitcast.22, ...), custom_call_target="tpu_custom_call" | custom-call | tf_op jit(solution)/shard_map/spread/pallas_call | solution.py:1446
  759.6 0.0 copy-done.1
  759.6 1.0 copy.32
  760.6 0.0 copy-done
  760.6 1.3 copy.33
  (1 shorter events, 0.0 us)
Async XLA Ops:
  7.2 726.2 %all-gather.3.cloned.1.call-start = ((), (), s32[]{:S(2)}) async-start(), calls=%async_computation | async-start | bytes 14155776 | tf_op jit(solution)/shard_map/all_gather | solution.py:1491
  733.3 26.3 %copy-start.1 = (bf16[256,2048]{1,0:T(8,128)(2,1)S(1)}, bf16[256,2048]{1,0:T(8,128)(2,1)}, u32[]{:S(2)}) copy-start(bf16[256,2048]{1,0:T(8,128)(2,1)} %get-tuple-element.61) | copy-start | bytes 3145732
  733.3 27.2 %copy-start = (f32[256,2048]{1,0:T(8,128)S(1)}, f32[256,2048]{1,0:T(8,128)}, u32[]{:S(2)}) copy-start(f32[256,2048]{1,0:T(8,128)} %get-tuple-element.79) | copy-start | bytes 6291460
Sparse Core Ops, SparseCore 0:
  508.6 156.9 all-gather.2

commit v13 on v12

--- a/solution.py
+++ b/solution.py
@@ -1145,18 +1145,37 @@
     )
 
 
-def last_kernel(*refs):
-    back, weights, x, grad_middle, gain_rows, gain_two, gain_heads, context, normed, low = refs[:10]
-    hidden, gain_out, head_grad, land = refs[10:14]
-    weight, weight_sem, total, gain_one, pack, pack_in, shard_sum, shard_in = refs[14:22]
-    slabs_in, slab_out, slab_sems, own_head, refs = refs[22:24], refs[24], refs[25], refs[26], refs[27:]
+PAIR_PARTS = 4
+
+
+def last_kernel(heads, *refs):
+    queries, keys, values, out_grad, inverse, context, proj, cosine, sine, token_info = refs[:10]
+    weights, x, grad_middle, gain_rows, gain_two, normed, low, pair_sum = refs[10:18]
+    hidden, gain_out, head_grad, land, pair_land = refs[18:23]
+    back, gain_heads, key_grad, value_grad, query_grad, pair_own, pair_sem = refs[23:30]
+    pair_sems, refs = refs[30:36], refs[36:]
+    weight, weight_sem, total, gain_one, pack, pack_in, shard_sum, shard_in = refs[:8]
+    slabs_in, slab_out, slab_sems, own_head, refs = refs[8:10], refs[10], refs[11], refs[12], refs[13:]
     small, head_refs, refs = refs[:4], (refs[4:7], refs[7:10]), refs[10:]
     gather_sems, scratch = (refs[:6], refs[6:12]), refs[12:]
     me, _, _, chips = line_position()
     shard = lax.axis_index("fsdp")
     shards, ahead, _ = peers_of("fsdp")
     parts, next_part, _ = peers_of("ctx")
+    tokens = queries.shape[0]
+    key_at = heads * HEAD_SIZE
     copy = copy_in(weights, weight, weight_sem)
+    pair_copy = copy_in(pair_sum, pair_own, pair_sem)
+    pair_size = pair_own.shape[0] // PAIR_PARTS
+
+    def pump(begin, end):
+        def one(index, carry):
+            part = index % PAIR_PARTS
+            sems = [ref.at[part] for ref in pair_sems]
+            Gather(pair_land, sems, part=tile(part, pair_size)).step(index // PAIR_PARTS)
+            return carry
+
+        lax.fori_loop(begin, end, one, 0)
 
     def produce(piece, chunk):
         return rdot(back[piece], weight[pl.ds(pl.multiple_of(chunk * WIDE, WIDE), WIDE), :])
@@ -1174,23 +1193,99 @@
         return (rest // inner) * 2 * inner + side * inner + rest % inner
 
     slabs = Slabs((normed, low), slabs_in, slab_out, head_grad, slab_sems, products, place)
-    heads = [
+    head_sums = [
         FsdpSum(head_grad, *head_refs[h], own=own_head.at[halves[h]], part=halves[h]) for h in range(2)
     ]
     gathers = [Gather(land, gather_sems[h], part=halves[h]) for h in range(2)]
 
     def head_ready(h):
-        heads[h].collect(land.at[me, halves[h]])
+        head_sums[h].collect(land.at[me, halves[h]])
         gathers[h].step(0)
     scatter = Scatter(scratch, produce, total)
     scatter.begin()
     slabs.fetch(0)
     full_barrier()
+    pair_copy.wait()
+    pair_copy = copy_in(pair_own, pair_land.at[me], pair_sem)
+    pair_copy.wait()
+    pump(0, PAIR_PARTS)
+    key_grad[...] = jnp.zeros_like(key_grad)
+    value_grad[...] = jnp.zeros_like(value_grad)
+    gain_heads[...] = jnp.zeros_like(gain_heads)
+
+    def through(index, lanes, grad, row):
+        block = tile(index, QUERY_TILE)
+        turned = pltpu.roll(grad, HEAD_SIZE // 2, 1)
+        unrotated = grad * cosine[block, :] - turned * sine[block, :]
+        result, terms = rms_back(proj[index, :, lanes], gain_rows[row + 2 : row + 3, :HEAD_SIZE], unrotated)
+        back[index, :, lanes] = result.astype(BF16)
+        gain_heads[row : row + 1, :] += jnp.sum(terms, axis=0, keepdims=True)
+
+    count = token_info.shape[2]
+    each = KEY_TILE // count
+
+    def attend(index):
+        block = tile(index, QUERY_TILE)
+        query_ids = token_info[index, 1:2, :].astype(F32)
+        shifts = []
+        for h in range(heads):
+            lanes = slice(h * HEAD_SIZE, (h + 1) * HEAD_SIZE)
+            products = out_grad[index, :, lanes].astype(F32) * context[index, :, lanes].astype(F32)
+            shift = lax.dot_general(
+                jnp.ones((8, HEAD_SIZE), F32),
+                products,
+                (((1,), (1,)), ((), ())),
+                precision=lax.Precision.HIGHEST,
+                preferred_element_type=F32,
+            )[0:1, :]
+            shifts.append(shift)
+        query_grad[...] = jnp.zeros_like(query_grad)
+
+        def one(key_tile):
+            span = tile(key_tile, KEY_TILE)
+            key, value = keys[span, :], values[span, :]
+            key_ids = jnp.concatenate(
+                [
+                    jnp.broadcast_to(
+                        token_info[key_tile * each + j, 1:2, :].astype(F32), (128, count)
+                    ).T[:, 0:1]
+                    for j in range(each)
+                ],
+                axis=0,
+            )
+            allowed = key_ids <= query_ids
+            for h in range(heads):
+                lanes = slice(h * HEAD_SIZE, (h + 1) * HEAD_SIZE)
+                query, grad = queries[block, lanes], out_grad[index, :, lanes]
+                expon = jnp.exp(rdot(key, query)) * inverse[h : h + 1, block]
+                probs = jnp.where(allowed, expon, 0.0)
+                grad_scores = (probs * (rdot(value, grad) - shifts[h])).astype(BF16)
+                value_grad[span, :] += dot(probs.astype(BF16), grad)
+                key_grad[span, :] += dot(grad_scores, query)
+                query_grad[:, lanes] += tdot(grad_scores, key)
+
+        loop(reach(index, tokens), one)
+        for h in range(heads):
+            lanes = slice(h * HEAD_SIZE, (h + 1) * HEAD_SIZE)
+            through(index, lanes, query_grad[:, lanes] * HEAD_SIZE ** (-0.5), 0)
+
+    def finish_keys(index):
+        block = tile(index, QUERY_TILE)
+        through(index, slice(key_at, key_at + HEAD_SIZE), key_grad[block, :], 1)
+        back[index, :, key_at + HEAD_SIZE :] = value_grad[block, :].astype(BF16)
+
+    tiles = tokens // QUERY_TILE
+    marks = (0, 3 * tiles // 8, 5 * tiles // 8, 6 * tiles // 8, tiles)
+    for i in range(4):
+        loop(marks[i + 1] - marks[i], lambda index, i=i: attend(marks[i] + index))
+        pump(PAIR_PARTS + i, PAIR_PARTS + i + 1)
+    loop(tiles, finish_keys)
     copy.wait()
     for h in range(2):
         slabs.run(h * per_half, (h + 1) * per_half)
         slabs.settle((h + 1) * per_half)
-        heads[h].start()
+        head_sums[h].start()
+        pump(2 * PAIR_PARTS + h, 2 * PAIR_PARTS + h + 1)
     own = copy_in(head_grad.at[shard], own_head, weight_sem)
     own.wait()
     scatter.prepare(0)
@@ -1198,6 +1293,9 @@
     def step(time):
         scatter.step(time)
         scatter.prepare(time + 1)
+        begin = 2 * PAIR_PARTS + 2
+        span = PAIR_PARTS * (chips - 3)
+        pump(begin + time * span // (chips - 1), begin + (time + 1) * span // (chips - 1))
 
         @pl.when(time == 0)
         def _():
@@ -1261,29 +1359,52 @@
 
     loop(parts, add_sum)
     gathers[1].step(chips - 1)
+    pump(PAIR_PARTS * (chips - 1) + 2, PAIR_PARTS * chips)
+
+    def settle_pair(part):
+        sems = [ref.at[part] for ref in pair_sems]
+        Gather(pair_land, sems, part=tile(part, pair_size)).finish()
+
+    loop(PAIR_PARTS, settle_pair)
     for h in range(2):
         gathers[h].finish()
-        heads[h].finish()
+        head_sums[h].finish()
     loop(shards, lambda i: pack_copy(i).wait_send())
     loop(parts, lambda i: sum_copy(i).wait_send())
 
 
-def last(back, weights, hidden, grad_middle, gain_rows, gain_two, gain_heads, context, normed, low, shards):
-    parts, count, width = back.shape
-    rows = D // shards
-    query_width = context.shape[2]
+def last(*operands):
+    tokens, query_width = operands[0].shape
+    heads = query_width // HEAD_SIZE
+    parts = operands[5].shape[0]
+    count = tokens // parts
+    width = query_width + 2 * HEAD_SIZE
     head_width = width + query_width
+    rows, pair_width = operands[-1].shape
+    shards = D // rows
+    chips = parts // 2
     return pl.pallas_call(
-        last_kernel,
+        functools.partial(last_kernel, heads),
         out_shape=(
             jax.ShapeDtypeStruct((count, D), F32),
             jax.ShapeDtypeStruct((16, 128), F32),
             jax.ShapeDtypeStruct((shards, rows, head_width), BF16),
             jax.ShapeDtypeStruct((parts, rows, head_width), BF16),
+            jax.ShapeDtypeStruct((parts, rows, pair_width), BF16),
         ),
-        in_specs=[WHOLE, HBM] + [WHOLE] * 6 + [HBM] * 2,
-        out_specs=(WHOLE, WHOLE, HBM, WHOLE),
+        in_specs=[WHOLE] * 10 + [HBM] + [WHOLE] * 4 + [HBM] * 3,
+        out_specs=(WHOLE, WHOLE, HBM, WHOLE, HBM),
         scratch_shapes=[
+            VMEM((parts, count, width), BF16),
+            VMEM((8, HEAD_SIZE), F32),
+            VMEM((tokens, HEAD_SIZE), F32),
+            VMEM((tokens, HEAD_SIZE), F32),
+            VMEM((QUERY_TILE, query_width), F32),
+            VMEM((rows, pair_width), BF16),
+            pltpu.SemaphoreType.DMA,
+        ]
+        + [pltpu.SemaphoreType.DMA((PAIR_PARTS, chips)) for _ in range(6)]
+        + [
             VMEM((D, width), BF16),
             pltpu.SemaphoreType.DMA,
             VMEM((count, D), F32),
@@ -1302,108 +1423,12 @@
         + [pltpu.SemaphoreType.DMA((parts,))] * 2
         + fsdp_scratch(shards, rows // 2, head_width)
         + fsdp_scratch(shards, rows // 2, head_width)
-        + gather_scratch(parts // 2)
-        + gather_scratch(parts // 2)
-        + scatter_scratch(parts // 2, count),
-        compiler_params=params(5, 60),
-        cost_estimate=cost(90),
+        + gather_scratch(chips)
+        + gather_scratch(chips)
+        + scatter_scratch(chips, count),
+        compiler_params=params(5, 63),
+        cost_estimate=cost(190),
         name="last",
-    )(back, weights, hidden, grad_middle, gain_rows, gain_two, gain_heads, context, normed, low)
-
-
-def attention_back_kernel(heads, *refs):
-    queries, keys, values, out_grad, inverse, context, proj, cosine, sine, gain_rows = refs[:10]
-    token_info, back, gain_sum, key_grad, value_grad, query_grad = refs[10:]
-    tokens = proj.shape[0]
-    key_at = heads * HEAD_SIZE
-    key_grad[...] = jnp.zeros_like(key_grad)
-    value_grad[...] = jnp.zeros_like(value_grad)
-    gain_sum[...] = jnp.zeros_like(gain_sum)
-
-    def through(block, lanes, grad, row):
-        turned = pltpu.roll(grad, HEAD_SIZE // 2, 1)
-        unrotated = grad * cosine[block, :] - turned * sine[block, :]
-        result, terms = rms_back(proj[block, lanes], gain_rows[row + 2 : row + 3, :HEAD_SIZE], unrotated)
-        back[block, lanes] = result.astype(BF16)
-        gain_sum[row : row + 1, :] += jnp.sum(terms, axis=0, keepdims=True)
-
-    count = token_info.shape[2]
-    each = KEY_TILE // count
-
-    def attend(index):
-        block = tile(index, QUERY_TILE)
-        query_ids = token_info[index, 1:2, :].astype(F32)
-        shifts = []
-        for h in range(heads):
-            lanes = slice(h * HEAD_SIZE, (h + 1) * HEAD_SIZE)
-            products = out_grad[block, lanes].astype(F32) * context[block, lanes].astype(F32)
-            shift = lax.dot_general(
-                jnp.ones((8, HEAD_SIZE), F32),
-                products,
-                (((1,), (1,)), ((), ())),
-                precision=lax.Precision.HIGHEST,
-                preferred_element_type=F32,
-            )[0:1, :]
-            shifts.append(shift)
-        query_grad[...] = jnp.zeros_like(query_grad)
-
-        def one(key_tile):
-            span = tile(key_tile, KEY_TILE)
-            key, value = keys[span, :], values[span, :]
-            key_ids = jnp.concatenate(
-                [
-                    jnp.broadcast_to(
-                        token_info[key_tile * each + j, 1:2, :].astype(F32), (128, count)
-                    ).T[:, 0:1]
-                    for j in range(each)
-                ],
-                axis=0,
-            )
-            allowed = key_ids <= query_ids
-            for h in range(heads):
-                lanes = slice(h * HEAD_SIZE, (h + 1) * HEAD_SIZE)
-                query, grad = queries[block, lanes], out_grad[block, lanes]
-                expon = jnp.exp(rdot(key, query)) * inverse[h : h + 1, block]
-                probs = jnp.where(allowed, expon, 0.0)
-                grad_scores = (probs * (rdot(value, grad) - shifts[h])).astype(BF16)
-                value_grad[span, :] += dot(probs.astype(BF16), grad)
-                key_grad[span, :] += dot(grad_scores, query)
-                query_grad[:, lanes] += tdot(grad_scores, key)
-
-        loop(reach(index, tokens), one)
-        for h in range(heads):
-            lanes = slice(h * HEAD_SIZE, (h + 1) * HEAD_SIZE)
-            through(block, lanes, query_grad[:, lanes] * HEAD_SIZE ** (-0.5), 0)
-
-    loop(tokens // QUERY_TILE, attend)
-
-    def finish(index):
-        block = pl.ds(pl.multiple_of(index * QUERY_TILE, QUERY_TILE), QUERY_TILE)
-        through(block, slice(key_at, key_at + HEAD_SIZE), key_grad[block, :], 1)
-        back[block, key_at + HEAD_SIZE : key_at + 2 * HEAD_SIZE] = value_grad[block, :].astype(BF16)
-
-    loop(tokens // QUERY_TILE, finish)
-
-
-def attention_back(heads, *operands):
-    tokens = operands[0].shape[0]
-    width = heads * HEAD_SIZE
-    return pl.pallas_call(
-        functools.partial(attention_back_kernel, heads),
-        out_shape=(
-            jax.ShapeDtypeStruct((tokens, width + 2 * HEAD_SIZE), BF16),
-            jax.ShapeDtypeStruct((8, HEAD_SIZE), F32),
-        ),
-        in_specs=[WHOLE] * len(operands),
-        out_specs=(WHOLE,) * 2,
-        scratch_shapes=[
-            VMEM((tokens, HEAD_SIZE), F32),
-            VMEM((tokens, HEAD_SIZE), F32),
-            VMEM((QUERY_TILE, width), F32),
-        ],
-        compiler_params=pltpu.CompilerParams(vmem_limit_bytes=62 * 1024 * 1024),
-        cost_estimate=cost(38),
-        name="attention_back",
     )(*operands)
 
 
@@ -1486,9 +1511,6 @@
     head_rows = HEAD_SIZE // shards
     count = hidden_in.shape[1]
     tokens = parts * count
-
-    def gather_parts(piece):
-        return lax.all_gather(piece, "ctx", axis=0)
 
     own_gains = jnp.concatenate([gain_attention, gain_feed, gain_query, gain_key]).astype(F32)
     own_gains = jnp.pad(own_gains, (0, 2048 - own_gains.shape[0])).reshape(16, 128)
@@ -1529,7 +1551,6 @@
         pair_weight,
         down_weight,
     ) = forward(hidden, grad, own_gains, own_tokens, freq, weights, shards, parts, heads)
-    proj = proj.reshape(tokens, width + 2 * HEAD_SIZE)
 
     flat_grad = grad_all.reshape(tokens, D)
     flat_activation = activation.reshape(tokens, feed_width)
@@ -1546,34 +1567,25 @@
         down_grad.reshape(shards, rows, feed_width),
         normed_two_all,
     )
-    feed_parts = gather_parts(feed_shard)
-    context_grad = context_grad.reshape(tokens, width)
-    grad_qkv, gain_heads = attention_back(
-        heads,
+    grad_hidden, gain_sums, _, head_parts, feed_parts = last(
         queries,
         keys,
         values,
         context_grad,
         inverse,
-        context,
+        context.reshape(parts, count, width),
         proj,
         cosine,
         sine,
-        gain_rows,
         whole,
-    )
-    grad_hidden, gain_sums, _, head_parts = last(
-        grad_qkv.reshape(parts, count, -1),
         heads_weight,
         hidden,
         grad_middle,
         gain_rows,
         gain_two,
-        gain_heads,
-        context.reshape(parts, count, width),
         normed_all,
         low_all,
-        shards,
+        feed_shard,
     )
 
     gain_sums = gain_sums.reshape(-1)

time: 770 us -> 732 us (0.951)
  Pallas kernels: 733 us -> 710 us
  between operations: 14.1 us -> 0.7 us
    pallas_call x2 -> x1, Pallas kernels: 222 us -> 199 us  [last(): pl.pallas_call(functools.partial(last_kernel, heads), out_shape=(jax.Shap...]
  transfers between devices with their start and end apart: 1 -> 0, of which waited for: 0 -> 0; matrix products, arithmetic and copies ran while one was open for 0% -> 0% of each run, Pallas kernels for 29% -> 0%
where the time goes in v13:
time: 732 us; the launch traced here: 731 us
  Pallas kernels  710 us (97%)
  matrix products  11.4 us (2%)
  local copies, waits for them, and re-layouts  7.48 us (1%)
    pallas_call x1, Pallas kernels, forward(): pl.pallas_call(functools.partial(forward_kernel, heads), out_shape=(shape...  272 us
    pallas_call x1, Pallas kernels, turn(): pl.pallas_call(turn_kernel, out_shape=(jax.ShapeDtypeStruct((count, D), F...  212 us
    pallas_call x1, Pallas kernels, last(): pl.pallas_call(functools.partial(last_kernel, heads), out_shape=(jax.Shap...  199 us
    pallas_call x1, Pallas kernels, spread(): pl.pallas_call(functools.partial(spread_kernel, width), out_shape=tuple((...  26.3 us

profile of v13, /device:TPU:0, one launch (start us, length us, event | category | flops | bytes accessed | tf_op | source)
XLA Modules:
  0.0 730.7 jit_solution(13478057025601190549)
XLA Ops:
  0.6 2.8 concatenate.6
  3.4 0.6 bitcast_convert_fusion.1.refs_2_
  4.0 0.7 pad_add_fusion
  4.8 0.6 pad.10.refs_3_
  5.4 0.1 pad_maximum_fusion
  5.4 0.6 broadcast_in_dim.9.refs_4_
  6.0 272.2 %forward.1 = (bf16[8,256,2048]{2,1,0:T(8,128)(2,1)}, bf16[8,256,2048]{2,1,0:T(8,128)(2,1)}, bf16[8,256,2048]{2,1,0:T(8,128)(2,1)}, bf16[8,256,768]{2,1,0:T(8,128...) custom-call(bf16[256,2048]{1,0:T(8,128)(2,1)} %bitcast.23, ...), custom_call_target="tpu_custom_call" | custom-call | flops 321999994880 | bytes 1024 | tf_op jit(solution)/shard_map/forward/pallas_call | solution.py:763
  278.3 11.4 %bitcast_convert_fusion = bf16[2048,768]{1,0:T(8,128)(2,1)} fusion(bf16[8,256,2048]{2,1,0:T(8,128)(2,1)} %get-tuple-element.58, bf16[8,256,768]{2,1,0:T(8,128)(2,1)} %get-tuple-element.54.refs_3_), kind=kOutput, calls=%fused_computation | convolution fusion | flops 6444023808 | bytes 14680064 | tf_op jit(solution)/shard_map/dot_general | solution.py:33
  289.6 212.5 %turn.1 = (f32[256,2048]{1,0:T(8,128)}, bf16[8,256,2048]{2,1,0:T(8,128)(2,1)}, f32[8,2048]{1,0:T(8,128)}, bf16[8,512,768]{2,1,0:T(8,128)(2,1)}, bf16[8,256,256]{...) custom-call(bf16[8,256,1536]{2,1,0:T(8,128)(2,1)} %get-tuple-element, ...), custom_call_target="tpu_custom_call" | custom-call | flops 212749991936 | bytes 1024 | tf_op jit(solution)/shard_map/turn/pallas_call | solution.py:1096
  502.1 198.7 %last.1 = (f32[256,2048]{1,0:T(8,128)}, f32[16,128]{1,0:T(8,128)}, bf16[4,512,768]{2,1,0:T(8,128)(2,1)}, bf16[8,512,768]{2,1,0:T(8,128)(2,1)}, bf16[8,512,1536]{2,1,0:T(8,128)(2,1)}) custom-call(bf16[2048,256]{1,0:T(8,128)(2,1)} %get-tuple-element.61.refs_0_, bf16[2048,128]{1,0:T(8,128)(2,1)} %get-tuple-element.62.refs_1_, ...), custom_call_target="tpu_custom_call" | custom-call | flops 218500005888 | bytes 1024 | tf_op jit(solution)/shard_map/last/pallas_call | solution.py:1386
  700.8 0.0 copy-start.2
  700.8 0.0 copy-start.1
  700.9 0.0 copy-start
  700.9 26.3 %spread.1 = (f32[512,2048]{1,0:T(8,128)}, f32[512,1024]{1,0:T(8,128)}, f32[512,1024]{1,0:T(8,128)}, f32[2048,512]{1,0:T(8,128)}, f32[512,6144]{1,0:T(8,128)}, /*index=5*/f32[512,6144]{1,0:T(8,128)}, f32[6144,512]{1,0:T(8,128)}) custom-call(bf16[8,512,768]{2,1,0:T(8,128)(2,1)} %get-tuple-element.78.head_source, ...), custom_call_target="tpu_custom_call" | custom-call | tf_op jit(solution)/shard_map/spread/pallas_call | solution.py:1471
  727.2 0.0 copy-done.2
  727.2 0.6 fusion
  727.8 0.6 slice_bitcast_fusion
  728.4 0.0 copy-done.1
  728.4 1.0 copy.32
  729.3 0.0 copy-done
  729.3 1.3 copy.33
  (1 shorter events, 0.0 us)
Async XLA Ops:
  700.8 26.4 %copy-start.2 = (f32[16,128]{1,0:T(8,128)S(1)}, f32[16,128]{1,0:T(8,128)}, u32[]{:S(2)}) copy-start(f32[16,128]{1,0:T(8,128)} %get-tuple-element.88) | copy-start | bytes 24580
  700.8 27.5 %copy-start.1 = (bf16[256,2048]{1,0:T(8,128)(2,1)S(1)}, bf16[256,2048]{1,0:T(8,128)(2,1)}, u32[]{:S(2)}) copy-start(bf16[256,2048]{1,0:T(8,128)(2,1)} %get-tuple-element.60) | copy-start | bytes 3145732
  700.9 28.5 %copy-start = (f32[256,2048]{1,0:T(8,128)S(1)}, f32[256,2048]{1,0:T(8,128)}, u32[]{:S(2)}) copy-start(f32[256,2048]{1,0:T(8,128)} %get-tuple-element.77) | copy-start | bytes 6291460

commit v14 on v13

--- a/solution.py
+++ b/solution.py
@@ -4,7 +4,6 @@
 import jax.numpy as jnp
 from jax import lax
 from jax.experimental import pallas as pl
-from jax.experimental.layout import Layout, with_layout_constraint
 from jax.experimental.pallas import tpu as pltpu
 from jax.sharding import PartitionSpec as P
 
@@ -517,7 +516,8 @@
     pair, down, own, piece_in, grad_in, act_out, back_out, total, sems = refs[:9]
     small, refs = refs[9:13], refs[13:]
     share_own, share_sems, refs = refs[0], refs[1:15], refs[15:]
-    first_sems, grad_sems, two_sems, scratch = refs[:6], refs[6:12], refs[12:18], refs[18:]
+    first_sems, grad_sems, refs = refs[:6], (refs[6:12], refs[12:18]), refs[18:]
+    two_sems, scratch = refs[:6], refs[6:]
     me, _, _, chips = line_position()
     shard = lax.axis_index("fsdp")
     shards, ahead, behind = peers_of("fsdp")
@@ -617,7 +617,9 @@
         values[block, :] = proj[piece, :, width + HEAD_SIZE : width + 2 * HEAD_SIZE].astype(BF16)
 
     first_gather = Gather(normed_land, first_sems, project)
-    grad_gather = Gather(grad_land, grad_sems)
+    grad_gathers = [
+        Gather(grad_land, grad_sems[h], part=pl.ds(h * (count // 2), count // 2)) for h in range(2)
+    ]
     first_gather.move(0)
     loop(parts, lambda i: token_copy(i, past_part(i)).wait_recv())
 
@@ -635,7 +637,8 @@
 
     loop(chips - 1, first_step)
     grad_copy.wait()
-    grad_gather.step(0)
+    for gather in grad_gathers:
+        gather.step(0)
     first_gather.use(chips - 1)
 
     def attend(index):
@@ -678,8 +681,9 @@
 
     def scatter_step(time):
         scatter.step(time)
+        grad_gathers[0].step(time + 1)
         scatter.prepare(time + 1)
-        grad_gather.step(time + 1)
+        grad_gathers[1].step(time + 1)
 
     loop(chips - 1, scatter_step)
     scatter.finish()
@@ -742,7 +746,8 @@
     act_copy(0).wait()
     back_copy(0).wait()
     first_gather.finish()
-    grad_gather.finish()
+    for gather in grad_gathers:
+        gather.finish()
     two_gather.finish()
     for out in outs:
         out.wait()
@@ -804,6 +809,7 @@
         + gather_scratch(chips)
         + gather_scratch(chips)
         + gather_scratch(chips)
+        + gather_scratch(chips)
         + scatter_scratch(chips, count),
         compiler_params=params(0, 63),
         cost_estimate=cost(280),
@@ -871,6 +877,17 @@
         self.leave(index - 1).wait()
 
 
+def halves_first(half, size):
+    inner = half // size
+    per_half = D // size // 2
+
+    def place(index):
+        side, rest = index // per_half, index % per_half
+        return (rest // inner) * 2 * inner + side * inner + rest % inner
+
+    return place
+
+
 def rms_back(value, gain, grad):
     inverse = inverse_norm(value)
     scaled = grad * gain
@@ -881,17 +898,21 @@
 
 def turn_kernel(*refs):
     back, pair_weight, down_weight, activation, out_weight = refs[:5]
-    middle, grad, gain_rows, down_grad, normed = refs[5:10]
-    grad_middle, land, gain_sum, down_land, context_grad, hidden, pair_in, pair_grad, pair_sum = refs[10:19]
-    weight, data, total, low, own_down, sems = refs[19:25]
-    slab, slab_out, slab_sems, sum_sems = refs[25:29]
-    down_refs, down_sems = (refs[29:32], refs[32:35]), (refs[35:41], refs[41:47])
-    gather_sems, pair_sems, first_scratch, second_scratch = refs[47:53], refs[53:55], refs[55:64], refs[64:]
+    middle, gain_rows, grads, normed = refs[5:9]
+    grad_middle, land, gain_sum, down_land, context_grad, hidden = refs[9:15]
+    pair_in, pair_grad, pair_sum, down_grad, refs = *refs[15:19], refs[19:]
+    weight, data, act, mid, total, low, own_down, sems = refs[:8]
+    slab, slab_out, down_out, slab_sems, sum_sems, refs = *refs[8:13], refs[13:]
+    down_refs, down_sems, refs = (refs[:3], refs[3:6]), (refs[6:12], refs[12:18]), refs[18:]
+    gather_sems, pair_sems, refs = (refs[:6], refs[6:12]), refs[12:14], refs[14:]
+    first_scratch, second_scratch = refs[:9], refs[9:]
     me, _, _, chips = line_position()
     width = back.shape[2] // 2
     weight_copy = copy_in(pair_weight, weight, sems.at[0])
     data_copy = copy_in(back, data, sems.at[1])
-    own_copy = copy_in(down_grad.at[lax.axis_index("fsdp")], own_down, sems.at[3])
+    act_copy = copy_in(activation, act, sems.at[3])
+    mid_copy = copy_in(middle, mid, sems.at[2])
+    low_copy = copy_in(grads.at[me], low, sems.at[4])
 
     def produce(piece, chunk):
         return rdot(data[piece], weight[pl.ds(pl.multiple_of(chunk * WIDE, WIDE), WIDE), :])
@@ -906,42 +927,52 @@
         return pltpu.make_async_copy(source, weight.at[down_block(chunk)], sems.at[5 + chunk])
 
     def produce_hidden(piece, chunk):
-        return dot(data[piece, :, :width], weight[down_block(chunk)])
-
-    def consume(piece):
-        copy = copy_in(land.at[piece], low, sems.at[4])
-        copy.wait()
-        context_grad[piece] = rdot(low[...], out_weight[...]).astype(BF16)
+        return dot(act[piece], weight[down_block(chunk)])
+
+    side = low.shape[0] // 2
+
+    def consume_of(part):
+        def consume(piece):
+            copy = copy_in(land.at[piece, part], low.at[part], sems.at[4])
+            copy.wait()
+            context_grad[piece, part] = rdot(low[part, :], out_weight[...]).astype(BF16)
+
+        return consume
+
+    sides = [pl.ds(h * side, side) for h in range(2)]
+    gathers = [
+        Gather(land, gather_sems[h], consume_of(sides[h]), part=sides[h]) for h in range(2)
+    ]
 
     def products(slot):
         return ((slab[slot], data[...]),)
+
+    def down_products(slot):
+        return ((slab[slot], act[...]),)
 
     slabs = Slabs((normed,), (slab,), slab_out, pair_grad, slab_sems, products)
     half = own_down.shape[0] // 2
     halves = [pl.ds(h * half, half) for h in range(2)]
+    order = halves_first(half, down_out.shape[0])
+    down_slabs = Slabs((grads,), (slab,), down_out, down_grad, slab_sems, down_products, order)
     downs = [
         FsdpSum(down_grad, *down_refs[h], own=own_down.at[halves[h]], part=halves[h]) for h in range(2)
     ]
     down_gathers = [Gather(down_land, down_sems[h], part=halves[h]) for h in range(2)]
 
     def down_ready(h):
-        downs[h].arrive()
-        if h == 0:
-            downs[1].start()
-        downs[h].add(own_down.at[halves[h]])
+        downs[h].collect(own_down.at[halves[h]])
         copy = copy_in(own_down.at[halves[h]], down_land.at[me, halves[h]], sems.at[3])
         copy.wait()
         down_gathers[h].step(0)
 
     pair = FsdpSum(pair_grad, pair_in, *pair_sems, own=own_down)
-    gather = Gather(land, gather_sems, consume)
     scatter = Scatter(first_scratch, produce, total)
     hidden_scatter = Scatter(second_scratch, produce_hidden, total)
     scatter.begin()
     hidden_scatter.begin()
     full_barrier()
-    downs[0].start()
-    slabs.fetch(0)
+    down_slabs.fetch(0)
     weight_copy.wait()
     data_copy.wait()
     scatter.prepare(0)
@@ -952,25 +983,36 @@
 
         @pl.when(time == 0)
         def _():
+            act_copy.wait()
+            for h in range(2):
+                begin, end = h * down_slabs.count // 2, (h + 1) * down_slabs.count // 2
+                down_slabs.run(begin, end)
+                down_slabs.settle(end)
+                downs[h].start()
+            slabs.fetch(0)
+            own_copy = copy_in(down_grad.at[lax.axis_index("fsdp")], own_down, sems.at[3])
             own_copy.wait()
+
+        @pl.when(time == 1)
+        def _():
             down_ready(0)
 
-        @pl.when(time >= 1)
-        def _():
-            down_gathers[0].step(time)
-
-        @pl.when(time == 1)
+        @pl.when(time >= 2)
+        def _():
+            down_gathers[0].step(time - 1)
+
+        @pl.when(time == 2)
         def _():
             down_ready(1)
 
-        @pl.when(time >= 2)
-        def _():
-            down_gathers[1].step(time - 1)
-
-        @pl.when(time < 3)
-        def _():
-            slabs.run(time * slabs.count // 3, (time + 1) * slabs.count // 3)
-            slabs.settle((time + 1) * slabs.count // 3)
+        @pl.when(time >= 3)
+        def _():
+            down_gathers[1].step(time - 2)
+
+        @pl.when(jnp.logical_or(time == 1, time == 2))
+        def _():
+            slabs.run((time - 1) * slabs.count // 2, time * slabs.count // 2)
+            slabs.settle(time * slabs.count // 2)
 
         @pl.when(time == 2)
         def _():
@@ -978,28 +1020,32 @@
 
     loop(chips - 1, step)
     scatter.finish()
-    down_gathers[0].step(chips - 1)
-    down_gathers[1].step(chips - 2)
+    down_gathers[0].step(chips - 2)
+    down_gathers[1].step(chips - 3)
     for chunk in range(CHUNKS):
         down_copy(chunk).start()
-    act_copy = copy_in(activation, data.at[:, :, pl.ds(0, width)], sems.at[1])
+    mid_copy.wait()
+    low_copy.wait()
     gain_sum[...] = jnp.zeros_like(gain_sum)
 
     def norm(block):
-        through, terms = rms_back(middle[block, :], gain_rows[1:2, :], total[block, :])
-        value = grad[block, :].astype(F32) + through
-        grad_middle[block, :] = value
+        through, terms = rms_back(mid[block, :], gain_rows[1:2, :], total[block, :])
+        value = low[block, :].astype(F32) + through
+        mid[block, :] = value
         low[block, :] = value.astype(BF16)
         gain_sum[0:1, :] += jnp.sum(terms, axis=0, keepdims=True)
 
-    row_blocks(middle.shape[0], norm)
+    row_blocks(mid.shape[0], norm)
+    mid_out = copy_in(mid, grad_middle, sems.at[2])
     low_copy = copy_in(low, land.at[me], sems.at[3])
     low_copy.wait()
-    gather.step(0)
+    for gather in gathers:
+        gather.step(0)
     for chunk in range(CHUNKS):
         down_copy(chunk).wait()
-    act_copy.wait()
     hidden_scatter.prepare(0)
+    mid_out.wait()
+    mid_copy = copy_in(middle, mid, sems.at[2])
 
     def add_pairs():
         pair.arrive()
@@ -1063,13 +1109,19 @@
 
     def turn_step(time):
         hidden_scatter.step(time)
+        gathers[0].step(time + 1)
         hidden_scatter.prepare(time + 1)
 
         @pl.when(time == chips - 2)
         def _():
             add_pairs()
 
-        gather.step(time + 1)
+        gathers[1].step(time + 1)
+
+        @pl.when(time == 0)
+        def _():
+            down_gathers[0].step(chips - 1)
+            down_gathers[1].step(chips - 2)
 
         @pl.when(time == 1)
         def _():
@@ -1077,21 +1129,22 @@
 
     loop(chips - 1, turn_step)
     hidden_scatter.finish()
-    gather.finish()
     for h in range(2):
+        gathers[h].finish()
         down_gathers[h].finish()
         downs[h].finish()
     pair.finish()
+    mid_copy.wait()
 
     def add(block):
-        hidden[block, :] = (middle[block, :] + total[block, :]).astype(BF16)
-
-    row_blocks(middle.shape[0], add)
-
-
-def turn(back, pair_weight, down_weight, activation, out_weight, middle, grad, gain_rows, down_grad, normed):
+        hidden[block, :] = (mid[block, :] + total[block, :]).astype(BF16)
+
+    row_blocks(mid.shape[0], add)
+
+
+def turn(back, pair_weight, down_weight, activation, out_weight, middle, gain_rows, grads, normed, shards):
     parts, count, feed_width = activation.shape
-    shards, rows, _ = down_grad.shape
+    rows = D // shards
     width = out_weight.shape[0]
     return pl.pallas_call(
         turn_kernel,
@@ -1105,23 +1158,28 @@
             jax.ShapeDtypeStruct((shards - 1, rows, 2 * feed_width), BF16),
             jax.ShapeDtypeStruct((shards, rows, 2 * feed_width), BF16),
             jax.ShapeDtypeStruct((rows, 2 * feed_width), BF16),
+            jax.ShapeDtypeStruct((shards, rows, feed_width), BF16),
         ),
-        in_specs=[HBM] * 4 + [WHOLE] * 4 + [HBM] * 2,
-        out_specs=(WHOLE, HBM, WHOLE, HBM, WHOLE, WHOLE, HBM, HBM, HBM),
+        in_specs=[HBM] * 4 + [WHOLE, HBM, WHOLE] + [HBM] * 2,
+        out_specs=(HBM, HBM, WHOLE, HBM, WHOLE, WHOLE) + (HBM,) * 4,
         scratch_shapes=[
             VMEM((D, 2 * feed_width), BF16),
             VMEM((parts, count, 2 * feed_width), BF16),
+            VMEM((parts, count, feed_width), BF16),
+            VMEM((count, D), F32),
             VMEM((count, D), F32),
             VMEM((count, D), BF16),
             VMEM((rows, feed_width), BF16),
             pltpu.SemaphoreType.DMA((5 + CHUNKS,)),
             VMEM((2, parts, count, slab_size(parts)), BF16),
             VMEM((slab_size(parts), 2 * feed_width), BF16),
+            VMEM((slab_size(parts), feed_width), BF16),
             pltpu.SemaphoreType.DMA((3,)),
             pltpu.SemaphoreType.DMA((2, parts)),
         ]
         + fsdp_scratch(shards, rows // 2, feed_width)
         + fsdp_scratch(shards, rows // 2, feed_width)
+        + gather_scratch(parts // 2)
         + gather_scratch(parts // 2)
         + gather_scratch(parts // 2)
         + gather_scratch(parts // 2)
@@ -1138,9 +1196,8 @@
         activation,
         out_weight,
         middle,
-        grad,
         gain_rows,
-        down_grad,
+        grads,
         normed,
     )
 
@@ -1185,13 +1242,8 @@
 
     half = own_head.shape[0] // 2
     halves = [pl.ds(h * half, half) for h in range(2)]
-    per_half = (D // half) // 2 * half // slab_out.shape[0]
-    inner = half // slab_out.shape[0]
-
-    def place(index):
-        side, rest = index // per_half, index % per_half
-        return (rest // inner) * 2 * inner + side * inner + rest % inner
-
+    per_half = D // slab_out.shape[0] // 2
+    place = halves_first(half, slab_out.shape[0])
     slabs = Slabs((normed, low), slabs_in, slab_out, head_grad, slab_sems, products, place)
     head_sums = [
         FsdpSum(head_grad, *head_refs[h], own=own_head.at[halves[h]], part=halves[h]) for h in range(2)
@@ -1479,10 +1531,6 @@
     )(*sources)
 
 
-def by_row(array):
-    return with_layout_constraint(array, Layout(major_to_minor=(0, 1)))
-
-
 def local(
     hidden_in,
     weight_query,
@@ -1552,20 +1600,17 @@
         down_weight,
     ) = forward(hidden, grad, own_gains, own_tokens, freq, weights, shards, parts, heads)
 
-    flat_grad = grad_all.reshape(tokens, D)
-    flat_activation = activation.reshape(tokens, feed_width)
-    down_grad = by_row(tdot(flat_grad, flat_activation).astype(BF16))
-    grad_middle, low_all, gain_two, down_parts, context_grad, hidden_out, _, _, feed_shard = turn(
+    grad_middle, low_all, gain_two, down_parts, context_grad, hidden_out, _, _, feed_shard, _ = turn(
         back,
         pair_weight,
         down_weight,
         activation,
         out_weight,
         middle,
-        grad,
         gain_rows,
-        down_grad.reshape(shards, rows, feed_width),
+        grad_all,
         normed_two_all,
+        shards,
     )
     grad_hidden, gain_sums, _, head_parts, feed_parts = last(
         queries,

time: 732 us -> 732 us (level)
  matrix products: 11.4 us -> 0 us
  Pallas kernels: 710 us -> 720 us
    dot_general x1 -> x0, matrix products: 11.4 us -> none  [tdot(): lax.dot_general(left, right, (((0,), (0,)), ((), ())), preferred_element_...]
where the time goes in v14:
time: 732 us; the launch traced here: 730 us
  Pallas kernels  720 us (98%)
  local copies, waits for them, and re-layouts  7.48 us (1%)
    pallas_call x1, Pallas kernels, forward(): pl.pallas_call(functools.partial(forward_kernel, heads), out_shape=(shape...  279 us
    pallas_call x1, Pallas kernels, turn(): pl.pallas_call(turn_kernel, out_shape=(jax.ShapeDtypeStruct((count, D), F...  218 us
    pallas_call x1, Pallas kernels, last(): pl.pallas_call(functools.partial(last_kernel, heads), out_shape=(jax.Shap...  197 us
    pallas_call x1, Pallas kernels, spread(): pl.pallas_call(functools.partial(spread_kernel, width), out_shape=tuple((...  26.3 us

profile of v14, /device:TPU:0, one launch (start us, length us, event | category | flops | bytes accessed | tf_op | source)
XLA Modules:
  0.0 729.8 jit_solution(12873152018059683490)
XLA Ops:
  0.6 2.8 concatenate.6
  3.4 0.6 bitcast_convert_fusion.refs_2_
  4.0 0.7 pad_add_fusion
  4.8 0.6 pad.10.refs_3_
  5.4 0.1 pad_maximum_fusion
  5.4 0.6 broadcast_in_dim.9.refs_4_
  6.0 278.7 %forward.1 = (bf16[8,256,2048]{2,1,0:T(8,128)(2,1)}, bf16[8,256,2048]{2,1,0:T(8,128)(2,1)}, bf16[8,256,2048]{2,1,0:T(8,128)(2,1)}, bf16[8,256,768]{2,1,0:T(8,128...) custom-call(bf16[256,2048]{1,0:T(8,128)(2,1)} %bitcast.17, ...), custom_call_target="tpu_custom_call" | custom-call | flops 321999994880 | bytes 1024 | tf_op jit(solution)/shard_map/forward/pallas_call | solution.py:768
  284.7 218.3 %turn.1 = (f32[256,2048]{1,0:T(8,128)}, bf16[8,256,2048]{2,1,0:T(8,128)(2,1)}, f32[8,2048]{1,0:T(8,128)}, bf16[8,512,768]{2,1,0:T(8,128)(2,1)}, bf16[8,256,256]{...) custom-call(bf16[8,256,1536]{2,1,0:T(8,128)(2,1)} %get-tuple-element, ...), custom_call_target="tpu_custom_call" | custom-call | flops 212749991936 | bytes 1024 | tf_op jit(solution)/shard_map/turn/pallas_call | solution.py:1149
  503.0 196.9 %last.1 = (f32[256,2048]{1,0:T(8,128)}, f32[16,128]{1,0:T(8,128)}, bf16[4,512,768]{2,1,0:T(8,128)(2,1)}, bf16[8,512,768]{2,1,0:T(8,128)(2,1)}, bf16[8,512,1536]{2,1,0:T(8,128)(2,1)}) custom-call(bf16[2048,256]{1,0:T(8,128)(2,1)} %get-tuple-element.61.refs_0_, bf16[2048,128]{1,0:T(8,128)(2,1)} %get-tuple-element.62.refs_1_, ...), custom_call_target="tpu_custom_call" | custom-call | flops 218500005888 | bytes 1024 | tf_op jit(solution)/shard_map/last/pallas_call | solution.py:1438
  699.9 0.0 copy-start.2
  699.9 0.0 copy-start.1
  699.9 0.0 copy-start
  700.0 26.3 %spread.1 = (f32[512,2048]{1,0:T(8,128)}, f32[512,1024]{1,0:T(8,128)}, f32[512,1024]{1,0:T(8,128)}, f32[2048,512]{1,0:T(8,128)}, f32[512,6144]{1,0:T(8,128)}, /*index=5*/f32[512,6144]{1,0:T(8,128)}, f32[6144,512]{1,0:T(8,128)}) custom-call(bf16[8,512,768]{2,1,0:T(8,128)(2,1)} %get-tuple-element.78.head_source, ...), custom_call_target="tpu_custom_call" | custom-call | tf_op jit(solution)/shard_map/spread/pallas_call | solution.py:1523
  726.3 0.0 copy-done.2
  726.3 0.6 fusion
  726.9 0.6 slice_bitcast_fusion
  727.5 0.0 copy-done.1
  727.5 1.0 copy.30
  728.4 0.0 copy-done
  728.4 1.3 copy.31
  (1 shorter events, 0.0 us)
Async XLA Ops:
  699.9 26.4 %copy-start.2 = (f32[16,128]{1,0:T(8,128)S(1)}, f32[16,128]{1,0:T(8,128)}, u32[]{:S(2)}) copy-start(f32[16,128]{1,0:T(8,128)} %get-tuple-element.88) | copy-start | bytes 24580
  699.9 27.5 %copy-start.1 = (bf16[256,2048]{1,0:T(8,128)(2,1)S(1)}, bf16[256,2048]{1,0:T(8,128)(2,1)}, u32[]{:S(2)}) copy-start(bf16[256,2048]{1,0:T(8,128)(2,1)} %get-tuple-element.60) | copy-start | bytes 3145732
  699.9 28.5 %copy-start = (f32[256,2048]{1,0:T(8,128)S(1)}, f32[256,2048]{1,0:T(8,128)}, u32[]{:S(2)}) copy-start(f32[256,2048]{1,0:T(8,128)} %get-tuple-element.77) | copy-start | bytes 6291460

commit v15 on v14

--- a/solution.py
+++ b/solution.py
@@ -516,8 +516,7 @@
     pair, down, own, piece_in, grad_in, act_out, back_out, total, sems = refs[:9]
     small, refs = refs[9:13], refs[13:]
     share_own, share_sems, refs = refs[0], refs[1:15], refs[15:]
-    first_sems, grad_sems, refs = refs[:6], (refs[6:12], refs[12:18]), refs[18:]
-    two_sems, scratch = refs[:6], refs[6:]
+    first_sems, grad_sems, two_sems, scratch = refs[:6], refs[6:12], refs[12:18], refs[18:]
     me, _, _, chips = line_position()
     shard = lax.axis_index("fsdp")
     shards, ahead, behind = peers_of("fsdp")
@@ -617,9 +616,7 @@
         values[block, :] = proj[piece, :, width + HEAD_SIZE : width + 2 * HEAD_SIZE].astype(BF16)
 
     first_gather = Gather(normed_land, first_sems, project)
-    grad_gathers = [
-        Gather(grad_land, grad_sems[h], part=pl.ds(h * (count // 2), count // 2)) for h in range(2)
-    ]
+    grad_gather = Gather(grad_land, grad_sems)
     first_gather.move(0)
     loop(parts, lambda i: token_copy(i, past_part(i)).wait_recv())
 
@@ -637,8 +634,7 @@
 
     loop(chips - 1, first_step)
     grad_copy.wait()
-    for gather in grad_gathers:
-        gather.step(0)
+    grad_gather.step(0)
     first_gather.use(chips - 1)
 
     def attend(index):
@@ -681,9 +677,8 @@
 
     def scatter_step(time):
         scatter.step(time)
-        grad_gathers[0].step(time + 1)
         scatter.prepare(time + 1)
-        grad_gathers[1].step(time + 1)
+        grad_gather.step(time + 1)
 
     loop(chips - 1, scatter_step)
     scatter.finish()
@@ -746,8 +741,7 @@
     act_copy(0).wait()
     back_copy(0).wait()
     first_gather.finish()
-    for gather in grad_gathers:
-        gather.finish()
+    grad_gather.finish()
     two_gather.finish()
     for out in outs:
         out.wait()
@@ -809,7 +803,6 @@
         + gather_scratch(chips)
         + gather_scratch(chips)
         + gather_scratch(chips)
-        + gather_scratch(chips)
         + scatter_scratch(chips, count),
         compiler_params=params(0, 63),
         cost_estimate=cost(280),
@@ -1108,8 +1101,8 @@
             copy.wait()
 
     def turn_step(time):
+        gathers[0].step(time + 1)
         hidden_scatter.step(time)
-        gathers[0].step(time + 1)
         hidden_scatter.prepare(time + 1)
 
         @pl.when(time == chips - 2)

time: 732 us -> 725 us (level)
  no operation moved by 1% of the time
where the time goes in v15:
time: 725 us; the launch traced here: 723 us
  Pallas kernels  714 us (98%)
  local copies, waits for them, and re-layouts  7.48 us (1%)
    pallas_call x1, Pallas kernels, forward(): pl.pallas_call(functools.partial(forward_kernel, heads), out_shape=(shape...  272 us
    pallas_call x1, Pallas kernels, turn(): pl.pallas_call(turn_kernel, out_shape=(jax.ShapeDtypeStruct((count, D), F...  218 us
    pallas_call x1, Pallas kernels, last(): pl.pallas_call(functools.partial(last_kernel, heads), out_shape=(jax.Shap...  197 us
    pallas_call x1, Pallas kernels, spread(): pl.pallas_call(functools.partial(spread_kernel, width), out_shape=tuple((...  26.3 us

profile of v15, /device:TPU:0, one launch (start us, length us, event | category | flops | bytes accessed | tf_op | source)
XLA Modules:
  0.0 723.2 jit_solution(4813351272590270025)
XLA Ops:
  0.6 2.8 concatenate.6
  3.4 0.6 bitcast_convert_fusion.refs_2_
  4.0 0.7 pad_add_fusion
  4.8 0.6 pad.10.refs_3_
  5.4 0.1 pad_maximum_fusion
  5.4 0.6 broadcast_in_dim.9.refs_4_
  6.0 272.1 %forward.1 = (bf16[8,256,2048]{2,1,0:T(8,128)(2,1)}, bf16[8,256,2048]{2,1,0:T(8,128)(2,1)}, bf16[8,256,2048]{2,1,0:T(8,128)(2,1)}, bf16[8,256,768]{2,1,0:T(8,128...) custom-call(bf16[256,2048]{1,0:T(8,128)(2,1)} %bitcast.17, ...), custom_call_target="tpu_custom_call" | custom-call | flops 321999994880 | bytes 1024 | tf_op jit(solution)/shard_map/forward/pallas_call | solution.py:762
  278.1 218.3 %turn.1 = (f32[256,2048]{1,0:T(8,128)}, bf16[8,256,2048]{2,1,0:T(8,128)(2,1)}, f32[8,2048]{1,0:T(8,128)}, bf16[8,512,768]{2,1,0:T(8,128)(2,1)}, bf16[8,256,256]{...) custom-call(bf16[8,256,1536]{2,1,0:T(8,128)(2,1)} %get-tuple-element, ...), custom_call_target="tpu_custom_call" | custom-call | flops 212749991936 | bytes 1024 | tf_op jit(solution)/shard_map/turn/pallas_call | solution.py:1142
  496.4 196.9 %last.1 = (f32[256,2048]{1,0:T(8,128)}, f32[16,128]{1,0:T(8,128)}, bf16[4,512,768]{2,1,0:T(8,128)(2,1)}, bf16[8,512,768]{2,1,0:T(8,128)(2,1)}, bf16[8,512,1536]{2,1,0:T(8,128)(2,1)}) custom-call(bf16[2048,256]{1,0:T(8,128)(2,1)} %get-tuple-element.61.refs_0_, bf16[2048,128]{1,0:T(8,128)(2,1)} %get-tuple-element.62.refs_1_, ...), custom_call_target="tpu_custom_call" | custom-call | flops 218500005888 | bytes 1024 | tf_op jit(solution)/shard_map/last/pallas_call | solution.py:1431
  693.4 0.0 copy-start.2
  693.4 0.0 copy-start.1
  693.4 0.0 copy-start
  693.4 26.3 %spread.1 = (f32[512,2048]{1,0:T(8,128)}, f32[512,1024]{1,0:T(8,128)}, f32[512,1024]{1,0:T(8,128)}, f32[2048,512]{1,0:T(8,128)}, f32[512,6144]{1,0:T(8,128)}, /*index=5*/f32[512,6144]{1,0:T(8,128)}, f32[6144,512]{1,0:T(8,128)}) custom-call(bf16[8,512,768]{2,1,0:T(8,128)(2,1)} %get-tuple-element.78.head_source, ...), custom_call_target="tpu_custom_call" | custom-call | tf_op jit(solution)/shard_map/spread/pallas_call | solution.py:1516
  719.7 0.0 copy-done.2
  719.7 0.6 fusion
  720.3 0.6 slice_bitcast_fusion
  720.9 0.0 copy-done.1
  720.9 1.0 copy.30
  721.9 0.0 copy-done
  721.9 1.3 copy.31
  (1 shorter events, 0.0 us)
Async XLA Ops:
  693.4 26.4 %copy-start.2 = (f32[16,128]{1,0:T(8,128)S(1)}, f32[16,128]{1,0:T(8,128)}, u32[]{:S(2)}) copy-start(f32[16,128]{1,0:T(8,128)} %get-tuple-element.88) | copy-start | bytes 24580
  693.4 27.5 %copy-start.1 = (bf16[256,2048]{1,0:T(8,128)(2,1)S(1)}, bf16[256,2048]{1,0:T(8,128)(2,1)}, u32[]{:S(2)}) copy-start(bf16[256,2048]{1,0:T(8,128)(2,1)} %get-tuple-element.60) | copy-start | bytes 3145732
  693.4 28.5 %copy-start = (f32[256,2048]{1,0:T(8,128)S(1)}, f32[256,2048]{1,0:T(8,128)}, u32[]{:S(2)}) copy-start(f32[256,2048]{1,0:T(8,128)} %get-tuple-element.77) | copy-start | bytes 6291460

commit v16 on v15

--- a/solution.py
+++ b/solution.py
@@ -1326,6 +1326,7 @@
         pump(PAIR_PARTS + i, PAIR_PARTS + i + 1)
     loop(tiles, finish_keys)
     copy.wait()
+    scatter.prepare(0)
     for h in range(2):
         slabs.run(h * per_half, (h + 1) * per_half)
         slabs.settle((h + 1) * per_half)
@@ -1333,7 +1334,6 @@
         pump(2 * PAIR_PARTS + h, 2 * PAIR_PARTS + h + 1)
     own = copy_in(head_grad.at[shard], own_head, weight_sem)
     own.wait()
-    scatter.prepare(0)
 
     def step(time):
         scatter.step(time)

time: 725 us -> 725 us (level)
  no operation moved by 1% of the time
where the time goes in v16:
time: 725 us; the launch traced here: 723 us
  Pallas kernels  714 us (98%)
  local copies, waits for them, and re-layouts  7.48 us (1%)
    pallas_call x1, Pallas kernels, forward(): pl.pallas_call(functools.partial(forward_kernel, heads), out_shape=(shape...  272 us
    pallas_call x1, Pallas kernels, turn(): pl.pallas_call(turn_kernel, out_shape=(jax.ShapeDtypeStruct((count, D), F...  218 us
    pallas_call x1, Pallas kernels, last(): pl.pallas_call(functools.partial(last_kernel, heads), out_shape=(jax.Shap...  197 us
    pallas_call x1, Pallas kernels, spread(): pl.pallas_call(functools.partial(spread_kernel, width), out_shape=tuple((...  26.3 us

profile of v16, /device:TPU:0, one launch (start us, length us, event | category | flops | bytes accessed | tf_op | source)
XLA Modules:
  0.0 723.2 jit_solution(13748734748429302333)
XLA Ops:
  0.6 2.8 concatenate.6
  3.4 0.6 bitcast_convert_fusion.refs_2_
  4.0 0.7 pad_add_fusion
  4.8 0.6 pad.10.refs_3_
  5.4 0.1 pad_maximum_fusion
  5.4 0.6 broadcast_in_dim.9.refs_4_
  6.0 272.1 %forward.1 = (bf16[8,256,2048]{2,1,0:T(8,128)(2,1)}, bf16[8,256,2048]{2,1,0:T(8,128)(2,1)}, bf16[8,256,2048]{2,1,0:T(8,128)(2,1)}, bf16[8,256,768]{2,1,0:T(8,128...) custom-call(bf16[256,2048]{1,0:T(8,128)(2,1)} %bitcast.17, ...), custom_call_target="tpu_custom_call" | custom-call | flops 321999994880 | bytes 1024 | tf_op jit(solution)/shard_map/forward/pallas_call | solution.py:762
  278.1 218.3 %turn.1 = (f32[256,2048]{1,0:T(8,128)}, bf16[8,256,2048]{2,1,0:T(8,128)(2,1)}, f32[8,2048]{1,0:T(8,128)}, bf16[8,512,768]{2,1,0:T(8,128)(2,1)}, bf16[8,256,256]{...) custom-call(bf16[8,256,1536]{2,1,0:T(8,128)(2,1)} %get-tuple-element, ...), custom_call_target="tpu_custom_call" | custom-call | flops 212749991936 | bytes 1024 | tf_op jit(solution)/shard_map/turn/pallas_call | solution.py:1142
  496.4 196.9 %last.1 = (f32[256,2048]{1,0:T(8,128)}, f32[16,128]{1,0:T(8,128)}, bf16[4,512,768]{2,1,0:T(8,128)(2,1)}, bf16[8,512,768]{2,1,0:T(8,128)(2,1)}, bf16[8,512,1536]{2,1,0:T(8,128)(2,1)}) custom-call(bf16[2048,256]{1,0:T(8,128)(2,1)} %get-tuple-element.61.refs_0_, bf16[2048,128]{1,0:T(8,128)(2,1)} %get-tuple-element.62.refs_1_, ...), custom_call_target="tpu_custom_call" | custom-call | flops 218500005888 | bytes 1024 | tf_op jit(solution)/shard_map/last/pallas_call | solution.py:1431
  693.4 0.0 copy-start.2
  693.4 0.0 copy-start.1
  693.4 0.0 copy-start
  693.4 26.3 %spread.1 = (f32[512,2048]{1,0:T(8,128)}, f32[512,1024]{1,0:T(8,128)}, f32[512,1024]{1,0:T(8,128)}, f32[2048,512]{1,0:T(8,128)}, f32[512,6144]{1,0:T(8,128)}, /*index=5*/f32[512,6144]{1,0:T(8,128)}, f32[6144,512]{1,0:T(8,128)}) custom-call(bf16[8,512,768]{2,1,0:T(8,128)(2,1)} %get-tuple-element.78.head_source, ...), custom_call_target="tpu_custom_call" | custom-call | tf_op jit(solution)/shard_map/spread/pallas_call | solution.py:1516
  719.7 0.0 copy-done.2
  719.7 0.6 fusion
  720.3 0.6 slice_bitcast_fusion
  720.9 0.0 copy-done.1
  720.9 1.0 copy.30
  721.9 0.0 copy-done
  721.9 1.3 copy.31
  (1 shorter events, 0.0 us)
Async XLA Ops:
  693.4 26.4 %copy-start.2 = (f32[16,128]{1,0:T(8,128)S(1)}, f32[16,128]{1,0:T(8,128)}, u32[]{:S(2)}) copy-start(f32[16,128]{1,0:T(8,128)} %get-tuple-element.88) | copy-start | bytes 24580
  693.4 27.5 %copy-start.1 = (bf16[256,2048]{1,0:T(8,128)(2,1)S(1)}, bf16[256,2048]{1,0:T(8,128)(2,1)}, u32[]{:S(2)}) copy-start(bf16[256,2048]{1,0:T(8,128)(2,1)} %get-tuple-element.60) | copy-start | bytes 3145732
  693.4 28.5 %copy-start = (f32[256,2048]{1,0:T(8,128)S(1)}, f32[256,2048]{1,0:T(8,128)}, u32[]{:S(2)}) copy-start(f32[256,2048]{1,0:T(8,128)} %get-tuple-element.77) | copy-start | bytes 6291460
